TPU v7x, 512 devices: a whole 4x8x8 slice. The times are simulated.
512 devices in a mesh: seq: 64 (over z, x, y_lo), tp: 8 (over y_hi, core).
Axes of the slice: x: 4, y: 8 (y_hi: 4, y_lo: 2; y = y_hi * 2 + y_lo), z: 8, core: 2. Of those that a mesh axis runs over, the one named last changes fastest.
Arguments:
- tokens: bfloat16 [16384, 4096], P('seq', 'tp'), may hold values from -6 to 6
- x_weight: bfloat16 [4096, 8192], P('seq', 'tp'), may hold values from -0.09375 to 0.09375
- bc_weight: bfloat16 [4096, 256], P('seq', 'tp'), may hold values from -0.09375 to 0.09375
- dt_weight: bfloat16 [4096, 128], P('seq', 'tp'), may hold values from -0.09375 to 0.09375
- conv_x: float32 [4, 8192], P(None, 'tp'), may hold values from -2.5 to 2.5
- conv_bc: float32 [4, 256], replicated, may hold values from -2.5 to 2.5
- dt_bias: float32 [128], P('tp'), may hold values from -3 to 0
- decay_rate: float32 [128], P('tp'), may hold values from 6.1035155e-07 to 0.07
- d_skip: float32 [128], P('tp'), may hold values from 0.5 to 2
- norm_gain: float32 [8192], P('tp'), may hold values from 0.5 to 1.5
- initial_state: float32 [128, 64, 128], P('tp'), may hold values from -16 to 16
- steer: float32 [8192], P('tp'), may hold values from -6 to 6
Outputs:
- steered: bfloat16 [16384, 8192], P('seq', 'tp')
All inputs are finite; a program needn't handle non-finite values.
Results may differ from a plain program's by a relative error of at most 0.0055.
Values may be sent and summed in bfloat16 or wider, within the bound.
No kernel may reach another device: no remote copies, remote signals or barrier semaphores. Data moves between devices by JAX's collectives and lax.ppermute only.
A program may use at most 64 MiB of HBM per device.

v0:
```python
import jax
import jax.numpy as jnp
from jax import lax
from jax.sharding import PartitionSpec as P

N = 128
GROUP = 128


EPSILON = 1e-05


def passed_along(value, axis, steps):
    count = lax.axis_size(axis)
    first, last = (max(0, -steps), min(count, count - steps))
    return lax.ppermute(value, axis, [(source, source + steps) for source in range(first, last)])


def prefix(x, axis, combine, identity):
    count, mine = (lax.axis_size(axis), lax.axis_index(axis))
    everything = jax.tree.map(
        lambda part, kind: lax.all_gather(part.astype(kind), axis), x, (jnp.bfloat16, jnp.bfloat16)
    )
    start = jax.tree.map(
        lambda part, zero: jnp.broadcast_to(jnp.asarray(zero, part.dtype), part.shape), x, identity
    )

    def turn(k, before):
        reached = k < mine
        new = combine(
            before, jax.tree.map(lambda part, own: part[k].astype(own.dtype), everything, x)
        )
        return jax.tree.map(lambda a, b: jnp.where(reached, a, b), new, before)

    return lax.fori_loop(0, count, turn, start)


def convolve(extended, kernel):
    kernel_rows = kernel.shape[0]
    length = extended.shape[0] - kernel_rows + 1
    summed = kernel[0] * extended[0:length].astype(jnp.float32)
    for offset in range(1, kernel_rows):
        summed = summed + kernel[offset] * extended[offset : offset + length].astype(jnp.float32)
    return jax.nn.silu(summed).astype(jnp.bfloat16)


def block_update(carry_state, inputs):
    x_block, b_block, c_block, a_block, dt_block = inputs
    length = a_block.shape[0]
    cumulative = jnp.cumsum(a_block, axis=0)
    scores = jnp.dot(c_block, b_block.T, preferred_element_type=jnp.float32)
    causal = lax.broadcasted_iota(jnp.int32, (length, length), 0) >= lax.broadcasted_iota(
        jnp.int32, (length, length), 1
    )
    differ = cumulative[:, None, :] - cumulative[None, :, :]
    decays = jnp.where(causal[:, :, None], jnp.exp(jnp.where(causal[:, :, None], differ, 0.0)), 0.0)
    mixing = (scores[:, :, None] * decays * dt_block[None, :, :]).astype(jnp.bfloat16)
    inside = jnp.einsum("tsh,shp->thp", mixing, x_block, preferred_element_type=jnp.float32)
    carried_in = jnp.einsum(
        "tn,hpn->thp", c_block.astype(jnp.float32), carry_state, precision=lax.Precision.HIGHEST
    )
    outputs = inside + jnp.exp(cumulative)[:, :, None] * carried_in
    to_end = jnp.exp(cumulative[-1][None, :] - cumulative) * dt_block
    scaled = (x_block.astype(jnp.float32) * to_end[:, :, None]).astype(jnp.bfloat16)
    added_state = jnp.einsum("shp,sn->hpn", scaled, b_block, preferred_element_type=jnp.float32)
    return (jnp.exp(cumulative[-1])[:, None, None] * carry_state + added_state, outputs)


def combine_carry(earlier, later):
    return (earlier[0] * later[0], later[0][:, None, None] * earlier[1] + later[1])


def per_device(
    tokens,
    x_weight,
    bc_weight,
    dt_weight,
    conv_x,
    conv_bc,
    dt_bias,
    decay_rate,
    d_skip,
    norm_gain,
    initial_state,
    steer,
):
    features = lax.all_gather(tokens, "tp", axis=1, tiled=True)
    rim_rows = conv_x.shape[0] - 1
    local_tokens = features.shape[0]
    head_count = dt_weight.shape[1]
    channels = x_weight.shape[1]
    head_size = channels // head_count
    bc_panel = lax.all_gather(bc_weight, "tp", axis=1, tiled=True)
    x_sums = jnp.dot(
        features,
        lax.all_gather(x_weight, "seq", axis=0, tiled=True),
        preferred_element_type=jnp.float32,
    )
    bc_sums = jnp.dot(
        features,
        lax.all_gather(bc_panel, "seq", axis=0, tiled=True),
        preferred_element_type=jnp.float32,
    )
    dt_sums = jnp.dot(
        features,
        lax.all_gather(dt_weight, "seq", axis=0, tiled=True),
        preferred_element_type=jnp.float32,
    )
    x_pre = x_sums.astype(jnp.bfloat16)
    bc_pre = bc_sums.astype(jnp.bfloat16)
    joined = jnp.concatenate(
        [x_pre[local_tokens - rim_rows :], bc_pre[local_tokens - rim_rows :]], 1
    )
    arrived = passed_along(joined, "seq", 1)
    x_extended = jnp.concatenate([arrived[:, :channels], x_pre], 0)
    bc_extended = jnp.concatenate([arrived[:, channels:], bc_pre], 0)
    x_conv = convolve(x_extended, conv_x)
    bc_conv = convolve(bc_extended, conv_bc)
    b_values = bc_conv[:, :N]
    c_values = bc_conv[:, N:]
    step_size = jax.nn.softplus(dt_sums + dt_bias[None, :])
    log_decay = -step_size * decay_rate[None, :]
    blocks = local_tokens // GROUP
    x_heads = x_conv.reshape(local_tokens, head_count, head_size)
    inputs = (
        x_heads.reshape(blocks, GROUP, head_count, head_size),
        b_values.reshape(blocks, GROUP, N),
        c_values.reshape(blocks, GROUP, N),
        log_decay.reshape(blocks, GROUP, head_count),
        step_size.reshape(blocks, GROUP, head_count),
    )
    zero_state = jnp.zeros((head_count, head_size, N), jnp.float32)
    local_state, local_out = lax.scan(block_update, zero_state, inputs)
    running = jnp.cumsum(log_decay, axis=0)
    local_decay = jnp.exp(running[-1])
    identity = (
        jnp.ones((head_count,), jnp.float32),
        jnp.zeros((head_count, head_size, N), jnp.float32),
    )
    prefix_decay, prefix_state = prefix((local_decay, local_state), "seq", combine_carry, identity)
    entering = prefix_decay[:, None, None] * initial_state + prefix_state
    from_entering = jnp.einsum(
        "tn,hpn->thp", c_values.astype(jnp.float32), entering, precision=lax.Precision.HIGHEST
    )
    outputs = (
        local_out.reshape(local_tokens, head_count, head_size)
        + jnp.exp(running)[:, :, None] * from_entering
        + d_skip[None, :, None] * x_heads.astype(jnp.float32)
    )
    mean_square = jnp.mean(outputs * outputs, axis=-1, keepdims=True)
    normed = (outputs * lax.rsqrt(mean_square + EPSILON)).reshape(
        local_tokens, channels
    ) * norm_gain[None, :]
    partial_dot = jnp.sum(normed * steer[None, :], axis=1)
    total_dot = lax.psum(partial_dot, "tp")
    penalty = total_dot / jnp.sqrt(jnp.float32(channels * lax.axis_size("tp")))
    return (normed - penalty[:, None] * steer[None, :]).astype(jnp.bfloat16)


def solution(mesh):
    placed = (
        P("seq", "tp"),
        P("seq", "tp"),
        P("seq", "tp"),
        P("seq", "tp"),
        P(None, "tp"),
        P(),
        P("tp"),
        P("tp"),
        P("tp"),
        P("tp"),
        P("tp", None, None),
        P("tp"),
    )
    return jax.shard_map(
        per_device, mesh=mesh, in_specs=placed, out_specs=P("seq", "tp"), check_vma=False
    )
```

profile of v0, /device:TPU:1, one launch (start us, length us, event | category | flops | bytes accessed | tf_op | source)
XLA Modules:
  0.0 1208.3 jit_solution(8973249411349206538)
XLA Ops:
  7.3 21.4 %all_gather.28 = bf16[64,256]{0,1:T(8,128)(2,1)S(1)} all-gather(bf16[64,32]{0,1:T(8,128)(2,1)} %param.18), channel_id=1, replica_groups=mesh['seq'=64,'tp'=8] {'tp'}, dimensions={1}, use_global_device_ids=true | all-gather | bytes 36864 | tf_op jit(solution)/shard_map/all_gather | solution.py:93
  30.3 134.9 %all-gather.1 = bf16[64,64,16]{1,2,0:T(8,128)(2,1)S(1)} all-gather(bf16[1,64,16]{1,2,0:T(8,128)(2,1)} %bitcast.146), channel_id=1, replica_groups=mesh['seq'=64,'tp'=8] {'seq'}, dimensions={0}, use_global_device_ids=true | all-gather | bytes 133120 | tf_op jit(solution)/shard_map/all_gather | solution.py:106
  167.3 147.8 %all-gather.12.cloned.1.call-done = bf16[4096,256]{1,0:T(8,128)(2,1)} async-done(((bf16[64,256]{1,0:T(8,128)(2,1)}), bf16[4096,256]{1,0:T(8,128)(2,1)}) %all-gather.12.cloned.1.call-update) | async-done | bytes 2097168 | tf_op jit(solution)/shard_map/all_gather | solution.py:101
  315.1 2.9 convolution_convert_fusion.1
  318.1 328.3 %all-gather.10.cloned.1.call-done = bf16[4096,1024]{1,0:T(8,128)(2,1)} async-done(((bf16[64,1024]{1,0:T(8,128)(2,1)}), bf16[4096,1024]{1,0:T(8,128)(2,1)}) %all-gather.10.cloned.1.call-update) | async-done | bytes 8388624 | tf_op jit(solution)/shard_map/all_gather | solution.py:96
  646.4 5.7 convolution_convert_fusion
  652.2 1.9 collective-permute-start
  657.4 29.9 %while.29 = (s32[]{:T(128)}, f32[16,64,128]{2,1,0:T(8,128)S(1)}, f32[2,128,16,64]{1,0,3,2:T(2,128)}, f32[2,128,16]{2,1,0:T(8,128)S(1)}, bf16[2,128,16,64]{1,3,2,...) while((s32[]{:T(128)}, f32[16,64,128]{2,1,0:T(8,128)S(1)}, ...), condition=%wide.region_2.3_spmd.clone, body=%wide.region_0.2_spmd.clone.sunk | while | flops 275662848 | bytes 5196752 | solution.py:133
  659.0 13.0 %dynamic_update_slice.6 = f32[2,128,16,64]{1,0,3,2:T(2,128)} dynamic-update-slice(f32[2,128,16,64]{1,0,3,2:T(2,128)} %get-tuple-element.433, f32[1,128,16,64]{1,0,3,2:T(1,128)S(1)} %bitcast.133, s32[]{:T(128)} %get-tuple-element.431, s32[]{:T(128)} %constant.65.clone.1..sunk, s32[]{:T(128)} %constant.65.clone.1..sunk, s32[]{:T(128)} %constant.65.clone.1..sunk) | dynamic-update-slice | bytes 1048580 | tf_op jit(solution)/shard_map/while/body/jit(dynamic_update_index_in_dim)/dynamic_update_slice | solution.py:133
  674.0 13.0 %dynamic_update_slice.6 = f32[2,128,16,64]{1,0,3,2:T(2,128)} dynamic-update-slice(f32[2,128,16,64]{1,0,3,2:T(2,128)} %get-tuple-element.433, f32[1,128,16,64]{1,0,3,2:T(1,128)S(1)} %bitcast.133, s32[]{:T(128)} %get-tuple-element.431, s32[]{:T(128)} %constant.65.clone.1..sunk, s32[]{:T(128)} %constant.65.clone.1..sunk, s32[]{:T(128)} %constant.65.clone.1..sunk) | dynamic-update-slice | bytes 1048580 | tf_op jit(solution)/shard_map/while/body/jit(dynamic_update_index_in_dim)/dynamic_update_slice | solution.py:133
  689.4 133.3 %all-gather.2 = bf16[64,1,16]{2,1,0:T(2,128)(2,1)S(1)} all-gather(bf16[1,1,16]{2,1,0:T(2,128)(2,1)S(1)} %bitcast.151), channel_id=1, replica_groups=mesh['seq'=64,'tp'=8] {'seq'}, dimensions={0}, use_global_device_ids=true | all-gather | bytes 2080 | tf_op jit(solution)/shard_map/all_gather | solution.py:22
  823.0 2.1 reshape.112
  825.1 286.8 %all-gather.14.cloned.1.call-done = bf16[1024,64,128]{2,1,0:T(8,128)(2,1)} async-done(((bf16[16,64,128]{2,1,0:T(8,128)(2,1)}), bf16[1024,64,128]{2,1,0:T(8,128)(2,1)}) %all-gather.14.cloned.1.call-update) | async-done | bytes 16777232 | tf_op jit(solution)/shard_map/all_gather | solution.py:22
  1111.9 73.0 %while.30 = (s32[]{:T(128)}, f32[16]{0:T(128)S(1)}, f32[16,64,128]{2,1,0:T(8,128)S(1)}, s32[]{:T(128)}, bf16[64,16]{1,0:T(8,128)(2,1)S(1)}, /*index=5*/bf16[64,16,64,128]{3,2,1,0:T(8,128)(2,1)}, s32[]{:T(128)}, s32[]{:T(128)}) while((s32[]{:T(128)}, f32[16]{0:T(128)S(1)}, f32[16,64,128]{2,1,0:T(8,128)S(1)}, s32[]{:T(128)}, ...), condition=%wide.region_6.7_spmd.clone, body=%wide.region_5.6_spmd.clone.sunk | while | flops 655428 | bytes 1311123 | solution.py:35
  1111.9 1.1 fusion.85
  1113.1 1.1 fusion.85
  1114.2 1.1 fusion.85
  1115.4 1.1 fusion.85
  1116.5 1.1 fusion.85
  1117.7 1.1 fusion.85
  1118.8 1.1 fusion.85
  1119.9 1.1 fusion.85
  1121.1 1.1 fusion.85
  1122.2 1.1 fusion.85
  1123.4 1.1 fusion.85
  1124.5 1.1 fusion.85
  1125.6 1.1 fusion.85
  1126.8 1.1 fusion.85
  1127.9 1.1 fusion.85
  1129.1 1.1 fusion.85
  1130.2 1.1 fusion.85
  1131.3 1.1 fusion.85
  1132.5 1.1 fusion.85
  1133.6 1.1 fusion.85
  1134.8 1.1 fusion.85
  1135.9 1.1 fusion.85
  1137.0 1.1 fusion.85
  1138.2 1.1 fusion.85
  1139.3 1.1 fusion.85
  1140.4 1.1 fusion.85
  1141.6 1.1 fusion.85
  1142.7 1.1 fusion.85
  1143.9 1.1 fusion.85
  1145.0 1.1 fusion.85
  1146.1 1.1 fusion.85
  1148.4 1.1 fusion.85
  1151.8 1.1 fusion.85
  1153.0 1.1 fusion.85
  1155.3 1.1 fusion.85
  1156.4 1.1 fusion.85
  1158.7 1.1 fusion.85
  1159.8 1.1 fusion.85
  1162.1 1.1 fusion.85
  1163.2 1.1 fusion.85
  1166.7 1.1 fusion.85
  1170.1 1.1 fusion.85
  1173.5 1.1 fusion.85
  1174.6 1.1 fusion.85
  1176.9 1.1 fusion.85
  1178.0 1.1 fusion.85
  1180.3 1.1 fusion.85
  1181.5 1.1 fusion.85
  1183.7 1.1 fusion.85
  1186.3 14.5 %psum.7 = f32[256]{0:T(256)S(1)} all-reduce(f32[256]{0:T(256)S(1)} %get-tuple-element.306), channel_id=1, replica_groups=mesh['seq'=64,'tp'=8] {'tp'}, use_global_device_ids=true, to_apply=%region_9.10 | all-reduce | flops 256 | bytes 2048 | tf_op jit(solution)/shard_map/psum | solution.py:155
  (172 shorter events, 33.7 us)
Async XLA Ops:
  6.5 160.7 %all-gather.8.cloned.1.call-start = ((), (), s32[]{:S(2)}) async-start(), calls=%async_computation | async-start | bytes 2359296 | tf_op jit(solution)/shard_map/all_gather | solution.py:87
  7.3 307.9 %all-gather.12.cloned.1.call-start = ((), (), s32[]{:S(2)}) async-start(), calls=%async_computation.2 | async-start | bytes 2129920 | tf_op jit(solution)/shard_map/all_gather | solution.py:101
  29.5 616.9 %all-gather.10.cloned.1.call-start = ((), (), s32[]{:S(2)}) async-start(), calls=%async_computation.1 | async-start | bytes 8519680 | tf_op jit(solution)/shard_map/all_gather | solution.py:96
  30.2 1081.7 %all-gather.14.cloned.1.call-start = ((), (), s32[]{:S(2)}) async-start(), calls=%async_computation.3 | async-start | bytes 17039360 | tf_op jit(solution)/shard_map/all_gather | solution.py:22
  167.3 479.1 %copy-start = (bf16[256,4096]{1,0:T(8,128)(2,1)S(1)}, bf16[256,4096]{1,0:T(8,128)(2,1)}, u32[]{:S(2)}) copy-start(bf16[256,4096]{1,0:T(8,128)(2,1)} %all-gather.8.cloned.1.call-done) | copy-start | bytes 6291460
  318.1 336.0 %copy-start.4 = (f32[16]{0:T(128)S(1)}, f32[16]{0:T(128)}, u32[]{:S(2)}) copy-start(f32[16]{0:T(128)} %param.23) | copy-start | bytes 196
  318.1 336.0 %copy-start.6 = (f32[16]{0:T(128)S(1)}, f32[16]{0:T(128)}, u32[]{:S(2)}) copy-start(f32[16]{0:T(128)} %param.22) | copy-start | bytes 196
  652.2 2.8 collective-permute-start
  657.4 30.8 %copy-start.3 = (f32[1024]{0:T(1024)S(1)}, f32[1024]{0:T(1024)}, u32[]{:S(2)}) copy-start(f32[1024]{0:T(1024)} %param.25) | copy-start | bytes 12292
  657.4 30.8 %copy-start.2 = (f32[1024]{0:T(1024)S(1)}, f32[1024]{0:T(1024)}, u32[]{:S(2)}) copy-start(f32[1024]{0:T(1024)} %param.27) | copy-start | bytes 12292
  1111.9 73.0 %copy-start.1 = (f32[16,64,128]{2,1,0:T(8,128)S(1)}, f32[16,64,128]{2,1,0:T(8,128)}, u32[]{:S(2)}) copy-start(f32[16,64,128]{2,1,0:T(8,128)} %param.26) | copy-start | bytes 1572868
  1111.9 73.0 %copy-start.5 = (f32[16]{0:T(128)S(1)}, f32[16]{0:T(128)}, u32[]{:S(2)}) copy-start(f32[16]{0:T(128)} %param.24) | copy-start | bytes 196
Sparse Core Ops, SparseCore 0:
  9.5 44.7 all-gather.7
  56.3 258.7 all-gather.11
  317.2 329.1 all-gather.9
  688.3 423.5 all-gather.13
where the time goes:
time: 1210 us
  waiting for transfers between devices  764 us (63%)
  blocking collectives  304 us (25%)
  other arithmetic  75.7 us (6%)
  local copies, waits for them, and re-layouts  34.1 us (3%)
  between operations  13.4 us (1%)
  matrix products  12.8 us (1%)
    all_gather x1, waiting for transfers between devices, per_device(): lax.all_gather(x_weight, 'seq', axis=0, tiled=True)  328 us
    all_gather x1, waiting for transfers between devices, prefix(): lax.all_gather(part.astype(kind), axis)  287 us
    all_gather x1, waiting for transfers between devices, per_device(): lax.all_gather(bc_panel, 'seq', axis=0, tiled=True)  148 us
    all_gather x1, blocking collectives, per_device(): lax.all_gather(dt_weight, 'seq', axis=0, tiled=True)  135 us
    all_gather x1, blocking collectives, prefix(): lax.all_gather(part.astype(kind), axis)  133 us
    select_n x128, other arithmetic, turn(): return jax.tree.map(lambda a, b: jnp.where(reached, a, b), new, before)  71.3 us
    dynamic_update_slice x2, local copies, waits for them, and re-layouts, per_device(): local_state, local_out = lax.scan(block_update, zero_state, inputs)  26.1 us
  transfers between devices with their start and end apart: 5, of which 3 were waited for; matrix products, arithmetic and copies ran while one was open for 1% of the time, Pallas kernels for 0%

commit v1 on v0

v1 whole, which is shorter than its diff:
```python
import functools
import math

import jax
import jax.numpy as jnp
from jax import lax
from jax.experimental import pallas as pl
from jax.experimental.pallas import tpu as pltpu
from jax.sharding import Mesh, PartitionSpec as P

EPSILON = 1e-05
GROUP = 128
N = 128
HALO = 16
HEAD = 64
HIGHEST = lax.Precision.HIGHEST

SEQ = ("z", "x", "yl")
TP = ("yh", "c")
SIZES = {"z": 8, "x": 4, "yl": 2, "yh": 4, "c": 2}


def call(kernel, outs, *args, flops=0, bytes_accessed=0, smem=()):
    specs = [
        pl.BlockSpec(memory_space=pltpu.SMEM if at in smem else pltpu.VMEM)
        for at in range(len(args))
    ]
    return pl.pallas_call(
        kernel,
        out_shape=outs,
        in_specs=specs,
        out_specs=jax.tree.map(lambda _: pl.BlockSpec(memory_space=pltpu.VMEM), outs),
        compiler_params=pltpu.CompilerParams(vmem_limit_bytes=48 * 1024 * 1024),
        cost_estimate=pl.CostEstimate(
            flops=flops, bytes_accessed=bytes_accessed, transcendentals=0
        ),
    )(*args)


def dot(a, b, dims, precision=None):
    return lax.dot_general(
        a, b, (dims, ((), ())), precision=precision, preferred_element_type=jnp.float32
    )


def expander(heads, channels):
    row = lax.broadcasted_iota(jnp.int32, (heads, channels), 0)
    column = lax.broadcasted_iota(jnp.int32, (heads, channels), 1)
    return jnp.where(column // (channels // heads) == row, 1.0, 0.0)


def project_kernel(mine_ref, feats_ref, w_ref, keep_ref, send_ref, bc_ref, dt_ref, acc, bc_acc, dt_acc):
    step = pl.program_id(0)
    mine = mine_ref[0]
    channels = keep_ref.shape[1]
    bc_rows = bc_ref.shape[0]

    @pl.when(step == 0)
    def _():
        acc[...] = jnp.zeros_like(acc)
        bc_acc[...] = jnp.zeros_like(bc_acc)
        dt_acc[...] = jnp.zeros_like(dt_acc)

    weights = w_ref[0, 0:channels, :]
    for half in range(2):
        acc[half] += dot(feats_ref[0, half, 0], weights, ((1,), (0,)))
    own = feats_ref[0, mine, 0]
    bc_acc[...] += dot(w_ref[0, channels : channels + bc_rows, :], own, ((1,), (1,)))
    dt_acc[...] += dot(w_ref[0, channels + bc_rows :, :], own[HALO:], ((1,), (1,)))

    @pl.when(step == pl.num_programs(0) - 1)
    def _():
        keep_ref[...] = acc[mine].astype(jnp.bfloat16)
        send_ref[...] = acc[1 - mine].astype(jnp.bfloat16)
        bc_ref[...] = bc_acc[...].astype(jnp.bfloat16)
        dt_ref[...] = dt_acc[...]


def project(mine, feats, weights, bc_rows, dt_rows):
    _, _, _, rows, depth = feats.shape
    blocks, height, channels = weights.shape
    tokens = rows - HALO
    return pl.pallas_call(
        project_kernel,
        grid_spec=pltpu.PrefetchScalarGridSpec(
            num_scalar_prefetch=1,
            grid=(blocks,),
            in_specs=[
                pl.BlockSpec((1, 2, 1, rows, depth), lambda j, m: (j // 2, 0, j % 2, 0, 0)),
                pl.BlockSpec((1, height, channels), lambda j, m: (j, 0, 0)),
            ],
            out_specs=[
                pl.BlockSpec((rows, channels), lambda j, m: (0, 0)),
                pl.BlockSpec((rows, channels), lambda j, m: (0, 0)),
                pl.BlockSpec((bc_rows, rows), lambda j, m: (0, 0)),
                pl.BlockSpec((dt_rows, tokens), lambda j, m: (0, 0)),
            ],
            scratch_shapes=[
                pltpu.VMEM((2, rows, channels), jnp.float32),
                pltpu.VMEM((bc_rows, rows), jnp.float32),
                pltpu.VMEM((dt_rows, tokens), jnp.float32),
            ],
        ),
        out_shape=[
            jax.ShapeDtypeStruct((rows, channels), jnp.bfloat16),
            jax.ShapeDtypeStruct((rows, channels), jnp.bfloat16),
            jax.ShapeDtypeStruct((bc_rows, rows), jnp.bfloat16),
            jax.ShapeDtypeStruct((dt_rows, tokens), jnp.float32),
        ],
        compiler_params=pltpu.CompilerParams(vmem_limit_bytes=48 * 1024 * 1024),
    )(mine, feats, weights)


def convolved(values, taps, tokens):
    summed = taps[0:1] * values[HALO - 3 : HALO - 3 + tokens]
    for k in range(1, 4):
        summed = summed + taps[k : k + 1] * values[HALO - 3 + k : HALO - 3 + k + tokens]
    return (summed / (1.0 + jnp.exp(-summed))).astype(jnp.bfloat16)


def state_kernel(
    mine_ref, keep_ref, got_ref, bc_ref, dt_ref, conv_x_ref, conv_bc_ref, bias_ref, rate_ref,
    x_ref, bconv_ref, cum_ref, step_ref, pay_ref, added_ref,
):
    mine = mine_ref[0]
    tokens, channels = x_ref.shape
    half = channels // 2
    heads = dt_ref.shape[0]
    for lane in range(0, channels, 128):
        at = lane % half
        own, got = keep_ref[:, at : at + 128], got_ref[:, at : at + 128]
        values = jnp.where(mine == lane // half, own, got).astype(jnp.float32)
        x_ref[:, lane : lane + 128] = convolved(values, conv_x_ref[:, lane : lane + 128], tokens)
    for lane in range(0, 2 * N, 128):
        values = bc_ref[:, lane : lane + 128].astype(jnp.float32)
        bconv_ref[:, lane : lane + 128] = convolved(
            values, conv_bc_ref[:, lane : lane + 128], tokens
        )
    raw = dt_ref[...] + bias_ref[...]
    step_size = jnp.maximum(raw, 0.0) + jnp.log1p(jnp.exp(-jnp.abs(raw)))
    log_decay = -step_size * rate_ref[...]
    step_ref[...] = step_size
    upper = jnp.where(
        lax.broadcasted_iota(jnp.int32, (GROUP, GROUP), 0)
        <= lax.broadcasted_iota(jnp.int32, (GROUP, GROUP), 1),
        1.0,
        0.0,
    )
    spread = expander(heads, channels)
    ends = []
    for block in range(tokens // GROUP):
        at = slice(block * GROUP, (block + 1) * GROUP)
        cumulative = dot(log_decay[:, at], upper, ((1,), (0,)), HIGHEST)
        cum_ref[:, at] = cumulative
        end = cumulative[:, GROUP - 1 : GROUP]
        to_end = jnp.exp(end - cumulative) * step_size[:, at]
        wide = dot(to_end.T, spread, ((1,), (0,)), HIGHEST)
        scaled = (x_ref[at, :].astype(jnp.float32) * wide).astype(jnp.bfloat16)
        added_ref[block] = dot(scaled, bconv_ref[at, 0:N], ((0,), (0,)))
        ends.append(end)
    second = jnp.exp(ends[1])
    total = jnp.exp(ends[0] + ends[1])
    high = total.astype(jnp.bfloat16).astype(jnp.float32)
    low = total - high
    share = pay_ref.shape[0] // heads
    row = lax.broadcasted_iota(jnp.int32, (16, N), 0)
    for head in range(heads):
        at = slice(head * HEAD, (head + 1) * HEAD)
        state = added_ref[0, at] * second[head : head + 1] + added_ref[1, at]
        tail = jnp.where(
            row == 0, high[head : head + 1], jnp.where(row == 1, low[head : head + 1], 0.0)
        ).astype(jnp.bfloat16)
        for part in range(share):
            pay_ref[head * share + part, 0:16] = state[part * 16 : (part + 1) * 16].astype(
                jnp.bfloat16
            )
            pay_ref[head * share + part, 16:32] = tail


def prefix_kernel(got_ref, start_ref, out_ref):
    running = start_ref[...]
    for source in range(got_ref.shape[0]):
        out_ref[source] = running.astype(jnp.bfloat16)
        tail = got_ref[source, 16:32].astype(jnp.float32)
        running = (tail[0:1] + tail[1:2]) * running + got_ref[source, 0:16].astype(jnp.float32)


def inside_kernel(x_ref, bc_ref, cum_ref, step_ref, out_ref):
    tokens, channels = x_ref.shape
    heads = cum_ref.shape[0]
    causal = lax.broadcasted_iota(jnp.int32, (GROUP, GROUP), 0) >= lax.broadcasted_iota(
        jnp.int32, (GROUP, GROUP), 1
    )
    for block in range(tokens // GROUP):
        at = slice(block * GROUP, (block + 1) * GROUP)
        scores = dot(bc_ref[at, N:], bc_ref[at, 0:N], ((1,), (1,)))
        cumulative = cum_ref[:, at]
        columns = cumulative.T
        for pair in range(0, heads, 2):
            parts = []
            for head in (pair, pair + 1):
                differ = columns[:, head : head + 1] - cumulative[head : head + 1]
                decays = jnp.exp(jnp.where(causal, differ, -1e30))
                mixing = (scores * decays * step_ref[head : head + 1, at]).astype(jnp.bfloat16)
                parts.append(
                    dot(mixing, x_ref[at, head * HEAD : (head + 1) * HEAD], ((1,), (0,)))
                )
            out_ref[at, pair * HEAD : (pair + 2) * HEAD] = jnp.concatenate(parts, 1)


def output_kernel(
    inside_ref, x_ref, bc_ref, cum_ref, entering_ref, added_ref, skip_ref, gain_ref, steer_ref,
    normed_ref, dot_ref, state_ref,
):
    tokens, channels = x_ref.shape
    heads = cum_ref.shape[0]
    spread = expander(heads, channels)
    end = jnp.exp(cum_ref[:, GROUP - 1 : GROUP])
    state_ref[0] = entering_ref[...].astype(jnp.float32)
    for head in range(heads):
        at = slice(head * HEAD, (head + 1) * HEAD)
        state_ref[1, at] = state_ref[0, at] * end[head : head + 1] + added_ref[at]
    for block in range(tokens // GROUP):
        at = slice(block * GROUP, (block + 1) * GROUP)
        carried = dot(
            bc_ref[at, N:].astype(jnp.float32), state_ref[block], ((1,), (1,)), HIGHEST
        )
        growth = dot(jnp.exp(cum_ref[:, at]).T, spread, ((1,), (0,)), HIGHEST)
        y = inside_ref[at] + growth * carried + skip_ref[...] * x_ref[at].astype(jnp.float32)
        squares = dot(y * y, spread, ((1,), (1,)), HIGHEST) * (1.0 / HEAD)
        scale = dot(lax.rsqrt(squares + EPSILON), spread, ((1,), (0,)), HIGHEST)
        normed = y * scale * gain_ref[...]
        normed_ref[at] = normed
        dot_ref[:, at] = dot(steer_ref[...], normed, ((1,), (1,)), HIGHEST)


def steer_kernel(factor, normed_ref, dots_ref, steer_ref, out_ref):
    for lane in range(0, normed_ref.shape[1], 256):
        at = slice(lane, lane + 256)
        penalty = dot(dots_ref[...], steer_ref[:, at], ((0,), (0,)), HIGHEST)
        out_ref[:, at] = (normed_ref[:, at] - penalty * factor).astype(jnp.bfloat16)


def per_device(
    tokens, x_weight, bc_weight, dt_weight, conv_x, conv_bc, dt_bias, decay_rate, d_skip,
    norm_gain, initial_state, steer,
):
    local, width = tokens.shape
    k_rows, channels = x_weight.shape
    half = channels // 2
    heads = dt_weight.shape[1]
    bc_rows = bc_weight.shape[1]
    small = bc_rows + heads
    seq_count = SIZES["z"] * SIZES["x"] * SIZES["yl"]
    tp_count = SIZES["yh"] * SIZES["c"]
    mine = lax.axis_index("yl").astype(jnp.int32).reshape(1)

    earlier = lax.ppermute(
        tokens[local - HALO :], SEQ, [(i, i + 1) for i in range(seq_count - 1)]
    )
    extended = jnp.concatenate([earlier, tokens], 0)
    feats = lax.all_gather(extended, ("yh", "yl", "c"), axis=0, tiled=False)
    feats = feats.reshape(SIZES["yh"], 2, SIZES["c"], local + HALO, width)

    fan = SIZES["x"] * SIZES["yl"]
    packed_rows = small * k_rows // half
    packed = jnp.concatenate([bc_weight, dt_weight], 1).T.reshape(packed_rows, half)
    panel = jnp.concatenate(
        [
            x_weight.reshape(k_rows, 2, half).transpose(1, 0, 2),
            jnp.broadcast_to(packed[None], (2, packed_rows, half)),
            jnp.zeros((2, -packed_rows % 8, half), jnp.bfloat16),
        ],
        1,
    )
    panel = jnp.broadcast_to(panel[None], (SIZES["x"],) + panel.shape).reshape(
        fan, panel.shape[1], half
    )
    got = lax.all_to_all(panel, ("x", "yl"), 0, 0)
    tall = got[:, :k_rows].reshape(fan * k_rows, half)
    flat = got[:, k_rows : k_rows + packed_rows].reshape(
        fan, packed_rows, half // k_rows, k_rows
    )
    flat = flat.transpose(1, 2, 0, 3).reshape(small, fan * k_rows)
    block = jnp.concatenate([tall, flat], 0)
    weights = lax.all_gather(block, "z", axis=0, tiled=False)

    keep, send, bc_pre, dt_raw = project(mine, feats, weights, bc_rows, heads)
    other = lax.ppermute(send, "yl", [(0, 1), (1, 0)])
    bc_all = lax.all_to_all(jnp.broadcast_to(bc_pre[None], (tp_count,) + bc_pre.shape), TP, 0, 0)
    bc_all = bc_all.reshape(tp_count * bc_rows, local + HALO).T

    f32, bf16 = jnp.float32, jnp.bfloat16
    x_conv, bc_conv, cumulative, step_size, payload, added = call(
        state_kernel,
        [
            jax.ShapeDtypeStruct((local, channels), bf16),
            jax.ShapeDtypeStruct((local, 2 * N), bf16),
            jax.ShapeDtypeStruct((heads, local), f32),
            jax.ShapeDtypeStruct((heads, local), f32),
            jax.ShapeDtypeStruct((seq_count, 32, N), bf16),
            jax.ShapeDtypeStruct((local // GROUP, channels, N), f32),
        ],
        mine, keep, other, bc_all, dt_raw, conv_x, conv_bc, dt_bias[:, None], decay_rate[:, None],
        smem=(0,),
    )
    states = lax.all_to_all(payload, SEQ, 0, 0)
    share = channels // seq_count
    start = lax.dynamic_slice_in_dim(
        initial_state.reshape(channels, N), lax.axis_index(SEQ) * share, share, 0
    )
    pieces = call(prefix_kernel, jax.ShapeDtypeStruct((seq_count, share, N), bf16), states, start)
    entering = lax.all_to_all(pieces, SEQ, 0, 0).reshape(channels, N)

    inside = call(
        inside_kernel,
        jax.ShapeDtypeStruct((local, channels), f32),
        x_conv, bc_conv, cumulative, step_size,
        flops=2 * heads * local * GROUP * HEAD, bytes_accessed=4 * local * channels,
    )
    normed, dots, _ = call(
        output_kernel,
        [
            jax.ShapeDtypeStruct((local, channels), f32),
            jax.ShapeDtypeStruct((1, local), f32),
            jax.ShapeDtypeStruct((2, channels, N), f32),
        ],
        inside, x_conv, bc_conv, cumulative, entering, added[0],
        jnp.repeat(d_skip, HEAD)[None], norm_gain[None], steer[None],
    )
    partials = lax.all_to_all(jnp.broadcast_to(dots[None], (tp_count, 1, local)), TP, 0, 0)
    factor = 1.0 / math.sqrt(channels * tp_count)
    return call(
        functools.partial(steer_kernel, factor),
        jax.ShapeDtypeStruct((local, channels), bf16),
        normed, partials.reshape(tp_count, local),
        jnp.broadcast_to(steer[None], (tp_count, channels)),
    )


def solution(mesh):
    fine = Mesh(mesh.devices.reshape(tuple(SIZES.values())), tuple(SIZES))
    both = P(SEQ, TP)
    placed = (
        both, both, both, both, P(None, TP), P(), P(TP), P(TP), P(TP), P(TP),
        P(TP, None, None), P(TP),
    )
    return jax.shard_map(
        per_device, mesh=fine, in_specs=placed, out_specs=both, check_vma=False
    )
```

time: 1210 us -> 237 us (0.20)
  waiting for transfers between devices: 764 us -> 131 us
  blocking collectives: 304 us -> 26.6 us
  other arithmetic: 75.7 us -> 3.47 us
  starting transfers between devices: 1.98 us -> 30.2 us
  local copies, waits for them, and re-layouts: 34.1 us -> 7.86 us
  Pallas kernels: 0 us -> 23.7 us
  matrix products: 12.8 us -> 0 us
    all_gather x4 -> x2, waiting for transfers between devices: 763 us -> 99.5 us  [the longest x1 62.8 us: per_device(): weights = lax.all_gather(block, 'z', axis=0, tiled=False)]
    all_gather x3 -> x0, blocking collectives: 290 us -> none  [the longest x1 135 us: per_device(): lax.all_gather(dt_weight, 'seq', axis=0, tiled=True)]
    select_n x128 -> x0, other arithmetic: 71.3 us -> none  [turn(): return jax.tree.map(lambda a, b: jnp.where(reached, a, b), new, before)]
    all_to_all x0 -> x3, waiting for transfers between devices: none -> 30.3 us  [the longest x1 15.9 us: per_device(): states = lax.all_to_all(payload, SEQ, 0, 0)]
    all_to_all x0 -> x2, blocking collectives: none -> 26.6 us  [the longest x1 13.4 us: per_device(): lax.all_to_all(jnp.broadcast_to(dots[None], (tp_count, 1, local)), TP, 0, 0)]
    dynamic_update_slice x2 -> x0, local copies, waits for them, and re-layouts: 26.1 us -> none  [per_device(): local_state, local_out = lax.scan(block_update, zero_state, inputs)]
    pallas_call x0 -> x6, Pallas kernels: none -> 23.7 us  [the longest x5 16 us: call(): pl.pallas_call(kernel, out_shape=outs, in_specs=specs, out_specs=jax.tree...]
    all_to_all x0 -> x3, starting transfers between devices: none -> 23 us  [the longest x1 8.74 us: per_device(): states = lax.all_to_all(payload, SEQ, 0, 0)]
  transfers between devices with their start and end apart: 5 -> 7, of which waited for: 3 -> 6; matrix products, arithmetic and copies ran while one was open for 1% -> 2% of each run, Pallas kernels for 0% -> 1%
where the time goes in v1:
time: 237 us; the launch traced here: 236 us
  waiting for transfers between devices  131 us (55%)
  starting transfers between devices  30.2 us (13%)
  blocking collectives  26.6 us (11%)
  Pallas kernels  23.7 us (10%)
  between operations  13.6 us (6%)
  local copies, waits for them, and re-layouts  7.86 us (3%)
  other arithmetic  3.47 us (1%)
    all_gather x1, waiting for transfers between devices, per_device(): weights = lax.all_gather(block, 'z', axis=0, tiled=False)  62.8 us
    all_gather x1, waiting for transfers between devices, per_device(): feats = lax.all_gather(extended, ('yh', 'yl', 'c'), axis=0, tiled=False)  36.7 us
    pallas_call x5, Pallas kernels, call(): pl.pallas_call(kernel, out_shape=outs, in_specs=specs, out_specs=jax.tree...  16 us
    all_to_all x1, waiting for transfers between devices, per_device(): states = lax.all_to_all(payload, SEQ, 0, 0)  15.9 us
    all_to_all x1, blocking collectives, per_device(): lax.all_to_all(jnp.broadcast_to(dots[None], (tp_count, 1, local)), TP, 0, 0)  13.4 us
    all_to_all x1, blocking collectives, per_device(): got = lax.all_to_all(panel, ('x', 'yl'), 0, 0)  13.3 us
    all_to_all x1, waiting for transfers between devices, per_device(): lax.all_to_all(jnp.broadcast_to(bc_pre[None], (tp_count,) + bc_pre.shape)...  8.83 us
    all_to_all x1, starting transfers between devices, per_device(): states = lax.all_to_all(payload, SEQ, 0, 0)  8.74 us
  transfers between devices with their start and end apart: 7, of which 6 were waited for; matrix products, arithmetic and copies ran while one was open for 2% of the time, Pallas kernels for 1%

profile of v1, /device:TPU:1, one launch (start us, length us, event | category | flops | bytes accessed | tf_op | source)
XLA Modules:
  0.0 236.1 jit_solution(10348565744659837140)
XLA Ops:
  6.5 0.0 copy-start
  6.5 0.0 all-gather.5.cloned.1.call-start
  6.5 0.8 slice.12
  7.3 4.0 %collective-permute-start = (bf16[16,512]{1,0:T(8,128)(2,1)S(1)}, bf16[16,512]{1,0:T(8,128)(2,1)S(1)}, u32[]{:S(2)}, u32[]{:S(2)}) collective-permute-start(bf16[16,512]{1,0:T(8,128)(2,1)S(1)} %slice.12), channel_id=1, source_target_pairs={{0,8},{8,16},{16,24},{24,32},{32,40},{40,48},{48,56},{56,64},{64,7... | collective-permute-start | bytes 49160 | tf_op jit(solution)/shard_map/ppermute | solution.py:258
  11.3 0.9 collective-permute-done
  12.2 1.7 pad_maximum_fusion.1
  13.9 0.0 all-gather.5.cloned.1.call-update
  13.9 0.0 all-gather.7.cloned.1.call-start
  13.9 1.0 reshape.42
  14.9 0.7 maximum_bitcast_fusion
  15.7 0.1 broadcast_in_dim.51
  15.8 0.1 pad.4.clone
  15.8 0.2 maximum_maximum_fusion
  16.2 13.3 %all_to_all.25 = bf16[8,72,512]{2,1,0:T(8,128)(2,1)S(1)} all-to-all(bf16[8,72,512]{2,1,0:T(8,128)(2,1)S(1)} %bitcast.36), channel_id=1, replica_groups=mesh['z'=8,'x'=4,'yl'=2,'yh'=4,'c'=2] {'x','yl'}, dimensions={0} | all-to-all | bytes 1179648 | tf_op jit(solution)/shard_map/all_to_all | solution.py:279
  29.5 0.1 reshape.45
  29.6 0.1 reshape.46
  29.8 0.8 pad_maximum_fusion
  30.6 0.0 all-gather.7.cloned.1.call-update
  30.6 36.7 %all-gather.5.cloned.1.call-done = bf16[4352,512]{1,0:T(8,128)(2,1)} async-done(((bf16[272,512]{1,0:T(8,128)(2,1)}), bf16[4352,512]{1,0:T(8,128)(2,1)}) %all-gather.5.cloned.1.call-update) | async-done | bytes 4456464 | tf_op jit(solution)/shard_map/all_gather | solution.py:262
  67.4 62.8 %all-gather.7.cloned.1.call-done = bf16[4480,512]{1,0:T(8,128)(2,1)} async-done(((bf16[560,512]{1,0:T(8,128)(2,1)}), bf16[4480,512]{1,0:T(8,128)(2,1)}) %all-gather.7.cloned.1.call-update) | async-done | bytes 4587536 | tf_op jit(solution)/shard_map/all_gather | solution.py:286
  130.1 0.0 copy-start.1
  130.1 2.3 copy-done.1
  132.4 0.0 copy-start.7
  132.4 0.0 copy-start.8
  132.4 0.0 copy-start.4
  132.4 0.0 copy-start.5
  132.4 7.6 %shard_map.118 = (bf16[272,512]{1,0:T(8,128)(2,1)S(1)}, bf16[272,512]{1,0:T(8,128)(2,1)S(1)}, bf16[32,272]{1,0:T(8,128)(2,1)S(1)}, f32[16,256]{1,0:T(8,128)S(1)}) custom-call(s32[1]{0:T(128)} %bitcast.mine_ref, bf16[4,2,2,272,512]{4,3,2,1,0:T(8,128)(2,1)S(1)} %bitcast.28, bf16[8,560,512]{2,1,0:T(8,128)(2,1)} %bitcast.35), custom_call_target="tpu_custom_call" | custom-call | tf_op jit(solution)/shard_map/pallas_call | solution.py:83
  140.1 3.1 %collective-permute-start.1 = (bf16[272,512]{1,0:T(8,128)(2,1)S(1)}, bf16[272,512]{1,0:T(8,128)(2,1)S(1)}, u32[]{:S(2)}, u32[]{:S(2)}) collective-permute-start(bf16[272,512]{1,0:T(8,128)(2,1)S(1)} %get-tuple-element.18), channel_id=1, source_target_pairs={{0,8},{8,0},{1,9},{9,1},{2,10},{10,2},{3,11},{11,3},{4,12},{12,4},... | collective-permute-start | bytes 835592 | tf_op jit(solution)/shard_map/ppermute | solution.py:289
  143.2 0.7 broadcast_in_dim.55
  143.9 6.8 %all-to-all-start.1 = ((bf16[8,32,272]{2,1,0:T(8,128)(2,1)}), bf16[8,32,272]{2,1,0:T(8,128)(2,1)S(1)}, u32[]{:S(2)}, u32[]{:S(2)}) async-start(bf16[8,32,272]{2,1,0:T(8,128)(2,1)} %broadcast_in_dim.55), calls=%async_computation.1 | async-start | bytes 393216 | tf_op jit(solution)/shard_map/all_to_all | solution.py:290
  150.7 0.0 copy-done.7
  150.7 0.1 copy.30.bias_ref
  150.8 0.0 copy-done.8
  150.8 0.1 copy.31.rate_ref
  150.9 8.8 %all-to-all-done.1 = bf16[8,32,272]{2,1,0:T(8,128)(2,1)S(1)} async-done(((bf16[8,32,272]{2,1,0:T(8,128)(2,1)}), bf16[8,32,272]{2,1,0:T(8,128)(2,1)S(1)}, u32[]{:S(2)}, u32[]{:S(2)}) %all-to-all-start.1) | async-done | bytes 139296 | tf_op jit(solution)/shard_map/all_to_all | solution.py:290
  159.7 0.1 copy.29
  159.8 0.0 collective-permute-done.1.got_ref
  159.8 0.0 copy-done.4
  159.8 0.0 copy-done.5
  159.8 3.8 %shard_map.119 = (bf16[256,1024]{1,0:T(8,128)(2,1)S(1)}, bf16[256,256]{1,0:T(8,128)(2,1)S(1)}, f32[16,256]{1,0:T(8,128)S(1)}, f32[16,256]{1,0:T(8,128)S(1)}, bf1...) custom-call(s32[1]{0:T(128)} %bitcast.mine_ref, bf16[272,512]{1,0:T(8,128)(2,1)S(1)} %get-tuple-element.17.keep_ref, ...), custom_call_target="tpu_custom_call" | custom-call | tf_op jit(solution)/shard_map/pallas_call | solution.py:28
  163.7 0.0 copy-start.2
  163.7 1.0 copy-done.2
  164.7 0.0 copy-start.9
  164.7 8.7 %all-to-all-start.2 = ((bf16[64,32,128]{2,1,0:T(8,128)(2,1)}), bf16[64,32,128]{2,1,0:T(8,128)(2,1)S(1)}, u32[]{:S(2)}, u32[]{:S(2)}) async-start(bf16[64,32,128]{2,1,0:T(8,128)(2,1)} %get-tuple-element.25), calls=%async_computation.2 | async-start | bytes 1048576 | tf_op jit(solution)/shard_map/all_to_all | solution.py:307
  173.4 0.0 copy-done
  173.5 15.9 %all-to-all-done.2.got_ref = bf16[64,32,128]{2,1,0:T(8,128)(2,1)S(1)} async-done(((bf16[64,32,128]{2,1,0:T(8,128)(2,1)}), bf16[64,32,128]{2,1,0:T(8,128)(2,1)S(1)}, u32[]{:S(2)}, u32[]{:S(2)}) %all-to-all-start.2) | async-done | bytes 524320 | tf_op jit(solution)/shard_map/all_to_all | solution.py:307
  189.4 0.8 shard_map.121
  190.3 7.4 %all-to-all-start.3 = ((bf16[64,16,128]{2,1,0:T(8,128)(2,1)}), bf16[64,16,128]{2,1,0:T(8,128)(2,1)S(1)}, u32[]{:S(2)}, u32[]{:S(2)}) async-start(bf16[64,16,128]{2,1,0:T(8,128)(2,1)} %shard_map.121), calls=%async_computation.3 | async-start | bytes 524288 | tf_op jit(solution)/shard_map/all_to_all | solution.py:313
  197.7 0.0 copy-done.9
  197.7 0.1 broadcast_in_dim.58
  197.8 0.1 broadcast_in_dim_reshape.4.skip_ref
  197.8 0.0 copy-start.3
  197.9 0.0 copy-start.6
  197.9 3.1 %shard_map.120.inside_ref = f32[256,1024]{1,0:T(8,128)S(1)} custom-call(bf16[256,1024]{1,0:T(8,128)(2,1)S(1)} %get-tuple-element.21.x_ref, bf16[256,256]{1,0:T(8,128)(2,1)S(1)} %get-tuple-element.22.bc_ref, f32[16,256]{1,0:T(8,128)S(1)} %get-tuple-element.23.cum_ref, f32[16,256]{1,0:T(8,128)S(1)} %get-tuple-element.24.step_ref), custom_call_target="tpu_custom_call" | custom-call | flops 67108864 | bytes 1048576 | tf_op jit(solution)/shard_map/pallas_call | solution.py:28
  200.9 1.1 slice_bitcast_fusion.added_ref
  202.0 5.6 %all-to-all-done.3 = bf16[64,16,128]{2,1,0:T(8,128)(2,1)S(1)} async-done(((bf16[64,16,128]{2,1,0:T(8,128)(2,1)}), bf16[64,16,128]{2,1,0:T(8,128)(2,1)S(1)}, u32[]{:S(2)}, u32[]{:S(2)}) %all-to-all-start.3) | async-done | bytes 262176 | tf_op jit(solution)/shard_map/all_to_all | solution.py:313
  207.6 0.0 copy-done.3
  207.6 0.0 copy-done.6
  207.6 6.5 %shard_map.122 = (f32[256,1024]{1,0:T(8,128)S(1)}, f32[1,256]{1,0:T(1,128)S(1)}, f32[2,1024,128]{2,1,0:T(8,128)}) custom-call(f32[256,1024]{1,0:T(8,128)S(1)} %shard_map.120.inside_ref, bf16[256,1024]{1,0:T(8,128)(2,1)S(1)} %get-tuple-element.21.x_ref, bf16[256,256]{1,0:T(8,128)(2,1)S(1)} %get-tuple-element.22.bc_ref, ...), custom_call_target="tpu_custom_call" | custom-call | tf_op jit(solution)/shard_map/pallas_call | solution.py:28
  214.1 13.4 %all_to_all.26 = f32[8,1,256]{2,1,0:T(1,128)S(1)} all-to-all(f32[8,1,256]{2,1,0:T(1,128)S(1)} %broadcast_in_dim.62), channel_id=1, replica_groups=mesh['z'=8,'x'=4,'yl'=2,'yh'=4,'c'=2] {'yh','c'}, dimensions={0} | all-to-all | bytes 16384 | tf_op jit(solution)/shard_map/all_to_all | solution.py:331
  227.5 1.8 shard_map.123
  (12 shorter events, 0.2 us)
Async XLA Ops:
  6.5 166.9 %copy-start = (f32[16,64,128]{2,1,0:T(8,128)S(1)}, f32[16,64,128]{2,1,0:T(8,128)}, u32[]{:S(2)}) copy-start(f32[16,64,128]{2,1,0:T(8,128)} %param.22) | copy-start | bytes 1572868
  6.5 60.8 %all-gather.5.cloned.1.call-start = ((), (), s32[]{:S(2)}) async-start(), calls=%async_computation.5 | async-start | bytes 4734976 | tf_op jit(solution)/shard_map/all_gather | solution.py:262
  7.3 4.9 %collective-permute-start = (bf16[16,512]{1,0:T(8,128)(2,1)S(1)}, bf16[16,512]{1,0:T(8,128)(2,1)S(1)}, u32[]{:S(2)}, u32[]{:S(2)}) collective-permute-start(bf16[16,512]{1,0:T(8,128)(2,1)S(1)} %slice.12), channel_id=1, source_target_pairs={{0,8},{8,16},{16,24},{24,32},{32,40},{40,48},{48,56},{56,64},{64,7... | collective-permute-start | bytes 49160 | tf_op jit(solution)/shard_map/ppermute | solution.py:258
  13.9 116.2 %all-gather.7.cloned.1.call-start = ((), (), s32[]{:S(2)}) async-start(), calls=%async_computation.6 | async-start | bytes 5160960 | tf_op jit(solution)/shard_map/all_gather | solution.py:286
  130.1 2.3 copy-start.1
  132.4 18.3 %copy-start.7 = (f32[16]{0:T(128)S(1)}, f32[16]{0:T(128)}, u32[]{:S(2)}) copy-start(f32[16]{0:T(128)} %param.18) | copy-start | bytes 196
  132.4 18.4 %copy-start.8 = (f32[16]{0:T(128)S(1)}, f32[16]{0:T(128)}, u32[]{:S(2)}) copy-start(f32[16]{0:T(128)} %param.19) | copy-start | bytes 196
  132.4 27.4 %copy-start.4 = (f32[4,1024]{1,0:T(4,128)S(1)}, f32[4,1024]{1,0:T(4,128)}, u32[]{:S(2)}) copy-start(f32[4,1024]{1,0:T(4,128)} %conv_x_ref.1) | copy-start | bytes 49156
  132.4 27.4 %copy-start.5 = (f32[4,256]{1,0:T(4,128)S(1)}, f32[4,256]{1,0:T(4,128)}, u32[]{:S(2)}) copy-start(f32[4,256]{1,0:T(4,128)} %conv_bc_ref.1) | copy-start | bytes 12292
  140.1 19.8 %collective-permute-start.1 = (bf16[272,512]{1,0:T(8,128)(2,1)S(1)}, bf16[272,512]{1,0:T(8,128)(2,1)S(1)}, u32[]{:S(2)}, u32[]{:S(2)}) collective-permute-start(bf16[272,512]{1,0:T(8,128)(2,1)S(1)} %get-tuple-element.18), channel_id=1, source_target_pairs={{0,8},{8,0},{1,9},{9,1},{2,10},{10,2},{3,11},{11,3},{4,12},{12,4},... | collective-permute-start | bytes 835592 | tf_op jit(solution)/shard_map/ppermute | solution.py:289
  143.9 15.8 %all-to-all-start.1 = ((bf16[8,32,272]{2,1,0:T(8,128)(2,1)}), bf16[8,32,272]{2,1,0:T(8,128)(2,1)S(1)}, u32[]{:S(2)}, u32[]{:S(2)}) async-start(bf16[8,32,272]{2,1,0:T(8,128)(2,1)} %broadcast_in_dim.55), calls=%async_computation.1 | async-start | bytes 393216 | tf_op jit(solution)/shard_map/all_to_all | solution.py:290
  163.7 1.0 copy-start.2
  164.7 33.0 %copy-start.9 = (f32[16]{0:T(128)S(1)}, f32[16]{0:T(128)}, u32[]{:S(2)}) copy-start(f32[16]{0:T(128)} %param.20) | copy-start | bytes 196
  164.7 24.7 %all-to-all-start.2 = ((bf16[64,32,128]{2,1,0:T(8,128)(2,1)}), bf16[64,32,128]{2,1,0:T(8,128)(2,1)S(1)}, u32[]{:S(2)}, u32[]{:S(2)}) async-start(bf16[64,32,128]{2,1,0:T(8,128)(2,1)} %get-tuple-element.25), calls=%async_computation.2 | async-start | bytes 1048576 | tf_op jit(solution)/shard_map/all_to_all | solution.py:307
  190.3 17.3 %all-to-all-start.3 = ((bf16[64,16,128]{2,1,0:T(8,128)(2,1)}), bf16[64,16,128]{2,1,0:T(8,128)(2,1)S(1)}, u32[]{:S(2)}, u32[]{:S(2)}) async-start(bf16[64,16,128]{2,1,0:T(8,128)(2,1)} %shard_map.121), calls=%async_computation.3 | async-start | bytes 524288 | tf_op jit(solution)/shard_map/all_to_all | solution.py:313
  197.8 9.7 %copy-start.3 = (f32[1024]{0:T(1024)S(1)}, f32[1024]{0:T(1024)}, u32[]{:S(2)}) copy-start(f32[1024]{0:T(1024)} %param.23) | copy-start | bytes 12292
  197.9 9.7 %copy-start.6 = (f32[1024]{0:T(1024)S(1)}, f32[1024]{0:T(1024)}, u32[]{:S(2)}) copy-start(f32[1024]{0:T(1024)} %param.21) | copy-start | bytes 12292
Sparse Core Ops, SparseCore 0:
  14.0 53.3 all-gather.4
  69.5 60.6 all-gather.6

commit v2 on v1

v2 whole, which is shorter than its diff:
```python
import functools
import math

import jax
import jax.numpy as jnp
from jax import lax
from jax.experimental import pallas as pl
from jax.experimental.pallas import tpu as pltpu
from jax.sharding import Mesh, PartitionSpec as P

EPSILON = 1e-05
GROUP = 128
N = 128
HALO = 16
HEAD = 64
HIGHEST = lax.Precision.HIGHEST

SEQ = ("z", "x", "yl")
TP = ("yh", "c")
SIZES = {"z": 8, "x": 4, "yl": 2, "yh": 4, "c": 2}


def call(kernel, outs, scalars, *args, blocks=None, scratch=(), flops=0, bytes_accessed=0):
    blocks = blocks or {}
    specs = [
        pl.BlockSpec(*blocks[at])
        if at in blocks
        else pl.BlockSpec(arg.shape, functools.partial(lambda rank, i, s: (0,) * rank, arg.ndim))
        for at, arg in enumerate(args)
    ]
    whole = [
        pl.BlockSpec(out.shape, functools.partial(lambda rank, i, s: (0,) * rank, len(out.shape)))
        for out in outs
    ]
    return pl.pallas_call(
        kernel,
        grid_spec=pltpu.PrefetchScalarGridSpec(
            num_scalar_prefetch=1,
            grid=(1,),
            in_specs=specs,
            out_specs=whole,
            scratch_shapes=list(scratch),
        ),
        out_shape=outs,
        compiler_params=pltpu.CompilerParams(vmem_limit_bytes=48 * 1024 * 1024),
        cost_estimate=pl.CostEstimate(
            flops=flops, bytes_accessed=bytes_accessed, transcendentals=0
        ),
    )(scalars, *args)


def dot(a, b, dims, precision=None):
    return lax.dot_general(
        a, b, (dims, ((), ())), precision=precision, preferred_element_type=jnp.float32
    )


def expander(heads, channels):
    row = lax.broadcasted_iota(jnp.int32, (heads, channels), 0)
    column = lax.broadcasted_iota(jnp.int32, (heads, channels), 1)
    return jnp.where(column // (channels // heads) == row, 1.0, 0.0)


def project_kernel(
    where_ref, own_ref, other_ref, w0, w1, w2, w3, w4, w5, w6, w7, w8,
    x_ref, bc_ref, dt_ref, weights, acc, bc_acc, dt_acc, sem,
):
    step = pl.program_id(0)
    blocks = weights.shape[0]
    channels = x_ref.shape[2]
    bc_rows, dt_rows = bc_ref.shape[0], dt_ref.shape[0]
    rows = x_ref.shape[1]
    tokens = rows - HALO
    cut = w7.shape[0]
    copies = [
        [pltpu.make_async_copy(ref, weights.at[at], sem.at[at])]
        for at, ref in enumerate((w0, w1, w2, w3, w4, w5, w6))
    ]
    copies.append(
        [
            pltpu.make_async_copy(w7, weights.at[7, 0:cut], sem.at[7]),
            pltpu.make_async_copy(w8, weights.at[7, cut:], sem.at[8]),
        ]
    )

    @pl.when(step == 0)
    def _():
        for group in copies:
            for copy in group:
                copy.start()
        acc[...] = jnp.zeros_like(acc)
        bc_acc[...] = jnp.zeros_like(bc_acc)
        dt_acc[...] = jnp.zeros_like(dt_acc)

    for at, group in enumerate(copies):

        @pl.when(step == at)
        def _():
            for copy in group:
                copy.wait()

    mine = where_ref[blocks + step] == 1
    for half in range(2):
        feats = jnp.where(mine, own_ref[0, half], other_ref[0, half])
        acc[half] += dot(feats, weights[step, 0:channels], ((1,), (0,)))
        bc_acc[half] += dot(
            weights[step, channels : channels + bc_rows], feats, ((1,), (1,))
        )
        dt_acc[half] += dot(weights[step, channels + bc_rows :], feats[HALO:], ((1,), (1,)))

    @pl.when(step == blocks - 1)
    def _():
        x_ref[...] = acc[...].astype(jnp.bfloat16)
        for half in range(2):
            bc_ref[:, half, :] = bc_acc[half].astype(jnp.bfloat16)
            dt_ref[:, half * tokens : (half + 1) * tokens] = dt_acc[half]


def project(where, own, other, weights, bc_rows, dt_rows):
    _, _, rows, depth = own.shape
    height, channels = weights[0].shape
    blocks = len(weights) - 1
    tokens = rows - HALO
    feat = pl.BlockSpec((1, 2, rows, depth), lambda j, m: (m[j], 0, 0, 0))
    return pl.pallas_call(
        project_kernel,
        grid_spec=pltpu.PrefetchScalarGridSpec(
            num_scalar_prefetch=1,
            grid=(blocks,),
            in_specs=[feat, feat] + [pl.BlockSpec(memory_space=pl.ANY)] * len(weights),
            out_specs=[
                pl.BlockSpec((2, rows, channels), lambda j, m: (0, 0, 0)),
                pl.BlockSpec((bc_rows, 2, rows), lambda j, m: (0, 0, 0)),
                pl.BlockSpec((dt_rows, 2 * tokens), lambda j, m: (0, 0)),
            ],
            scratch_shapes=[
                pltpu.VMEM((blocks, height, channels), jnp.bfloat16),
                pltpu.VMEM((2, rows, channels), jnp.float32),
                pltpu.VMEM((2, bc_rows, rows), jnp.float32),
                pltpu.VMEM((2, dt_rows, tokens), jnp.float32),
                pltpu.SemaphoreType.DMA((blocks + 1,)),
            ],
        ),
        out_shape=[
            jax.ShapeDtypeStruct((2, rows, channels), jnp.bfloat16),
            jax.ShapeDtypeStruct((bc_rows, 2, rows), jnp.bfloat16),
            jax.ShapeDtypeStruct((dt_rows, 2 * tokens), jnp.float32),
        ],
        compiler_params=pltpu.CompilerParams(vmem_limit_bytes=48 * 1024 * 1024),
    )(where, own, other, *weights)


def convolved(values, taps, tokens):
    summed = taps[0:1] * values[HALO - 3 : HALO - 3 + tokens]
    for k in range(1, 4):
        summed = summed + taps[k : k + 1] * values[HALO - 3 + k : HALO - 3 + k + tokens]
    return (summed / (1.0 + jnp.exp(-summed))).astype(jnp.bfloat16)


def state_kernel(
    mine_ref, pre_ref, bc_ref, dt_ref, conv_x_ref, conv_bc_ref, bias_ref, rate_ref,
    x_ref, bconv_ref, cum_ref, step_ref, pay_ref, added_ref,
):
    tokens, channels = x_ref.shape
    halves, rows, _ = pre_ref.shape
    local = tokens // halves
    heads = dt_ref.shape[0]
    for part in range(halves):
        at = slice(part * local, (part + 1) * local)
        for lane in range(0, channels, 128):
            on = slice(lane, lane + 128)
            values = pre_ref[part, :, on].astype(jnp.float32)
            x_ref[at, on] = convolved(values, conv_x_ref[:, on], local)
        for lane in range(0, 2 * N, 128):
            on = slice(lane, lane + 128)
            values = bc_ref[part, :, on].astype(jnp.float32)
            bconv_ref[at, on] = convolved(values, conv_bc_ref[:, on], local)
    raw = dt_ref[...] + bias_ref[...]
    step_size = jnp.maximum(raw, 0.0) + jnp.log1p(jnp.exp(-jnp.abs(raw)))
    log_decay = -step_size * rate_ref[...]
    step_ref[...] = step_size
    upper = jnp.where(
        lax.broadcasted_iota(jnp.int32, (GROUP, GROUP), 0)
        <= lax.broadcasted_iota(jnp.int32, (GROUP, GROUP), 1),
        1.0,
        0.0,
    )
    spread = expander(heads, channels)
    ends = []
    for block in range(tokens // GROUP):
        at = slice(block * GROUP, (block + 1) * GROUP)
        cumulative = dot(log_decay[:, at], upper, ((1,), (0,)), HIGHEST)
        cum_ref[:, at] = cumulative
        end = cumulative[:, GROUP - 1 : GROUP]
        to_end = jnp.exp(end - cumulative) * step_size[:, at]
        wide = dot(to_end.T, spread, ((1,), (0,)), HIGHEST)
        scaled = (x_ref[at, :].astype(jnp.float32) * wide).astype(jnp.bfloat16)
        added_ref[block] = dot(scaled, bconv_ref[at, 0:N], ((0,), (0,)))
        ends.append(end)
    growths = [jnp.exp(end) for end in ends]
    total = jnp.exp(functools.reduce(lambda p, q: p + q, ends))
    high = total.astype(jnp.bfloat16).astype(jnp.float32)
    low = total - high
    share = pay_ref.shape[0] // heads
    tail_rows = pay_ref.shape[1] - 16
    row = lax.broadcasted_iota(jnp.int32, (tail_rows, N), 0)
    for head in range(heads):
        at = slice(head * HEAD, (head + 1) * HEAD)
        state = added_ref[0, at]
        for block in range(1, tokens // GROUP):
            state = state * growths[block][head : head + 1] + added_ref[block, at]
        tail = jnp.where(
            row == 0, high[head : head + 1], jnp.where(row == 1, low[head : head + 1], 0.0)
        ).astype(jnp.bfloat16)
        for part in range(share):
            pay_ref[head * share + part, 0:16] = state[part * 16 : (part + 1) * 16].astype(
                jnp.bfloat16
            )
            pay_ref[head * share + part, 16:] = tail


def prefix_kernel(at_ref, got_ref, start_ref, out_ref):
    running = start_ref[...]
    for source in range(got_ref.shape[0]):
        out_ref[source] = running.astype(jnp.bfloat16)
        tail = got_ref[source, 16:].astype(jnp.float32)
        running = (tail[0:1] + tail[1:2]) * running + got_ref[source, 0:16].astype(jnp.float32)


def inside_kernel(mine_ref, x_ref, bc_ref, cum_ref, step_ref, out_ref):
    tokens, channels = x_ref.shape
    heads = cum_ref.shape[0]
    causal = lax.broadcasted_iota(jnp.int32, (GROUP, GROUP), 0) >= lax.broadcasted_iota(
        jnp.int32, (GROUP, GROUP), 1
    )
    for block in range(tokens // GROUP):
        at = slice(block * GROUP, (block + 1) * GROUP)
        scores = dot(bc_ref[at, N:], bc_ref[at, 0:N], ((1,), (1,)))
        cumulative = cum_ref[:, at]
        columns = cumulative.T
        for pair in range(0, heads, 2):
            parts = []
            for head in (pair, pair + 1):
                differ = columns[:, head : head + 1] - cumulative[head : head + 1]
                decays = jnp.exp(jnp.where(causal, differ, -1e30))
                mixing = (scores * decays * step_ref[head : head + 1, at]).astype(jnp.bfloat16)
                parts.append(
                    dot(mixing, x_ref[at, head * HEAD : (head + 1) * HEAD], ((1,), (0,)))
                )
            out_ref[at, pair * HEAD : (pair + 2) * HEAD] = jnp.concatenate(parts, 1)


def output_kernel(
    mine_ref, inside_ref, x_ref, bc_ref, cum_ref, entering_ref, added_ref, skip_ref, gain_ref,
    steer_ref, keep_ref, send_ref, dot_ref, state_ref,
):
    mine = mine_ref[0]
    tokens, channels = x_ref.shape
    local = tokens // 2
    heads = cum_ref.shape[0]
    spread = expander(heads, channels)
    state_ref[...] = entering_ref[...].astype(jnp.float32)
    for block in range(tokens // GROUP):
        at = slice(block * GROUP, (block + 1) * GROUP)
        carried = dot(bc_ref[at, N:].astype(jnp.float32), state_ref[...], ((1,), (1,)), HIGHEST)
        growth = dot(jnp.exp(cum_ref[:, at]).T, spread, ((1,), (0,)), HIGHEST)
        y = inside_ref[at] + growth * carried + skip_ref[...] * x_ref[at].astype(jnp.float32)
        squares = dot(y * y, spread, ((1,), (1,)), HIGHEST) * (1.0 / HEAD)
        scale = dot(lax.rsqrt(squares + EPSILON), spread, ((1,), (0,)), HIGHEST)
        normed = y * scale * gain_ref[...]
        part = block * GROUP // local
        on = slice(block * GROUP - part * local, (block + 1) * GROUP - part * local)

        @pl.when(mine == part)
        def _():
            keep_ref[on] = normed

        @pl.when(mine != part)
        def _():
            send_ref[on] = normed.astype(jnp.bfloat16)

        dot_ref[part, :, on] = dot(steer_ref[...], normed, ((1,), (1,)), HIGHEST)
        if block + 1 < tokens // GROUP:
            end = jnp.exp(cum_ref[:, (block + 1) * GROUP - 1 : (block + 1) * GROUP])
            for head in range(heads):
                rows = slice(head * HEAD, (head + 1) * HEAD)
                state_ref[rows] = state_ref[rows] * end[head : head + 1] + added_ref[block, rows]


def steer_kernel(factor, mine_ref, keep_ref, other_ref, dots_ref, steer_ref, out_ref):
    first = mine_ref[0] == 0
    half = keep_ref.shape[1]
    for lane in range(0, half, 256):
        at = slice(lane, lane + 256)
        later = slice(half + lane, half + lane + 256)
        own, other = keep_ref[:, at], other_ref[:, at].astype(jnp.float32)
        left, right = jnp.where(first, own, other), jnp.where(first, other, own)
        for on, normed in ((at, left), (later, right)):
            penalty = dot(dots_ref[...], steer_ref[:, on], ((0,), (0,)), HIGHEST)
            out_ref[:, on] = (normed - penalty * factor).astype(jnp.bfloat16)


def ring(block, axis):
    count = SIZES[axis]
    forward = [(i, (i + 1) % count) for i in range(count)]
    backward = [(i, (i - 1) % count) for i in range(count)]
    pieces, offsets = [block], [0]
    ahead = behind = block
    for hop in range(1, count // 2):
        ahead = lax.ppermute(ahead, axis, forward)
        behind = lax.ppermute(behind, axis, backward)
        pieces += [ahead, behind]
        offsets += [-hop, hop]
    cut = (block.shape[0] // 2 + 15) // 16 * 16
    pieces.append(lax.ppermute(ahead[:cut], axis, forward))
    pieces.append(lax.ppermute(behind[cut:], axis, backward))
    offsets.append(count // 2)
    return pieces, offsets


def per_device(
    tokens, x_weight, bc_weight, dt_weight, conv_x, conv_bc, dt_bias, decay_rate, d_skip,
    norm_gain, initial_state, steer,
):
    local, width = tokens.shape
    k_rows, channels = x_weight.shape
    half = channels // 2
    heads = dt_weight.shape[1] // 2
    bc_rows = bc_weight.shape[1] // 2
    small = bc_rows + heads
    seq_count = SIZES["z"] * SIZES["x"] * SIZES["yl"]
    tp_count = SIZES["yh"] * SIZES["c"]
    z, core = lax.axis_index("z"), lax.axis_index("c")
    mine = lax.axis_index("yl").astype(jnp.int32).reshape(1)
    f32, bf16 = jnp.float32, jnp.bfloat16

    earlier = lax.ppermute(
        tokens[local - HALO :], SEQ, [(i, i + 1) for i in range(seq_count - 1)]
    )
    extended = jnp.concatenate([earlier, tokens], 0)
    line = SIZES["yh"] * 2
    own = lax.all_to_all(
        jnp.broadcast_to(extended[None], (line,) + extended.shape), ("yh", "yl"), 0, 0
    ).reshape(SIZES["yh"], 2, local + HALO, width)
    other = lax.ppermute(own, "c", [(0, 1), (1, 0)])

    fan = SIZES["x"] * SIZES["yl"]
    packed_rows = small * k_rows // half
    packed = jnp.concatenate(
        [
            bc_weight.reshape(k_rows, 2, bc_rows).transpose(1, 2, 0),
            dt_weight.reshape(k_rows, 2, heads).transpose(1, 2, 0),
        ],
        1,
    ).reshape(2, packed_rows, half)
    panel = jnp.concatenate(
        [
            x_weight.reshape(k_rows, 2, half).transpose(1, 0, 2),
            packed,
            jnp.zeros((2, -packed_rows % 8, half), bf16),
        ],
        1,
    )
    panel = jnp.broadcast_to(panel[None], (SIZES["x"],) + panel.shape).reshape(
        fan, panel.shape[1], half
    )
    got = lax.all_to_all(panel, ("x", "yl"), 0, 0)
    tall = got[:, :k_rows].reshape(fan * k_rows, half)
    flat = got[:, k_rows : k_rows + packed_rows].reshape(
        fan, packed_rows, half // k_rows, k_rows
    )
    flat = flat.transpose(1, 2, 0, 3).reshape(small, fan * k_rows)
    pieces, offsets = ring(jnp.concatenate([tall, flat], 0), "z")
    source = (z + jnp.array(offsets, jnp.int32)) % SIZES["z"]
    where = jnp.concatenate([source // 2, (source % 2 == core).astype(jnp.int32)])

    x_pre, bc_pre, dt_raw = project(where, own, other, pieces, bc_rows, heads)
    bc_all = lax.all_to_all(
        jnp.broadcast_to(
            bc_pre.reshape(1, bc_rows, -1), (2 * tp_count, bc_rows, 2 * (local + HALO))
        ),
        ("yh", "c", "yl"), 0, 0,
    )
    bc_all = bc_all.reshape(2 * N, -1).T.reshape(2, local + HALO, 2 * N)

    pair = 2 * local
    plane = SIZES["z"] * SIZES["x"]
    share = half // plane
    halves = {
        3: ((conv_x.shape[0], half), lambda i, s: (0, s[0])),
        5: ((heads, 1), lambda i, s: (s[0], 0)),
        6: ((heads, 1), lambda i, s: (s[0], 0)),
    }
    x_conv, bc_conv, cumulative, step_size, payload, added = call(
        state_kernel,
        [
            jax.ShapeDtypeStruct((pair, half), bf16),
            jax.ShapeDtypeStruct((pair, 2 * N), bf16),
            jax.ShapeDtypeStruct((heads, pair), f32),
            jax.ShapeDtypeStruct((heads, pair), f32),
            jax.ShapeDtypeStruct((plane, share + 8, N), bf16),
            jax.ShapeDtypeStruct((pair // GROUP, half, N), f32),
        ],
        mine, x_pre, bc_all, dt_raw, conv_x, conv_bc, dt_bias[:, None], decay_rate[:, None],
        blocks=halves,
    )
    states = lax.all_to_all(payload, ("z", "x"), 0, 0)
    place = mine * plane + lax.axis_index(("z", "x")).astype(jnp.int32)
    (prefixes,) = call(
        prefix_kernel,
        [jax.ShapeDtypeStruct((plane, share, N), bf16)],
        place, states, initial_state.reshape(channels, N),
        blocks={1: ((share, N), lambda i, s: (s[0], 0))},
    )
    entering = lax.all_to_all(prefixes, ("z", "x"), 0, 0).reshape(half, N)

    (inside,) = call(
        inside_kernel,
        [jax.ShapeDtypeStruct((pair, half), f32)],
        mine, x_conv, bc_conv, cumulative, step_size,
        flops=2 * heads * pair * GROUP * HEAD, bytes_accessed=4 * pair * half,
    )
    lanes = ((1, half), lambda i, s: (0, s[0]))
    keep, send, dots = call(
        output_kernel,
        [
            jax.ShapeDtypeStruct((local, half), f32),
            jax.ShapeDtypeStruct((local, half), bf16),
            jax.ShapeDtypeStruct((2, 1, local), f32),
        ],
        mine, inside, x_conv, bc_conv, cumulative, entering, added,
        jnp.repeat(d_skip, HEAD)[None], norm_gain[None], steer[None],
        blocks={6: lanes, 7: lanes, 8: lanes},
        scratch=[pltpu.VMEM((half, N), f32)],
    )
    swapped = lax.ppermute(send, "yl", [(0, 1), (1, 0)])
    shape = (SIZES["yh"], 2, SIZES["c"], 1, local)
    partials = lax.all_to_all(
        jnp.broadcast_to(dots[None, :, None], shape).reshape(2 * tp_count, 1, local),
        ("yh", "yl", "c"), 0, 0,
    )
    factor = 1.0 / math.sqrt(channels * tp_count)
    (out,) = call(
        functools.partial(steer_kernel, factor),
        [jax.ShapeDtypeStruct((local, channels), bf16)],
        mine, keep, swapped, partials.reshape(2 * tp_count, local),
        jnp.broadcast_to(steer[None], (2 * tp_count, channels)),
    )
    return out


def solution(mesh):
    fine = Mesh(mesh.devices.reshape(tuple(SIZES.values())), tuple(SIZES))
    both = P(SEQ, TP)
    placed = (
        both, both, both, both, P(None, TP), P(), P(TP), P(TP), P(TP), P(TP),
        P(TP, None, None), P(TP),
    )
    return jax.shard_map(
        per_device, mesh=fine, in_specs=placed, out_specs=both, check_vma=False
    )
```

time: 237 us -> 250 us (1.055)
  starting transfers between devices: 30.2 us -> 77.5 us
  waiting for transfers between devices: 131 us -> 116 us
  between operations: 13.6 us -> 0.39 us
  blocking collectives: 26.6 us -> 14 us
  Pallas kernels: 23.7 us -> 28.4 us
  local copies, waits for them, and re-layouts: 7.86 us -> 10.9 us
    all_gather x2 -> x0, waiting for transfers between devices: 99.5 us -> none  [the longest x1 62.8 us: per_device(): weights = lax.all_gather(block, 'z', axis=0, tiled=False)]
    all_to_all x3 -> x5, waiting for transfers between devices: 30.3 us -> 87.2 us  [the longest x1 54 us: per_device(): lax.all_to_all(jnp.broadcast_to(extended[None], (line,) + extended.shape)...]
    ppermute x1 -> x10, starting transfers between devices: 3.11 us -> 39.9 us  [the longest x3 17.7 us: ring(): behind = lax.ppermute(behind, axis, backward)]
    ppermute x1 -> x10, waiting for transfers between devices: 0.01 us -> 27.8 us  [the longest x3 24.5 us: ring(): ahead = lax.ppermute(ahead, axis, forward)]
    all_to_all x2 -> x1, blocking collectives: 26.6 us -> 14 us  [per_device(): lax.all_to_all(jnp.broadcast_to(dots[None, :, None], shape).reshape(2 * t...]
    all_to_all x3 -> x5, starting transfers between devices: 23 us -> 33.5 us  [the longest x1 8.65 us: per_device(): lax.all_to_all(jnp.broadcast_to(bc_pre.reshape(1, bc_rows, -1), (2 * tp_c...]
  transfers between devices with their start and end apart: 7 -> 16, of which waited for: 6 -> 10; matrix products, arithmetic and copies ran while one was open for 2% -> 1% of each run, Pallas kernels for 1% -> 1%
where the time goes in v2:
time: 250 us; the launch traced here: 248 us
  waiting for transfers between devices  116 us (46%)
  starting transfers between devices  77.5 us (31%)
  Pallas kernels  28.4 us (11%)
  blocking collectives  14 us (6%)
  local copies, waits for them, and re-layouts  10.9 us (4%)
    all_to_all x1, waiting for transfers between devices, per_device(): lax.all_to_all(jnp.broadcast_to(extended[None], (line,) + extended.shape)...  54 us
    ppermute x3, waiting for transfers between devices, ring(): ahead = lax.ppermute(ahead, axis, forward)  24.5 us
    pallas_call x5, Pallas kernels, call(): pl.pallas_call(kernel, grid_spec=pltpu.PrefetchScalarGridSpec(num_scalar_...  18.4 us
    ppermute x3, starting transfers between devices, ring(): behind = lax.ppermute(behind, axis, backward)  17.7 us
    all_to_all x1, blocking collectives, per_device(): lax.all_to_all(jnp.broadcast_to(dots[None, :, None], shape).reshape(2 * t...  14 us
    all_to_all x1, waiting for transfers between devices, per_device(): lax.all_to_all(jnp.broadcast_to(bc_pre.reshape(1, bc_rows, -1), (2 * tp_c...  11.3 us
    all_to_all x1, waiting for transfers between devices, per_device(): states = lax.all_to_all(payload, ('z', 'x'), 0, 0)  10.6 us
    pallas_call x1, Pallas kernels, project(): pl.pallas_call(project_kernel, grid_spec=pltpu.PrefetchScalarGridSpec(num...  9.98 us
  transfers between devices with their start and end apart: 16, of which 10 were waited for; matrix products, arithmetic and copies ran while one was open for 1% of the time, Pallas kernels for 1%

profile of v2, /device:TPU:1, one launch (start us, length us, event | category | flops | bytes accessed | tf_op | source)
XLA Modules:
  0.0 248.3 jit_solution(17271983272693216943)
XLA Ops:
  0.0 0.7 slice.15
  0.7 4.0 %collective-permute-start = (bf16[16,512]{1,0:T(8,128)(2,1)S(1)}, bf16[16,512]{1,0:T(8,128)(2,1)S(1)}, u32[]{:S(2)}, u32[]{:S(2)}) collective-permute-start(bf16[16,512]{1,0:T(8,128)(2,1)S(1)} %slice.15), channel_id=1, source_target_pairs={{0,8},{8,16},{16,24},{24,32},{32,40},{40,48},{48,56},{56,64},{64,7... | collective-permute-start | bytes 49160 | tf_op jit(solution)/shard_map/ppermute | solution.py:337
  4.7 0.9 collective-permute-done
  5.6 1.0 pad_maximum_fusion.1
  6.6 1.6 broadcast_in_dim.53
  8.2 6.9 %all-to-all-start = ((bf16[8,272,512]{2,1,0:T(8,128)(2,1)}), bf16[8,272,512]{2,1,0:T(8,128)(2,1)}, u32[]{:S(2)}, u32[]{:S(2)}) async-start(bf16[8,272,512]{2,1,0:T(8,128)(2,1)} %broadcast_in_dim.53), calls=%async_computation | async-start | bytes 4456448 | tf_op jit(solution)/shard_map/all_to_all | solution.py:342
  15.0 0.1 reshape.59
  15.1 0.1 reshape.62
  15.3 0.1 pad.4.clone
  15.3 0.2 maximum_maximum_fusion
  15.6 0.0 copy-start.15
  15.6 54.0 %all-to-all-done = bf16[8,272,512]{2,1,0:T(8,128)(2,1)} async-done(((bf16[8,272,512]{2,1,0:T(8,128)(2,1)}), bf16[8,272,512]{2,1,0:T(8,128)(2,1)}, u32[]{:S(2)}, u32[]{:S(2)}) %all-to-all-start) | async-done | bytes 2228256 | tf_op jit(solution)/shard_map/all_to_all | solution.py:342
  69.6 0.9 broadcast_in_dim.55
  70.5 5.4 %all-to-all-start.1 = ((bf16[8,72,512]{2,1,0:T(8,128)(2,1)}), bf16[8,72,512]{2,1,0:T(8,128)(2,1)S(1)}, u32[]{:S(2)}, u32[]{:S(2)}) async-start(bf16[8,72,512]{2,1,0:T(8,128)(2,1)} %bitcast.7), calls=%async_computation.1 | async-start | bytes 1179648 | tf_op jit(solution)/shard_map/all_to_all | solution.py:367
  75.9 2.7 %collective-permute-start.1 = (bf16[4,2,272,512]{3,2,1,0:T(8,128)(2,1)}, bf16[4,2,272,512]{3,2,1,0:T(8,128)(2,1)}, u32[]{:S(2)}, u32[]{:S(2)}) collective-permute-start(bf16[4,2,272,512]{3,2,1,0:T(8,128)(2,1)} %bitcast.1.own_ref), channel_id=1, source_target_pairs={{0,1},{1,0},{2,3},{3,2},{4,5},{5,4},{6,7},{7,6},{8,9},{9,8},{10,11... | collective-permute-start | bytes 6684680 | tf_op jit(solution)/shard_map/ppermute | solution.py:345
  78.6 7.1 %all-to-all-done.1 = bf16[8,72,512]{2,1,0:T(8,128)(2,1)S(1)} async-done(((bf16[8,72,512]{2,1,0:T(8,128)(2,1)}), bf16[8,72,512]{2,1,0:T(8,128)(2,1)S(1)}, u32[]{:S(2)}, u32[]{:S(2)}) %all-to-all-start.1) | async-done | bytes 589856 | tf_op jit(solution)/shard_map/all_to_all | solution.py:367
  85.7 0.1 reshape.65
  85.8 0.1 reshape.66
  86.0 5.8 %collective-permute-start.2 = (bf16[536,512]{1,0:T(8,128)(2,1)S(1)}, bf16[536,512]{1,0:T(8,128)(2,1)S(1)}, u32[]{:S(2)}, u32[]{:S(2)}) collective-permute-start(bf16[536,512]{1,0:T(8,128)(2,1)S(1)} %pad_maximum_fusion.w0), channel_id=1, source_target_pairs={{0,64},{64,128},{128,192},{192,256},{256,320},{320,384},{384,448},... | collective-permute-start | bytes 1646600 | tf_op jit(solution)/shard_map/ppermute | solution.py:310
  91.9 8.6 %collective-permute-start.3 = (bf16[536,512]{1,0:T(8,128)(2,1)S(1)}, bf16[536,512]{1,0:T(8,128)(2,1)S(1)}, u32[]{:S(2)}, u32[]{:S(2)}) collective-permute-start(bf16[536,512]{1,0:T(8,128)(2,1)S(1)} %pad_maximum_fusion.w0), channel_id=1, source_target_pairs={{0,448},{64,0},{128,64},{192,128},{256,192},{320,256},{384,320},{4... | collective-permute-start | bytes 1646600 | tf_op jit(solution)/shard_map/ppermute | solution.py:311
  100.5 9.1 %collective-permute-done.2.w1 = bf16[536,512]{1,0:T(8,128)(2,1)S(1)} collective-permute-done((bf16[536,512]{1,0:T(8,128)(2,1)S(1)}, bf16[536,512]{1,0:T(8,128)(2,1)S(1)}, u32[]{:S(2)}, u32[]{:S(2)}) %collective-permute-start.2) | collective-permute-done | bytes 548896 | tf_op jit(solution)/shard_map/ppermute | solution.py:310
  109.6 1.9 collective-permute-start.4
  111.5 4.6 %collective-permute-start.5 = (bf16[536,512]{1,0:T(8,128)(2,1)S(1)}, bf16[536,512]{1,0:T(8,128)(2,1)}, u32[]{:S(2)}, u32[]{:S(2)}) collective-permute-start(bf16[536,512]{1,0:T(8,128)(2,1)S(1)} %collective-permute-done.3.w2), channel_id=1, source_target_pairs={{0,448},{64,0},{128,64},{192,128},{256,192},{320,256},{384,320},{4... | collective-permute-start | bytes 1646600 | tf_op jit(solution)/shard_map/ppermute | solution.py:311
  116.1 8.2 %collective-permute-done.4.w3 = bf16[536,512]{1,0:T(8,128)(2,1)S(1)} collective-permute-done((bf16[536,512]{1,0:T(8,128)(2,1)S(1)}, bf16[536,512]{1,0:T(8,128)(2,1)S(1)}, u32[]{:S(2)}, u32[]{:S(2)}) %collective-permute-start.4) | collective-permute-done | bytes 548896 | tf_op jit(solution)/shard_map/ppermute | solution.py:310
  124.3 1.9 collective-permute-start.6
  126.2 0.0 collective-permute-done.5.w4
  126.2 4.6 %collective-permute-start.7 = (bf16[536,512]{1,0:T(8,128)(2,1)}, bf16[536,512]{1,0:T(8,128)(2,1)S(1)}, u32[]{:S(2)}, u32[]{:S(2)}) collective-permute-start(bf16[536,512]{1,0:T(8,128)(2,1)} %collective-permute-done.5.w4), channel_id=1, source_target_pairs={{0,448},{64,0},{128,64},{192,128},{256,192},{320,256},{384,320},{4... | collective-permute-start | bytes 1646600 | tf_op jit(solution)/shard_map/ppermute | solution.py:311
  130.8 7.2 %collective-permute-done.6.w5 = bf16[536,512]{1,0:T(8,128)(2,1)S(1)} collective-permute-done((bf16[536,512]{1,0:T(8,128)(2,1)S(1)}, bf16[536,512]{1,0:T(8,128)(2,1)S(1)}, u32[]{:S(2)}, u32[]{:S(2)}) %collective-permute-start.6) | collective-permute-done | bytes 548896 | tf_op jit(solution)/shard_map/ppermute | solution.py:310
  138.1 1.9 collective-permute-start.8
  140.1 4.6 %collective-permute-start.9 = (bf16[264,512]{1,0:T(8,128)(2,1)S(1)}, bf16[264,512]{1,0:T(8,128)(2,1)S(1)}, u32[]{:S(2)}, u32[]{:S(2)}) collective-permute-start(bf16[264,512]{1,0:T(8,128)(2,1)S(1)} %slice.23), channel_id=1, source_target_pairs={{0,448},{64,0},{128,64},{192,128},{256,192},{320,256},{384,320},{4... | collective-permute-start | bytes 811016 | tf_op jit(solution)/shard_map/ppermute | solution.py:316
  144.7 0.0 copy-start.13
  144.7 0.0 copy-start.14
  144.7 0.1 pad_add_fusion.where_ref
  144.8 3.3 %collective-permute-done.9.w8 = bf16[264,512]{1,0:T(8,128)(2,1)S(1)} collective-permute-done((bf16[264,512]{1,0:T(8,128)(2,1)S(1)}, bf16[264,512]{1,0:T(8,128)(2,1)S(1)}, u32[]{:S(2)}, u32[]{:S(2)}) %collective-permute-start.9) | collective-permute-done | bytes 270368 | tf_op jit(solution)/shard_map/ppermute | solution.py:316
  148.0 0.0 collective-permute-done.1.other_ref
  148.1 1.0 copy-done.1
  149.1 10.0 %shard_map.127 = (bf16[2,272,512]{2,1,0:T(8,128)(2,1)S(1)}, bf16[16,2,272]{2,1,0:T(2,128)(2,1)S(1)}, f32[8,512]{1,0:T(8,128)S(1)}) custom-call(s32[16]{0:T(128)S(1)} %pad_add_fusion.where_ref, bf16[4,2,272,512]{3,2,1,0:T(8,128)(2,1)} %bitcast.1.own_ref, bf16[4,2,272,512]{3,2,1,0:T(8,128)(2,1)} %collective-permute-done.1.other_ref, ...), custom_call_target="tpu_custom_call" | custom-call | tf_op jit(solution)/shard_map/pallas_call | solution.py:125
  159.1 0.0 copy-start.2
  159.1 0.1 broadcast_in_dim.56
  159.2 0.8 broadcast_in_dim.57
  159.9 8.7 %all-to-all-start.2 = ((bf16[16,16,544]{2,1,0:T(8,128)(2,1)}), bf16[16,16,544]{2,1,0:T(8,128)(2,1)S(1)}, u32[]{:S(2)}, u32[]{:S(2)}) async-start(bf16[16,16,544]{2,1,0:T(8,128)(2,1)} %broadcast_in_dim.57), calls=%async_computation.2 | async-start | bytes 655360 | tf_op jit(solution)/shard_map/all_to_all | solution.py:378
  168.6 0.1 copy.30.bias_ref
  168.7 0.1 copy.31.rate_ref
  168.8 11.3 %all-to-all-done.2 = bf16[16,16,544]{2,1,0:T(8,128)(2,1)S(1)} async-done(((bf16[16,16,544]{2,1,0:T(8,128)(2,1)}), bf16[16,16,544]{2,1,0:T(8,128)(2,1)S(1)}, u32[]{:S(2)}, u32[]{:S(2)}) %all-to-all-start.2) | async-done | bytes 278560 | tf_op jit(solution)/shard_map/all_to_all | solution.py:378
  180.1 0.2 copy.29
  180.3 5.0 %shard_map.128 = (bf16[512,512]{1,0:T(8,128)(2,1)S(1)}, bf16[512,256]{1,0:T(8,128)(2,1)S(1)}, f32[8,512]{1,0:T(8,128)S(1)}, f32[8,512]{1,0:T(8,128)S(1)}, bf16[3...) custom-call(s32[1]{0:T(128)} %bitcast.mine_ref, bf16[2,272,512]{2,1,0:T(8,128)(2,1)S(1)} %get-tuple-element.17.pre_ref, ...), custom_call_target="tpu_custom_call" | custom-call | tf_op jit(solution)/shard_map/pallas_call | solution.py:35
  185.3 8.4 %all-to-all-start.3 = ((bf16[32,24,128]{2,1,0:T(8,128)(2,1)}), bf16[32,24,128]{2,1,0:T(8,128)(2,1)S(1)}, u32[]{:S(2)}, u32[]{:S(2)}) async-start(bf16[32,24,128]{2,1,0:T(8,128)(2,1)} %get-tuple-element.24), calls=%async_computation.3 | async-start | bytes 393216 | tf_op jit(solution)/shard_map/all_to_all | solution.py:407
  193.7 10.6 %all-to-all-done.3.got_ref = bf16[32,24,128]{2,1,0:T(8,128)(2,1)S(1)} async-done(((bf16[32,24,128]{2,1,0:T(8,128)(2,1)}), bf16[32,24,128]{2,1,0:T(8,128)(2,1)S(1)}, u32[]{:S(2)}, u32[]{:S(2)}) %all-to-all-start.3) | async-done | bytes 196640 | tf_op jit(solution)/shard_map/all_to_all | solution.py:407
  204.3 0.7 shard_map.130
  205.0 4.2 %all-to-all-start.4 = ((bf16[32,16,128]{2,1,0:T(8,128)(2,1)}), bf16[32,16,128]{2,1,0:T(8,128)(2,1)S(1)}, u32[]{:S(2)}, u32[]{:S(2)}) async-start(bf16[32,16,128]{2,1,0:T(8,128)(2,1)} %shard_map.130), calls=%async_computation.4 | async-start | bytes 262144 | tf_op jit(solution)/shard_map/all_to_all | solution.py:415
  209.2 0.7 broadcast_in_dim.60
  209.9 0.7 broadcast_in_dim_reshape.3.skip_ref
  210.6 0.7 copy-done.4
  211.3 3.0 %shard_map.129.inside_ref = f32[512,512]{1,0:T(8,128)S(1)} custom-call(s32[1]{0:T(128)} %bitcast.mine_ref, bf16[512,512]{1,0:T(8,128)(2,1)S(1)} %get-tuple-element.20.x_ref, bf16[512,256]{1,0:T(8,128)(2,1)S(1)} %get-tuple-element.21.bc_ref, f32[8,512]{1,0:T(8,128)S(1)} %get-tuple-element.22.cum_ref, f32[8,512]{1,0:T(8,128)S(1)} %copy-done.4), custom_call_target="tpu_custom_call" | custom-call | flops 67108864 | bytes 1048576 | tf_op jit(solution)/shard_map/pallas_call | solution.py:35
  214.3 4.2 %all-to-all-done.4 = bf16[32,16,128]{2,1,0:T(8,128)(2,1)S(1)} async-done(((bf16[32,16,128]{2,1,0:T(8,128)(2,1)}), bf16[32,16,128]{2,1,0:T(8,128)(2,1)S(1)}, u32[]{:S(2)}, u32[]{:S(2)}) %all-to-all-start.4) | async-done | bytes 131104 | tf_op jit(solution)/shard_map/all_to_all | solution.py:415
  218.5 0.7 copy-done.5
  219.2 0.7 copy-done.6
  219.9 0.7 copy-done.9
  220.6 7.8 %shard_map.131 = (f32[256,512]{1,0:T(8,128)S(1)}, bf16[256,512]{1,0:T(8,128)(2,1)}, f32[2,1,256]{2,1,0:T(1,128)S(1)}) custom-call(s32[1]{0:T(128)} %bitcast.mine_ref, f32[512,512]{1,0:T(8,128)S(1)} %shard_map.129.inside_ref, bf16[512,512]{1,0:T(8,128)(2,1)S(1)} %get-tuple-element.20.x_ref, bf16[512,256]{1,0:T(8,128)(2,1)S(1)} %get-tuple-element.21.bc_ref, ...), custom_call_target="tpu_custom_call" | custom-call | tf_op jit(solution)/shard_map/pallas_call | solution.py:35
  228.4 3.3 %collective-permute-start.10 = (bf16[256,512]{1,0:T(8,128)(2,1)}, bf16[256,512]{1,0:T(8,128)(2,1)S(1)}, u32[]{:S(2)}, u32[]{:S(2)}) collective-permute-start(bf16[256,512]{1,0:T(8,128)(2,1)} %get-tuple-element.27), channel_id=1, source_target_pairs={{0,8},{8,0},{1,9},{9,1},{2,10},{10,2},{3,11},{11,3},{4,12},{12,4},... | collective-permute-start | bytes 786440 | tf_op jit(solution)/shard_map/ppermute | solution.py:436
  231.8 14.0 %all_to_all.30 = f32[16,1,256]{2,1,0:T(1,128)S(1)} all-to-all(f32[16,1,256]{2,1,0:T(1,128)S(1)} %broadcast_in_dim.65), channel_id=1, replica_groups=mesh['z'=8,'x'=4,'yl'=2,'yh'=4,'c'=2] {'yh','yl','c'}, dimensions={0} | all-to-all | bytes 32768 | tf_op jit(solution)/shard_map/all_to_all | solution.py:438
  245.8 0.0 collective-permute-done.10.other_ref
  245.8 0.7 broadcast_in_dim.66.steer_ref
  246.5 1.8 shard_map.132
  (43 shorter events, 0.3 us)
Async XLA Ops:
  0.7 4.9 %collective-permute-start = (bf16[16,512]{1,0:T(8,128)(2,1)S(1)}, bf16[16,512]{1,0:T(8,128)(2,1)S(1)}, u32[]{:S(2)}, u32[]{:S(2)}) collective-permute-start(bf16[16,512]{1,0:T(8,128)(2,1)S(1)} %slice.15), channel_id=1, source_target_pairs={{0,8},{8,16},{16,24},{24,32},{32,40},{40,48},{48,56},{56,64},{64,7... | collective-permute-start | bytes 49160 | tf_op jit(solution)/shard_map/ppermute | solution.py:337
  8.2 6.9 %copy-start.10 = (bf16[64,1024]{1,0:T(8,128)(2,1)S(1)}, bf16[64,1024]{1,0:T(8,128)(2,1)}, u32[]{:S(2)}) copy-start(bf16[64,1024]{1,0:T(8,128)(2,1)} %param.14) | copy-start | bytes 393220
  8.2 7.0 %copy-start.11 = (bf16[64,32]{0,1:T(8,128)(2,1)S(1)}, bf16[64,32]{0,1:T(8,128)(2,1)}, u32[]{:S(2)}) copy-start(bf16[64,32]{0,1:T(8,128)(2,1)} %param.15) | copy-start | bytes 12292
  8.2 7.0 %copy-start.12 = (bf16[64,16]{0,1:T(8,128)(2,1)S(1)}, bf16[64,16]{0,1:T(8,128)(2,1)}, u32[]{:S(2)}) copy-start(bf16[64,16]{0,1:T(8,128)(2,1)} %param.16) | copy-start | bytes 6148
  8.2 61.4 %all-to-all-start = ((bf16[8,272,512]{2,1,0:T(8,128)(2,1)}), bf16[8,272,512]{2,1,0:T(8,128)(2,1)}, u32[]{:S(2)}, u32[]{:S(2)}) async-start(bf16[8,272,512]{2,1,0:T(8,128)(2,1)} %broadcast_in_dim.53), calls=%async_computation | async-start | bytes 4456448 | tf_op jit(solution)/shard_map/all_to_all | solution.py:342
  15.6 115.2 %copy-start.15 = (s32[8]{0:T(128)S(1)}, s32[8]{0:T(128)}, u32[]{:S(2)}) copy-start(s32[8]{0:T(128)} %constant.63.clone) | copy-start | bytes 100
  70.5 15.2 %all-to-all-start.1 = ((bf16[8,72,512]{2,1,0:T(8,128)(2,1)}), bf16[8,72,512]{2,1,0:T(8,128)(2,1)S(1)}, u32[]{:S(2)}, u32[]{:S(2)}) async-start(bf16[8,72,512]{2,1,0:T(8,128)(2,1)} %bitcast.7), calls=%async_computation.1 | async-start | bytes 1179648 | tf_op jit(solution)/shard_map/all_to_all | solution.py:367
  75.9 72.1 %collective-permute-start.1 = (bf16[4,2,272,512]{3,2,1,0:T(8,128)(2,1)}, bf16[4,2,272,512]{3,2,1,0:T(8,128)(2,1)}, u32[]{:S(2)}, u32[]{:S(2)}) collective-permute-start(bf16[4,2,272,512]{3,2,1,0:T(8,128)(2,1)} %bitcast.1.own_ref), channel_id=1, source_target_pairs={{0,1},{1,0},{2,3},{3,2},{4,5},{5,4},{6,7},{7,6},{8,9},{9,8},{10,11... | collective-permute-start | bytes 6684680 | tf_op jit(solution)/shard_map/ppermute | solution.py:345
  86.0 23.6 %collective-permute-start.2 = (bf16[536,512]{1,0:T(8,128)(2,1)S(1)}, bf16[536,512]{1,0:T(8,128)(2,1)S(1)}, u32[]{:S(2)}, u32[]{:S(2)}) collective-permute-start(bf16[536,512]{1,0:T(8,128)(2,1)S(1)} %pad_maximum_fusion.w0), channel_id=1, source_target_pairs={{0,64},{64,128},{128,192},{192,256},{256,320},{320,384},{384,448},... | collective-permute-start | bytes 1646600 | tf_op jit(solution)/shard_map/ppermute | solution.py:310
  91.9 19.6 %collective-permute-start.3 = (bf16[536,512]{1,0:T(8,128)(2,1)S(1)}, bf16[536,512]{1,0:T(8,128)(2,1)S(1)}, u32[]{:S(2)}, u32[]{:S(2)}) collective-permute-start(bf16[536,512]{1,0:T(8,128)(2,1)S(1)} %pad_maximum_fusion.w0), channel_id=1, source_target_pairs={{0,448},{64,0},{128,64},{192,128},{256,192},{320,256},{384,320},{4... | collective-permute-start | bytes 1646600 | tf_op jit(solution)/shard_map/ppermute | solution.py:311
  109.6 14.7 %collective-permute-start.4 = (bf16[536,512]{1,0:T(8,128)(2,1)S(1)}, bf16[536,512]{1,0:T(8,128)(2,1)S(1)}, u32[]{:S(2)}, u32[]{:S(2)}) collective-permute-start(bf16[536,512]{1,0:T(8,128)(2,1)S(1)} %collective-permute-done.2.w1), channel_id=1, source_target_pairs={{0,64},{64,128},{128,192},{192,256},{256,320},{320,384},{384,448},... | collective-permute-start | bytes 1646600 | tf_op jit(solution)/shard_map/ppermute | solution.py:310
  111.5 14.7 %collective-permute-start.5 = (bf16[536,512]{1,0:T(8,128)(2,1)S(1)}, bf16[536,512]{1,0:T(8,128)(2,1)}, u32[]{:S(2)}, u32[]{:S(2)}) collective-permute-start(bf16[536,512]{1,0:T(8,128)(2,1)S(1)} %collective-permute-done.3.w2), channel_id=1, source_target_pairs={{0,448},{64,0},{128,64},{192,128},{256,192},{320,256},{384,320},{4... | collective-permute-start | bytes 1646600 | tf_op jit(solution)/shard_map/ppermute | solution.py:311
  124.3 23.7 %copy-start = (bf16[536,512]{1,0:T(8,128)(2,1)}, bf16[536,512]{1,0:T(8,128)(2,1)S(1)}, u32[]{:S(2)}) copy-start(bf16[536,512]{1,0:T(8,128)(2,1)S(1)} %collective-permute-done.4.w3) | copy-start | bytes 1646596
  124.3 13.8 %collective-permute-start.6 = (bf16[536,512]{1,0:T(8,128)(2,1)S(1)}, bf16[536,512]{1,0:T(8,128)(2,1)S(1)}, u32[]{:S(2)}, u32[]{:S(2)}) collective-permute-start(bf16[536,512]{1,0:T(8,128)(2,1)S(1)} %collective-permute-done.4.w3), channel_id=1, source_target_pairs={{0,64},{64,128},{128,192},{192,256},{256,320},{320,384},{384,448},... | collective-permute-start | bytes 1646600 | tf_op jit(solution)/shard_map/ppermute | solution.py:310
  126.2 13.8 %collective-permute-start.7 = (bf16[536,512]{1,0:T(8,128)(2,1)}, bf16[536,512]{1,0:T(8,128)(2,1)S(1)}, u32[]{:S(2)}, u32[]{:S(2)}) collective-permute-start(bf16[536,512]{1,0:T(8,128)(2,1)} %collective-permute-done.5.w4), channel_id=1, source_target_pairs={{0,448},{64,0},{128,64},{192,128},{256,192},{320,256},{384,320},{4... | collective-permute-start | bytes 1646600 | tf_op jit(solution)/shard_map/ppermute | solution.py:311
  138.1 9.9 %collective-permute-start.8 = (bf16[272,512]{1,0:T(8,128)(2,1)S(1)}, bf16[272,512]{1,0:T(8,128)(2,1)S(1)}, u32[]{:S(2)}, u32[]{:S(2)}) collective-permute-start(bf16[272,512]{1,0:T(8,128)(2,1)S(1)} %slice.22), channel_id=1, source_target_pairs={{0,64},{64,128},{128,192},{192,256},{256,320},{320,384},{384,448},... | collective-permute-start | bytes 835592 | tf_op jit(solution)/shard_map/ppermute | solution.py:315
  140.1 8.0 %collective-permute-start.9 = (bf16[264,512]{1,0:T(8,128)(2,1)S(1)}, bf16[264,512]{1,0:T(8,128)(2,1)S(1)}, u32[]{:S(2)}, u32[]{:S(2)}) collective-permute-start(bf16[264,512]{1,0:T(8,128)(2,1)S(1)} %slice.23), channel_id=1, source_target_pairs={{0,448},{64,0},{128,64},{192,128},{256,192},{320,256},{384,320},{4... | collective-permute-start | bytes 811016 | tf_op jit(solution)/shard_map/ppermute | solution.py:316
  144.7 23.9 %copy-start.13 = (f32[16]{0:T(128)S(1)}, f32[16]{0:T(128)}, u32[]{:S(2)}) copy-start(f32[16]{0:T(128)} %param.19) | copy-start | bytes 196
  144.7 24.0 %copy-start.14 = (f32[16]{0:T(128)S(1)}, f32[16]{0:T(128)}, u32[]{:S(2)}) copy-start(f32[16]{0:T(128)} %param.20) | copy-start | bytes 196
  148.0 1.1 copy-start.1
  149.1 31.2 %copy-start.7 = (f32[4,1024]{1,0:T(4,128)S(1)}, f32[4,1024]{1,0:T(4,128)}, u32[]{:S(2)}) copy-start(f32[4,1024]{1,0:T(4,128)} %conv_x_ref.1) | copy-start | bytes 49156
  149.1 31.2 %copy-start.8 = (f32[4,256]{1,0:T(4,128)S(1)}, f32[4,256]{1,0:T(4,128)}, u32[]{:S(2)}) copy-start(f32[4,256]{1,0:T(4,128)} %conv_bc_ref.1) | copy-start | bytes 12292
  159.1 45.2 %copy-start.2 = (f32[16,64,128]{2,1,0:T(8,128)S(1)}, f32[16,64,128]{2,1,0:T(8,128)}, u32[]{:S(2)}) copy-start(f32[16,64,128]{2,1,0:T(8,128)} %param.23) | copy-start | bytes 1572868
  159.9 20.1 %all-to-all-start.2 = ((bf16[16,16,544]{2,1,0:T(8,128)(2,1)}), bf16[16,16,544]{2,1,0:T(8,128)(2,1)S(1)}, u32[]{:S(2)}, u32[]{:S(2)}) async-start(bf16[16,16,544]{2,1,0:T(8,128)(2,1)} %broadcast_in_dim.57), calls=%async_computation.2 | async-start | bytes 655360 | tf_op jit(solution)/shard_map/all_to_all | solution.py:378
  185.3 19.7 %copy-start.3 = (f32[8,512]{1,0:T(8,128)}, f32[8,512]{1,0:T(8,128)S(1)}, u32[]{:S(2)}) copy-start(f32[8,512]{1,0:T(8,128)S(1)} %get-tuple-element.23.step_ref) | copy-start | bytes 49156
  185.3 19.0 %all-to-all-start.3 = ((bf16[32,24,128]{2,1,0:T(8,128)(2,1)}), bf16[32,24,128]{2,1,0:T(8,128)(2,1)S(1)}, u32[]{:S(2)}, u32[]{:S(2)}) async-start(bf16[32,24,128]{2,1,0:T(8,128)(2,1)} %get-tuple-element.24), calls=%async_computation.3 | async-start | bytes 393216 | tf_op jit(solution)/shard_map/all_to_all | solution.py:407
  205.0 13.5 %all-to-all-start.4 = ((bf16[32,16,128]{2,1,0:T(8,128)(2,1)}), bf16[32,16,128]{2,1,0:T(8,128)(2,1)S(1)}, u32[]{:S(2)}, u32[]{:S(2)}) async-start(bf16[32,16,128]{2,1,0:T(8,128)(2,1)} %shard_map.130), calls=%async_computation.4 | async-start | bytes 262144 | tf_op jit(solution)/shard_map/all_to_all | solution.py:415
  210.6 0.7 copy-start.4
  218.5 0.7 copy-start.5
  219.2 0.7 copy-start.6
  219.9 0.7 copy-start.9
  228.4 17.4 %collective-permute-start.10 = (bf16[256,512]{1,0:T(8,128)(2,1)}, bf16[256,512]{1,0:T(8,128)(2,1)S(1)}, u32[]{:S(2)}, u32[]{:S(2)}) collective-permute-start(bf16[256,512]{1,0:T(8,128)(2,1)} %get-tuple-element.27), channel_id=1, source_target_pairs={{0,8},{8,0},{1,9},{9,1},{2,10},{10,2},{3,11},{11,3},{4,12},{12,4},... | collective-permute-start | bytes 786440 | tf_op jit(solution)/shard_map/ppermute | solution.py:436

commit v3 on v2

--- a/solution.py
+++ b/solution.py
@@ -55,15 +55,31 @@
     )
 
 
+def parts(value):
+    high = value.astype(jnp.bfloat16)
+    rest = value - high.astype(jnp.float32)
+    middle = rest.astype(jnp.bfloat16)
+    low = (rest - middle.astype(jnp.float32)).astype(jnp.bfloat16)
+    return high, middle, low
+
+
+def left_dot(value, exact, dims):
+    return sum(dot(part, exact, dims) for part in parts(value))
+
+
+def right_dot(exact, value, dims):
+    return sum(dot(exact, part, dims) for part in parts(value))
+
+
 def expander(heads, channels):
     row = lax.broadcasted_iota(jnp.int32, (heads, channels), 0)
     column = lax.broadcasted_iota(jnp.int32, (heads, channels), 1)
-    return jnp.where(column // (channels // heads) == row, 1.0, 0.0)
+    return jnp.where(column // (channels // heads) == row, 1.0, 0.0).astype(jnp.bfloat16)
 
 
 def project_kernel(
     where_ref, own_ref, other_ref, w0, w1, w2, w3, w4, w5, w6, w7, w8,
-    x_ref, bc_ref, dt_ref, weights, acc, bc_acc, dt_acc, sem,
+    x_ref, bc_ref, dt_ref, weights, acc, small, sem,
 ):
     step = pl.program_id(0)
     blocks = weights.shape[0]
@@ -89,8 +105,7 @@
             for copy in group:
                 copy.start()
         acc[...] = jnp.zeros_like(acc)
-        bc_acc[...] = jnp.zeros_like(bc_acc)
-        dt_acc[...] = jnp.zeros_like(dt_acc)
+        small[...] = jnp.zeros_like(small)
 
     for at, group in enumerate(copies):
 
@@ -103,17 +118,18 @@
     for half in range(2):
         feats = jnp.where(mine, own_ref[0, half], other_ref[0, half])
         acc[half] += dot(feats, weights[step, 0:channels], ((1,), (0,)))
-        bc_acc[half] += dot(
-            weights[step, channels : channels + bc_rows], feats, ((1,), (1,))
+        small[half, 0:rows, 0 : bc_rows + dt_rows] += dot(
+            feats, weights[step, channels:], ((1,), (1,))
         )
-        dt_acc[half] += dot(weights[step, channels + bc_rows :], feats[HALO:], ((1,), (1,)))
 
     @pl.when(step == blocks - 1)
     def _():
         x_ref[...] = acc[...].astype(jnp.bfloat16)
         for half in range(2):
-            bc_ref[:, half, :] = bc_acc[half].astype(jnp.bfloat16)
-            dt_ref[:, half * tokens : (half + 1) * tokens] = dt_acc[half]
+            turned = small[half].T
+            bc_ref[:, half, :] = turned[0:bc_rows, 0:rows].astype(jnp.bfloat16)
+            turned = small[half, HALO:rows].T
+            dt_ref[:, half * tokens : (half + 1) * tokens] = turned[bc_rows : bc_rows + dt_rows]
 
 
 def project(where, own, other, weights, bc_rows, dt_rows):
@@ -136,8 +152,7 @@
             scratch_shapes=[
                 pltpu.VMEM((blocks, height, channels), jnp.bfloat16),
                 pltpu.VMEM((2, rows, channels), jnp.float32),
-                pltpu.VMEM((2, bc_rows, rows), jnp.float32),
-                pltpu.VMEM((2, dt_rows, tokens), jnp.float32),
+                pltpu.VMEM((2, (rows + 127) // 128 * 128, 128), jnp.float32),
                 pltpu.SemaphoreType.DMA((blocks + 1,)),
             ],
         ),
@@ -157,9 +172,8 @@
     return (summed / (1.0 + jnp.exp(-summed))).astype(jnp.bfloat16)
 
 
-def state_kernel(
-    mine_ref, pre_ref, bc_ref, dt_ref, conv_x_ref, conv_bc_ref, bias_ref, rate_ref,
-    x_ref, bconv_ref, cum_ref, step_ref, pay_ref, added_ref,
+def conv_kernel(
+    mine_ref, pre_ref, dt_ref, conv_ref, head_ref, x_ref, cum_ref, step_ref, scaled_ref
 ):
     tokens, channels = x_ref.shape
     halves, rows, _ = pre_ref.shape
@@ -170,53 +184,72 @@
         for lane in range(0, channels, 128):
             on = slice(lane, lane + 128)
             values = pre_ref[part, :, on].astype(jnp.float32)
-            x_ref[at, on] = convolved(values, conv_x_ref[:, on], local)
-        for lane in range(0, 2 * N, 128):
-            on = slice(lane, lane + 128)
-            values = bc_ref[part, :, on].astype(jnp.float32)
-            bconv_ref[at, on] = convolved(values, conv_bc_ref[:, on], local)
-    raw = dt_ref[...] + bias_ref[...]
+            x_ref[at, on] = convolved(values, conv_ref[:, on], local)
+    raw = dt_ref[...] + head_ref[:, 0:1]
     step_size = jnp.maximum(raw, 0.0) + jnp.log1p(jnp.exp(-jnp.abs(raw)))
-    log_decay = -step_size * rate_ref[...]
+    log_decay = -step_size * head_ref[:, 1:2]
     step_ref[...] = step_size
     upper = jnp.where(
         lax.broadcasted_iota(jnp.int32, (GROUP, GROUP), 0)
         <= lax.broadcasted_iota(jnp.int32, (GROUP, GROUP), 1),
         1.0,
         0.0,
-    )
+    ).astype(jnp.bfloat16)
     spread = expander(heads, channels)
-    ends = []
     for block in range(tokens // GROUP):
         at = slice(block * GROUP, (block + 1) * GROUP)
-        cumulative = dot(log_decay[:, at], upper, ((1,), (0,)), HIGHEST)
+        cumulative = left_dot(log_decay[:, at], upper, ((1,), (0,)))
         cum_ref[:, at] = cumulative
-        end = cumulative[:, GROUP - 1 : GROUP]
-        to_end = jnp.exp(end - cumulative) * step_size[:, at]
-        wide = dot(to_end.T, spread, ((1,), (0,)), HIGHEST)
-        scaled = (x_ref[at, :].astype(jnp.float32) * wide).astype(jnp.bfloat16)
-        added_ref[block] = dot(scaled, bconv_ref[at, 0:N], ((0,), (0,)))
-        ends.append(end)
-    growths = [jnp.exp(end) for end in ends]
-    total = jnp.exp(functools.reduce(lambda p, q: p + q, ends))
+        to_end = jnp.exp(cumulative[:, GROUP - 1 : GROUP] - cumulative) * step_size[:, at]
+        wide = left_dot(to_end.T, spread, ((1,), (0,)))
+        scaled = x_ref[at, :].astype(jnp.float32) * wide
+        scaled_ref[:, at] = scaled.T.astype(jnp.bfloat16)
+
+
+def state_kernel(
+    mine_ref, bc_ref, conv_ref, cum_ref, scaled_ref, bconv_ref, pay_ref, local_ref
+):
+    halves, rows, _ = bc_ref.shape
+    channels, tokens = scaled_ref.shape
+    local = tokens // halves
+    heads = cum_ref.shape[0]
+    for part in range(halves):
+        at = slice(part * local, (part + 1) * local)
+        for lane in range(0, 2 * N, 128):
+            on = slice(lane, lane + 128)
+            values = bc_ref[part, :, on].astype(jnp.float32)
+            bconv_ref[at, on] = convolved(values, conv_ref[:, on], local)
+    total = jnp.zeros((heads, 1), jnp.float32)
+    blocks = tokens // GROUP
+    for block in range(blocks):
+        at = slice(block * GROUP, (block + 1) * GROUP)
+        added = dot(scaled_ref[:, at], bconv_ref[at, 0:N], ((1,), (0,)))
+        end = cum_ref[:, (block + 1) * GROUP - 1 : (block + 1) * GROUP]
+        total = total + end
+        growth = jnp.exp(end)
+        for head in range(heads):
+            on = slice(head * HEAD, (head + 1) * HEAD)
+            if block:
+                local_ref[block, on] = (
+                    local_ref[block - 1, on] * growth[head : head + 1] + added[on]
+                )
+            else:
+                local_ref[block, on] = added[on]
+    total = jnp.exp(total)
     high = total.astype(jnp.bfloat16).astype(jnp.float32)
     low = total - high
     share = pay_ref.shape[0] // heads
     tail_rows = pay_ref.shape[1] - 16
     row = lax.broadcasted_iota(jnp.int32, (tail_rows, N), 0)
     for head in range(heads):
-        at = slice(head * HEAD, (head + 1) * HEAD)
-        state = added_ref[0, at]
-        for block in range(1, tokens // GROUP):
-            state = state * growths[block][head : head + 1] + added_ref[block, at]
         tail = jnp.where(
             row == 0, high[head : head + 1], jnp.where(row == 1, low[head : head + 1], 0.0)
         ).astype(jnp.bfloat16)
-        for part in range(share):
-            pay_ref[head * share + part, 0:16] = state[part * 16 : (part + 1) * 16].astype(
+        for part in range(head * share, (head + 1) * share):
+            pay_ref[part, 0:16] = local_ref[blocks - 1, part * 16 : (part + 1) * 16].astype(
                 jnp.bfloat16
             )
-            pay_ref[head * share + part, 16:] = tail
+            pay_ref[part, 16:] = tail
 
 
 def prefix_kernel(at_ref, got_ref, start_ref, out_ref):
@@ -227,47 +260,56 @@
         running = (tail[0:1] + tail[1:2]) * running + got_ref[source, 0:16].astype(jnp.float32)
 
 
-def inside_kernel(mine_ref, x_ref, bc_ref, cum_ref, step_ref, out_ref):
+def inside_kernel(
+    mine_ref, x_ref, bc_ref, cum_ref, step_ref, local_ref, chan_ref, out_ref, growth_ref
+):
     tokens, channels = x_ref.shape
     heads = cum_ref.shape[0]
+    spread = expander(heads, channels)
     causal = lax.broadcasted_iota(jnp.int32, (GROUP, GROUP), 0) >= lax.broadcasted_iota(
         jnp.int32, (GROUP, GROUP), 1
     )
+    before = jnp.zeros((heads, 1), jnp.float32)
     for block in range(tokens // GROUP):
         at = slice(block * GROUP, (block + 1) * GROUP)
-        scores = dot(bc_ref[at, N:], bc_ref[at, 0:N], ((1,), (1,)))
+        c_block = bc_ref[at, N:]
+        scores = dot(c_block, bc_ref[at, 0:N], ((1,), (1,)))
         cumulative = cum_ref[:, at]
         columns = cumulative.T
+        growth_ref[at] = left_dot(jnp.exp(cumulative + before).T, spread, ((1,), (0,)))
+        before = before + cumulative[:, GROUP - 1 : GROUP]
+        rest = chan_ref[0:1] * x_ref[at].astype(jnp.float32)
+        if block:
+            carried = right_dot(c_block, local_ref[block - 1], ((1,), (1,)))
+            rest = rest + left_dot(jnp.exp(columns), spread, ((1,), (0,))) * carried
         for pair in range(0, heads, 2):
-            parts = []
+            found = []
             for head in (pair, pair + 1):
                 differ = columns[:, head : head + 1] - cumulative[head : head + 1]
                 decays = jnp.exp(jnp.where(causal, differ, -1e30))
                 mixing = (scores * decays * step_ref[head : head + 1, at]).astype(jnp.bfloat16)
-                parts.append(
+                found.append(
                     dot(mixing, x_ref[at, head * HEAD : (head + 1) * HEAD], ((1,), (0,)))
                 )
-            out_ref[at, pair * HEAD : (pair + 2) * HEAD] = jnp.concatenate(parts, 1)
+            on = slice(pair * HEAD, (pair + 2) * HEAD)
+            out_ref[at, on] = jnp.concatenate(found, 1) + rest[:, on]
 
 
 def output_kernel(
-    mine_ref, inside_ref, x_ref, bc_ref, cum_ref, entering_ref, added_ref, skip_ref, gain_ref,
-    steer_ref, keep_ref, send_ref, dot_ref, state_ref,
+    mine_ref, inside_ref, growth_ref, bc_ref, entering_ref, chan_ref, keep_ref, send_ref, dot_ref
 ):
     mine = mine_ref[0]
-    tokens, channels = x_ref.shape
+    tokens, channels = inside_ref.shape
     local = tokens // 2
-    heads = cum_ref.shape[0]
-    spread = expander(heads, channels)
-    state_ref[...] = entering_ref[...].astype(jnp.float32)
+    spread = expander(channels // HEAD, channels)
+    gain, steer = chan_ref[1:2], chan_ref[2:3]
     for block in range(tokens // GROUP):
         at = slice(block * GROUP, (block + 1) * GROUP)
-        carried = dot(bc_ref[at, N:].astype(jnp.float32), state_ref[...], ((1,), (1,)), HIGHEST)
-        growth = dot(jnp.exp(cum_ref[:, at]).T, spread, ((1,), (0,)), HIGHEST)
-        y = inside_ref[at] + growth * carried + skip_ref[...] * x_ref[at].astype(jnp.float32)
-        squares = dot(y * y, spread, ((1,), (1,)), HIGHEST) * (1.0 / HEAD)
-        scale = dot(lax.rsqrt(squares + EPSILON), spread, ((1,), (0,)), HIGHEST)
-        normed = y * scale * gain_ref[...]
+        carried = dot(bc_ref[at, N:], entering_ref[...], ((1,), (1,)))
+        y = inside_ref[at] + growth_ref[at] * carried
+        squares = left_dot(y * y, spread, ((1,), (1,))) * (1.0 / HEAD)
+        scale = left_dot(lax.rsqrt(squares + EPSILON), spread, ((1,), (0,)))
+        normed = y * scale * gain
         part = block * GROUP // local
         on = slice(block * GROUP - part * local, (block + 1) * GROUP - part * local)
 
@@ -279,24 +321,25 @@
         def _():
             send_ref[on] = normed.astype(jnp.bfloat16)
 
-        dot_ref[part, :, on] = dot(steer_ref[...], normed, ((1,), (1,)), HIGHEST)
-        if block + 1 < tokens // GROUP:
-            end = jnp.exp(cum_ref[:, (block + 1) * GROUP - 1 : (block + 1) * GROUP])
-            for head in range(heads):
-                rows = slice(head * HEAD, (head + 1) * HEAD)
-                state_ref[rows] = state_ref[rows] * end[head : head + 1] + added_ref[block, rows]
-
-
-def steer_kernel(factor, mine_ref, keep_ref, other_ref, dots_ref, steer_ref, out_ref):
+        terms = normed * steer
+        folded = terms[:, 0:128]
+        for lane in range(128, channels, 128):
+            folded = folded + terms[:, lane : lane + 128]
+        dot_ref[part, :, on] = jnp.sum(folded.T, axis=0, keepdims=True)
+
+
+def steer_kernel(factor, mine_ref, keep_ref, other_ref, dots_ref, chan_ref, out_ref):
     first = mine_ref[0] == 0
     half = keep_ref.shape[1]
+    dots = dots_ref[...]
     for lane in range(0, half, 256):
         at = slice(lane, lane + 256)
         later = slice(half + lane, half + lane + 256)
         own, other = keep_ref[:, at], other_ref[:, at].astype(jnp.float32)
         left, right = jnp.where(first, own, other), jnp.where(first, other, own)
         for on, normed in ((at, left), (later, right)):
-            penalty = dot(dots_ref[...], steer_ref[:, on], ((0,), (0,)), HIGHEST)
+            steer = jnp.broadcast_to(chan_ref[2:3, on], (dots.shape[0], 256))
+            penalty = dot(dots, steer, ((0,), (0,)), HIGHEST)
             out_ref[:, on] = (normed - penalty * factor).astype(jnp.bfloat16)
 
 
@@ -309,6 +352,7 @@
     for hop in range(1, count // 2):
         ahead = lax.ppermute(ahead, axis, forward)
         behind = lax.ppermute(behind, axis, backward)
+        ahead, behind = lax.optimization_barrier((ahead, behind))
         pieces += [ahead, behind]
         offsets += [-hop, hop]
     cut = (block.shape[0] // 2 + 15) // 16 * 16
@@ -339,10 +383,7 @@
     )
     extended = jnp.concatenate([earlier, tokens], 0)
     line = SIZES["yh"] * 2
-    own = lax.all_to_all(
-        jnp.broadcast_to(extended[None], (line,) + extended.shape), ("yh", "yl"), 0, 0
-    ).reshape(SIZES["yh"], 2, local + HALO, width)
-    other = lax.ppermute(own, "c", [(0, 1), (1, 0)])
+    copies = jnp.broadcast_to(extended[None], (line,) + extended.shape)
 
     fan = SIZES["x"] * SIZES["yl"]
     packed_rows = small * k_rows // half
@@ -371,6 +412,25 @@
     )
     flat = flat.transpose(1, 2, 0, 3).reshape(small, fan * k_rows)
     pieces, offsets = ring(jnp.concatenate([tall, flat], 0), "z")
+
+    copies = lax.optimization_barrier((copies, got))[0]
+    own = lax.all_to_all(copies, ("yh", "yl"), 0, 0).reshape(
+        SIZES["yh"], 2, local + HALO, width
+    )
+    own = lax.optimization_barrier((own, pieces[5], pieces[6]))[0]
+    other = lax.ppermute(own, "c", [(0, 1), (1, 0)])
+
+    channel_rows = jnp.concatenate(
+        [
+            jnp.repeat(d_skip, HEAD)[None], norm_gain[None], steer[None],
+            jnp.zeros((5, channels), f32),
+        ],
+        0,
+    )
+    head_columns = jnp.stack([dt_bias, decay_rate], 1)
+    channel_rows, head_columns, _ = lax.optimization_barrier(
+        (channel_rows, head_columns, pieces[3])
+    )
     source = (z + jnp.array(offsets, jnp.int32)) % SIZES["z"]
     where = jnp.concatenate([source // 2, (source % 2 == core).astype(jnp.int32)])
 
@@ -386,23 +446,29 @@
     pair = 2 * local
     plane = SIZES["z"] * SIZES["x"]
     share = half // plane
-    halves = {
-        3: ((conv_x.shape[0], half), lambda i, s: (0, s[0])),
-        5: ((heads, 1), lambda i, s: (s[0], 0)),
-        6: ((heads, 1), lambda i, s: (s[0], 0)),
-    }
-    x_conv, bc_conv, cumulative, step_size, payload, added = call(
-        state_kernel,
+    x_conv, cumulative, step_size, scaled = call(
+        conv_kernel,
         [
             jax.ShapeDtypeStruct((pair, half), bf16),
-            jax.ShapeDtypeStruct((pair, 2 * N), bf16),
             jax.ShapeDtypeStruct((heads, pair), f32),
             jax.ShapeDtypeStruct((heads, pair), f32),
+            jax.ShapeDtypeStruct((half, pair), bf16),
+        ],
+        mine, x_pre, dt_raw, conv_x, head_columns,
+        blocks={
+            2: ((conv_x.shape[0], half), lambda i, s: (0, s[0])),
+            3: ((heads, 2), lambda i, s: (s[0], 0)),
+        },
+        flops=10**9, bytes_accessed=8 * pair * half,
+    )
+    bc_conv, payload, locals_ = call(
+        state_kernel,
+        [
+            jax.ShapeDtypeStruct((pair, 2 * N), bf16),
             jax.ShapeDtypeStruct((plane, share + 8, N), bf16),
             jax.ShapeDtypeStruct((pair // GROUP, half, N), f32),
         ],
-        mine, x_pre, bc_all, dt_raw, conv_x, conv_bc, dt_bias[:, None], decay_rate[:, None],
-        blocks=halves,
+        mine, bc_all, conv_bc, cumulative, scaled,
     )
     states = lax.all_to_all(payload, ("z", "x"), 0, 0)
     place = mine * plane + lax.axis_index(("z", "x")).astype(jnp.int32)
@@ -414,13 +480,14 @@
     )
     entering = lax.all_to_all(prefixes, ("z", "x"), 0, 0).reshape(half, N)
 
-    (inside,) = call(
+    lanes = ((8, half), lambda i, s: (0, s[0]))
+    inside, growth = call(
         inside_kernel,
-        [jax.ShapeDtypeStruct((pair, half), f32)],
-        mine, x_conv, bc_conv, cumulative, step_size,
-        flops=2 * heads * pair * GROUP * HEAD, bytes_accessed=4 * pair * half,
-    )
-    lanes = ((1, half), lambda i, s: (0, s[0]))
+        [jax.ShapeDtypeStruct((pair, half), f32), jax.ShapeDtypeStruct((pair, half), f32)],
+        mine, x_conv, bc_conv, cumulative, step_size, locals_, channel_rows,
+        blocks={5: lanes},
+        flops=10**9, bytes_accessed=12 * pair * half,
+    )
     keep, send, dots = call(
         output_kernel,
         [
@@ -428,10 +495,8 @@
             jax.ShapeDtypeStruct((local, half), bf16),
             jax.ShapeDtypeStruct((2, 1, local), f32),
         ],
-        mine, inside, x_conv, bc_conv, cumulative, entering, added,
-        jnp.repeat(d_skip, HEAD)[None], norm_gain[None], steer[None],
-        blocks={6: lanes, 7: lanes, 8: lanes},
-        scratch=[pltpu.VMEM((half, N), f32)],
+        mine, inside, growth, bc_conv, entering, channel_rows,
+        blocks={4: lanes},
     )
     swapped = lax.ppermute(send, "yl", [(0, 1), (1, 0)])
     shape = (SIZES["yh"], 2, SIZES["c"], 1, local)
@@ -444,7 +509,7 @@
         functools.partial(steer_kernel, factor),
         [jax.ShapeDtypeStruct((local, channels), bf16)],
         mine, keep, swapped, partials.reshape(2 * tp_count, local),
-        jnp.broadcast_to(steer[None], (2 * tp_count, channels)),
+        channel_rows,
     )
     return out
 

time: 250 us -> 188 us (0.75)
  waiting for transfers between devices: 116 us -> 59.2 us
  Pallas kernels: 28.4 us -> 21.5 us
    all_to_all x1, waiting for transfers between devices: 54 us -> 1.36 us  [per_device(): lax.all_to_all(copies, ('yh', 'yl'), 0, 0)]
    pallas_call x5 -> x6, Pallas kernels: 18.4 us -> 11.8 us  [call(): pl.pallas_call(kernel, grid_spec=pltpu.PrefetchScalarGridSpec(num_scalar_...]
    all_to_all x1, starting transfers between devices: 8.65 us -> 4.84 us  [per_device(): lax.all_to_all(jnp.broadcast_to(bc_pre.reshape(1, bc_rows, -1), (2 * tp_c...]
    all_to_all x1, waiting for transfers between devices: 11.3 us -> 7.55 us  [per_device(): lax.all_to_all(jnp.broadcast_to(bc_pre.reshape(1, bc_rows, -1), (2 * tp_c...]
    all_to_all x1, waiting for transfers between devices: 7.07 us -> 3.63 us  [per_device(): got = lax.all_to_all(panel, ('x', 'yl'), 0, 0)]
    unnamed x34 -> x38, local copies, waits for them, and re-layouts: 3.86 us -> 7.03 us
    ppermute x1, starting transfers between devices: 2.72 us -> 5.52 us  [per_device(): other = lax.ppermute(own, 'c', [(0, 1), (1, 0)])]
  transfers between devices with their start and end apart: 16 -> 16, of which waited for: 10 -> 13; matrix products, arithmetic and copies ran while one was open for 1% -> 0% of each run, Pallas kernels for 1% -> 2%
where the time goes in v3:
time: 188 us; the launch traced here: 187 us
  starting transfers between devices  78.1 us (42%)
  waiting for transfers between devices  59.2 us (31%)
  Pallas kernels  21.5 us (11%)
  blocking collectives  13.9 us (7%)
  local copies, waits for them, and re-layouts  12.4 us (7%)
    ppermute x3, waiting for transfers between devices, ring(): ahead = lax.ppermute(ahead, axis, forward)  22.2 us
    ppermute x3, starting transfers between devices, ring(): behind = lax.ppermute(behind, axis, backward)  18.5 us
    all_to_all x1, blocking collectives, per_device(): lax.all_to_all(jnp.broadcast_to(dots[None, :, None], shape).reshape(2 * t...  13.9 us
    pallas_call x6, Pallas kernels, call(): pl.pallas_call(kernel, grid_spec=pltpu.PrefetchScalarGridSpec(num_scalar_...  11.8 us
    all_to_all x1, waiting for transfers between devices, per_device(): states = lax.all_to_all(payload, ('z', 'x'), 0, 0)  10.5 us
    pallas_call x1, Pallas kernels, project(): pl.pallas_call(project_kernel, grid_spec=pltpu.PrefetchScalarGridSpec(num...  9.7 us
    ppermute x3, starting transfers between devices, ring(): ahead = lax.ppermute(ahead, axis, forward)  8.87 us
    all_to_all x1, starting transfers between devices, per_device(): lax.all_to_all(copies, ('yh', 'yl'), 0, 0)  7.91 us
  transfers between devices with their start and end apart: 16, of which 13 were waited for; matrix products, arithmetic and copies ran while one was open for 0% of the time, Pallas kernels for 2%

profile of v3, /device:TPU:1, one launch (start us, length us, event | category | flops | bytes accessed | tf_op | source)
XLA Modules:
  0.0 186.8 jit_solution(9881658203849447174)
XLA Ops:
  0.0 1.0 reshape.57
  1.0 0.7 pad_maximum_fusion.2
  1.8 0.1 reshape.60
  1.9 0.1 pad.10.clone
  1.9 0.2 maximum_maximum_fusion
  2.2 0.9 broadcast_in_dim.46
  3.1 5.9 %all-to-all-start = ((bf16[8,72,512]{2,1,0:T(8,128)(2,1)}), bf16[8,72,512]{2,1,0:T(8,128)(2,1)S(1)}, u32[]{:S(2)}, u32[]{:S(2)}) async-start(bf16[8,72,512]{2,1,0:T(8,128)(2,1)} %bitcast.6), calls=%async_computation | async-start | bytes 1179648 | tf_op jit(solution)/shard_map/all_to_all | solution.py:408
  8.9 3.4 %collective-permute-start = (bf16[16,512]{1,0:T(8,128)(2,1)S(1)}, bf16[16,512]{1,0:T(8,128)(2,1)S(1)}, u32[]{:S(2)}, u32[]{:S(2)}) collective-permute-start(bf16[16,512]{1,0:T(8,128)(2,1)S(1)} %slice.15), channel_id=1, source_target_pairs={{0,8},{8,16},{16,24},{24,32},{32,40},{40,48},{48,56},{56,64},{64,7... | collective-permute-start | bytes 49160 | tf_op jit(solution)/shard_map/ppermute | solution.py:381
  12.3 0.9 collective-permute-done
  13.2 3.6 %all-to-all-done = bf16[8,72,512]{2,1,0:T(8,128)(2,1)S(1)} async-done(((bf16[8,72,512]{2,1,0:T(8,128)(2,1)}), bf16[8,72,512]{2,1,0:T(8,128)(2,1)S(1)}, u32[]{:S(2)}, u32[]{:S(2)}) %all-to-all-start) | async-done | bytes 589856 | tf_op jit(solution)/shard_map/all_to_all | solution.py:408
  16.8 1.6 broadcast_in_dim.44
  18.4 7.9 %all-to-all-start.1 = ((bf16[8,272,512]{2,1,0:T(8,128)(2,1)}), bf16[8,272,512]{2,1,0:T(8,128)(2,1)}, u32[]{:S(2)}, u32[]{:S(2)}) async-start(bf16[8,272,512]{2,1,0:T(8,128)(2,1)} %broadcast_in_dim.44), calls=%async_computation.1 | async-start | bytes 4456448 | tf_op jit(solution)/shard_map/all_to_all | solution.py:417
  26.4 0.1 reshape.64
  26.5 0.1 reshape.65
  26.7 4.0 %collective-permute-start.1 = (bf16[536,512]{1,0:T(8,128)(2,1)S(1)}, bf16[536,512]{1,0:T(8,128)(2,1)S(1)}, u32[]{:S(2)}, u32[]{:S(2)}) collective-permute-start(bf16[536,512]{1,0:T(8,128)(2,1)S(1)} %pad_maximum_fusion.w0), channel_id=1, source_target_pairs={{0,64},{64,128},{128,192},{192,256},{256,320},{320,384},{384,448},... | collective-permute-start | bytes 1646600 | tf_op jit(solution)/shard_map/ppermute | solution.py:353
  30.7 8.7 %collective-permute-start.2 = (bf16[536,512]{1,0:T(8,128)(2,1)S(1)}, bf16[536,512]{1,0:T(8,128)(2,1)S(1)}, u32[]{:S(2)}, u32[]{:S(2)}) collective-permute-start(bf16[536,512]{1,0:T(8,128)(2,1)S(1)} %pad_maximum_fusion.w0), channel_id=1, source_target_pairs={{0,448},{64,0},{128,64},{192,128},{256,192},{320,256},{384,320},{4... | collective-permute-start | bytes 1646600 | tf_op jit(solution)/shard_map/ppermute | solution.py:354
  39.4 8.5 %collective-permute-done.1.w1 = bf16[536,512]{1,0:T(8,128)(2,1)S(1)} collective-permute-done((bf16[536,512]{1,0:T(8,128)(2,1)S(1)}, bf16[536,512]{1,0:T(8,128)(2,1)S(1)}, u32[]{:S(2)}, u32[]{:S(2)}) %collective-permute-start.1) | collective-permute-done | bytes 548896 | tf_op jit(solution)/shard_map/ppermute | solution.py:353
  47.9 0.8 collective-permute-done.2.w2
  48.7 1.9 %collective-permute-start.3 = (bf16[536,512]{1,0:T(8,128)(2,1)S(1)}, bf16[536,512]{1,0:T(8,128)(2,1)S(1)}, u32[]{:S(2)}, u32[]{:S(2)}) collective-permute-start(bf16[536,512]{1,0:T(8,128)(2,1)S(1)} %collective-permute-done.1.w1), channel_id=1, source_target_pairs={{0,64},{64,128},{128,192},{192,256},{256,320},{320,384},{384,448},... | collective-permute-start | bytes 1646600 | tf_op jit(solution)/shard_map/ppermute | solution.py:353
  50.6 5.4 %collective-permute-start.4 = (bf16[536,512]{1,0:T(8,128)(2,1)S(1)}, bf16[536,512]{1,0:T(8,128)(2,1)S(1)}, u32[]{:S(2)}, u32[]{:S(2)}) collective-permute-start(bf16[536,512]{1,0:T(8,128)(2,1)S(1)} %collective-permute-done.2.w2), channel_id=1, source_target_pairs={{0,448},{64,0},{128,64},{192,128},{256,192},{320,256},{384,320},{4... | collective-permute-start | bytes 1646600 | tf_op jit(solution)/shard_map/ppermute | solution.py:354
  56.0 7.7 %collective-permute-done.3.w3 = bf16[536,512]{1,0:T(8,128)(2,1)S(1)} collective-permute-done((bf16[536,512]{1,0:T(8,128)(2,1)S(1)}, bf16[536,512]{1,0:T(8,128)(2,1)S(1)}, u32[]{:S(2)}, u32[]{:S(2)}) %collective-permute-start.3) | collective-permute-done | bytes 548896 | tf_op jit(solution)/shard_map/ppermute | solution.py:353
  63.7 0.8 collective-permute-done.4.w4
  64.5 3.0 %collective-permute-start.5 = (bf16[536,512]{1,0:T(8,128)(2,1)S(1)}, bf16[536,512]{1,0:T(8,128)(2,1)S(1)}, u32[]{:S(2)}, u32[]{:S(2)}) collective-permute-start(bf16[536,512]{1,0:T(8,128)(2,1)S(1)} %collective-permute-done.3.w3), channel_id=1, source_target_pairs={{0,64},{64,128},{128,192},{192,256},{256,320},{320,384},{384,448},... | collective-permute-start | bytes 1646600 | tf_op jit(solution)/shard_map/ppermute | solution.py:353
  67.5 4.4 %collective-permute-start.6 = (bf16[536,512]{1,0:T(8,128)(2,1)S(1)}, bf16[536,512]{1,0:T(8,128)(2,1)S(1)}, u32[]{:S(2)}, u32[]{:S(2)}) collective-permute-start(bf16[536,512]{1,0:T(8,128)(2,1)S(1)} %collective-permute-done.4.w4), channel_id=1, source_target_pairs={{0,448},{64,0},{128,64},{192,128},{256,192},{320,256},{384,320},{4... | collective-permute-start | bytes 1646600 | tf_op jit(solution)/shard_map/ppermute | solution.py:354
  71.9 0.8 copy-done
  72.7 6.1 %collective-permute-done.5.w5 = bf16[536,512]{1,0:T(8,128)(2,1)S(1)} collective-permute-done((bf16[536,512]{1,0:T(8,128)(2,1)S(1)}, bf16[536,512]{1,0:T(8,128)(2,1)S(1)}, u32[]{:S(2)}, u32[]{:S(2)}) %collective-permute-start.5) | collective-permute-done | bytes 548896 | tf_op jit(solution)/shard_map/ppermute | solution.py:353
  78.8 0.8 collective-permute-done.6.w6
  79.5 1.4 all-to-all-done.1
  80.9 5.5 %collective-permute-start.7 = (bf16[4,2,272,512]{3,2,1,0:T(8,128)(2,1)}, bf16[4,2,272,512]{3,2,1,0:T(8,128)(2,1)}, u32[]{:S(2)}, u32[]{:S(2)}) collective-permute-start(bf16[4,2,272,512]{3,2,1,0:T(8,128)(2,1)} %bitcast.7.own_ref), channel_id=1, source_target_pairs={{0,1},{1,0},{2,3},{3,2},{4,5},{5,4},{6,7},{7,6},{8,9},{9,8},{10,11... | collective-permute-start | bytes 6684680 | tf_op jit(solution)/shard_map/ppermute | solution.py:421
  86.5 2.8 %collective-permute-start.8 = (bf16[272,512]{1,0:T(8,128)(2,1)S(1)}, bf16[272,512]{1,0:T(8,128)(2,1)S(1)}, u32[]{:S(2)}, u32[]{:S(2)}) collective-permute-start(bf16[272,512]{1,0:T(8,128)(2,1)S(1)} %slice.18), channel_id=1, source_target_pairs={{0,64},{64,128},{128,192},{192,256},{256,320},{320,384},{384,448},... | collective-permute-start | bytes 835592 | tf_op jit(solution)/shard_map/ppermute | solution.py:359
  89.4 6.7 %collective-permute-start.9 = (bf16[264,512]{1,0:T(8,128)(2,1)S(1)}, bf16[264,512]{1,0:T(8,128)(2,1)S(1)}, u32[]{:S(2)}, u32[]{:S(2)}) collective-permute-start(bf16[264,512]{1,0:T(8,128)(2,1)S(1)} %slice.19), channel_id=1, source_target_pairs={{0,448},{64,0},{128,64},{192,128},{256,192},{320,256},{384,320},{4... | collective-permute-start | bytes 811016 | tf_op jit(solution)/shard_map/ppermute | solution.py:360
  96.1 0.0 copy-start.14
  96.1 0.0 copy-start.15
  96.2 0.1 pad_add_fusion.where_ref
  96.2 5.7 %collective-permute-done.9.w8 = bf16[264,512]{1,0:T(8,128)(2,1)S(1)} collective-permute-done((bf16[264,512]{1,0:T(8,128)(2,1)S(1)}, bf16[264,512]{1,0:T(8,128)(2,1)S(1)}, u32[]{:S(2)}, u32[]{:S(2)}) %collective-permute-start.9) | collective-permute-done | bytes 270368 | tf_op jit(solution)/shard_map/ppermute | solution.py:360
  102.0 1.1 copy-done.1
  103.0 9.7 %shard_map.127 = (bf16[2,272,512]{2,1,0:T(8,128)(2,1)S(1)}, bf16[16,2,272]{2,1,0:T(2,128)(2,1)S(1)}, f32[8,512]{1,0:T(8,128)S(1)}) custom-call(s32[16]{0:T(128)S(1)} %pad_add_fusion.where_ref, bf16[4,2,272,512]{3,2,1,0:T(8,128)(2,1)} %bitcast.7.own_ref, bf16[4,2,272,512]{3,2,1,0:T(8,128)(2,1)} %collective-permute-done.7.other_ref, ...), custom_call_target="tpu_custom_call" | custom-call | tf_op jit(solution)/shard_map/pallas_call | solution.py:141
  112.8 0.8 copy-done.6
  113.6 0.1 broadcast_in_dim.51
  113.7 0.8 broadcast_in_dim.52
  114.4 4.8 %all-to-all-start.2 = ((bf16[16,16,544]{2,1,0:T(8,128)(2,1)}), bf16[16,16,544]{2,1,0:T(8,128)(2,1)S(1)}, u32[]{:S(2)}, u32[]{:S(2)}) async-start(bf16[16,16,544]{2,1,0:T(8,128)(2,1)} %broadcast_in_dim.52), calls=%async_computation.2 | async-start | bytes 655360 | tf_op jit(solution)/shard_map/all_to_all | solution.py:438
  119.3 0.1 broadcast_in_dim.47
  119.4 0.1 broadcast_in_dim_reshape.3
  119.5 0.1 pad.5.clone
  119.6 0.1 maximum_maximum_fusion.1.chan_ref
  119.6 0.1 copy.29.head_ref
  119.7 1.1 copy-done.7
  120.8 2.3 %shard_map.128 = (bf16[512,512]{1,0:T(8,128)(2,1)S(1)}, f32[8,512]{1,0:T(8,128)S(1)}, f32[8,512]{1,0:T(8,128)S(1)}, bf16[512,512]{1,0:T(8,128)(2,1)S(1)}) custom-call(s32[1]{0:T(128)} %bitcast.mine_ref, bf16[2,272,512]{2,1,0:T(8,128)(2,1)S(1)} %copy-done.7, f32[8,512]{1,0:T(8,128)S(1)} %get-tuple-element.39.dt_ref, f32[4,1024]{1,0:T(4,128)S(1)} %copy-done.8, ...), custom_call_target="tpu_custom_call" | custom-call | flops 1000000000 | bytes 2097152 | tf_op jit(solution)/shard_map/pallas_call | solution.py:35
  123.1 7.6 %all-to-all-done.2 = bf16[16,16,544]{2,1,0:T(8,128)(2,1)S(1)} async-done(((bf16[16,16,544]{2,1,0:T(8,128)(2,1)}), bf16[16,16,544]{2,1,0:T(8,128)(2,1)S(1)}, u32[]{:S(2)}, u32[]{:S(2)}) %all-to-all-start.2) | async-done | bytes 278560 | tf_op jit(solution)/shard_map/all_to_all | solution.py:438
  130.7 0.2 copy.30
  130.9 1.5 shard_map.129
  132.4 1.0 copy-done.4
  133.3 6.2 %all-to-all-start.3 = ((bf16[32,24,128]{2,1,0:T(8,128)(2,1)}), bf16[32,24,128]{2,1,0:T(8,128)(2,1)S(1)}, u32[]{:S(2)}, u32[]{:S(2)}) async-start(bf16[32,24,128]{2,1,0:T(8,128)(2,1)} %get-tuple-element.51), calls=%async_computation.3 | async-start | bytes 393216 | tf_op jit(solution)/shard_map/all_to_all | solution.py:473
  139.5 10.5 %all-to-all-done.3.got_ref = bf16[32,24,128]{2,1,0:T(8,128)(2,1)S(1)} async-done(((bf16[32,24,128]{2,1,0:T(8,128)(2,1)}), bf16[32,24,128]{2,1,0:T(8,128)(2,1)S(1)}, u32[]{:S(2)}, u32[]{:S(2)}) %all-to-all-start.3) | async-done | bytes 196640 | tf_op jit(solution)/shard_map/all_to_all | solution.py:473
  150.1 0.7 shard_map.131
  150.8 4.2 %all-to-all-start.4 = ((bf16[32,16,128]{2,1,0:T(8,128)(2,1)}), bf16[32,16,128]{2,1,0:T(8,128)(2,1)S(1)}, u32[]{:S(2)}, u32[]{:S(2)}) async-start(bf16[32,16,128]{2,1,0:T(8,128)(2,1)} %shard_map.131), calls=%async_computation.4 | async-start | bytes 262144 | tf_op jit(solution)/shard_map/all_to_all | solution.py:481
  155.0 1.2 copy-done.5
  156.2 1.0 copy-done.10
  157.2 2.2 %shard_map.130 = (f32[512,512]{1,0:T(8,128)S(1)}, f32[512,512]{1,0:T(8,128)S(1)}) custom-call(s32[1]{0:T(128)} %bitcast.mine_ref, bf16[512,512]{1,0:T(8,128)(2,1)S(1)} %copy-done.10, bf16[512,256]{1,0:T(8,128)(2,1)S(1)} %get-tuple-element.45.bc_ref, f32[8,512]{1,0:T(8,128)S(1)} %get-tuple-element.43.cum_ref, f32[8,512]{1,0:T(8,128)S(1)} %get-tuple-element.46.step_ref, ...), custom_call_target="tpu_custom_call" | custom-call | flops 1000000000 | bytes 3145728 | tf_op jit(solution)/shard_map/pallas_call | solution.py:35
  159.4 4.9 %all-to-all-done.4 = bf16[32,16,128]{2,1,0:T(8,128)(2,1)S(1)} async-done(((bf16[32,16,128]{2,1,0:T(8,128)(2,1)}), bf16[32,16,128]{2,1,0:T(8,128)(2,1)S(1)}, u32[]{:S(2)}, u32[]{:S(2)}) %all-to-all-start.4) | async-done | bytes 131104 | tf_op jit(solution)/shard_map/all_to_all | solution.py:481
  164.3 3.3 %shard_map.132 = (f32[256,512]{1,0:T(8,128)S(1)}, bf16[256,512]{1,0:T(8,128)(2,1)S(1)}, f32[2,1,256]{2,1,0:T(1,128)S(1)}) custom-call(s32[1]{0:T(128)} %bitcast.mine_ref, f32[512,512]{1,0:T(8,128)S(1)} %get-tuple-element.49.inside_ref, f32[512,512]{1,0:T(8,128)S(1)} %get-tuple-element.50.growth_ref, bf16[512,256]{1,0:T(8,128)(2,1)S(1)} %get-tuple-element.45.bc_ref, ...), custom_call_target="tpu_custom_call" | custom-call | tf_op jit(solution)/shard_map/pallas_call | solution.py:35
  167.6 3.3 %collective-permute-start.10 = (bf16[256,512]{1,0:T(8,128)(2,1)S(1)}, bf16[256,512]{1,0:T(8,128)(2,1)S(1)}, u32[]{:S(2)}, u32[]{:S(2)}) collective-permute-start(bf16[256,512]{1,0:T(8,128)(2,1)S(1)} %get-tuple-element.53), channel_id=1, source_target_pairs={{0,8},{8,0},{1,9},{9,1},{2,10},{10,2},{3,11},{11,3},{4,12},{12,4},... | collective-permute-start | bytes 786440 | tf_op jit(solution)/shard_map/ppermute | solution.py:501
  171.0 13.9 %all_to_all.30 = f32[16,1,256]{2,1,0:T(1,128)S(1)} all-to-all(f32[16,1,256]{2,1,0:T(1,128)S(1)} %broadcast_in_dim.55), channel_id=1, replica_groups=mesh['z'=8,'x'=4,'yl'=2,'yh'=4,'c'=2] {'yh','yl','c'}, dimensions={0} | all-to-all | bytes 32768 | tf_op jit(solution)/shard_map/all_to_all | solution.py:503
  184.9 1.8 shard_map.133
  (50 shorter events, 0.4 us)
Async XLA Ops:
  0.0 8.9 %copy-start.11 = (bf16[256,512]{1,0:T(8,128)(2,1)S(1)}, bf16[256,512]{1,0:T(8,128)(2,1)}, u32[]{:S(2)}) copy-start(bf16[256,512]{1,0:T(8,128)(2,1)} %param.13) | copy-start | bytes 786436
  3.1 13.8 %all-to-all-start = ((bf16[8,72,512]{2,1,0:T(8,128)(2,1)}), bf16[8,72,512]{2,1,0:T(8,128)(2,1)S(1)}, u32[]{:S(2)}, u32[]{:S(2)}) async-start(bf16[8,72,512]{2,1,0:T(8,128)(2,1)} %bitcast.6), calls=%async_computation | async-start | bytes 1179648 | tf_op jit(solution)/shard_map/all_to_all | solution.py:408
  8.9 4.2 %collective-permute-start = (bf16[16,512]{1,0:T(8,128)(2,1)S(1)}, bf16[16,512]{1,0:T(8,128)(2,1)S(1)}, u32[]{:S(2)}, u32[]{:S(2)}) collective-permute-start(bf16[16,512]{1,0:T(8,128)(2,1)S(1)} %slice.15), channel_id=1, source_target_pairs={{0,8},{8,16},{16,24},{24,32},{32,40},{40,48},{48,56},{56,64},{64,7... | collective-permute-start | bytes 49160 | tf_op jit(solution)/shard_map/ppermute | solution.py:381
  18.4 62.5 %all-to-all-start.1 = ((bf16[8,272,512]{2,1,0:T(8,128)(2,1)}), bf16[8,272,512]{2,1,0:T(8,128)(2,1)}, u32[]{:S(2)}, u32[]{:S(2)}) async-start(bf16[8,272,512]{2,1,0:T(8,128)(2,1)} %broadcast_in_dim.44), calls=%async_computation.1 | async-start | bytes 4456448 | tf_op jit(solution)/shard_map/all_to_all | solution.py:417
  26.3 60.1 %copy-start.17 = (s32[8]{0:T(128)S(1)}, s32[8]{0:T(128)}, u32[]{:S(2)}) copy-start(s32[8]{0:T(128)} %constant.65.clone) | copy-start | bytes 100
  26.7 21.2 %collective-permute-start.1 = (bf16[536,512]{1,0:T(8,128)(2,1)S(1)}, bf16[536,512]{1,0:T(8,128)(2,1)S(1)}, u32[]{:S(2)}, u32[]{:S(2)}) collective-permute-start(bf16[536,512]{1,0:T(8,128)(2,1)S(1)} %pad_maximum_fusion.w0), channel_id=1, source_target_pairs={{0,64},{64,128},{128,192},{192,256},{256,320},{320,384},{384,448},... | collective-permute-start | bytes 1646600 | tf_op jit(solution)/shard_map/ppermute | solution.py:353
  30.7 18.0 %collective-permute-start.2 = (bf16[536,512]{1,0:T(8,128)(2,1)S(1)}, bf16[536,512]{1,0:T(8,128)(2,1)S(1)}, u32[]{:S(2)}, u32[]{:S(2)}) collective-permute-start(bf16[536,512]{1,0:T(8,128)(2,1)S(1)} %pad_maximum_fusion.w0), channel_id=1, source_target_pairs={{0,448},{64,0},{128,64},{192,128},{256,192},{320,256},{384,320},{4... | collective-permute-start | bytes 1646600 | tf_op jit(solution)/shard_map/ppermute | solution.py:354
  48.7 15.0 %collective-permute-start.3 = (bf16[536,512]{1,0:T(8,128)(2,1)S(1)}, bf16[536,512]{1,0:T(8,128)(2,1)S(1)}, u32[]{:S(2)}, u32[]{:S(2)}) collective-permute-start(bf16[536,512]{1,0:T(8,128)(2,1)S(1)} %collective-permute-done.1.w1), channel_id=1, source_target_pairs={{0,64},{64,128},{128,192},{192,256},{256,320},{320,384},{384,448},... | collective-permute-start | bytes 1646600 | tf_op jit(solution)/shard_map/ppermute | solution.py:353
  50.6 13.9 %collective-permute-start.4 = (bf16[536,512]{1,0:T(8,128)(2,1)S(1)}, bf16[536,512]{1,0:T(8,128)(2,1)S(1)}, u32[]{:S(2)}, u32[]{:S(2)}) collective-permute-start(bf16[536,512]{1,0:T(8,128)(2,1)S(1)} %collective-permute-done.2.w2), channel_id=1, source_target_pairs={{0,448},{64,0},{128,64},{192,128},{256,192},{320,256},{384,320},{4... | collective-permute-start | bytes 1646600 | tf_op jit(solution)/shard_map/ppermute | solution.py:354
  64.5 14.2 %collective-permute-start.5 = (bf16[536,512]{1,0:T(8,128)(2,1)S(1)}, bf16[536,512]{1,0:T(8,128)(2,1)S(1)}, u32[]{:S(2)}, u32[]{:S(2)}) collective-permute-start(bf16[536,512]{1,0:T(8,128)(2,1)S(1)} %collective-permute-done.3.w3), channel_id=1, source_target_pairs={{0,64},{64,128},{128,192},{192,256},{256,320},{320,384},{384,448},... | collective-permute-start | bytes 1646600 | tf_op jit(solution)/shard_map/ppermute | solution.py:353
  67.5 12.0 %collective-permute-start.6 = (bf16[536,512]{1,0:T(8,128)(2,1)S(1)}, bf16[536,512]{1,0:T(8,128)(2,1)S(1)}, u32[]{:S(2)}, u32[]{:S(2)}) collective-permute-start(bf16[536,512]{1,0:T(8,128)(2,1)S(1)} %collective-permute-done.4.w4), channel_id=1, source_target_pairs={{0,448},{64,0},{128,64},{192,128},{256,192},{320,256},{384,320},{4... | collective-permute-start | bytes 1646600 | tf_op jit(solution)/shard_map/ppermute | solution.py:354
  71.9 0.8 copy-start
  80.9 21.1 %collective-permute-start.7 = (bf16[4,2,272,512]{3,2,1,0:T(8,128)(2,1)}, bf16[4,2,272,512]{3,2,1,0:T(8,128)(2,1)}, u32[]{:S(2)}, u32[]{:S(2)}) collective-permute-start(bf16[4,2,272,512]{3,2,1,0:T(8,128)(2,1)} %bitcast.7.own_ref), channel_id=1, source_target_pairs={{0,1},{1,0},{2,3},{3,2},{4,5},{5,4},{6,7},{7,6},{8,9},{9,8},{10,11... | collective-permute-start | bytes 6684680 | tf_op jit(solution)/shard_map/ppermute | solution.py:421
  86.5 15.5 %collective-permute-start.8 = (bf16[272,512]{1,0:T(8,128)(2,1)S(1)}, bf16[272,512]{1,0:T(8,128)(2,1)S(1)}, u32[]{:S(2)}, u32[]{:S(2)}) collective-permute-start(bf16[272,512]{1,0:T(8,128)(2,1)S(1)} %slice.18), channel_id=1, source_target_pairs={{0,64},{64,128},{128,192},{192,256},{256,320},{320,384},{384,448},... | collective-permute-start | bytes 835592 | tf_op jit(solution)/shard_map/ppermute | solution.py:359
  89.4 12.6 %collective-permute-start.9 = (bf16[264,512]{1,0:T(8,128)(2,1)S(1)}, bf16[264,512]{1,0:T(8,128)(2,1)S(1)}, u32[]{:S(2)}, u32[]{:S(2)}) collective-permute-start(bf16[264,512]{1,0:T(8,128)(2,1)S(1)} %slice.19), channel_id=1, source_target_pairs={{0,448},{64,0},{128,64},{192,128},{256,192},{320,256},{384,320},{4... | collective-permute-start | bytes 811016 | tf_op jit(solution)/shard_map/ppermute | solution.py:360
  96.1 23.2 %copy-start.14 = (f32[16]{0:T(128)S(1)}, f32[16]{0:T(128)}, u32[]{:S(2)}) copy-start(f32[16]{0:T(128)} %param.21) | copy-start | bytes 196
  96.1 23.4 %copy-start.15 = (f32[16]{0:T(128)S(1)}, f32[16]{0:T(128)}, u32[]{:S(2)}) copy-start(f32[16]{0:T(128)} %param.20) | copy-start | bytes 196
  96.1 23.4 %copy-start.16 = (f32[16]{0:T(128)S(1)}, f32[16]{0:T(128)}, u32[]{:S(2)}) copy-start(f32[16]{0:T(128)} %param.19) | copy-start | bytes 196
  102.0 1.1 copy-start.1
  103.0 16.5 %copy-start.12 = (f32[1024]{0:T(1024)S(1)}, f32[1024]{0:T(1024)}, u32[]{:S(2)}) copy-start(f32[1024]{0:T(1024)} %param.24) | copy-start | bytes 12292
  103.0 16.5 %copy-start.13 = (f32[1024]{0:T(1024)S(1)}, f32[1024]{0:T(1024)}, u32[]{:S(2)}) copy-start(f32[1024]{0:T(1024)} %param.22) | copy-start | bytes 12292
  103.0 16.7 %copy-start.8 = (f32[4,1024]{1,0:T(4,128)S(1)}, f32[4,1024]{1,0:T(4,128)}, u32[]{:S(2)}) copy-start(f32[4,1024]{1,0:T(4,128)} %conv_ref.2) | copy-start | bytes 49156
  112.8 0.8 copy-start.6
  114.4 16.3 %all-to-all-start.2 = ((bf16[16,16,544]{2,1,0:T(8,128)(2,1)}), bf16[16,16,544]{2,1,0:T(8,128)(2,1)S(1)}, u32[]{:S(2)}, u32[]{:S(2)}) async-start(bf16[16,16,544]{2,1,0:T(8,128)(2,1)} %broadcast_in_dim.52), calls=%async_computation.2 | async-start | bytes 655360 | tf_op jit(solution)/shard_map/all_to_all | solution.py:438
  119.3 11.6 %copy-start.3 = (f32[4,256]{1,0:T(4,128)S(1)}, f32[4,256]{1,0:T(4,128)}, u32[]{:S(2)}) copy-start(f32[4,256]{1,0:T(4,128)} %conv_ref.3) | copy-start | bytes 12292
  119.7 1.1 copy-start.7
  120.8 29.3 %copy-start.2 = (f32[16,64,128]{2,1,0:T(8,128)S(1)}, f32[16,64,128]{2,1,0:T(8,128)}, u32[]{:S(2)}) copy-start(f32[16,64,128]{2,1,0:T(8,128)} %param.23) | copy-start | bytes 1572868
  123.1 7.7 %copy-start.9 = (bf16[512,512]{1,0:T(8,128)(2,1)}, bf16[512,512]{1,0:T(8,128)(2,1)S(1)}, u32[]{:S(2)}) copy-start(bf16[512,512]{1,0:T(8,128)(2,1)S(1)} %get-tuple-element.41.x_ref) | copy-start | bytes 1572868
  132.4 1.0 copy-start.4
  133.3 16.7 %all-to-all-start.3 = ((bf16[32,24,128]{2,1,0:T(8,128)(2,1)}), bf16[32,24,128]{2,1,0:T(8,128)(2,1)S(1)}, u32[]{:S(2)}, u32[]{:S(2)}) async-start(bf16[32,24,128]{2,1,0:T(8,128)(2,1)} %get-tuple-element.51), calls=%async_computation.3 | async-start | bytes 393216 | tf_op jit(solution)/shard_map/all_to_all | solution.py:473
  150.8 13.5 %all-to-all-start.4 = ((bf16[32,16,128]{2,1,0:T(8,128)(2,1)}), bf16[32,16,128]{2,1,0:T(8,128)(2,1)S(1)}, u32[]{:S(2)}, u32[]{:S(2)}) async-start(bf16[32,16,128]{2,1,0:T(8,128)(2,1)} %shard_map.131), calls=%async_computation.4 | async-start | bytes 262144 | tf_op jit(solution)/shard_map/all_to_all | solution.py:481
  155.0 1.2 copy-start.5
  156.2 1.0 copy-start.10
  167.6 17.4 %collective-permute-start.10 = (bf16[256,512]{1,0:T(8,128)(2,1)S(1)}, bf16[256,512]{1,0:T(8,128)(2,1)S(1)}, u32[]{:S(2)}, u32[]{:S(2)}) collective-permute-start(bf16[256,512]{1,0:T(8,128)(2,1)S(1)} %get-tuple-element.53), channel_id=1, source_target_pairs={{0,8},{8,0},{1,9},{9,1},{2,10},{10,2},{3,11},{11,3},{4,12},{12,4},... | collective-permute-start | bytes 786440 | tf_op jit(solution)/shard_map/ppermute | solution.py:501

commit v4 on v3

--- a/solution.py
+++ b/solution.py
@@ -13,6 +13,7 @@
 N = 128
 HALO = 16
 HEAD = 64
+ALL_VMEM = 67043328
 HIGHEST = lax.Precision.HIGHEST
 
 SEQ = ("z", "x", "yl")
@@ -42,7 +43,7 @@
             scratch_shapes=list(scratch),
         ),
         out_shape=outs,
-        compiler_params=pltpu.CompilerParams(vmem_limit_bytes=48 * 1024 * 1024),
+        compiler_params=pltpu.CompilerParams(vmem_limit_bytes=20 * 1024 * 1024),
         cost_estimate=pl.CostEstimate(
             flops=flops, bytes_accessed=bytes_accessed, transcendentals=0
         ),
@@ -77,92 +78,122 @@
     return jnp.where(column // (channels // heads) == row, 1.0, 0.0).astype(jnp.bfloat16)
 
 
+def panel_kernel(x_ref, bc_ref, dt_ref, panel_ref, side_ref):
+    k_rows, channels = x_ref.shape
+    half, quarter = channels // 2, channels // 4
+    bc_rows, heads = bc_ref.shape[1] // 2, dt_ref.shape[1] // 2
+    row = lax.broadcasted_iota(jnp.int32, (k_rows, k_rows), 0)
+    column = lax.broadcasted_iota(jnp.int32, (k_rows, k_rows), 1)
+    same = jnp.where(row == column, 1.0, 0.0).astype(jnp.bfloat16)
+    bc = dot(bc_ref[...], same, ((0,), (0,))).astype(jnp.bfloat16)
+    dt = dot(dt_ref[...], same, ((0,), (0,)))
+    small = bc_rows + heads
+    for part in range(2):
+        top = x_ref[:, part * half : part * half + quarter]
+        rest = x_ref[:, part * half + quarter : (part + 1) * half]
+        narrow = jnp.concatenate(
+            [
+                bc[part * bc_rows : (part + 1) * bc_rows].astype(jnp.float32),
+                dt[part * heads : (part + 1) * heads],
+            ],
+            0,
+        )
+        narrow = jnp.concatenate([narrow, jnp.zeros((small, quarter - k_rows), jnp.float32)], 1)
+        narrow = narrow.astype(jnp.bfloat16)
+        for at in range(part, panel_ref.shape[0], 2):
+            panel_ref[at, 0:k_rows] = top
+            panel_ref[at, k_rows:] = narrow
+        for at in range(part, side_ref.shape[0], 2):
+            side_ref[at] = rest
+
+
 def project_kernel(
-    where_ref, own_ref, other_ref, w0, w1, w2, w3, w4, w5, w6, w7, w8,
-    x_ref, bc_ref, dt_ref, weights, acc, small, sem,
+    where_ref, feats_ref, side_ref, w0, w1, w2, w3, w4, w5, w6, w7, w8,
+    x_ref, bc_ref, dt_ref, feats, first, second, acc, small, sem,
 ):
-    step = pl.program_id(0)
-    blocks = weights.shape[0]
-    channels = x_ref.shape[2]
+    blocks = first.shape[0]
     bc_rows, dt_rows = bc_ref.shape[0], dt_ref.shape[0]
     rows = x_ref.shape[1]
+    depth = feats.shape[3]
+    half = first.shape[2]
+    flat = dt_rows + bc_rows
     tokens = rows - HALO
     cut = w7.shape[0]
-    copies = [
-        [pltpu.make_async_copy(ref, weights.at[at], sem.at[at])]
-        for at, ref in enumerate((w0, w1, w2, w3, w4, w5, w6))
-    ]
-    copies.append(
-        [
-            pltpu.make_async_copy(w7, weights.at[7, 0:cut], sem.at[7]),
-            pltpu.make_async_copy(w8, weights.at[7, cut:], sem.at[8]),
-        ]
-    )
-
-    @pl.when(step == 0)
-    def _():
-        for group in copies:
-            for copy in group:
-                copy.start()
-        acc[...] = jnp.zeros_like(acc)
-        small[...] = jnp.zeros_like(small)
-
-    for at, group in enumerate(copies):
-
-        @pl.when(step == at)
-        def _():
-            for copy in group:
-                copy.wait()
-
-    mine = where_ref[blocks + step] == 1
-    for half in range(2):
-        feats = jnp.where(mine, own_ref[0, half], other_ref[0, half])
-        acc[half] += dot(feats, weights[step, 0:channels], ((1,), (0,)))
-        small[half, 0:rows, 0 : bc_rows + dt_rows] += dot(
-            feats, weights[step, channels:], ((1,), (1,))
-        )
-
-    @pl.when(step == blocks - 1)
-    def _():
-        x_ref[...] = acc[...].astype(jnp.bfloat16)
-        for half in range(2):
-            turned = small[half].T
-            bc_ref[:, half, :] = turned[0:bc_rows, 0:rows].astype(jnp.bfloat16)
-            turned = small[half, HALO:rows].T
-            dt_ref[:, half * tokens : (half + 1) * tokens] = turned[bc_rows : bc_rows + dt_rows]
-
-
-def project(where, own, other, weights, bc_rows, dt_rows):
-    _, _, rows, depth = own.shape
-    height, channels = weights[0].shape
+    parts = ((0, w0), (1, w1), (2, w2), (3, w3), (4, w4), (5, w5), (6, w6))
+    for step in range(blocks):
+        at = where_ref[step]
+        pltpu.make_async_copy(
+            feats_ref.at[at // 2, :, at % 2], feats.at[step], sem.at[0, step]
+        ).start()
+        if step < blocks - 1:
+            pltpu.make_async_copy(parts[step][1], first.at[step], sem.at[1, step]).start()
+        else:
+            pltpu.make_async_copy(w7, first.at[step, 0:cut], sem.at[1, step]).start()
+            pltpu.make_async_copy(w8, first.at[step, cut:], sem.at[1, step + 1]).start()
+        pltpu.make_async_copy(
+            side_ref.at[:, at], second.at[step], sem.at[2, step]
+        ).start()
+    small[...] = jnp.zeros_like(small)
+    for step in range(blocks):
+        pltpu.make_async_copy(feats_ref.at[0, :, 0], feats.at[step], sem.at[0, step]).wait()
+        if step < blocks - 1:
+            pltpu.make_async_copy(parts[step][1], first.at[step], sem.at[1, step]).wait()
+        else:
+            pltpu.make_async_copy(w7, first.at[step, 0:cut], sem.at[1, step]).wait()
+            pltpu.make_async_copy(w8, first.at[step, cut:], sem.at[1, step + 1]).wait()
+        pltpu.make_async_copy(side_ref.at[:, 0], second.at[step], sem.at[2, step]).wait()
+        for part in range(2):
+            values = feats[step, part]
+            left = dot(values, first[step, 0:depth], ((1,), (0,)))
+            right = dot(values, second[step].reshape(depth, half), ((1,), (0,)))
+            if step:
+                acc[part, :, 0:half] += left
+                acc[part, :, half:] += right
+            else:
+                acc[part, :, 0:half] = left
+                acc[part, :, half:] = right
+            narrow = small[part, 0:rows, 0:flat]
+            for at in range(depth // half):
+                narrow = narrow + dot(
+                    values[:, at * half : (at + 1) * half],
+                    first[step, depth + at * flat : depth + (at + 1) * flat],
+                    ((1,), (1,)),
+                )
+            small[part, 0:rows, 0:flat] = narrow
+    x_ref[...] = acc[...].astype(jnp.bfloat16)
+    for part in range(2):
+        turned = small[part].T
+        bc_ref[:, part, :] = turned[0:bc_rows, 0:rows].astype(jnp.bfloat16)
+        turned = small[part, HALO:rows].T
+        dt_ref[:, part * tokens : (part + 1) * tokens] = turned[bc_rows:flat]
+
+
+def project(where, tokens_by_block, side, weights, bc_rows, dt_rows):
+    _, _, _, rows, depth = tokens_by_block.shape
+    height, half = weights[0].shape
     blocks = len(weights) - 1
     tokens = rows - HALO
-    feat = pl.BlockSpec((1, 2, rows, depth), lambda j, m: (m[j], 0, 0, 0))
+    outs = [
+        jax.ShapeDtypeStruct((2, rows, 2 * half), jnp.bfloat16),
+        jax.ShapeDtypeStruct((bc_rows, 2, rows), jnp.bfloat16),
+        jax.ShapeDtypeStruct((dt_rows, 2 * tokens), jnp.float32),
+    ]
     return pl.pallas_call(
         project_kernel,
-        grid_spec=pltpu.PrefetchScalarGridSpec(
-            num_scalar_prefetch=1,
-            grid=(blocks,),
-            in_specs=[feat, feat] + [pl.BlockSpec(memory_space=pl.ANY)] * len(weights),
-            out_specs=[
-                pl.BlockSpec((2, rows, channels), lambda j, m: (0, 0, 0)),
-                pl.BlockSpec((bc_rows, 2, rows), lambda j, m: (0, 0, 0)),
-                pl.BlockSpec((dt_rows, 2 * tokens), lambda j, m: (0, 0)),
-            ],
-            scratch_shapes=[
-                pltpu.VMEM((blocks, height, channels), jnp.bfloat16),
-                pltpu.VMEM((2, rows, channels), jnp.float32),
-                pltpu.VMEM((2, (rows + 127) // 128 * 128, 128), jnp.float32),
-                pltpu.SemaphoreType.DMA((blocks + 1,)),
-            ],
-        ),
-        out_shape=[
-            jax.ShapeDtypeStruct((2, rows, channels), jnp.bfloat16),
-            jax.ShapeDtypeStruct((bc_rows, 2, rows), jnp.bfloat16),
-            jax.ShapeDtypeStruct((dt_rows, 2 * tokens), jnp.float32),
+        in_specs=[pl.BlockSpec(memory_space=pltpu.SMEM)]
+        + [pl.BlockSpec(memory_space=pltpu.HBM)] * (len(weights) + 2),
+        out_specs=[pl.BlockSpec(memory_space=pltpu.VMEM)] * 3,
+        scratch_shapes=[
+            pltpu.VMEM((blocks, 2, rows, depth), jnp.bfloat16),
+            pltpu.VMEM((blocks, height, half), jnp.bfloat16),
+            pltpu.VMEM((blocks,) + (side.shape[0],) + side.shape[2:], jnp.bfloat16),
+            pltpu.VMEM((2, rows, 2 * half), jnp.float32),
+            pltpu.VMEM((2, (rows + 127) // 128 * 128, 128), jnp.float32),
+            pltpu.SemaphoreType.DMA((3, blocks + 1)),
         ],
-        compiler_params=pltpu.CompilerParams(vmem_limit_bytes=48 * 1024 * 1024),
-    )(where, own, other, *weights)
+        out_shape=outs,
+        compiler_params=pltpu.CompilerParams(vmem_limit_bytes=ALL_VMEM),
+    )(where, tokens_by_block, side, *weights)
 
 
 def convolved(values, taps, tokens):
@@ -374,7 +405,7 @@
     small = bc_rows + heads
     seq_count = SIZES["z"] * SIZES["x"] * SIZES["yl"]
     tp_count = SIZES["yh"] * SIZES["c"]
-    z, core = lax.axis_index("z"), lax.axis_index("c")
+    z = lax.axis_index("z")
     mine = lax.axis_index("yl").astype(jnp.int32).reshape(1)
     f32, bf16 = jnp.float32, jnp.bfloat16
 
@@ -382,44 +413,32 @@
         tokens[local - HALO :], SEQ, [(i, i + 1) for i in range(seq_count - 1)]
     )
     extended = jnp.concatenate([earlier, tokens], 0)
-    line = SIZES["yh"] * 2
-    copies = jnp.broadcast_to(extended[None], (line,) + extended.shape)
-
+    feats = lax.all_gather(extended, ("yh", "yl", "c"), axis=0, tiled=False).reshape(
+        SIZES["yh"], 2, SIZES["c"], local + HALO, width
+    )
+
+    quarter = half // 2
     fan = SIZES["x"] * SIZES["yl"]
-    packed_rows = small * k_rows // half
-    packed = jnp.concatenate(
-        [
-            bc_weight.reshape(k_rows, 2, bc_rows).transpose(1, 2, 0),
-            dt_weight.reshape(k_rows, 2, heads).transpose(1, 2, 0),
+    panel, side = pl.pallas_call(
+        panel_kernel,
+        out_shape=[
+            jax.ShapeDtypeStruct((fan, k_rows + small, quarter), bf16),
+            jax.ShapeDtypeStruct((2 * SIZES["z"], k_rows, quarter), bf16),
         ],
-        1,
-    ).reshape(2, packed_rows, half)
-    panel = jnp.concatenate(
-        [
-            x_weight.reshape(k_rows, 2, half).transpose(1, 0, 2),
-            packed,
-            jnp.zeros((2, -packed_rows % 8, half), bf16),
-        ],
-        1,
-    )
-    panel = jnp.broadcast_to(panel[None], (SIZES["x"],) + panel.shape).reshape(
-        fan, panel.shape[1], half
-    )
+        compiler_params=pltpu.CompilerParams(vmem_limit_bytes=ALL_VMEM),
+    )(x_weight, bc_weight, dt_weight)
     got = lax.all_to_all(panel, ("x", "yl"), 0, 0)
-    tall = got[:, :k_rows].reshape(fan * k_rows, half)
-    flat = got[:, k_rows : k_rows + packed_rows].reshape(
-        fan, packed_rows, half // k_rows, k_rows
-    )
-    flat = flat.transpose(1, 2, 0, 3).reshape(small, fan * k_rows)
-    pieces, offsets = ring(jnp.concatenate([tall, flat], 0), "z")
-
-    copies = lax.optimization_barrier((copies, got))[0]
-    own = lax.all_to_all(copies, ("yh", "yl"), 0, 0).reshape(
-        SIZES["yh"], 2, local + HALO, width
-    )
-    own = lax.optimization_barrier((own, pieces[5], pieces[6]))[0]
-    other = lax.ppermute(own, "c", [(0, 1), (1, 0)])
-
+    tall = got[:, :k_rows].reshape(fan * k_rows, quarter)
+    flat = got[:, k_rows:, :k_rows].reshape(2, fan // 2, small, k_rows)
+    flat = flat.transpose(0, 2, 1, 3).reshape(2 * small, quarter)
+    block = jnp.concatenate([tall, flat], 0)
+    pieces, offsets = ring(block, "z")
+    side = lax.optimization_barrier((side, block))[0]
+    side = lax.all_to_all(side, ("z", "yl"), 0, 0).reshape(SIZES["z"], 2 * k_rows, quarter)
+    side = lax.optimization_barrier((side, pieces[1], pieces[2]))[0]
+    side = lax.all_to_all(
+        jnp.broadcast_to(side[None], (SIZES["x"],) + side.shape), "x", 0, 0
+    )
     channel_rows = jnp.concatenate(
         [
             jnp.repeat(d_skip, HEAD)[None], norm_gain[None], steer[None],
@@ -432,9 +451,7 @@
         (channel_rows, head_columns, pieces[3])
     )
     source = (z + jnp.array(offsets, jnp.int32)) % SIZES["z"]
-    where = jnp.concatenate([source // 2, (source % 2 == core).astype(jnp.int32)])
-
-    x_pre, bc_pre, dt_raw = project(where, own, other, pieces, bc_rows, heads)
+    x_pre, bc_pre, dt_raw = project(source, feats, side, pieces, bc_rows, heads)
     bc_all = lax.all_to_all(
         jnp.broadcast_to(
             bc_pre.reshape(1, bc_rows, -1), (2 * tp_count, bc_rows, 2 * (local + HALO))

time: 188 us -> 202 us (1.074)
  between operations: 0.42 us -> 13.7 us
  waiting for transfers between devices: 59.2 us -> 46.4 us
  blocking collectives: 13.9 us -> 26.2 us
  starting transfers between devices: 78.1 us -> 73.8 us
  local copies, waits for them, and re-layouts: 12.4 us -> 15.3 us
  other arithmetic: 1.2 us -> 3.75 us
    all_to_all x0 -> x1, blocking collectives: none -> 12.2 us  [per_device(): got = lax.all_to_all(panel, ('x', 'yl'), 0, 0)]
    ppermute x3, starting transfers between devices: 18.5 us -> 9.78 us  [ring(): behind = lax.ppermute(behind, axis, backward)]
    all_to_all x1, starting transfers between devices: 4.84 us -> 11.1 us  [per_device(): lax.all_to_all(jnp.broadcast_to(bc_pre.reshape(1, bc_rows, -1), (2 * tp_c...]
    ppermute x1 -> x0, starting transfers between devices: 5.52 us -> none  [per_device(): other = lax.ppermute(own, 'c', [(0, 1), (1, 0)])]
    all_to_all x2, waiting for transfers between devices: 4.99 us -> 0.01 us  [the longest x1 0.01 us: per_device(): lax.all_to_all(side, ('z', 'yl'), 0, 0)]
    ppermute x1, waiting for transfers between devices: 5.75 us -> 1.38 us  [ring(): pieces.append(lax.ppermute(behind[cut:], axis, backward))]
    all_to_all x1, waiting for transfers between devices: 7.55 us -> 3.36 us  [per_device(): lax.all_to_all(jnp.broadcast_to(bc_pre.reshape(1, bc_rows, -1), (2 * tp_c...]
    all_to_all x2, starting transfers between devices: 13.8 us -> 17.4 us  [the longest x1 12.8 us: per_device(): lax.all_to_all(side, ('z', 'yl'), 0, 0)]
  transfers between devices with their start and end apart: 16 -> 16, of which waited for: 13 -> 11; matrix products, arithmetic and copies ran while one was open for 0% -> 4% of each run, Pallas kernels for 2% -> 3%
where the time goes in v4:
time: 202 us; the launch traced here: 201 us
  starting transfers between devices  73.8 us (37%)
  waiting for transfers between devices  46.4 us (23%)
  blocking collectives  26.2 us (13%)
  Pallas kernels  21.4 us (11%)
  local copies, waits for them, and re-layouts  15.3 us (8%)
  between operations  13.7 us (7%)
  other arithmetic  3.75 us (2%)
    ppermute x3, waiting for transfers between devices, ring(): ahead = lax.ppermute(ahead, axis, forward)  21.1 us
    all_to_all x1, blocking collectives, per_device(): lax.all_to_all(jnp.broadcast_to(dots[None, :, None], shape).reshape(2 * t...  14 us
    all_to_all x1, starting transfers between devices, per_device(): lax.all_to_all(side, ('z', 'yl'), 0, 0)  12.8 us
    all_to_all x1, blocking collectives, per_device(): got = lax.all_to_all(panel, ('x', 'yl'), 0, 0)  12.2 us
    pallas_call x6, Pallas kernels, call(): pl.pallas_call(kernel, grid_spec=pltpu.PrefetchScalarGridSpec(num_scalar_...  11.7 us
    all_to_all x1, starting transfers between devices, per_device(): lax.all_to_all(jnp.broadcast_to(bc_pre.reshape(1, bc_rows, -1), (2 * tp_c...  11.1 us
    all_to_all x1, waiting for transfers between devices, per_device(): states = lax.all_to_all(payload, ('z', 'x'), 0, 0)  10.5 us
    unnamed x42, local copies, waits for them, and re-layouts  10 us
  transfers between devices with their start and end apart: 16, of which 11 were waited for; matrix products, arithmetic and copies ran while one was open for 4% of the time, Pallas kernels for 3%

profile of v4, /device:TPU:1, one launch (start us, length us, event | category | flops | bytes accessed | tf_op | source)
XLA Modules:
  0.0 200.6 jit_solution(756727146647298286)
XLA Ops:
  6.5 0.7 slice.15
  7.3 4.0 %collective-permute-start = (bf16[16,512]{1,0:T(8,128)(2,1)S(1)}, bf16[16,512]{1,0:T(8,128)(2,1)S(1)}, u32[]{:S(2)}, u32[]{:S(2)}) collective-permute-start(bf16[16,512]{1,0:T(8,128)(2,1)S(1)} %slice.15), channel_id=1, source_target_pairs={{0,8},{8,16},{16,24},{24,32},{32,40},{40,48},{48,56},{56,64},{64,7... | collective-permute-start | bytes 49160 | tf_op jit(solution)/shard_map/ppermute | solution.py:412
  11.3 0.9 collective-permute-done
  12.1 1.7 pad_maximum_fusion.1
  13.8 0.0 all-gather.3.cloned.1.call-update
  13.8 1.4 copy.26.bc_ref
  15.2 1.4 copy.27.dt_ref
  16.6 1.9 shard_map.127
  18.5 12.2 %all_to_all.35 = bf16[8,88,256]{2,1,0:T(8,128)(2,1)S(1)} all-to-all(bf16[8,88,256]{2,1,0:T(8,128)(2,1)} %get-tuple-element.33), channel_id=1, replica_groups=mesh['z'=8,'x'=4,'yl'=2,'yh'=4,'c'=2] {'x','yl'}, dimensions={0} | all-to-all | bytes 720896 | tf_op jit(solution)/shard_map/all_to_all | solution.py:430
  30.7 0.1 reshape.47
  30.9 12.8 %all-to-all-start.1 = ((bf16[16,64,256]{2,1,0:T(8,128)(2,1)}), bf16[16,64,256]{2,1,0:T(8,128)(2,1)S(1)}, u32[]{:S(2)}, u32[]{:S(2)}) async-start(bf16[16,64,256]{2,1,0:T(8,128)(2,1)} %get-tuple-element.34), calls=%async_computation.1 | async-start | bytes 1048576 | tf_op jit(solution)/shard_map/all_to_all | solution.py:437
  43.7 3.3 %collective-permute-start.1 = (bf16[560,256]{1,0:T(8,128)(2,1)S(1)}, bf16[560,256]{1,0:T(8,128)(2,1)S(1)}, u32[]{:S(2)}, u32[]{:S(2)}) collective-permute-start(bf16[560,256]{1,0:T(8,128)(2,1)S(1)} %pad_maximum_fusion.w0), channel_id=1, source_target_pairs={{0,64},{64,128},{128,192},{192,256},{256,320},{320,384},{384,448},... | collective-permute-start | bytes 860168 | tf_op jit(solution)/shard_map/ppermute | solution.py:384
  47.0 3.2 %collective-permute-start.2 = (bf16[560,256]{1,0:T(8,128)(2,1)S(1)}, bf16[560,256]{1,0:T(8,128)(2,1)S(1)}, u32[]{:S(2)}, u32[]{:S(2)}) collective-permute-start(bf16[560,256]{1,0:T(8,128)(2,1)S(1)} %pad_maximum_fusion.w0), channel_id=1, source_target_pairs={{0,448},{64,0},{128,64},{192,128},{256,192},{320,256},{384,320},{4... | collective-permute-start | bytes 860168 | tf_op jit(solution)/shard_map/ppermute | solution.py:385
  50.3 13.8 %collective-permute-done.1.w1 = bf16[560,256]{1,0:T(8,128)(2,1)S(1)} collective-permute-done((bf16[560,256]{1,0:T(8,128)(2,1)S(1)}, bf16[560,256]{1,0:T(8,128)(2,1)S(1)}, u32[]{:S(2)}, u32[]{:S(2)}) %collective-permute-start.1) | collective-permute-done | bytes 286752 | tf_op jit(solution)/shard_map/ppermute | solution.py:384
  64.1 0.3 collective-permute-done.2.w2
  64.4 1.6 broadcast_in_dim.35
  66.1 4.6 %all-to-all-start.2 = ((bf16[4,8,128,256]{3,2,1,0:T(8,128)(2,1)}), bf16[4,8,128,256]{3,2,1,0:T(8,128)(2,1)}, u32[]{:S(2)}, u32[]{:S(2)}) async-start(bf16[4,8,128,256]{3,2,1,0:T(8,128)(2,1)} %broadcast_in_dim.35), calls=%async_computation.2 | async-start | bytes 4194304 | tf_op jit(solution)/shard_map/all_to_all | solution.py:439
  70.7 3.8 %collective-permute-start.3 = (bf16[560,256]{1,0:T(8,128)(2,1)S(1)}, bf16[560,256]{1,0:T(8,128)(2,1)S(1)}, u32[]{:S(2)}, u32[]{:S(2)}) collective-permute-start(bf16[560,256]{1,0:T(8,128)(2,1)S(1)} %collective-permute-done.1.w1), channel_id=1, source_target_pairs={{0,64},{64,128},{128,192},{192,256},{256,320},{320,384},{384,448},... | collective-permute-start | bytes 860168 | tf_op jit(solution)/shard_map/ppermute | solution.py:384
  74.5 2.7 %collective-permute-start.4 = (bf16[560,256]{1,0:T(8,128)(2,1)S(1)}, bf16[560,256]{1,0:T(8,128)(2,1)S(1)}, u32[]{:S(2)}, u32[]{:S(2)}) collective-permute-start(bf16[560,256]{1,0:T(8,128)(2,1)S(1)} %collective-permute-done.2.w2), channel_id=1, source_target_pairs={{0,448},{64,0},{128,64},{192,128},{256,192},{320,256},{384,320},{4... | collective-permute-start | bytes 860168 | tf_op jit(solution)/shard_map/ppermute | solution.py:385
  77.2 3.9 %collective-permute-done.3.w3 = bf16[560,256]{1,0:T(8,128)(2,1)S(1)} collective-permute-done((bf16[560,256]{1,0:T(8,128)(2,1)S(1)}, bf16[560,256]{1,0:T(8,128)(2,1)S(1)}, u32[]{:S(2)}, u32[]{:S(2)}) %collective-permute-start.3) | collective-permute-done | bytes 286752 | tf_op jit(solution)/shard_map/ppermute | solution.py:384
  81.1 3.0 %collective-permute-done.4.w4 = bf16[560,256]{1,0:T(8,128)(2,1)S(1)} collective-permute-done((bf16[560,256]{1,0:T(8,128)(2,1)S(1)}, bf16[560,256]{1,0:T(8,128)(2,1)S(1)}, u32[]{:S(2)}, u32[]{:S(2)}) %collective-permute-start.4) | collective-permute-done | bytes 286752 | tf_op jit(solution)/shard_map/ppermute | solution.py:385
  84.0 2.6 %collective-permute-start.5 = (bf16[560,256]{1,0:T(8,128)(2,1)S(1)}, bf16[560,256]{1,0:T(8,128)(2,1)S(1)}, u32[]{:S(2)}, u32[]{:S(2)}) collective-permute-start(bf16[560,256]{1,0:T(8,128)(2,1)S(1)} %collective-permute-done.3.w3), channel_id=1, source_target_pairs={{0,64},{64,128},{128,192},{192,256},{256,320},{320,384},{384,448},... | collective-permute-start | bytes 860168 | tf_op jit(solution)/shard_map/ppermute | solution.py:384
  86.7 3.9 %collective-permute-start.6 = (bf16[560,256]{1,0:T(8,128)(2,1)S(1)}, bf16[560,256]{1,0:T(8,128)(2,1)S(1)}, u32[]{:S(2)}, u32[]{:S(2)}) collective-permute-start(bf16[560,256]{1,0:T(8,128)(2,1)S(1)} %collective-permute-done.4.w4), channel_id=1, source_target_pairs={{0,448},{64,0},{128,64},{192,128},{256,192},{320,256},{384,320},{4... | collective-permute-start | bytes 860168 | tf_op jit(solution)/shard_map/ppermute | solution.py:385
  90.5 3.4 %collective-permute-done.5.w5 = bf16[560,256]{1,0:T(8,128)(2,1)S(1)} collective-permute-done((bf16[560,256]{1,0:T(8,128)(2,1)S(1)}, bf16[560,256]{1,0:T(8,128)(2,1)S(1)}, u32[]{:S(2)}, u32[]{:S(2)}) %collective-permute-start.5) | collective-permute-done | bytes 286752 | tf_op jit(solution)/shard_map/ppermute | solution.py:384
  93.9 0.9 collective-permute-done.6.w6
  94.8 2.4 %collective-permute-start.7 = (bf16[288,256]{1,0:T(8,128)(2,1)S(1)}, bf16[288,256]{1,0:T(8,128)(2,1)S(1)}, u32[]{:S(2)}, u32[]{:S(2)}) collective-permute-start(bf16[288,256]{1,0:T(8,128)(2,1)S(1)} %slice.18), channel_id=1, source_target_pairs={{0,64},{64,128},{128,192},{192,256},{256,320},{320,384},{384,448},... | collective-permute-start | bytes 442376 | tf_op jit(solution)/shard_map/ppermute | solution.py:390
  97.3 4.8 %collective-permute-start.8 = (bf16[272,256]{1,0:T(8,128)(2,1)S(1)}, bf16[272,256]{1,0:T(8,128)(2,1)S(1)}, u32[]{:S(2)}, u32[]{:S(2)}) collective-permute-start(bf16[272,256]{1,0:T(8,128)(2,1)S(1)} %slice.19), channel_id=1, source_target_pairs={{0,448},{64,0},{128,64},{192,128},{256,192},{320,256},{384,320},{4... | collective-permute-start | bytes 417800 | tf_op jit(solution)/shard_map/ppermute | solution.py:391
  102.2 0.6 and_select_fusion.where_ref
  102.8 1.4 collective-permute-done.8.w8
  104.2 0.0 collective-permute-done.7.w7
  104.2 0.7 copy-done.16
  104.9 0.0 copy-done.17
  104.9 7.8 %shard_map.128 = (bf16[2,272,512]{2,1,0:T(8,128)(2,1)}, bf16[16,2,272]{2,1,0:T(2,128)(2,1)}, f32[8,512]{1,0:T(8,128)}) custom-call(s32[8]{0:T(128)} %and_select_fusion.where_ref, bf16[4,2,2,272,512]{4,3,2,1,0:T(8,128)(2,1)} %bitcast.29, bf16[4,8,128,256]{3,2,1,0:T(8,128)(2,1)} %all-to-all-done.2.side_ref, bf16[560,256]{1,0:T(8,128)(2,1)} %copy-done.9, ...), custom_call_target="tpu_custom_call" | custom-call | tf_op jit(solution)/shard_map/pallas_call | solution.py:181
  112.6 0.8 broadcast_in_dim.40
  113.5 0.7 broadcast_in_dim.41
  114.2 11.1 %all-to-all-start.3 = ((bf16[16,16,544]{2,1,0:T(8,128)(2,1)}), bf16[16,16,544]{2,1,0:T(8,128)(2,1)S(1)}, u32[]{:S(2)}, u32[]{:S(2)}) async-start(bf16[16,16,544]{2,1,0:T(8,128)(2,1)} %broadcast_in_dim.41), calls=%async_computation.3 | async-start | bytes 655360 | tf_op jit(solution)/shard_map/all_to_all | solution.py:455
  125.3 0.7 broadcast_in_dim.36
  126.0 0.1 broadcast_in_dim_reshape.3
  126.1 0.1 pad.5.clone
  126.2 0.7 pad_maximum_fusion.2
  126.9 0.8 maximum_maximum_fusion.chan_ref
  127.6 0.1 copy.29.head_ref
  127.7 1.1 copy-done.4
  128.8 0.7 copy-done.5
  129.5 0.7 copy-done.6
  130.2 2.3 %shard_map.129 = (bf16[512,512]{1,0:T(8,128)(2,1)S(1)}, f32[8,512]{1,0:T(8,128)S(1)}, f32[8,512]{1,0:T(8,128)S(1)}, bf16[512,512]{1,0:T(8,128)(2,1)S(1)}) custom-call(s32[1]{0:T(128)} %bitcast.mine_ref, bf16[2,272,512]{2,1,0:T(8,128)(2,1)S(1)} %copy-done.4, f32[8,512]{1,0:T(8,128)S(1)} %copy-done.6, f32[4,1024]{1,0:T(4,128)S(1)} %copy-done.5, ...), custom_call_target="tpu_custom_call" | custom-call | flops 1000000000 | bytes 2097152 | tf_op jit(solution)/shard_map/pallas_call | solution.py:36
  132.5 0.0 copy-start.7
  132.5 0.8 copy-done.7
  133.3 3.4 %all-to-all-done.3 = bf16[16,16,544]{2,1,0:T(8,128)(2,1)S(1)} async-done(((bf16[16,16,544]{2,1,0:T(8,128)(2,1)}), bf16[16,16,544]{2,1,0:T(8,128)(2,1)S(1)}, u32[]{:S(2)}, u32[]{:S(2)}) %all-to-all-start.3) | async-done | bytes 278560 | tf_op jit(solution)/shard_map/all_to_all | solution.py:455
  136.7 0.2 copy.30
  136.9 1.5 shard_map.130
  138.3 1.0 copy-done.2
  139.3 7.1 %all-to-all-start.4 = ((bf16[32,24,128]{2,1,0:T(8,128)(2,1)}), bf16[32,24,128]{2,1,0:T(8,128)(2,1)S(1)}, u32[]{:S(2)}, u32[]{:S(2)}) async-start(bf16[32,24,128]{2,1,0:T(8,128)(2,1)} %get-tuple-element.55), calls=%async_computation.4 | async-start | bytes 393216 | tf_op jit(solution)/shard_map/all_to_all | solution.py:490
  146.5 10.5 %all-to-all-done.4.got_ref = bf16[32,24,128]{2,1,0:T(8,128)(2,1)S(1)} async-done(((bf16[32,24,128]{2,1,0:T(8,128)(2,1)}), bf16[32,24,128]{2,1,0:T(8,128)(2,1)S(1)}, u32[]{:S(2)}, u32[]{:S(2)}) %all-to-all-start.4) | async-done | bytes 196640 | tf_op jit(solution)/shard_map/all_to_all | solution.py:490
  157.0 0.7 shard_map.132
  157.7 4.2 %all-to-all-start.5 = ((bf16[32,16,128]{2,1,0:T(8,128)(2,1)}), bf16[32,16,128]{2,1,0:T(8,128)(2,1)S(1)}, u32[]{:S(2)}, u32[]{:S(2)}) async-start(bf16[32,16,128]{2,1,0:T(8,128)(2,1)} %shard_map.132), calls=%async_computation.5 | async-start | bytes 262144 | tf_op jit(solution)/shard_map/all_to_all | solution.py:498
  161.9 1.2 copy-done.3
  163.1 1.0 copy-done.8
  164.1 2.1 %shard_map.131 = (f32[512,512]{1,0:T(8,128)S(1)}, f32[512,512]{1,0:T(8,128)S(1)}) custom-call(s32[1]{0:T(128)} %bitcast.mine_ref, bf16[512,512]{1,0:T(8,128)(2,1)S(1)} %copy-done.8, bf16[512,256]{1,0:T(8,128)(2,1)S(1)} %get-tuple-element.49.bc_ref, f32[8,512]{1,0:T(8,128)S(1)} %get-tuple-element.47.cum_ref, f32[8,512]{1,0:T(8,128)S(1)} %get-tuple-element.50.step_ref, ...), custom_call_target="tpu_custom_call" | custom-call | flops 1000000000 | bytes 3145728 | tf_op jit(solution)/shard_map/pallas_call | solution.py:36
  166.3 4.9 %all-to-all-done.5 = bf16[32,16,128]{2,1,0:T(8,128)(2,1)S(1)} async-done(((bf16[32,16,128]{2,1,0:T(8,128)(2,1)}), bf16[32,16,128]{2,1,0:T(8,128)(2,1)S(1)}, u32[]{:S(2)}, u32[]{:S(2)}) %all-to-all-start.5) | async-done | bytes 131104 | tf_op jit(solution)/shard_map/all_to_all | solution.py:498
  171.2 3.3 %shard_map.133 = (f32[256,512]{1,0:T(8,128)S(1)}, bf16[256,512]{1,0:T(8,128)(2,1)S(1)}, f32[2,1,256]{2,1,0:T(1,128)S(1)}) custom-call(s32[1]{0:T(128)} %bitcast.mine_ref, f32[512,512]{1,0:T(8,128)S(1)} %get-tuple-element.53.inside_ref, f32[512,512]{1,0:T(8,128)S(1)} %get-tuple-element.54.growth_ref, bf16[512,256]{1,0:T(8,128)(2,1)S(1)} %get-tuple-element.49.bc_ref, ...), custom_call_target="tpu_custom_call" | custom-call | tf_op jit(solution)/shard_map/pallas_call | solution.py:36
  174.5 3.3 %collective-permute-start.9 = (bf16[256,512]{1,0:T(8,128)(2,1)S(1)}, bf16[256,512]{1,0:T(8,128)(2,1)S(1)}, u32[]{:S(2)}, u32[]{:S(2)}) collective-permute-start(bf16[256,512]{1,0:T(8,128)(2,1)S(1)} %get-tuple-element.57), channel_id=1, source_target_pairs={{0,8},{8,0},{1,9},{9,1},{2,10},{10,2},{3,11},{11,3},{4,12},{12,4},... | collective-permute-start | bytes 786440 | tf_op jit(solution)/shard_map/ppermute | solution.py:518
  177.9 14.0 %all_to_all.36 = f32[16,1,256]{2,1,0:T(1,128)S(1)} all-to-all(f32[16,1,256]{2,1,0:T(1,128)S(1)} %broadcast_in_dim.44), channel_id=1, replica_groups=mesh['z'=8,'x'=4,'yl'=2,'yh'=4,'c'=2] {'yh','yl','c'}, dimensions={0} | all-to-all | bytes 32768 | tf_op jit(solution)/shard_map/all_to_all | solution.py:520
  191.9 1.8 shard_map.134
  (44 shorter events, 0.2 us)
Async XLA Ops:
  6.5 98.3 %all-gather.3.cloned.1.call-start = ((), (), s32[]{:S(2)}) async-start(), calls=%async_computation.7 | async-start | bytes 4734976 | tf_op jit(solution)/shard_map/all_gather | solution.py:416
  7.3 4.9 %collective-permute-start = (bf16[16,512]{1,0:T(8,128)(2,1)S(1)}, bf16[16,512]{1,0:T(8,128)(2,1)S(1)}, u32[]{:S(2)}, u32[]{:S(2)}) collective-permute-start(bf16[16,512]{1,0:T(8,128)(2,1)S(1)} %slice.15), channel_id=1, source_target_pairs={{0,8},{8,16},{16,24},{24,32},{32,40},{40,48},{48,56},{56,64},{64,7... | collective-permute-start | bytes 49160 | tf_op jit(solution)/shard_map/ppermute | solution.py:412
  30.9 35.2 %copy-start.9 = (bf16[560,256]{1,0:T(8,128)(2,1)}, bf16[560,256]{1,0:T(8,128)(2,1)S(1)}, u32[]{:S(2)}) copy-start(bf16[560,256]{1,0:T(8,128)(2,1)S(1)} %pad_maximum_fusion.w0) | copy-start | bytes 860164
  30.9 33.5 %all-to-all-start.1 = ((bf16[16,64,256]{2,1,0:T(8,128)(2,1)}), bf16[16,64,256]{2,1,0:T(8,128)(2,1)S(1)}, u32[]{:S(2)}, u32[]{:S(2)}) async-start(bf16[16,64,256]{2,1,0:T(8,128)(2,1)} %get-tuple-element.34), calls=%async_computation.1 | async-start | bytes 1048576 | tf_op jit(solution)/shard_map/all_to_all | solution.py:437
  43.7 20.3 %collective-permute-start.1 = (bf16[560,256]{1,0:T(8,128)(2,1)S(1)}, bf16[560,256]{1,0:T(8,128)(2,1)S(1)}, u32[]{:S(2)}, u32[]{:S(2)}) collective-permute-start(bf16[560,256]{1,0:T(8,128)(2,1)S(1)} %pad_maximum_fusion.w0), channel_id=1, source_target_pairs={{0,64},{64,128},{128,192},{192,256},{256,320},{320,384},{384,448},... | collective-permute-start | bytes 860168 | tf_op jit(solution)/shard_map/ppermute | solution.py:384
  47.0 17.4 %collective-permute-start.2 = (bf16[560,256]{1,0:T(8,128)(2,1)S(1)}, bf16[560,256]{1,0:T(8,128)(2,1)S(1)}, u32[]{:S(2)}, u32[]{:S(2)}) collective-permute-start(bf16[560,256]{1,0:T(8,128)(2,1)S(1)} %pad_maximum_fusion.w0), channel_id=1, source_target_pairs={{0,448},{64,0},{128,64},{192,128},{256,192},{320,256},{384,320},{4... | collective-permute-start | bytes 860168 | tf_op jit(solution)/shard_map/ppermute | solution.py:385
  64.1 6.6 %copy-start.12 = (bf16[560,256]{1,0:T(8,128)(2,1)}, bf16[560,256]{1,0:T(8,128)(2,1)S(1)}, u32[]{:S(2)}) copy-start(bf16[560,256]{1,0:T(8,128)(2,1)S(1)} %collective-permute-done.1.w1) | copy-start | bytes 860164
  64.4 10.1 %copy-start.13 = (bf16[560,256]{1,0:T(8,128)(2,1)}, bf16[560,256]{1,0:T(8,128)(2,1)S(1)}, u32[]{:S(2)}) copy-start(bf16[560,256]{1,0:T(8,128)(2,1)S(1)} %collective-permute-done.2.w2) | copy-start | bytes 860164
  66.1 36.1 %copy-start.18 = (s32[8]{0:T(128)S(1)}, s32[8]{0:T(128)}, u32[]{:S(2)}) copy-start(s32[8]{0:T(128)} %constant.39.clone) | copy-start | bytes 100
  66.1 38.8 %all-to-all-start.2 = ((bf16[4,8,128,256]{3,2,1,0:T(8,128)(2,1)}), bf16[4,8,128,256]{3,2,1,0:T(8,128)(2,1)}, u32[]{:S(2)}, u32[]{:S(2)}) async-start(bf16[4,8,128,256]{3,2,1,0:T(8,128)(2,1)} %broadcast_in_dim.35), calls=%async_computation.2 | async-start | bytes 4194304 | tf_op jit(solution)/shard_map/all_to_all | solution.py:439
  70.7 10.4 %collective-permute-start.3 = (bf16[560,256]{1,0:T(8,128)(2,1)S(1)}, bf16[560,256]{1,0:T(8,128)(2,1)S(1)}, u32[]{:S(2)}, u32[]{:S(2)}) collective-permute-start(bf16[560,256]{1,0:T(8,128)(2,1)S(1)} %collective-permute-done.1.w1), channel_id=1, source_target_pairs={{0,64},{64,128},{128,192},{192,256},{256,320},{320,384},{384,448},... | collective-permute-start | bytes 860168 | tf_op jit(solution)/shard_map/ppermute | solution.py:384
  74.5 9.5 %collective-permute-start.4 = (bf16[560,256]{1,0:T(8,128)(2,1)S(1)}, bf16[560,256]{1,0:T(8,128)(2,1)S(1)}, u32[]{:S(2)}, u32[]{:S(2)}) collective-permute-start(bf16[560,256]{1,0:T(8,128)(2,1)S(1)} %collective-permute-done.2.w2), channel_id=1, source_target_pairs={{0,448},{64,0},{128,64},{192,128},{256,192},{320,256},{384,320},{4... | collective-permute-start | bytes 860168 | tf_op jit(solution)/shard_map/ppermute | solution.py:385
  81.1 16.2 %copy-start.14 = (bf16[560,256]{1,0:T(8,128)(2,1)}, bf16[560,256]{1,0:T(8,128)(2,1)S(1)}, u32[]{:S(2)}) copy-start(bf16[560,256]{1,0:T(8,128)(2,1)S(1)} %collective-permute-done.3.w3) | copy-start | bytes 860164
  84.0 18.1 %copy-start.15 = (bf16[560,256]{1,0:T(8,128)(2,1)}, bf16[560,256]{1,0:T(8,128)(2,1)S(1)}, u32[]{:S(2)}) copy-start(bf16[560,256]{1,0:T(8,128)(2,1)S(1)} %collective-permute-done.4.w4) | copy-start | bytes 860164
  84.0 9.9 %collective-permute-start.5 = (bf16[560,256]{1,0:T(8,128)(2,1)S(1)}, bf16[560,256]{1,0:T(8,128)(2,1)S(1)}, u32[]{:S(2)}, u32[]{:S(2)}) collective-permute-start(bf16[560,256]{1,0:T(8,128)(2,1)S(1)} %collective-permute-done.3.w3), channel_id=1, source_target_pairs={{0,64},{64,128},{128,192},{192,256},{256,320},{320,384},{384,448},... | collective-permute-start | bytes 860168 | tf_op jit(solution)/shard_map/ppermute | solution.py:384
  86.7 8.2 %collective-permute-start.6 = (bf16[560,256]{1,0:T(8,128)(2,1)S(1)}, bf16[560,256]{1,0:T(8,128)(2,1)S(1)}, u32[]{:S(2)}, u32[]{:S(2)}) collective-permute-start(bf16[560,256]{1,0:T(8,128)(2,1)S(1)} %collective-permute-done.4.w4), channel_id=1, source_target_pairs={{0,448},{64,0},{128,64},{192,128},{256,192},{320,256},{384,320},{4... | collective-permute-start | bytes 860168 | tf_op jit(solution)/shard_map/ppermute | solution.py:385
  93.9 0.9 copy-start.10
  94.8 2.4 %copy-start.11 = (bf16[560,256]{1,0:T(8,128)(2,1)}, bf16[560,256]{1,0:T(8,128)(2,1)S(1)}, u32[]{:S(2)}) copy-start(bf16[560,256]{1,0:T(8,128)(2,1)S(1)} %collective-permute-done.6.w6) | copy-start | bytes 860164
  94.8 9.3 %collective-permute-start.7 = (bf16[288,256]{1,0:T(8,128)(2,1)S(1)}, bf16[288,256]{1,0:T(8,128)(2,1)S(1)}, u32[]{:S(2)}, u32[]{:S(2)}) collective-permute-start(bf16[288,256]{1,0:T(8,128)(2,1)S(1)} %slice.18), channel_id=1, source_target_pairs={{0,64},{64,128},{128,192},{192,256},{256,320},{320,384},{384,448},... | collective-permute-start | bytes 442376 | tf_op jit(solution)/shard_map/ppermute | solution.py:390
  97.3 6.9 %collective-permute-start.8 = (bf16[272,256]{1,0:T(8,128)(2,1)S(1)}, bf16[272,256]{1,0:T(8,128)(2,1)S(1)}, u32[]{:S(2)}, u32[]{:S(2)}) collective-permute-start(bf16[272,256]{1,0:T(8,128)(2,1)S(1)} %slice.19), channel_id=1, source_target_pairs={{0,448},{64,0},{128,64},{192,128},{256,192},{320,256},{384,320},{4... | collective-permute-start | bytes 417800 | tf_op jit(solution)/shard_map/ppermute | solution.py:391
  104.2 0.7 copy-start.17
  104.2 0.7 copy-start.16
  114.2 22.5 %all-to-all-start.3 = ((bf16[16,16,544]{2,1,0:T(8,128)(2,1)}), bf16[16,16,544]{2,1,0:T(8,128)(2,1)S(1)}, u32[]{:S(2)}, u32[]{:S(2)}) async-start(bf16[16,16,544]{2,1,0:T(8,128)(2,1)} %broadcast_in_dim.41), calls=%async_computation.3 | async-start | bytes 655360 | tf_op jit(solution)/shard_map/all_to_all | solution.py:455
  127.7 1.1 copy-start.4
  128.8 0.7 copy-start.5
  129.5 0.7 copy-start.6
  130.2 6.7 %copy-start.1 = (f32[4,256]{1,0:T(4,128)S(1)}, f32[4,256]{1,0:T(4,128)}, u32[]{:S(2)}) copy-start(f32[4,256]{1,0:T(4,128)} %conv_ref.3) | copy-start | bytes 12292
  130.2 26.8 %copy-start = (f32[16,64,128]{2,1,0:T(8,128)S(1)}, f32[16,64,128]{2,1,0:T(8,128)}, u32[]{:S(2)}) copy-start(f32[16,64,128]{2,1,0:T(8,128)} %param.23) | copy-start | bytes 1572868
  132.5 0.8 copy-start.7
  138.3 1.0 copy-start.2
  139.3 17.7 %all-to-all-start.4 = ((bf16[32,24,128]{2,1,0:T(8,128)(2,1)}), bf16[32,24,128]{2,1,0:T(8,128)(2,1)S(1)}, u32[]{:S(2)}, u32[]{:S(2)}) async-start(bf16[32,24,128]{2,1,0:T(8,128)(2,1)} %get-tuple-element.55), calls=%async_computation.4 | async-start | bytes 393216 | tf_op jit(solution)/shard_map/all_to_all | solution.py:490
  157.7 13.5 %all-to-all-start.5 = ((bf16[32,16,128]{2,1,0:T(8,128)(2,1)}), bf16[32,16,128]{2,1,0:T(8,128)(2,1)S(1)}, u32[]{:S(2)}, u32[]{:S(2)}) async-start(bf16[32,16,128]{2,1,0:T(8,128)(2,1)} %shard_map.132), calls=%async_computation.5 | async-start | bytes 262144 | tf_op jit(solution)/shard_map/all_to_all | solution.py:498
  161.9 1.2 copy-start.3
  163.1 1.0 copy-start.8
  174.5 17.4 %collective-permute-start.9 = (bf16[256,512]{1,0:T(8,128)(2,1)S(1)}, bf16[256,512]{1,0:T(8,128)(2,1)S(1)}, u32[]{:S(2)}, u32[]{:S(2)}) collective-permute-start(bf16[256,512]{1,0:T(8,128)(2,1)S(1)} %get-tuple-element.57), channel_id=1, source_target_pairs={{0,8},{8,0},{1,9},{9,1},{2,10},{10,2},{3,11},{11,3},{4,12},{12,4},... | collective-permute-start | bytes 786440 | tf_op jit(solution)/shard_map/ppermute | solution.py:518
Sparse Core Ops, SparseCore 0:
  14.0 56.8 all-gather.2

commit v5 on v3

--- a/solution.py
+++ b/solution.py
@@ -13,6 +13,7 @@
 N = 128
 HALO = 16
 HEAD = 64
+ALL_VMEM = 67043328
 HIGHEST = lax.Precision.HIGHEST
 
 SEQ = ("z", "x", "yl")
@@ -42,7 +43,7 @@
             scratch_shapes=list(scratch),
         ),
         out_shape=outs,
-        compiler_params=pltpu.CompilerParams(vmem_limit_bytes=48 * 1024 * 1024),
+        compiler_params=pltpu.CompilerParams(vmem_limit_bytes=ALL_VMEM),
         cost_estimate=pl.CostEstimate(
             flops=flops, bytes_accessed=bytes_accessed, transcendentals=0
         ),
@@ -77,91 +78,133 @@
     return jnp.where(column // (channels // heads) == row, 1.0, 0.0).astype(jnp.bfloat16)
 
 
+def fetch_tokens(where_ref, own_ref, other_ref, feats, sem):
+    for step in range(feats.shape[0]):
+        line, mine = where_ref[step], where_ref[feats.shape[0] + step] == 1
+
+        @pl.when(mine)
+        def _():
+            pltpu.make_async_copy(own_ref.at[line], feats.at[step], sem.at[step]).start()
+
+        @pl.when(jnp.logical_not(mine))
+        def _():
+            pltpu.make_async_copy(other_ref.at[line], feats.at[step], sem.at[step]).start()
+
+
+def narrow_kernel(
+    where_ref, own_ref, other_ref, w0, w1, w2, w3, w4, w5, w6, w7,
+    bc_ref, dt_ref, feats, weights, small, sem, weight_sem,
+):
+    bc_rows, dt_rows = bc_ref.shape[0], dt_ref.shape[0]
+    flat = bc_rows + dt_rows
+    rows = feats.shape[2]
+    tokens = rows - HALO
+    blocks = feats.shape[0]
+    fetch_tokens(where_ref, own_ref, other_ref, feats, sem)
+    copies = []
+    for at, ref in enumerate((w0, w1, w2, w3, w4, w5, w6, w7)):
+        tall = ref.shape[0] - flat
+        copies.append(
+            pltpu.make_async_copy(
+                ref.at[tall : tall + flat], weights.at[at], weight_sem.at[at]
+            )
+        )
+        copies[at].start()
+    small[...] = jnp.zeros_like(small)
+    for step in range(blocks):
+        pltpu.make_async_copy(own_ref.at[0], feats.at[step], sem.at[step]).wait()
+        copies[step].wait()
+        for part in range(2):
+            small[part, 0:rows, 0:flat] += dot(
+                feats[step, part], weights[step], ((1,), (1,))
+            )
+    for part in range(2):
+        turned = small[part].T
+        bc_ref[:, part, :] = turned[0:bc_rows, 0:rows].astype(jnp.bfloat16)
+        turned = small[part, HALO:rows].T
+        dt_ref[:, part * tokens : (part + 1) * tokens] = turned[bc_rows:flat]
+
+
 def project_kernel(
     where_ref, own_ref, other_ref, w0, w1, w2, w3, w4, w5, w6, w7, w8,
-    x_ref, bc_ref, dt_ref, weights, acc, small, sem,
-):
-    step = pl.program_id(0)
-    blocks = weights.shape[0]
-    channels = x_ref.shape[2]
-    bc_rows, dt_rows = bc_ref.shape[0], dt_ref.shape[0]
-    rows = x_ref.shape[1]
-    tokens = rows - HALO
+    x_ref, feats, weights, acc, sem, weight_sem,
+):
+    blocks, depth = weights.shape[0], weights.shape[1]
     cut = w7.shape[0]
+    fetch_tokens(where_ref, own_ref, other_ref, feats, sem)
     copies = [
-        [pltpu.make_async_copy(ref, weights.at[at], sem.at[at])]
+        [pltpu.make_async_copy(ref.at[0:depth], weights.at[at], weight_sem.at[at])]
         for at, ref in enumerate((w0, w1, w2, w3, w4, w5, w6))
     ]
     copies.append(
         [
-            pltpu.make_async_copy(w7, weights.at[7, 0:cut], sem.at[7]),
-            pltpu.make_async_copy(w8, weights.at[7, cut:], sem.at[8]),
+            pltpu.make_async_copy(w7, weights.at[7, 0:cut], weight_sem.at[7]),
+            pltpu.make_async_copy(w8, weights.at[7, cut:], weight_sem.at[8]),
         ]
     )
-
-    @pl.when(step == 0)
-    def _():
-        for group in copies:
-            for copy in group:
-                copy.start()
-        acc[...] = jnp.zeros_like(acc)
-        small[...] = jnp.zeros_like(small)
-
-    for at, group in enumerate(copies):
-
-        @pl.when(step == at)
-        def _():
-            for copy in group:
-                copy.wait()
-
-    mine = where_ref[blocks + step] == 1
-    for half in range(2):
-        feats = jnp.where(mine, own_ref[0, half], other_ref[0, half])
-        acc[half] += dot(feats, weights[step, 0:channels], ((1,), (0,)))
-        small[half, 0:rows, 0 : bc_rows + dt_rows] += dot(
-            feats, weights[step, channels:], ((1,), (1,))
-        )
-
-    @pl.when(step == blocks - 1)
-    def _():
-        x_ref[...] = acc[...].astype(jnp.bfloat16)
-        for half in range(2):
-            turned = small[half].T
-            bc_ref[:, half, :] = turned[0:bc_rows, 0:rows].astype(jnp.bfloat16)
-            turned = small[half, HALO:rows].T
-            dt_ref[:, half * tokens : (half + 1) * tokens] = turned[bc_rows : bc_rows + dt_rows]
-
-
-def project(where, own, other, weights, bc_rows, dt_rows):
+    for group in copies:
+        for copy in group:
+            copy.start()
+    for step in range(blocks):
+        pltpu.make_async_copy(own_ref.at[0], feats.at[step], sem.at[step]).wait()
+        for copy in copies[step]:
+            copy.wait()
+        for part in range(2):
+            found = dot(feats[step, part], weights[step], ((1,), (0,)))
+            if step == 0:
+                acc[part] = found
+            elif step < blocks - 1:
+                acc[part] += found
+            else:
+                x_ref[part] = (acc[part] + found).astype(jnp.bfloat16)
+
+
+def narrow_project(where, own, other, weights, bc_rows, dt_rows):
     _, _, rows, depth = own.shape
-    height, channels = weights[0].shape
+    blocks = len(weights)
+    flat = bc_rows + dt_rows
+    return pl.pallas_call(
+        narrow_kernel,
+        in_specs=[pl.BlockSpec(memory_space=pltpu.SMEM)]
+        + [pl.BlockSpec(memory_space=pl.ANY)] * (blocks + 2),
+        out_specs=[pl.BlockSpec(memory_space=pltpu.VMEM)] * 2,
+        scratch_shapes=[
+            pltpu.VMEM((blocks, 2, rows, depth), jnp.bfloat16),
+            pltpu.VMEM((blocks, flat, depth), jnp.bfloat16),
+            pltpu.VMEM((2, (rows + 127) // 128 * 128, 128), jnp.float32),
+            pltpu.SemaphoreType.DMA((blocks,)),
+            pltpu.SemaphoreType.DMA((blocks,)),
+        ],
+        out_shape=[
+            jax.ShapeDtypeStruct((bc_rows, 2, rows), jnp.bfloat16),
+            jax.ShapeDtypeStruct((dt_rows, 2 * (rows - HALO)), jnp.float32),
+        ],
+        compiler_params=pltpu.CompilerParams(vmem_limit_bytes=ALL_VMEM),
+        cost_estimate=pl.CostEstimate(flops=10**9, bytes_accessed=10**7, transcendentals=0),
+    )(where, own, other, *weights)
+
+
+def project(where, own, other, weights):
+    _, _, rows, depth = own.shape
+    channels = weights[0].shape[1]
     blocks = len(weights) - 1
-    tokens = rows - HALO
-    feat = pl.BlockSpec((1, 2, rows, depth), lambda j, m: (m[j], 0, 0, 0))
     return pl.pallas_call(
         project_kernel,
-        grid_spec=pltpu.PrefetchScalarGridSpec(
-            num_scalar_prefetch=1,
-            grid=(blocks,),
-            in_specs=[feat, feat] + [pl.BlockSpec(memory_space=pl.ANY)] * len(weights),
-            out_specs=[
-                pl.BlockSpec((2, rows, channels), lambda j, m: (0, 0, 0)),
-                pl.BlockSpec((bc_rows, 2, rows), lambda j, m: (0, 0, 0)),
-                pl.BlockSpec((dt_rows, 2 * tokens), lambda j, m: (0, 0)),
-            ],
-            scratch_shapes=[
-                pltpu.VMEM((blocks, height, channels), jnp.bfloat16),
-                pltpu.VMEM((2, rows, channels), jnp.float32),
-                pltpu.VMEM((2, (rows + 127) // 128 * 128, 128), jnp.float32),
-                pltpu.SemaphoreType.DMA((blocks + 1,)),
-            ],
+        in_specs=[pl.BlockSpec(memory_space=pltpu.SMEM)]
+        + [pl.BlockSpec(memory_space=pl.ANY)] * (len(weights) + 2),
+        out_specs=pl.BlockSpec(memory_space=pltpu.VMEM),
+        scratch_shapes=[
+            pltpu.VMEM((blocks, 2, rows, depth), jnp.bfloat16),
+            pltpu.VMEM((blocks, depth, channels), jnp.bfloat16),
+            pltpu.VMEM((2, rows, channels), jnp.float32),
+            pltpu.SemaphoreType.DMA((blocks,)),
+            pltpu.SemaphoreType.DMA((blocks + 1,)),
+        ],
+        out_shape=jax.ShapeDtypeStruct((2, rows, channels), jnp.bfloat16),
+        compiler_params=pltpu.CompilerParams(vmem_limit_bytes=ALL_VMEM),
+        cost_estimate=pl.CostEstimate(
+            flops=3 * 10**9, bytes_accessed=10**7, transcendentals=0
         ),
-        out_shape=[
-            jax.ShapeDtypeStruct((2, rows, channels), jnp.bfloat16),
-            jax.ShapeDtypeStruct((bc_rows, 2, rows), jnp.bfloat16),
-            jax.ShapeDtypeStruct((dt_rows, 2 * tokens), jnp.float32),
-        ],
-        compiler_params=pltpu.CompilerParams(vmem_limit_bytes=48 * 1024 * 1024),
     )(where, own, other, *weights)
 
 
@@ -252,6 +295,18 @@
             pay_ref[part, 16:] = tail
 
 
+def block_kernel(
+    mine_ref, pre_ref, bc_ref, dt_ref, conv_x_ref, conv_bc_ref, head_ref,
+    x_ref, bconv_ref, cum_ref, step_ref, pay_ref, local_ref, scaled_ref,
+):
+    conv_kernel(
+        mine_ref, pre_ref, dt_ref, conv_x_ref, head_ref, x_ref, cum_ref, step_ref, scaled_ref
+    )
+    state_kernel(
+        mine_ref, bc_ref, conv_bc_ref, cum_ref, scaled_ref, bconv_ref, pay_ref, local_ref
+    )
+
+
 def prefix_kernel(at_ref, got_ref, start_ref, out_ref):
     running = start_ref[...]
     for source in range(got_ref.shape[0]):
@@ -343,23 +398,31 @@
             out_ref[:, on] = (normed - penalty * factor).astype(jnp.bfloat16)
 
 
-def ring(block, axis):
+def ring(block, depth, axis):
     count = SIZES[axis]
     forward = [(i, (i + 1) % count) for i in range(count)]
     backward = [(i, (i - 1) % count) for i in range(count)]
+    across = [(i, (i + count // 2) % count) for i in range(count)]
     pieces, offsets = [block], [0]
     ahead = behind = block
+    far = None
     for hop in range(1, count // 2):
         ahead = lax.ppermute(ahead, axis, forward)
         behind = lax.ppermute(behind, axis, backward)
-        ahead, behind = lax.optimization_barrier((ahead, behind))
+        if far is None:
+            far = lax.ppermute(block[depth:], axis, across)
+            ahead, behind, far = lax.optimization_barrier((ahead, behind, far))
+        else:
+            ahead, behind = lax.optimization_barrier((ahead, behind))
         pieces += [ahead, behind]
         offsets += [-hop, hop]
-    cut = (block.shape[0] // 2 + 15) // 16 * 16
-    pieces.append(lax.ppermute(ahead[:cut], axis, forward))
-    pieces.append(lax.ppermute(behind[cut:], axis, backward))
+    cut = (depth // 2 + 15) // 16 * 16
+    last = [
+        lax.ppermute(ahead[:cut], axis, forward),
+        lax.ppermute(behind[cut:depth], axis, backward),
+    ]
     offsets.append(count // 2)
-    return pieces, offsets
+    return pieces, far, last, offsets
 
 
 def per_device(
@@ -411,7 +474,7 @@
         fan, packed_rows, half // k_rows, k_rows
     )
     flat = flat.transpose(1, 2, 0, 3).reshape(small, fan * k_rows)
-    pieces, offsets = ring(jnp.concatenate([tall, flat], 0), "z")
+    pieces, far, last, offsets = ring(jnp.concatenate([tall, flat], 0), fan * k_rows, "z")
 
     copies = lax.optimization_barrier((copies, got))[0]
     own = lax.all_to_all(copies, ("yh", "yl"), 0, 0).reshape(
@@ -434,7 +497,9 @@
     source = (z + jnp.array(offsets, jnp.int32)) % SIZES["z"]
     where = jnp.concatenate([source // 2, (source % 2 == core).astype(jnp.int32)])
 
-    x_pre, bc_pre, dt_raw = project(where, own, other, pieces, bc_rows, heads)
+    bc_pre, dt_raw = narrow_project(where, own, other, pieces + [far], bc_rows, heads)
+    last[0] = lax.optimization_barrier((last[0], bc_pre))[0]
+    x_pre = project(where, own, other, pieces + last)
     bc_all = lax.all_to_all(
         jnp.broadcast_to(
             bc_pre.reshape(1, bc_rows, -1), (2 * tp_count, bc_rows, 2 * (local + HALO))
@@ -446,29 +511,22 @@
     pair = 2 * local
     plane = SIZES["z"] * SIZES["x"]
     share = half // plane
-    x_conv, cumulative, step_size, scaled = call(
-        conv_kernel,
+    x_conv, bc_conv, cumulative, step_size, payload, locals_ = call(
+        block_kernel,
         [
             jax.ShapeDtypeStruct((pair, half), bf16),
+            jax.ShapeDtypeStruct((pair, 2 * N), bf16),
             jax.ShapeDtypeStruct((heads, pair), f32),
             jax.ShapeDtypeStruct((heads, pair), f32),
-            jax.ShapeDtypeStruct((half, pair), bf16),
-        ],
-        mine, x_pre, dt_raw, conv_x, head_columns,
-        blocks={
-            2: ((conv_x.shape[0], half), lambda i, s: (0, s[0])),
-            3: ((heads, 2), lambda i, s: (s[0], 0)),
-        },
-        flops=10**9, bytes_accessed=8 * pair * half,
-    )
-    bc_conv, payload, locals_ = call(
-        state_kernel,
-        [
-            jax.ShapeDtypeStruct((pair, 2 * N), bf16),
             jax.ShapeDtypeStruct((plane, share + 8, N), bf16),
             jax.ShapeDtypeStruct((pair // GROUP, half, N), f32),
         ],
-        mine, bc_all, conv_bc, cumulative, scaled,
+        mine, x_pre, bc_all, dt_raw, conv_x, conv_bc, head_columns,
+        blocks={
+            3: ((conv_x.shape[0], half), lambda i, s: (0, s[0])),
+            5: ((heads, 2), lambda i, s: (s[0], 0)),
+        },
+        scratch=[pltpu.VMEM((half, pair), bf16)],
     )
     states = lax.all_to_all(payload, ("z", "x"), 0, 0)
     place = mine * plane + lax.axis_index(("z", "x")).astype(jnp.int32)

time: 188 us -> 191 us (1.016)
  waiting for transfers between devices: 59.2 us -> 44.2 us
  Pallas kernels: 21.5 us -> 31.3 us
  starting transfers between devices: 78.1 us -> 82.9 us
  other arithmetic: 1.2 us -> 3.75 us
    ppermute x3, waiting for transfers between devices: 22.2 us -> 12.7 us  [ring(): ahead = lax.ppermute(ahead, axis, forward)]
    pallas_call x6 -> x5, Pallas kernels: 11.8 us -> 20 us  [call(): pl.pallas_call(kernel, grid_spec=pltpu.PrefetchScalarGridSpec(num_scalar_...]
    all_to_all x1, waiting for transfers between devices: 7.55 us -> 1.88 us  [per_device(): lax.all_to_all(jnp.broadcast_to(bc_pre.reshape(1, bc_rows, -1), (2 * tp_c...]
    unnamed x38 -> x24, local copies, waits for them, and re-layouts: 7.03 us -> 2.71 us
    ppermute x3, starting transfers between devices: 18.5 us -> 14.3 us  [ring(): behind = lax.ppermute(behind, axis, backward)]
    ppermute x3, starting transfers between devices: 8.87 us -> 12.6 us  [ring(): ahead = lax.ppermute(ahead, axis, forward)]
    ppermute x2 -> x3, starting transfers between devices: 9.56 us -> 12.4 us  [the longest x1 4.82 us: ring(): lax.ppermute(behind[cut:depth], axis, backward)]
    pallas_call x1 -> x2, Pallas kernels: 9.7 us -> 11.2 us  [the longest x1 6 us: project(): pl.pallas_call(project_kernel, in_specs=[pl.BlockSpec(memory_space=pltpu....]
  transfers between devices with their start and end apart: 16 -> 17, of which waited for: 13 -> 12; matrix products, arithmetic and copies ran while one was open for 0% -> 5% of each run, Pallas kernels for 2% -> 8%
where the time goes in v5:
time: 191 us; the launch traced here: 190 us
  starting transfers between devices  82.9 us (43%)
  waiting for transfers between devices  44.2 us (23%)
  Pallas kernels  31.3 us (16%)
  blocking collectives  14.3 us (7%)
  local copies, waits for them, and re-layouts  13.1 us (7%)
  other arithmetic  3.75 us (2%)
    pallas_call x5, Pallas kernels, call(): pl.pallas_call(kernel, grid_spec=pltpu.PrefetchScalarGridSpec(num_scalar_...  20 us
    all_to_all x1, blocking collectives, per_device(): lax.all_to_all(jnp.broadcast_to(dots[None, :, None], shape).reshape(2 * t...  14.3 us
    ppermute x3, starting transfers between devices, ring(): behind = lax.ppermute(behind, axis, backward)  14.3 us
    ppermute x3, waiting for transfers between devices, ring(): ahead = lax.ppermute(ahead, axis, forward)  12.7 us
    ppermute x3, starting transfers between devices, ring(): ahead = lax.ppermute(ahead, axis, forward)  12.6 us
    all_to_all x1, waiting for transfers between devices, per_device(): states = lax.all_to_all(payload, ('z', 'x'), 0, 0)  10.5 us
    all_to_all x1, starting transfers between devices, per_device(): lax.all_to_all(copies, ('yh', 'yl'), 0, 0)  7.91 us
    ppermute x1, starting transfers between devices, per_device(): other = lax.ppermute(own, 'c', [(0, 1), (1, 0)])  7.13 us
  transfers between devices with their start and end apart: 17, of which 12 were waited for; matrix products, arithmetic and copies ran while one was open for 5% of the time, Pallas kernels for 8%

profile of v5, /device:TPU:1, one launch (start us, length us, event | category | flops | bytes accessed | tf_op | source)
XLA Modules:
  0.0 189.9 jit_solution(2814851700678846653)
XLA Ops:
  0.0 1.0 reshape.57
  1.0 0.7 pad_maximum_fusion.2
  1.8 0.1 reshape.60
  1.9 0.1 pad.10.clone
  1.9 0.2 maximum_maximum_fusion
  2.2 0.9 broadcast_in_dim.46
  3.1 5.9 %all-to-all-start = ((bf16[8,72,512]{2,1,0:T(8,128)(2,1)}), bf16[8,72,512]{2,1,0:T(8,128)(2,1)S(1)}, u32[]{:S(2)}, u32[]{:S(2)}) async-start(bf16[8,72,512]{2,1,0:T(8,128)(2,1)} %bitcast.6), calls=%async_computation | async-start | bytes 1179648 | tf_op jit(solution)/shard_map/all_to_all | solution.py:471
  8.9 3.4 %collective-permute-start = (bf16[16,512]{1,0:T(8,128)(2,1)S(1)}, bf16[16,512]{1,0:T(8,128)(2,1)S(1)}, u32[]{:S(2)}, u32[]{:S(2)}) collective-permute-start(bf16[16,512]{1,0:T(8,128)(2,1)S(1)} %slice.15), channel_id=1, source_target_pairs={{0,8},{8,16},{16,24},{24,32},{32,40},{40,48},{48,56},{56,64},{64,7... | collective-permute-start | bytes 49160 | tf_op jit(solution)/shard_map/ppermute | solution.py:444
  12.3 0.9 collective-permute-done
  13.2 3.6 %all-to-all-done = bf16[8,72,512]{2,1,0:T(8,128)(2,1)S(1)} async-done(((bf16[8,72,512]{2,1,0:T(8,128)(2,1)}), bf16[8,72,512]{2,1,0:T(8,128)(2,1)S(1)}, u32[]{:S(2)}, u32[]{:S(2)}) %all-to-all-start) | async-done | bytes 589856 | tf_op jit(solution)/shard_map/all_to_all | solution.py:471
  16.8 1.6 broadcast_in_dim.44
  18.4 7.9 %all-to-all-start.1 = ((bf16[8,272,512]{2,1,0:T(8,128)(2,1)}), bf16[8,272,512]{2,1,0:T(8,128)(2,1)S(1)}, u32[]{:S(2)}, u32[]{:S(2)}) async-start(bf16[8,272,512]{2,1,0:T(8,128)(2,1)} %broadcast_in_dim.44), calls=%async_computation.1 | async-start | bytes 4456448 | tf_op jit(solution)/shard_map/all_to_all | solution.py:480
  26.3 0.1 reshape.64
  26.5 0.1 reshape.65
  26.7 4.0 %collective-permute-start.1 = (bf16[536,512]{1,0:T(8,128)(2,1)S(1)}, bf16[536,512]{1,0:T(8,128)(2,1)S(1)}, u32[]{:S(2)}, u32[]{:S(2)}) collective-permute-start(bf16[536,512]{1,0:T(8,128)(2,1)S(1)} %pad_maximum_fusion.w0), channel_id=1, source_target_pairs={{0,64},{64,128},{128,192},{192,256},{256,320},{320,384},{384,448},... | collective-permute-start | bytes 1646600 | tf_op jit(solution)/shard_map/ppermute | solution.py:410
  30.7 8.7 %collective-permute-start.2 = (bf16[536,512]{1,0:T(8,128)(2,1)S(1)}, bf16[536,512]{1,0:T(8,128)(2,1)S(1)}, u32[]{:S(2)}, u32[]{:S(2)}) collective-permute-start(bf16[536,512]{1,0:T(8,128)(2,1)S(1)} %pad_maximum_fusion.w0), channel_id=1, source_target_pairs={{0,448},{64,0},{128,64},{192,128},{256,192},{320,256},{384,320},{4... | collective-permute-start | bytes 1646600 | tf_op jit(solution)/shard_map/ppermute | solution.py:411
  39.4 4.4 %collective-permute-start.3 = (bf16[24,512]{1,0:T(8,128)(2,1)S(1)}, bf16[24,512]{1,0:T(8,128)(2,1)S(1)}, u32[]{:S(2)}, u32[]{:S(2)}) collective-permute-start(bf16[24,512]{1,0:T(8,128)(2,1)S(1)} %reshape.65), channel_id=1, source_target_pairs={{0,256},{64,320},{128,384},{192,448},{256,0},{320,64},{384,128},{4... | collective-permute-start | bytes 73736 | tf_op jit(solution)/shard_map/ppermute | solution.py:413
  43.8 5.2 %collective-permute-done.3.w7 = bf16[24,512]{1,0:T(8,128)(2,1)S(1)} collective-permute-done((bf16[24,512]{1,0:T(8,128)(2,1)S(1)}, bf16[24,512]{1,0:T(8,128)(2,1)S(1)}, u32[]{:S(2)}, u32[]{:S(2)}) %collective-permute-start.3) | collective-permute-done | bytes 24608 | tf_op jit(solution)/shard_map/ppermute | solution.py:413
  49.0 0.0 collective-permute-done.1.w1
  49.0 0.3 collective-permute-done.2.w2
  49.3 4.6 %collective-permute-start.4 = (bf16[536,512]{1,0:T(8,128)(2,1)S(1)}, bf16[536,512]{1,0:T(8,128)(2,1)S(1)}, u32[]{:S(2)}, u32[]{:S(2)}) collective-permute-start(bf16[536,512]{1,0:T(8,128)(2,1)S(1)} %collective-permute-done.1.w1), channel_id=1, source_target_pairs={{0,64},{64,128},{128,192},{192,256},{256,320},{320,384},{384,448},... | collective-permute-start | bytes 1646600 | tf_op jit(solution)/shard_map/ppermute | solution.py:410
  53.9 2.8 %collective-permute-start.5 = (bf16[536,512]{1,0:T(8,128)(2,1)S(1)}, bf16[536,512]{1,0:T(8,128)(2,1)S(1)}, u32[]{:S(2)}, u32[]{:S(2)}) collective-permute-start(bf16[536,512]{1,0:T(8,128)(2,1)S(1)} %collective-permute-done.2.w2), channel_id=1, source_target_pairs={{0,448},{64,0},{128,64},{192,128},{256,192},{320,256},{384,320},{4... | collective-permute-start | bytes 1646600 | tf_op jit(solution)/shard_map/ppermute | solution.py:411
  56.7 7.2 %collective-permute-done.4.w3 = bf16[536,512]{1,0:T(8,128)(2,1)S(1)} collective-permute-done((bf16[536,512]{1,0:T(8,128)(2,1)S(1)}, bf16[536,512]{1,0:T(8,128)(2,1)S(1)}, u32[]{:S(2)}, u32[]{:S(2)}) %collective-permute-start.4) | collective-permute-done | bytes 548896 | tf_op jit(solution)/shard_map/ppermute | solution.py:410
  63.9 1.2 collective-permute-done.5.w4
  65.2 4.0 %collective-permute-start.6 = (bf16[536,512]{1,0:T(8,128)(2,1)S(1)}, bf16[536,512]{1,0:T(8,128)(2,1)S(1)}, u32[]{:S(2)}, u32[]{:S(2)}) collective-permute-start(bf16[536,512]{1,0:T(8,128)(2,1)S(1)} %collective-permute-done.4.w3), channel_id=1, source_target_pairs={{0,64},{64,128},{128,192},{192,256},{256,320},{320,384},{384,448},... | collective-permute-start | bytes 1646600 | tf_op jit(solution)/shard_map/ppermute | solution.py:410
  69.2 2.9 %collective-permute-start.7 = (bf16[536,512]{1,0:T(8,128)(2,1)S(1)}, bf16[536,512]{1,0:T(8,128)(2,1)S(1)}, u32[]{:S(2)}, u32[]{:S(2)}) collective-permute-start(bf16[536,512]{1,0:T(8,128)(2,1)S(1)} %collective-permute-done.5.w4), channel_id=1, source_target_pairs={{0,448},{64,0},{128,64},{192,128},{256,192},{320,256},{384,320},{4... | collective-permute-start | bytes 1646600 | tf_op jit(solution)/shard_map/ppermute | solution.py:411
  72.1 5.4 %collective-permute-done.6.w5 = bf16[536,512]{1,0:T(8,128)(2,1)S(1)} collective-permute-done((bf16[536,512]{1,0:T(8,128)(2,1)S(1)}, bf16[536,512]{1,0:T(8,128)(2,1)S(1)}, u32[]{:S(2)}, u32[]{:S(2)}) %collective-permute-start.6) | collective-permute-done | bytes 548896 | tf_op jit(solution)/shard_map/ppermute | solution.py:410
  77.6 2.4 %collective-permute-done.7.w6 = bf16[536,512]{1,0:T(8,128)(2,1)S(1)} collective-permute-done((bf16[536,512]{1,0:T(8,128)(2,1)S(1)}, bf16[536,512]{1,0:T(8,128)(2,1)S(1)}, u32[]{:S(2)}, u32[]{:S(2)}) %collective-permute-start.7) | collective-permute-done | bytes 548896 | tf_op jit(solution)/shard_map/ppermute | solution.py:411
  79.9 0.8 all-to-all-done.1
  80.8 1.4 copy-done
  82.2 7.1 %collective-permute-start.8 = (bf16[4,2,272,512]{3,2,1,0:T(8,128)(2,1)S(1)}, bf16[4,2,272,512]{3,2,1,0:T(8,128)(2,1)}, u32[]{:S(2)}, u32[]{:S(2)}) collective-permute-start(bf16[4,2,272,512]{3,2,1,0:T(8,128)(2,1)S(1)} %bitcast.33), channel_id=1, source_target_pairs={{0,1},{1,0},{2,3},{3,2},{4,5},{5,4},{6,7},{7,6},{8,9},{9,8},{10,11... | collective-permute-start | bytes 6684680 | tf_op jit(solution)/shard_map/ppermute | solution.py:484
  89.4 0.7 pad_add_fusion.where_ref
  90.0 0.7 slice.18
  90.7 0.7 slice.19
  91.5 3.1 %collective-permute-start.9 = (bf16[256,512]{1,0:T(8,128)(2,1)}, bf16[256,512]{1,0:T(8,128)(2,1)}, u32[]{:S(2)}, u32[]{:S(2)}) collective-permute-start(bf16[256,512]{1,0:T(8,128)(2,1)} %slice.18), channel_id=1, source_target_pairs={{0,64},{64,128},{128,192},{192,256},{256,320},{320,384},{384,448},... | collective-permute-start | bytes 786440 | tf_op jit(solution)/shard_map/ppermute | solution.py:421
  94.6 4.8 %collective-permute-start.10 = (bf16[256,512]{1,0:T(8,128)(2,1)}, bf16[256,512]{1,0:T(8,128)(2,1)}, u32[]{:S(2)}, u32[]{:S(2)}) collective-permute-start(bf16[256,512]{1,0:T(8,128)(2,1)} %slice.19), channel_id=1, source_target_pairs={{0,448},{64,0},{128,64},{192,128},{256,192},{320,256},{384,320},{4... | collective-permute-start | bytes 786440 | tf_op jit(solution)/shard_map/ppermute | solution.py:422
  99.4 0.0 collective-permute-done.8.other_ref
  99.4 5.2 %shard_map.127 = (bf16[16,2,272]{2,1,0:T(2,128)(2,1)}, f32[8,512]{1,0:T(8,128)}) custom-call(s32[16]{0:T(128)} %pad_add_fusion.where_ref, bf16[4,2,272,512]{3,2,1,0:T(8,128)(2,1)} %bitcast.34, bf16[4,2,272,512]{3,2,1,0:T(8,128)(2,1)} %collective-permute-done.8.other_ref, bf16[536,512]{1,0:T(8,128)(2,1)} %copy-done.1, bf16[536,512]{1,0:T(8,128)(2,1)} %copy-done.4, ...), custom_call_target="tpu_custom_call" | custom-call | flops 1000000000 | bytes 10000000 | tf_op jit(solution)/shard_map/pallas_call | solution.py:166
  104.7 0.8 broadcast_in_dim.47
  105.5 0.8 broadcast_in_dim.48
  106.3 5.7 %all-to-all-start.2 = ((bf16[16,16,544]{2,1,0:T(8,128)(2,1)}), bf16[16,16,544]{2,1,0:T(8,128)(2,1)}, u32[]{:S(2)}, u32[]{:S(2)}) async-start(bf16[16,16,544]{2,1,0:T(8,128)(2,1)} %broadcast_in_dim.48), calls=%async_computation.2 | async-start | bytes 655360 | tf_op jit(solution)/shard_map/all_to_all | solution.py:503
  111.9 0.7 pad_maximum_fusion.3
  112.6 0.7 broadcast_in_dim.49
  113.3 0.1 broadcast_in_dim_reshape.3
  113.4 0.1 pad.5.clone
  113.5 1.4 maximum_maximum_fusion.1.chan_ref
  114.9 0.7 copy.30.head_ref
  115.6 0.0 collective-permute-done.9.w7
  115.6 6.0 %shard_map.128.pre_ref = bf16[2,272,512]{2,1,0:T(8,128)(2,1)} custom-call(s32[16]{0:T(128)} %pad_add_fusion.where_ref, bf16[4,2,272,512]{3,2,1,0:T(8,128)(2,1)} %bitcast.35, bf16[4,2,272,512]{3,2,1,0:T(8,128)(2,1)} %collective-permute-done.8.other_ref, bf16[536,512]{1,0:T(8,128)(2,1)} %copy-done.1, bf16[536,512]{1,0:T(8,128)(2,1)} %copy-done.4, ...), custom_call_target="tpu_custom_call" | custom-call | flops 3000000000 | bytes 10000000 | tf_op jit(solution)/shard_map/pallas_call | solution.py:191
  121.6 1.9 all-to-all-done.2
  123.5 1.8 copy.29
  125.3 5.1 %shard_map.129 = (bf16[512,512]{1,0:T(8,128)(2,1)}, bf16[512,256]{1,0:T(8,128)(2,1)}, f32[8,512]{1,0:T(8,128)}, f32[8,512]{1,0:T(8,128)}, bf16[32,24,128]{2,1,0:T(8,128)(2,1)}, /*index=5*/f32[4,512,128]{2,1,0:T(8,128)}) custom-call(s32[1]{0:T(128)} %bitcast.mine_ref, bf16[2,272,512]{2,1,0:T(8,128)(2,1)} %shard_map.128.pre_ref, ...), custom_call_target="tpu_custom_call" | custom-call | tf_op jit(solution)/shard_map/pallas_call | solution.py:36
  130.4 5.7 %all-to-all-start.3 = ((bf16[32,24,128]{2,1,0:T(8,128)(2,1)}), bf16[32,24,128]{2,1,0:T(8,128)(2,1)}, u32[]{:S(2)}, u32[]{:S(2)}) async-start(bf16[32,24,128]{2,1,0:T(8,128)(2,1)} %get-tuple-element.51), calls=%async_computation.3 | async-start | bytes 393216 | tf_op jit(solution)/shard_map/all_to_all | solution.py:531
  136.1 10.5 %all-to-all-done.3.got_ref = bf16[32,24,128]{2,1,0:T(8,128)(2,1)} async-done(((bf16[32,24,128]{2,1,0:T(8,128)(2,1)}), bf16[32,24,128]{2,1,0:T(8,128)(2,1)}, u32[]{:S(2)}, u32[]{:S(2)}) %all-to-all-start.3) | async-done | bytes 196640 | tf_op jit(solution)/shard_map/all_to_all | solution.py:531
  146.6 1.7 shard_map.131
  148.3 4.6 %all-to-all-start.4 = ((bf16[32,16,128]{2,1,0:T(8,128)(2,1)}), bf16[32,16,128]{2,1,0:T(8,128)(2,1)}, u32[]{:S(2)}, u32[]{:S(2)}) async-start(bf16[32,16,128]{2,1,0:T(8,128)(2,1)} %shard_map.131), calls=%async_computation.4 | async-start | bytes 262144 | tf_op jit(solution)/shard_map/all_to_all | solution.py:539
  152.9 4.7 %shard_map.130 = (f32[512,512]{1,0:T(8,128)}, f32[512,512]{1,0:T(8,128)}) custom-call(s32[1]{0:T(128)} %bitcast.mine_ref, bf16[512,512]{1,0:T(8,128)(2,1)} %get-tuple-element.43.x_ref, bf16[512,256]{1,0:T(8,128)(2,1)} %get-tuple-element.44.bc_ref, f32[8,512]{1,0:T(8,128)} %get-tuple-element.45.cum_ref, f32[8,512]{1,0:T(8,128)} %get-tuple-element.46.step_ref, ...), custom_call_target="tpu_custom_call" | custom-call | flops 1000000000 | bytes 3145728 | tf_op jit(solution)/shard_map/pallas_call | solution.py:36
  157.5 4.7 %all-to-all-done.4 = bf16[32,16,128]{2,1,0:T(8,128)(2,1)} async-done(((bf16[32,16,128]{2,1,0:T(8,128)(2,1)}), bf16[32,16,128]{2,1,0:T(8,128)(2,1)}, u32[]{:S(2)}, u32[]{:S(2)}) %all-to-all-start.4) | async-done | bytes 131104 | tf_op jit(solution)/shard_map/all_to_all | solution.py:539
  162.3 5.7 %shard_map.132 = (f32[256,512]{1,0:T(8,128)}, bf16[256,512]{1,0:T(8,128)(2,1)}, f32[2,1,256]{2,1,0:T(1,128)}) custom-call(s32[1]{0:T(128)} %bitcast.mine_ref, f32[512,512]{1,0:T(8,128)} %get-tuple-element.49.inside_ref, f32[512,512]{1,0:T(8,128)} %get-tuple-element.50.growth_ref, bf16[512,256]{1,0:T(8,128)(2,1)} %get-tuple-element.44.bc_ref, ...), custom_call_target="tpu_custom_call" | custom-call | tf_op jit(solution)/shard_map/pallas_call | solution.py:36
  167.9 3.4 %collective-permute-start.11 = (bf16[256,512]{1,0:T(8,128)(2,1)}, bf16[256,512]{1,0:T(8,128)(2,1)}, u32[]{:S(2)}, u32[]{:S(2)}) collective-permute-start(bf16[256,512]{1,0:T(8,128)(2,1)} %get-tuple-element.53), channel_id=1, source_target_pairs={{0,8},{8,0},{1,9},{9,1},{2,10},{10,2},{3,11},{11,3},{4,12},{12,4},... | collective-permute-start | bytes 786440 | tf_op jit(solution)/shard_map/ppermute | solution.py:559
  171.3 0.7 copy.36
  172.0 14.3 %all_to_all.30 = f32[16,1,256]{2,1,0:T(1,128)S(1)} all-to-all(f32[16,1,256]{2,1,0:T(1,128)S(1)} %broadcast_in_dim.55), channel_id=1, replica_groups=mesh['z'=8,'x'=4,'yl'=2,'yh'=4,'c'=2] {'yh','yl','c'}, dimensions={0} | all-to-all | bytes 32768 | tf_op jit(solution)/shard_map/all_to_all | solution.py:561
  186.4 0.6 copy.35
  187.0 2.9 %shard_map.133 = bf16[256,1024]{1,0:T(8,128)(2,1)} custom-call(s32[1]{0:T(128)} %bitcast.mine_ref, f32[256,512]{1,0:T(8,128)} %get-tuple-element.52.keep_ref, bf16[256,512]{1,0:T(8,128)(2,1)} %collective-permute-done.11.other_ref, f32[16,256]{1,0:T(8,128)} %bitcast.41, f32[8,1024]{1,0:T(8,128)} %maximum_maximum_fusion.1.chan_ref), custom_call_target="tpu_custom_call" | custom-call | tf_op jit(solution)/shard_map/pallas_call | solution.py:36
  (38 shorter events, 0.3 us)
Async XLA Ops:
  0.0 8.9 %copy-start.8 = (bf16[256,512]{1,0:T(8,128)(2,1)S(1)}, bf16[256,512]{1,0:T(8,128)(2,1)}, u32[]{:S(2)}) copy-start(bf16[256,512]{1,0:T(8,128)(2,1)} %param.13) | copy-start | bytes 786436
  3.1 13.8 %all-to-all-start = ((bf16[8,72,512]{2,1,0:T(8,128)(2,1)}), bf16[8,72,512]{2,1,0:T(8,128)(2,1)S(1)}, u32[]{:S(2)}, u32[]{:S(2)}) async-start(bf16[8,72,512]{2,1,0:T(8,128)(2,1)} %bitcast.6), calls=%async_computation | async-start | bytes 1179648 | tf_op jit(solution)/shard_map/all_to_all | solution.py:471
  8.9 4.2 %collective-permute-start = (bf16[16,512]{1,0:T(8,128)(2,1)S(1)}, bf16[16,512]{1,0:T(8,128)(2,1)S(1)}, u32[]{:S(2)}, u32[]{:S(2)}) collective-permute-start(bf16[16,512]{1,0:T(8,128)(2,1)S(1)} %slice.15), channel_id=1, source_target_pairs={{0,8},{8,16},{16,24},{24,32},{32,40},{40,48},{48,56},{56,64},{64,7... | collective-permute-start | bytes 49160 | tf_op jit(solution)/shard_map/ppermute | solution.py:444
  18.4 62.4 %all-to-all-start.1 = ((bf16[8,272,512]{2,1,0:T(8,128)(2,1)}), bf16[8,272,512]{2,1,0:T(8,128)(2,1)S(1)}, u32[]{:S(2)}, u32[]{:S(2)}) async-start(bf16[8,272,512]{2,1,0:T(8,128)(2,1)} %broadcast_in_dim.44), calls=%async_computation.1 | async-start | bytes 4456448 | tf_op jit(solution)/shard_map/all_to_all | solution.py:480
  26.3 63.0 %copy-start.10 = (s32[8]{0:T(128)S(1)}, s32[8]{0:T(128)}, u32[]{:S(2)}) copy-start(s32[8]{0:T(128)} %constant.65.clone) | copy-start | bytes 100
  26.7 50.9 %copy-start.1 = (bf16[536,512]{1,0:T(8,128)(2,1)}, bf16[536,512]{1,0:T(8,128)(2,1)S(1)}, u32[]{:S(2)}) copy-start(bf16[536,512]{1,0:T(8,128)(2,1)S(1)} %pad_maximum_fusion.w0) | copy-start | bytes 1646596
  26.7 22.3 %collective-permute-start.1 = (bf16[536,512]{1,0:T(8,128)(2,1)S(1)}, bf16[536,512]{1,0:T(8,128)(2,1)S(1)}, u32[]{:S(2)}, u32[]{:S(2)}) collective-permute-start(bf16[536,512]{1,0:T(8,128)(2,1)S(1)} %pad_maximum_fusion.w0), channel_id=1, source_target_pairs={{0,64},{64,128},{128,192},{192,256},{256,320},{320,384},{384,448},... | collective-permute-start | bytes 1646600 | tf_op jit(solution)/shard_map/ppermute | solution.py:410
  30.7 18.6 %collective-permute-start.2 = (bf16[536,512]{1,0:T(8,128)(2,1)S(1)}, bf16[536,512]{1,0:T(8,128)(2,1)S(1)}, u32[]{:S(2)}, u32[]{:S(2)}) collective-permute-start(bf16[536,512]{1,0:T(8,128)(2,1)S(1)} %pad_maximum_fusion.w0), channel_id=1, source_target_pairs={{0,448},{64,0},{128,64},{192,128},{256,192},{320,256},{384,320},{4... | collective-permute-start | bytes 1646600 | tf_op jit(solution)/shard_map/ppermute | solution.py:411
  39.4 9.6 %collective-permute-start.3 = (bf16[24,512]{1,0:T(8,128)(2,1)S(1)}, bf16[24,512]{1,0:T(8,128)(2,1)S(1)}, u32[]{:S(2)}, u32[]{:S(2)}) collective-permute-start(bf16[24,512]{1,0:T(8,128)(2,1)S(1)} %reshape.65), channel_id=1, source_target_pairs={{0,256},{64,320},{128,384},{192,448},{256,0},{320,64},{384,128},{4... | collective-permute-start | bytes 73736 | tf_op jit(solution)/shard_map/ppermute | solution.py:413
  49.0 14.9 %copy-start.9 = (bf16[24,512]{1,0:T(8,128)(2,1)}, bf16[24,512]{1,0:T(8,128)(2,1)S(1)}, u32[]{:S(2)}) copy-start(bf16[24,512]{1,0:T(8,128)(2,1)S(1)} %collective-permute-done.3.w7) | copy-start | bytes 73732
  49.0 28.5 %copy-start.4 = (bf16[536,512]{1,0:T(8,128)(2,1)}, bf16[536,512]{1,0:T(8,128)(2,1)S(1)}, u32[]{:S(2)}) copy-start(bf16[536,512]{1,0:T(8,128)(2,1)S(1)} %collective-permute-done.1.w1) | copy-start | bytes 1646596
  49.3 28.2 %copy-start.5 = (bf16[536,512]{1,0:T(8,128)(2,1)}, bf16[536,512]{1,0:T(8,128)(2,1)S(1)}, u32[]{:S(2)}) copy-start(bf16[536,512]{1,0:T(8,128)(2,1)S(1)} %collective-permute-done.2.w2) | copy-start | bytes 1646596
  49.3 14.6 %collective-permute-start.4 = (bf16[536,512]{1,0:T(8,128)(2,1)S(1)}, bf16[536,512]{1,0:T(8,128)(2,1)S(1)}, u32[]{:S(2)}, u32[]{:S(2)}) collective-permute-start(bf16[536,512]{1,0:T(8,128)(2,1)S(1)} %collective-permute-done.1.w1), channel_id=1, source_target_pairs={{0,64},{64,128},{128,192},{192,256},{256,320},{320,384},{384,448},... | collective-permute-start | bytes 1646600 | tf_op jit(solution)/shard_map/ppermute | solution.py:410
  53.9 11.3 %collective-permute-start.5 = (bf16[536,512]{1,0:T(8,128)(2,1)S(1)}, bf16[536,512]{1,0:T(8,128)(2,1)S(1)}, u32[]{:S(2)}, u32[]{:S(2)}) collective-permute-start(bf16[536,512]{1,0:T(8,128)(2,1)S(1)} %collective-permute-done.2.w2), channel_id=1, source_target_pairs={{0,448},{64,0},{128,64},{192,128},{256,192},{320,256},{384,320},{4... | collective-permute-start | bytes 1646600 | tf_op jit(solution)/shard_map/ppermute | solution.py:411
  63.9 13.6 %copy-start.6 = (bf16[536,512]{1,0:T(8,128)(2,1)}, bf16[536,512]{1,0:T(8,128)(2,1)S(1)}, u32[]{:S(2)}) copy-start(bf16[536,512]{1,0:T(8,128)(2,1)S(1)} %collective-permute-done.4.w3) | copy-start | bytes 1646596
  65.2 12.4 %copy-start.7 = (bf16[536,512]{1,0:T(8,128)(2,1)}, bf16[536,512]{1,0:T(8,128)(2,1)S(1)}, u32[]{:S(2)}) copy-start(bf16[536,512]{1,0:T(8,128)(2,1)S(1)} %collective-permute-done.5.w4) | copy-start | bytes 1646596
  65.2 12.3 %collective-permute-start.6 = (bf16[536,512]{1,0:T(8,128)(2,1)S(1)}, bf16[536,512]{1,0:T(8,128)(2,1)S(1)}, u32[]{:S(2)}, u32[]{:S(2)}) collective-permute-start(bf16[536,512]{1,0:T(8,128)(2,1)S(1)} %collective-permute-done.4.w3), channel_id=1, source_target_pairs={{0,64},{64,128},{128,192},{192,256},{256,320},{320,384},{384,448},... | collective-permute-start | bytes 1646600 | tf_op jit(solution)/shard_map/ppermute | solution.py:410
  69.2 10.7 %collective-permute-start.7 = (bf16[536,512]{1,0:T(8,128)(2,1)S(1)}, bf16[536,512]{1,0:T(8,128)(2,1)S(1)}, u32[]{:S(2)}, u32[]{:S(2)}) collective-permute-start(bf16[536,512]{1,0:T(8,128)(2,1)S(1)} %collective-permute-done.5.w4), channel_id=1, source_target_pairs={{0,448},{64,0},{128,64},{192,128},{256,192},{320,256},{384,320},{4... | collective-permute-start | bytes 1646600 | tf_op jit(solution)/shard_map/ppermute | solution.py:411
  77.6 12.5 %copy-start.2 = (bf16[536,512]{1,0:T(8,128)(2,1)}, bf16[536,512]{1,0:T(8,128)(2,1)S(1)}, u32[]{:S(2)}) copy-start(bf16[536,512]{1,0:T(8,128)(2,1)S(1)} %collective-permute-done.6.w5) | copy-start | bytes 1646596
  79.9 10.8 %copy-start.3 = (bf16[536,512]{1,0:T(8,128)(2,1)}, bf16[536,512]{1,0:T(8,128)(2,1)S(1)}, u32[]{:S(2)}) copy-start(bf16[536,512]{1,0:T(8,128)(2,1)S(1)} %collective-permute-done.7.w6) | copy-start | bytes 1646596
  80.8 1.4 copy-start
  82.2 17.3 %collective-permute-start.8 = (bf16[4,2,272,512]{3,2,1,0:T(8,128)(2,1)S(1)}, bf16[4,2,272,512]{3,2,1,0:T(8,128)(2,1)}, u32[]{:S(2)}, u32[]{:S(2)}) collective-permute-start(bf16[4,2,272,512]{3,2,1,0:T(8,128)(2,1)S(1)} %bitcast.33), channel_id=1, source_target_pairs={{0,1},{1,0},{2,3},{3,2},{4,5},{5,4},{6,7},{7,6},{8,9},{9,8},{10,11... | collective-permute-start | bytes 6684680 | tf_op jit(solution)/shard_map/ppermute | solution.py:484
  91.5 24.1 %collective-permute-start.9 = (bf16[256,512]{1,0:T(8,128)(2,1)}, bf16[256,512]{1,0:T(8,128)(2,1)}, u32[]{:S(2)}, u32[]{:S(2)}) collective-permute-start(bf16[256,512]{1,0:T(8,128)(2,1)} %slice.18), channel_id=1, source_target_pairs={{0,64},{64,128},{128,192},{192,256},{256,320},{320,384},{384,448},... | collective-permute-start | bytes 786440 | tf_op jit(solution)/shard_map/ppermute | solution.py:421
  94.6 21.0 %collective-permute-start.10 = (bf16[256,512]{1,0:T(8,128)(2,1)}, bf16[256,512]{1,0:T(8,128)(2,1)}, u32[]{:S(2)}, u32[]{:S(2)}) collective-permute-start(bf16[256,512]{1,0:T(8,128)(2,1)} %slice.19), channel_id=1, source_target_pairs={{0,448},{64,0},{128,64},{192,128},{256,192},{320,256},{384,320},{4... | collective-permute-start | bytes 786440 | tf_op jit(solution)/shard_map/ppermute | solution.py:422
  106.3 17.2 %all-to-all-start.2 = ((bf16[16,16,544]{2,1,0:T(8,128)(2,1)}), bf16[16,16,544]{2,1,0:T(8,128)(2,1)}, u32[]{:S(2)}, u32[]{:S(2)}) async-start(bf16[16,16,544]{2,1,0:T(8,128)(2,1)} %broadcast_in_dim.48), calls=%async_computation.2 | async-start | bytes 655360 | tf_op jit(solution)/shard_map/all_to_all | solution.py:503
  130.4 16.2 %all-to-all-start.3 = ((bf16[32,24,128]{2,1,0:T(8,128)(2,1)}), bf16[32,24,128]{2,1,0:T(8,128)(2,1)}, u32[]{:S(2)}, u32[]{:S(2)}) async-start(bf16[32,24,128]{2,1,0:T(8,128)(2,1)} %get-tuple-element.51), calls=%async_computation.3 | async-start | bytes 393216 | tf_op jit(solution)/shard_map/all_to_all | solution.py:531
  148.3 14.0 %all-to-all-start.4 = ((bf16[32,16,128]{2,1,0:T(8,128)(2,1)}), bf16[32,16,128]{2,1,0:T(8,128)(2,1)}, u32[]{:S(2)}, u32[]{:S(2)}) async-start(bf16[32,16,128]{2,1,0:T(8,128)(2,1)} %shard_map.131), calls=%async_computation.4 | async-start | bytes 262144 | tf_op jit(solution)/shard_map/all_to_all | solution.py:539
  167.9 19.1 %collective-permute-start.11 = (bf16[256,512]{1,0:T(8,128)(2,1)}, bf16[256,512]{1,0:T(8,128)(2,1)}, u32[]{:S(2)}, u32[]{:S(2)}) collective-permute-start(bf16[256,512]{1,0:T(8,128)(2,1)} %get-tuple-element.53), channel_id=1, source_target_pairs={{0,8},{8,0},{1,9},{9,1},{2,10},{10,2},{3,11},{11,3},{4,12},{12,4},... | collective-permute-start | bytes 786440 | tf_op jit(solution)/shard_map/ppermute | solution.py:559

commit v6 on v5

--- a/solution.py
+++ b/solution.py
@@ -18,10 +18,14 @@
 
 SEQ = ("z", "x", "yl")
 TP = ("yh", "c")
+OFFSETS = (0, -1, 1, -2, 2, -3, 3, 4)
 SIZES = {"z": 8, "x": 4, "yl": 2, "yh": 4, "c": 2}
 
 
-def call(kernel, outs, scalars, *args, blocks=None, scratch=(), flops=0, bytes_accessed=0):
+def call(
+    kernel, outs, scalars, *args, blocks=None, scratch=(), flops=0, bytes_accessed=0,
+    grant=20 * 1024 * 1024,
+):
     blocks = blocks or {}
     specs = [
         pl.BlockSpec(*blocks[at])
@@ -43,7 +47,7 @@
             scratch_shapes=list(scratch),
         ),
         out_shape=outs,
-        compiler_params=pltpu.CompilerParams(vmem_limit_bytes=ALL_VMEM),
+        compiler_params=pltpu.CompilerParams(vmem_limit_bytes=grant),
         cost_estimate=pl.CostEstimate(
             flops=flops, bytes_accessed=bytes_accessed, transcendentals=0
         ),
@@ -126,29 +130,20 @@
 
 
 def project_kernel(
-    where_ref, own_ref, other_ref, w0, w1, w2, w3, w4, w5, w6, w7, w8,
+    where_ref, own_ref, other_ref, w0, w1, w2, w3, w4, w5, w6, w7,
     x_ref, feats, weights, acc, sem, weight_sem,
 ):
     blocks, depth = weights.shape[0], weights.shape[1]
-    cut = w7.shape[0]
     fetch_tokens(where_ref, own_ref, other_ref, feats, sem)
     copies = [
-        [pltpu.make_async_copy(ref.at[0:depth], weights.at[at], weight_sem.at[at])]
-        for at, ref in enumerate((w0, w1, w2, w3, w4, w5, w6))
+        pltpu.make_async_copy(ref.at[0:depth], weights.at[at], weight_sem.at[at])
+        for at, ref in enumerate((w0, w1, w2, w3, w4, w5, w6, w7))
     ]
-    copies.append(
-        [
-            pltpu.make_async_copy(w7, weights.at[7, 0:cut], weight_sem.at[7]),
-            pltpu.make_async_copy(w8, weights.at[7, cut:], weight_sem.at[8]),
-        ]
-    )
-    for group in copies:
-        for copy in group:
-            copy.start()
+    for copy in copies:
+        copy.start()
     for step in range(blocks):
         pltpu.make_async_copy(own_ref.at[0], feats.at[step], sem.at[step]).wait()
-        for copy in copies[step]:
-            copy.wait()
+        copies[step].wait()
         for part in range(2):
             found = dot(feats[step, part], weights[step], ((1,), (0,)))
             if step == 0:
@@ -187,7 +182,7 @@
 def project(where, own, other, weights):
     _, _, rows, depth = own.shape
     channels = weights[0].shape[1]
-    blocks = len(weights) - 1
+    blocks = len(weights)
     return pl.pallas_call(
         project_kernel,
         in_specs=[pl.BlockSpec(memory_space=pltpu.SMEM)]
@@ -198,7 +193,7 @@
             pltpu.VMEM((blocks, depth, channels), jnp.bfloat16),
             pltpu.VMEM((2, rows, channels), jnp.float32),
             pltpu.SemaphoreType.DMA((blocks,)),
-            pltpu.SemaphoreType.DMA((blocks + 1,)),
+            pltpu.SemaphoreType.DMA((blocks,)),
         ],
         out_shape=jax.ShapeDtypeStruct((2, rows, channels), jnp.bfloat16),
         compiler_params=pltpu.CompilerParams(vmem_limit_bytes=ALL_VMEM),
@@ -398,31 +393,43 @@
             out_ref[:, on] = (normed - penalty * factor).astype(jnp.bfloat16)
 
 
-def ring(block, depth, axis):
+def prepare_parameters(d_skip, norm_gain, steer, dt_bias, decay_rate, z):
+    channel_rows = jnp.concatenate(
+        [
+            jnp.repeat(d_skip, HEAD)[None], norm_gain[None], steer[None],
+            jnp.zeros((5, steer.shape[0]), jnp.float32),
+        ],
+        0,
+    )
+    head_columns = jnp.stack([dt_bias, decay_rate], 1)
+    source = (z + jnp.array(OFFSETS, jnp.int32)) % SIZES["z"]
+    where = jnp.concatenate(
+        [source // 2, (source % 2 == lax.axis_index("c")).astype(jnp.int32)]
+    )
+    return channel_rows, head_columns, where
+
+
+def ring(block, depth, axis, prepare, raw):
     count = SIZES[axis]
     forward = [(i, (i + 1) % count) for i in range(count)]
     backward = [(i, (i - 1) % count) for i in range(count)]
     across = [(i, (i + count // 2) % count) for i in range(count)]
-    pieces, offsets = [block], [0]
+    pieces = [block]
     ahead = behind = block
-    far = None
     for hop in range(1, count // 2):
         ahead = lax.ppermute(ahead, axis, forward)
         behind = lax.ppermute(behind, axis, backward)
-        if far is None:
+        if hop == 1:
             far = lax.ppermute(block[depth:], axis, across)
+            ready = prepare(*lax.optimization_barrier((raw, far))[0])
             ahead, behind, far = lax.optimization_barrier((ahead, behind, far))
+        elif hop == 2:
+            ahead, behind, ready = lax.optimization_barrier((ahead, behind, ready))
         else:
             ahead, behind = lax.optimization_barrier((ahead, behind))
         pieces += [ahead, behind]
-        offsets += [-hop, hop]
-    cut = (depth // 2 + 15) // 16 * 16
-    last = [
-        lax.ppermute(ahead[:cut], axis, forward),
-        lax.ppermute(behind[cut:depth], axis, backward),
-    ]
-    offsets.append(count // 2)
-    return pieces, far, last, offsets
+    pieces.append(lax.ppermute(ahead, axis, forward))
+    return pieces, far, ready
 
 
 def per_device(
@@ -437,7 +444,7 @@
     small = bc_rows + heads
     seq_count = SIZES["z"] * SIZES["x"] * SIZES["yl"]
     tp_count = SIZES["yh"] * SIZES["c"]
-    z, core = lax.axis_index("z"), lax.axis_index("c")
+    z = lax.axis_index("z")
     mine = lax.axis_index("yl").astype(jnp.int32).reshape(1)
     f32, bf16 = jnp.float32, jnp.bfloat16
 
@@ -474,7 +481,12 @@
         fan, packed_rows, half // k_rows, k_rows
     )
     flat = flat.transpose(1, 2, 0, 3).reshape(small, fan * k_rows)
-    pieces, far, last, offsets = ring(jnp.concatenate([tall, flat], 0), fan * k_rows, "z")
+    block = jnp.concatenate([tall, flat], 0)
+    pieces, far, ready = ring(
+        block, fan * k_rows, "z", prepare_parameters,
+        (d_skip, norm_gain, steer, dt_bias, decay_rate, z.astype(jnp.int32)),
+    )
+    channel_rows, head_columns, where = ready
 
     copies = lax.optimization_barrier((copies, got))[0]
     own = lax.all_to_all(copies, ("yh", "yl"), 0, 0).reshape(
@@ -483,23 +495,9 @@
     own = lax.optimization_barrier((own, pieces[5], pieces[6]))[0]
     other = lax.ppermute(own, "c", [(0, 1), (1, 0)])
 
-    channel_rows = jnp.concatenate(
-        [
-            jnp.repeat(d_skip, HEAD)[None], norm_gain[None], steer[None],
-            jnp.zeros((5, channels), f32),
-        ],
-        0,
-    )
-    head_columns = jnp.stack([dt_bias, decay_rate], 1)
-    channel_rows, head_columns, _ = lax.optimization_barrier(
-        (channel_rows, head_columns, pieces[3])
-    )
-    source = (z + jnp.array(offsets, jnp.int32)) % SIZES["z"]
-    where = jnp.concatenate([source // 2, (source % 2 == core).astype(jnp.int32)])
-
-    bc_pre, dt_raw = narrow_project(where, own, other, pieces + [far], bc_rows, heads)
-    last[0] = lax.optimization_barrier((last[0], bc_pre))[0]
-    x_pre = project(where, own, other, pieces + last)
+    bc_pre, dt_raw = narrow_project(where, own, other, pieces[:-1] + [far], bc_rows, heads)
+    pieces[-1] = lax.optimization_barrier((pieces[-1], bc_pre))[0]
+    x_pre = project(where, own, other, pieces)
     bc_all = lax.all_to_all(
         jnp.broadcast_to(
             bc_pre.reshape(1, bc_rows, -1), (2 * tp_count, bc_rows, 2 * (local + HALO))
@@ -527,6 +525,7 @@
             5: ((heads, 2), lambda i, s: (s[0], 0)),
         },
         scratch=[pltpu.VMEM((half, pair), bf16)],
+        grant=ALL_VMEM,
     )
     states = lax.all_to_all(payload, ("z", "x"), 0, 0)
     place = mine * plane + lax.axis_index(("z", "x")).astype(jnp.int32)

time: 191 us -> 182 us (0.953)
  Pallas kernels: 31.3 us -> 24.6 us
  local copies, waits for them, and re-layouts: 13.1 us -> 17.7 us
  waiting for transfers between devices: 44.2 us -> 41.2 us
  starting transfers between devices: 82.9 us -> 80 us
    pallas_call x5, Pallas kernels: 20 us -> 13.1 us  [call(): pl.pallas_call(kernel, grid_spec=pltpu.PrefetchScalarGridSpec(num_scalar_...]
    unnamed x24 -> x44, local copies, waits for them, and re-layouts: 2.71 us -> 8.73 us
    ppermute x2 -> x1, starting transfers between devices: 7.94 us -> 3.13 us  [ring(): pieces.append(lax.ppermute(ahead, axis, forward))]
    all_to_all x1, waiting for transfers between devices: 4.73 us -> 1.79 us  [per_device(): entering = lax.all_to_all(prefixes, ('z', 'x'), 0, 0).reshape(half, N)]
    all_to_all x1, waiting for transfers between devices: 1.88 us -> 3.99 us  [per_device(): lax.all_to_all(jnp.broadcast_to(bc_pre.reshape(1, bc_rows, -1), (2 * tp_c...]
  transfers between devices with their start and end apart: 17 -> 16, of which waited for: 12 -> 13; matrix products, arithmetic and copies ran while one was open for 5% -> 3% of each run, Pallas kernels for 8% -> 8%
where the time goes in v6:
time: 182 us; the launch traced here: 181 us
  starting transfers between devices  80 us (44%)
  waiting for transfers between devices  41.2 us (23%)
  Pallas kernels  24.6 us (14%)
  local copies, waits for them, and re-layouts  17.7 us (10%)
  blocking collectives  14 us (8%)
  other arithmetic  2.9 us (2%)
    ppermute x3, starting transfers between devices, ring(): behind = lax.ppermute(behind, axis, backward)  14.5 us
    all_to_all x1, blocking collectives, per_device(): lax.all_to_all(jnp.broadcast_to(dots[None, :, None], shape).reshape(2 * t...  14 us
    pallas_call x5, Pallas kernels, call(): pl.pallas_call(kernel, grid_spec=pltpu.PrefetchScalarGridSpec(num_scalar_...  13.1 us
    ppermute x3, starting transfers between devices, ring(): ahead = lax.ppermute(ahead, axis, forward)  12.6 us
    ppermute x3, waiting for transfers between devices, ring(): ahead = lax.ppermute(ahead, axis, forward)  11 us
    all_to_all x1, waiting for transfers between devices, per_device(): states = lax.all_to_all(payload, ('z', 'x'), 0, 0)  10.5 us
    unnamed x44, local copies, waits for them, and re-layouts  8.73 us
    all_to_all x1, starting transfers between devices, per_device(): lax.all_to_all(copies, ('yh', 'yl'), 0, 0)  7.91 us
  transfers between devices with their start and end apart: 16, of which 13 were waited for; matrix products, arithmetic and copies ran while one was open for 3% of the time, Pallas kernels for 8%

profile of v6, /device:TPU:1, one launch (start us, length us, event | category | flops | bytes accessed | tf_op | source)
XLA Modules:
  0.0 180.6 jit_solution(5770387936750878272)
XLA Ops:
  0.0 0.8 pad_maximum_fusion.2
  0.8 0.1 reshape.60
  0.9 1.0 reshape.57
  1.9 0.1 pad.14.clone
  1.9 0.2 maximum_maximum_fusion
  2.2 0.9 broadcast_in_dim.45
  3.1 5.9 %all-to-all-start = ((bf16[8,72,512]{2,1,0:T(8,128)(2,1)}), bf16[8,72,512]{2,1,0:T(8,128)(2,1)S(1)}, u32[]{:S(2)}, u32[]{:S(2)}) async-start(bf16[8,72,512]{2,1,0:T(8,128)(2,1)} %bitcast.6), calls=%async_computation | async-start | bytes 1179648 | tf_op jit(solution)/shard_map/all_to_all | solution.py:478
  9.0 3.4 %collective-permute-start.5 = (bf16[16,512]{1,0:T(8,128)(2,1)S(1)}, bf16[16,512]{1,0:T(8,128)(2,1)S(1)}, u32[]{:S(2)}, u32[]{:S(2)}) collective-permute-start(bf16[16,512]{1,0:T(8,128)(2,1)S(1)} %slice.11), channel_id=1, source_target_pairs={{0,8},{8,16},{16,24},{24,32},{32,40},{40,48},{48,56},{56,64},{64,7... | collective-permute-start | bytes 49160 | tf_op jit(solution)/shard_map/ppermute | solution.py:451
  12.3 0.9 collective-permute-done.5
  13.2 3.6 %all-to-all-done = bf16[8,72,512]{2,1,0:T(8,128)(2,1)S(1)} async-done(((bf16[8,72,512]{2,1,0:T(8,128)(2,1)}), bf16[8,72,512]{2,1,0:T(8,128)(2,1)S(1)}, u32[]{:S(2)}, u32[]{:S(2)}) %all-to-all-start) | async-done | bytes 589856 | tf_op jit(solution)/shard_map/all_to_all | solution.py:478
  16.8 1.6 broadcast_in_dim.50
  18.4 7.9 %all-to-all-start.1 = ((bf16[8,272,512]{2,1,0:T(8,128)(2,1)}), bf16[8,272,512]{2,1,0:T(8,128)(2,1)S(1)}, u32[]{:S(2)}, u32[]{:S(2)}) async-start(bf16[8,272,512]{2,1,0:T(8,128)(2,1)} %broadcast_in_dim.50), calls=%async_computation.1 | async-start | bytes 4456448 | tf_op jit(solution)/shard_map/all_to_all | solution.py:492
  26.4 0.1 reshape.63
  26.5 0.1 reshape.64
  26.7 4.0 %collective-permute-start = (bf16[536,512]{1,0:T(8,128)(2,1)S(1)}, bf16[536,512]{1,0:T(8,128)(2,1)S(1)}, u32[]{:S(2)}, u32[]{:S(2)}) collective-permute-start(bf16[536,512]{1,0:T(8,128)(2,1)S(1)} %pad_maximum_fusion.w0), channel_id=1, source_target_pairs={{0,64},{64,128},{128,192},{192,256},{256,320},{320,384},{384,448},... | collective-permute-start | bytes 1646600 | tf_op jit(solution)/shard_map/ppermute | solution.py:420
  30.7 8.7 %collective-permute-start.1 = (bf16[536,512]{1,0:T(8,128)(2,1)S(1)}, bf16[536,512]{1,0:T(8,128)(2,1)}, u32[]{:S(2)}, u32[]{:S(2)}) collective-permute-start(bf16[536,512]{1,0:T(8,128)(2,1)S(1)} %pad_maximum_fusion.w0), channel_id=1, source_target_pairs={{0,448},{64,0},{128,64},{192,128},{256,192},{320,256},{384,320},{4... | collective-permute-start | bytes 1646600 | tf_op jit(solution)/shard_map/ppermute | solution.py:421
  39.4 4.4 %collective-permute-start.2 = (bf16[24,512]{1,0:T(8,128)(2,1)S(1)}, bf16[24,512]{1,0:T(8,128)(2,1)S(1)}, u32[]{:S(2)}, u32[]{:S(2)}) collective-permute-start(bf16[24,512]{1,0:T(8,128)(2,1)S(1)} %reshape.64), channel_id=1, source_target_pairs={{0,256},{64,320},{128,384},{192,448},{256,0},{320,64},{384,128},{4... | collective-permute-start | bytes 73736 | tf_op jit(solution)/shard_map/ppermute | solution.py:423
  43.9 0.1 pad.9.clone
  44.0 5.1 %collective-permute-done.2.w7 = bf16[24,512]{1,0:T(8,128)(2,1)S(1)} collective-permute-done((bf16[24,512]{1,0:T(8,128)(2,1)S(1)}, bf16[24,512]{1,0:T(8,128)(2,1)S(1)}, u32[]{:S(2)}, u32[]{:S(2)}) %collective-permute-start.2) | collective-permute-done | bytes 24608 | tf_op jit(solution)/shard_map/ppermute | solution.py:423
  49.1 0.3 collective-permute-done.1.w2
  49.4 4.6 %collective-permute-start.3 = (bf16[536,512]{1,0:T(8,128)(2,1)S(1)}, bf16[536,512]{1,0:T(8,128)(2,1)}, u32[]{:S(2)}, u32[]{:S(2)}) collective-permute-start(bf16[536,512]{1,0:T(8,128)(2,1)S(1)} %collective-permute-done.w1), channel_id=1, source_target_pairs={{0,64},{64,128},{128,192},{192,256},{256,320},{320,384},{384,448},... | collective-permute-start | bytes 1646600 | tf_op jit(solution)/shard_map/ppermute | solution.py:420
  54.0 2.9 %collective-permute-start.4 = (bf16[536,512]{1,0:T(8,128)(2,1)}, bf16[536,512]{1,0:T(8,128)(2,1)}, u32[]{:S(2)}, u32[]{:S(2)}) collective-permute-start(bf16[536,512]{1,0:T(8,128)(2,1)} %collective-permute-done.1.w2), channel_id=1, source_target_pairs={{0,448},{64,0},{128,64},{192,128},{256,192},{320,256},{384,320},{4... | collective-permute-start | bytes 1646600 | tf_op jit(solution)/shard_map/ppermute | solution.py:421
  57.0 0.1 broadcast_in_dim_reshape.3
  57.1 0.6 pad_add_fusion.where_ref
  57.6 0.6 pad_maximum_fusion.3
  58.2 0.7 maximum_maximum_fusion.1.chan_ref
  58.9 5.3 %collective-permute-done.3.w3 = bf16[536,512]{1,0:T(8,128)(2,1)} collective-permute-done((bf16[536,512]{1,0:T(8,128)(2,1)S(1)}, bf16[536,512]{1,0:T(8,128)(2,1)}, u32[]{:S(2)}, u32[]{:S(2)}) %collective-permute-start.3) | collective-permute-done | bytes 548896 | tf_op jit(solution)/shard_map/ppermute | solution.py:420
  64.2 1.4 collective-permute-done.4.w4
  65.6 4.0 %collective-permute-start.6 = (bf16[536,512]{1,0:T(8,128)(2,1)}, bf16[536,512]{1,0:T(8,128)(2,1)S(1)}, u32[]{:S(2)}, u32[]{:S(2)}) collective-permute-start(bf16[536,512]{1,0:T(8,128)(2,1)} %collective-permute-done.3.w3), channel_id=1, source_target_pairs={{0,64},{64,128},{128,192},{192,256},{256,320},{320,384},{384,448},... | collective-permute-start | bytes 1646600 | tf_op jit(solution)/shard_map/ppermute | solution.py:420
  69.6 2.9 %collective-permute-start.7 = (bf16[536,512]{1,0:T(8,128)(2,1)}, bf16[536,512]{1,0:T(8,128)(2,1)}, u32[]{:S(2)}, u32[]{:S(2)}) collective-permute-start(bf16[536,512]{1,0:T(8,128)(2,1)} %collective-permute-done.4.w4), channel_id=1, source_target_pairs={{0,448},{64,0},{128,64},{192,128},{256,192},{320,256},{384,320},{4... | collective-permute-start | bytes 1646600 | tf_op jit(solution)/shard_map/ppermute | solution.py:421
  72.6 5.7 %collective-permute-done.6.w5 = bf16[536,512]{1,0:T(8,128)(2,1)S(1)} collective-permute-done((bf16[536,512]{1,0:T(8,128)(2,1)}, bf16[536,512]{1,0:T(8,128)(2,1)S(1)}, u32[]{:S(2)}, u32[]{:S(2)}) %collective-permute-start.6) | collective-permute-done | bytes 548896 | tf_op jit(solution)/shard_map/ppermute | solution.py:420
  78.3 0.8 copy-done.12
  79.1 1.5 collective-permute-done.7.w6
  80.7 0.1 all-to-all-done.1
  80.8 1.4 copy-done.9
  82.2 7.8 %collective-permute-start.8 = (bf16[4,2,272,512]{3,2,1,0:T(8,128)(2,1)S(1)}, bf16[4,2,272,512]{3,2,1,0:T(8,128)(2,1)}, u32[]{:S(2)}, u32[]{:S(2)}) collective-permute-start(bf16[4,2,272,512]{3,2,1,0:T(8,128)(2,1)S(1)} %bitcast.36), channel_id=1, source_target_pairs={{0,1},{1,0},{2,3},{3,2},{4,5},{5,4},{6,7},{7,6},{8,9},{9,8},{10,11... | collective-permute-start | bytes 6684680 | tf_op jit(solution)/shard_map/ppermute | solution.py:496
  90.0 3.1 %collective-permute-start.9 = (bf16[536,512]{1,0:T(8,128)(2,1)}, bf16[536,512]{1,0:T(8,128)(2,1)}, u32[]{:S(2)}, u32[]{:S(2)}) collective-permute-start(bf16[536,512]{1,0:T(8,128)(2,1)} %copy-done.12), channel_id=1, source_target_pairs={{0,64},{64,128},{128,192},{192,256},{256,320},{320,384},{384,448},... | collective-permute-start | bytes 1646600 | tf_op jit(solution)/shard_map/ppermute | solution.py:431
  93.2 0.9 collective-permute-done.8.other_ref
  94.1 5.3 %shard_map.127 = (bf16[16,2,272]{2,1,0:T(2,128)(2,1)}, f32[8,512]{1,0:T(8,128)}) custom-call(s32[16]{0:T(128)} %pad_add_fusion.where_ref, bf16[4,2,272,512]{3,2,1,0:T(8,128)(2,1)} %bitcast.37, bf16[4,2,272,512]{3,2,1,0:T(8,128)(2,1)} %collective-permute-done.8.other_ref, bf16[536,512]{1,0:T(8,128)(2,1)} %copy-done.10, bf16[536,512]{1,0:T(8,128)(2,1)} %copy-done.11, ...), custom_call_target="tpu_custom_call" | custom-call | flops 1000000000 | bytes 10000000 | tf_op jit(solution)/shard_map/pallas_call | solution.py:161
  99.4 0.8 broadcast_in_dim.51
  100.2 0.8 broadcast_in_dim.52
  101.0 7.0 %all-to-all-start.2 = ((bf16[16,16,544]{2,1,0:T(8,128)(2,1)}), bf16[16,16,544]{2,1,0:T(8,128)(2,1)}, u32[]{:S(2)}, u32[]{:S(2)}) async-start(bf16[16,16,544]{2,1,0:T(8,128)(2,1)} %broadcast_in_dim.52), calls=%async_computation.2 | async-start | bytes 655360 | tf_op jit(solution)/shard_map/all_to_all | solution.py:501
  107.9 1.3 copy.30.head_ref
  109.3 6.2 %shard_map.128.pre_ref = bf16[2,272,512]{2,1,0:T(8,128)(2,1)} custom-call(s32[16]{0:T(128)} %pad_add_fusion.where_ref, bf16[4,2,272,512]{3,2,1,0:T(8,128)(2,1)} %bitcast.38, bf16[4,2,272,512]{3,2,1,0:T(8,128)(2,1)} %collective-permute-done.8.other_ref, bf16[536,512]{1,0:T(8,128)(2,1)} %copy-done.10, bf16[536,512]{1,0:T(8,128)(2,1)} %copy-done.11, ...), custom_call_target="tpu_custom_call" | custom-call | flops 3000000000 | bytes 10000000 | tf_op jit(solution)/shard_map/pallas_call | solution.py:186
  115.5 4.0 %all-to-all-done.2 = bf16[16,16,544]{2,1,0:T(8,128)(2,1)} async-done(((bf16[16,16,544]{2,1,0:T(8,128)(2,1)}), bf16[16,16,544]{2,1,0:T(8,128)(2,1)}, u32[]{:S(2)}, u32[]{:S(2)}) %all-to-all-start.2) | async-done | bytes 278560 | tf_op jit(solution)/shard_map/all_to_all | solution.py:501
  119.4 1.8 %copy.29 = bf16[544,256]{1,0:T(8,128)(2,1)} copy(bf16[544,256]{0,1:T(8,128)(2,1)} %bitcast.15) | data formatting | bytes 557056 | tf_op jit(solution)/shard_map/transpose | solution.py:507
  121.3 5.2 %shard_map.129 = (bf16[512,512]{1,0:T(8,128)(2,1)}, bf16[512,256]{1,0:T(8,128)(2,1)}, f32[8,512]{1,0:T(8,128)}, f32[8,512]{1,0:T(8,128)}, bf16[32,24,128]{2,1,0:T(8,128)(2,1)}, /*index=5*/f32[4,512,128]{2,1,0:T(8,128)}) custom-call(s32[1]{0:T(128)} %bitcast.mine_ref, bf16[2,272,512]{2,1,0:T(8,128)(2,1)} %shard_map.128.pre_ref, ...), custom_call_target="tpu_custom_call" | custom-call | tf_op jit(solution)/shard_map/pallas_call | solution.py:40
  126.4 5.9 %all-to-all-start.3 = ((bf16[32,24,128]{2,1,0:T(8,128)(2,1)}), bf16[32,24,128]{2,1,0:T(8,128)(2,1)S(1)}, u32[]{:S(2)}, u32[]{:S(2)}) async-start(bf16[32,24,128]{2,1,0:T(8,128)(2,1)} %get-tuple-element.65), calls=%async_computation.3 | async-start | bytes 393216 | tf_op jit(solution)/shard_map/all_to_all | solution.py:530
  132.3 10.5 %all-to-all-done.3.got_ref = bf16[32,24,128]{2,1,0:T(8,128)(2,1)S(1)} async-done(((bf16[32,24,128]{2,1,0:T(8,128)(2,1)}), bf16[32,24,128]{2,1,0:T(8,128)(2,1)S(1)}, u32[]{:S(2)}, u32[]{:S(2)}) %all-to-all-start.3) | async-done | bytes 196640 | tf_op jit(solution)/shard_map/all_to_all | solution.py:530
  142.9 1.0 copy-done
  143.9 0.7 shard_map.131
  144.6 4.2 %all-to-all-start.4 = ((bf16[32,16,128]{2,1,0:T(8,128)(2,1)}), bf16[32,16,128]{2,1,0:T(8,128)(2,1)S(1)}, u32[]{:S(2)}, u32[]{:S(2)}) async-start(bf16[32,16,128]{2,1,0:T(8,128)(2,1)} %shard_map.131), calls=%async_computation.4 | async-start | bytes 262144 | tf_op jit(solution)/shard_map/all_to_all | solution.py:538
  148.8 0.7 copy-done.1
  149.6 0.9 copy-done.3
  150.5 1.2 copy-done.5
  151.7 1.0 copy-done.6
  152.8 0.7 copy-done.7
  153.5 0.7 copy-done.8
  154.2 2.1 %shard_map.130 = (f32[512,512]{1,0:T(8,128)S(1)}, f32[512,512]{1,0:T(8,128)S(1)}) custom-call(s32[1]{0:T(128)} %bitcast.mine_ref, bf16[512,512]{1,0:T(8,128)(2,1)S(1)} %copy-done.6, bf16[512,256]{1,0:T(8,128)(2,1)S(1)} %copy-done.3, f32[8,512]{1,0:T(8,128)S(1)} %copy-done.7, f32[8,512]{1,0:T(8,128)S(1)} %copy-done.8, f32[4,512,128]{2,1,0:T(8,128)S(1)} %copy-done.5, ...), custom_call_target="tpu_custom_call" | custom-call | flops 1000000000 | bytes 3145728 | tf_op jit(solution)/shard_map/pallas_call | solution.py:40
  156.4 1.8 all-to-all-done.4
  158.2 3.3 %shard_map.132 = (f32[256,512]{1,0:T(8,128)S(1)}, bf16[256,512]{1,0:T(8,128)(2,1)S(1)}, f32[2,1,256]{2,1,0:T(1,128)S(1)}) custom-call(s32[1]{0:T(128)} %bitcast.mine_ref, f32[512,512]{1,0:T(8,128)S(1)} %get-tuple-element.63.inside_ref, f32[512,512]{1,0:T(8,128)S(1)} %get-tuple-element.64.growth_ref, bf16[512,256]{1,0:T(8,128)(2,1)S(1)} %copy-done.4, ...), custom_call_target="tpu_custom_call" | custom-call | tf_op jit(solution)/shard_map/pallas_call | solution.py:40
  161.4 3.3 %collective-permute-start.10 = (bf16[256,512]{1,0:T(8,128)(2,1)S(1)}, bf16[256,512]{1,0:T(8,128)(2,1)S(1)}, u32[]{:S(2)}, u32[]{:S(2)}) collective-permute-start(bf16[256,512]{1,0:T(8,128)(2,1)S(1)} %get-tuple-element.67), channel_id=1, source_target_pairs={{0,8},{8,0},{1,9},{9,1},{2,10},{10,2},{3,11},{11,3},{4,12},{12,4},... | collective-permute-start | bytes 786440 | tf_op jit(solution)/shard_map/ppermute | solution.py:558
  164.8 14.0 %all_to_all.30 = f32[16,1,256]{2,1,0:T(1,128)S(1)} all-to-all(f32[16,1,256]{2,1,0:T(1,128)S(1)} %broadcast_in_dim.55), channel_id=1, replica_groups=mesh['z'=8,'x'=4,'yl'=2,'yh'=4,'c'=2] {'yh','yl','c'}, dimensions={0} | all-to-all | bytes 32768 | tf_op jit(solution)/shard_map/all_to_all | solution.py:560
  178.8 1.8 %shard_map.133 = bf16[256,1024]{1,0:T(8,128)(2,1)} custom-call(s32[1]{0:T(128)} %bitcast.mine_ref, f32[256,512]{1,0:T(8,128)S(1)} %get-tuple-element.66.keep_ref, bf16[256,512]{1,0:T(8,128)(2,1)S(1)} %collective-permute-done.10.other_ref, f32[16,256]{1,0:T(8,128)S(1)} %bitcast.35, f32[8,1024]{1,0:T(8,128)S(1)} %copy-done.2), custom_call_target="tpu_custom_call" | custom-call | tf_op jit(solution)/shard_map/pallas_call | solution.py:40
  (54 shorter events, 0.4 us)
Async XLA Ops:
  0.0 8.9 %copy-start.13 = (bf16[256,512]{1,0:T(8,128)(2,1)S(1)}, bf16[256,512]{1,0:T(8,128)(2,1)}, u32[]{:S(2)}) copy-start(bf16[256,512]{1,0:T(8,128)(2,1)} %param.13) | copy-start | bytes 786436
  3.1 13.8 %all-to-all-start = ((bf16[8,72,512]{2,1,0:T(8,128)(2,1)}), bf16[8,72,512]{2,1,0:T(8,128)(2,1)S(1)}, u32[]{:S(2)}, u32[]{:S(2)}) async-start(bf16[8,72,512]{2,1,0:T(8,128)(2,1)} %bitcast.6), calls=%async_computation | async-start | bytes 1179648 | tf_op jit(solution)/shard_map/all_to_all | solution.py:478
  9.0 4.2 %collective-permute-start.5 = (bf16[16,512]{1,0:T(8,128)(2,1)S(1)}, bf16[16,512]{1,0:T(8,128)(2,1)S(1)}, u32[]{:S(2)}, u32[]{:S(2)}) collective-permute-start(bf16[16,512]{1,0:T(8,128)(2,1)S(1)} %slice.11), channel_id=1, source_target_pairs={{0,8},{8,16},{16,24},{24,32},{32,40},{40,48},{48,56},{56,64},{64,7... | collective-permute-start | bytes 49160 | tf_op jit(solution)/shard_map/ppermute | solution.py:451
  18.4 62.4 %all-to-all-start.1 = ((bf16[8,272,512]{2,1,0:T(8,128)(2,1)}), bf16[8,272,512]{2,1,0:T(8,128)(2,1)S(1)}, u32[]{:S(2)}, u32[]{:S(2)}) async-start(bf16[8,272,512]{2,1,0:T(8,128)(2,1)} %broadcast_in_dim.50), calls=%async_computation.1 | async-start | bytes 4456448 | tf_op jit(solution)/shard_map/all_to_all | solution.py:492
  26.3 22.8 %copy-start.20 = (s32[8]{0:T(128)S(1)}, s32[8]{0:T(128)}, u32[]{:S(2)}) copy-start(s32[8]{0:T(128)} %constant.65.clone) | copy-start | bytes 100
  26.3 30.6 %copy-start.17 = (f32[16]{0:T(128)S(1)}, f32[16]{0:T(128)}, u32[]{:S(2)}) copy-start(f32[16]{0:T(128)} %param.21) | copy-start | bytes 196
  26.3 31.3 %copy-start.18 = (f32[16]{0:T(128)S(1)}, f32[16]{0:T(128)}, u32[]{:S(2)}) copy-start(f32[16]{0:T(128)} %param.20) | copy-start | bytes 196
  26.3 31.3 %copy-start.19 = (f32[16]{0:T(128)S(1)}, f32[16]{0:T(128)}, u32[]{:S(2)}) copy-start(f32[16]{0:T(128)} %param.19) | copy-start | bytes 196
  26.3 31.9 %copy-start.15 = (f32[1024]{0:T(1024)S(1)}, f32[1024]{0:T(1024)}, u32[]{:S(2)}) copy-start(f32[1024]{0:T(1024)} %param.24) | copy-start | bytes 12292
  26.4 31.9 %copy-start.16 = (f32[1024]{0:T(1024)S(1)}, f32[1024]{0:T(1024)}, u32[]{:S(2)}) copy-start(f32[1024]{0:T(1024)} %param.22) | copy-start | bytes 12292
  26.7 63.3 %copy-start.10 = (bf16[536,512]{1,0:T(8,128)(2,1)}, bf16[536,512]{1,0:T(8,128)(2,1)S(1)}, u32[]{:S(2)}) copy-start(bf16[536,512]{1,0:T(8,128)(2,1)S(1)} %pad_maximum_fusion.w0) | copy-start | bytes 1646596
  26.7 22.4 %collective-permute-start = (bf16[536,512]{1,0:T(8,128)(2,1)S(1)}, bf16[536,512]{1,0:T(8,128)(2,1)S(1)}, u32[]{:S(2)}, u32[]{:S(2)}) collective-permute-start(bf16[536,512]{1,0:T(8,128)(2,1)S(1)} %pad_maximum_fusion.w0), channel_id=1, source_target_pairs={{0,64},{64,128},{128,192},{192,256},{256,320},{320,384},{384,448},... | collective-permute-start | bytes 1646600 | tf_op jit(solution)/shard_map/ppermute | solution.py:420
  30.7 18.6 %collective-permute-start.1 = (bf16[536,512]{1,0:T(8,128)(2,1)S(1)}, bf16[536,512]{1,0:T(8,128)(2,1)}, u32[]{:S(2)}, u32[]{:S(2)}) collective-permute-start(bf16[536,512]{1,0:T(8,128)(2,1)S(1)} %pad_maximum_fusion.w0), channel_id=1, source_target_pairs={{0,448},{64,0},{128,64},{192,128},{256,192},{320,256},{384,320},{4... | collective-permute-start | bytes 1646600 | tf_op jit(solution)/shard_map/ppermute | solution.py:421
  39.4 9.6 %collective-permute-start.2 = (bf16[24,512]{1,0:T(8,128)(2,1)S(1)}, bf16[24,512]{1,0:T(8,128)(2,1)S(1)}, u32[]{:S(2)}, u32[]{:S(2)}) collective-permute-start(bf16[24,512]{1,0:T(8,128)(2,1)S(1)} %reshape.64), channel_id=1, source_target_pairs={{0,256},{64,320},{128,384},{192,448},{256,0},{320,64},{384,128},{4... | collective-permute-start | bytes 73736 | tf_op jit(solution)/shard_map/ppermute | solution.py:423
  49.1 44.1 %copy-start.14 = (bf16[24,512]{1,0:T(8,128)(2,1)}, bf16[24,512]{1,0:T(8,128)(2,1)S(1)}, u32[]{:S(2)}) copy-start(bf16[24,512]{1,0:T(8,128)(2,1)S(1)} %collective-permute-done.2.w7) | copy-start | bytes 73732
  49.1 44.1 %copy-start.11 = (bf16[536,512]{1,0:T(8,128)(2,1)}, bf16[536,512]{1,0:T(8,128)(2,1)S(1)}, u32[]{:S(2)}) copy-start(bf16[536,512]{1,0:T(8,128)(2,1)S(1)} %collective-permute-done.w1) | copy-start | bytes 1646596
  49.4 14.8 %collective-permute-start.3 = (bf16[536,512]{1,0:T(8,128)(2,1)S(1)}, bf16[536,512]{1,0:T(8,128)(2,1)}, u32[]{:S(2)}, u32[]{:S(2)}) collective-permute-start(bf16[536,512]{1,0:T(8,128)(2,1)S(1)} %collective-permute-done.w1), channel_id=1, source_target_pairs={{0,64},{64,128},{128,192},{192,256},{256,320},{320,384},{384,448},... | collective-permute-start | bytes 1646600 | tf_op jit(solution)/shard_map/ppermute | solution.py:420
  54.0 11.6 %collective-permute-start.4 = (bf16[536,512]{1,0:T(8,128)(2,1)}, bf16[536,512]{1,0:T(8,128)(2,1)}, u32[]{:S(2)}, u32[]{:S(2)}) collective-permute-start(bf16[536,512]{1,0:T(8,128)(2,1)} %collective-permute-done.1.w2), channel_id=1, source_target_pairs={{0,448},{64,0},{128,64},{192,128},{256,192},{320,256},{384,320},{4... | collective-permute-start | bytes 1646600 | tf_op jit(solution)/shard_map/ppermute | solution.py:421
  65.6 12.7 %collective-permute-start.6 = (bf16[536,512]{1,0:T(8,128)(2,1)}, bf16[536,512]{1,0:T(8,128)(2,1)S(1)}, u32[]{:S(2)}, u32[]{:S(2)}) collective-permute-start(bf16[536,512]{1,0:T(8,128)(2,1)} %collective-permute-done.3.w3), channel_id=1, source_target_pairs={{0,64},{64,128},{128,192},{192,256},{256,320},{320,384},{384,448},... | collective-permute-start | bytes 1646600 | tf_op jit(solution)/shard_map/ppermute | solution.py:420
  69.6 11.0 %collective-permute-start.7 = (bf16[536,512]{1,0:T(8,128)(2,1)}, bf16[536,512]{1,0:T(8,128)(2,1)}, u32[]{:S(2)}, u32[]{:S(2)}) collective-permute-start(bf16[536,512]{1,0:T(8,128)(2,1)} %collective-permute-done.4.w4), channel_id=1, source_target_pairs={{0,448},{64,0},{128,64},{192,128},{256,192},{320,256},{384,320},{4... | collective-permute-start | bytes 1646600 | tf_op jit(solution)/shard_map/ppermute | solution.py:421
  78.3 0.8 copy-start.12
  80.8 1.4 copy-start.9
  82.2 11.9 %collective-permute-start.8 = (bf16[4,2,272,512]{3,2,1,0:T(8,128)(2,1)S(1)}, bf16[4,2,272,512]{3,2,1,0:T(8,128)(2,1)}, u32[]{:S(2)}, u32[]{:S(2)}) collective-permute-start(bf16[4,2,272,512]{3,2,1,0:T(8,128)(2,1)S(1)} %bitcast.36), channel_id=1, source_target_pairs={{0,1},{1,0},{2,3},{3,2},{4,5},{5,4},{6,7},{7,6},{8,9},{9,8},{10,11... | collective-permute-start | bytes 6684680 | tf_op jit(solution)/shard_map/ppermute | solution.py:496
  90.0 19.3 %collective-permute-start.9 = (bf16[536,512]{1,0:T(8,128)(2,1)}, bf16[536,512]{1,0:T(8,128)(2,1)}, u32[]{:S(2)}, u32[]{:S(2)}) collective-permute-start(bf16[536,512]{1,0:T(8,128)(2,1)} %copy-done.12), channel_id=1, source_target_pairs={{0,64},{64,128},{128,192},{192,256},{256,320},{320,384},{384,448},... | collective-permute-start | bytes 1646600 | tf_op jit(solution)/shard_map/ppermute | solution.py:431
  101.0 18.5 %all-to-all-start.2 = ((bf16[16,16,544]{2,1,0:T(8,128)(2,1)}), bf16[16,16,544]{2,1,0:T(8,128)(2,1)}, u32[]{:S(2)}, u32[]{:S(2)}) async-start(bf16[16,16,544]{2,1,0:T(8,128)(2,1)} %broadcast_in_dim.52), calls=%async_computation.2 | async-start | bytes 655360 | tf_op jit(solution)/shard_map/all_to_all | solution.py:501
  126.4 16.4 %all-to-all-start.3 = ((bf16[32,24,128]{2,1,0:T(8,128)(2,1)}), bf16[32,24,128]{2,1,0:T(8,128)(2,1)S(1)}, u32[]{:S(2)}, u32[]{:S(2)}) async-start(bf16[32,24,128]{2,1,0:T(8,128)(2,1)} %get-tuple-element.65), calls=%async_computation.3 | async-start | bytes 393216 | tf_op jit(solution)/shard_map/all_to_all | solution.py:530
  142.9 1.0 copy-start
  143.9 14.2 %copy-start.2 = (f32[8,1024]{1,0:T(8,128)S(1)}, f32[8,1024]{1,0:T(8,128)}, u32[]{:S(2)}) copy-start(f32[8,1024]{1,0:T(8,128)} %maximum_maximum_fusion.1.chan_ref) | copy-start | bytes 98308
  143.9 14.2 %copy-start.4 = (bf16[512,256]{1,0:T(8,128)(2,1)S(1)}, bf16[512,256]{1,0:T(8,128)(2,1)}, u32[]{:S(2)}) copy-start(bf16[512,256]{1,0:T(8,128)(2,1)} %get-tuple-element.58.bc_ref) | copy-start | bytes 786436
  144.6 13.5 %all-to-all-start.4 = ((bf16[32,16,128]{2,1,0:T(8,128)(2,1)}), bf16[32,16,128]{2,1,0:T(8,128)(2,1)S(1)}, u32[]{:S(2)}, u32[]{:S(2)}) async-start(bf16[32,16,128]{2,1,0:T(8,128)(2,1)} %shard_map.131), calls=%async_computation.4 | async-start | bytes 262144 | tf_op jit(solution)/shard_map/all_to_all | solution.py:538
  148.8 0.8 copy-start.1
  149.6 0.9 copy-start.3
  150.5 1.2 copy-start.5
  151.7 1.0 copy-start.6
  152.8 0.7 copy-start.7
  153.5 0.7 copy-start.8
  161.4 17.4 %collective-permute-start.10 = (bf16[256,512]{1,0:T(8,128)(2,1)S(1)}, bf16[256,512]{1,0:T(8,128)(2,1)S(1)}, u32[]{:S(2)}, u32[]{:S(2)}) collective-permute-start(bf16[256,512]{1,0:T(8,128)(2,1)S(1)} %get-tuple-element.67), channel_id=1, source_target_pairs={{0,8},{8,0},{1,9},{9,1},{2,10},{10,2},{3,11},{11,3},{4,12},{12,4},... | collective-permute-start | bytes 786440 | tf_op jit(solution)/shard_map/ppermute | solution.py:558

commit v7 on v6

--- a/solution.py
+++ b/solution.py
@@ -18,6 +18,7 @@
 
 SEQ = ("z", "x", "yl")
 TP = ("yh", "c")
+SHARES = 64
 OFFSETS = (0, -1, 1, -2, 2, -3, 3, 4)
 SIZES = {"z": 8, "x": 4, "yl": 2, "yh": 4, "c": 2}
 
@@ -99,7 +100,7 @@
     where_ref, own_ref, other_ref, w0, w1, w2, w3, w4, w5, w6, w7,
     bc_ref, dt_ref, feats, weights, small, sem, weight_sem,
 ):
-    bc_rows, dt_rows = bc_ref.shape[0], dt_ref.shape[0]
+    bc_rows, dt_rows = bc_ref.shape[1], dt_ref.shape[0]
     flat = bc_rows + dt_rows
     rows = feats.shape[2]
     tokens = rows - HALO
@@ -119,13 +120,14 @@
         pltpu.make_async_copy(own_ref.at[0], feats.at[step], sem.at[step]).wait()
         copies[step].wait()
         for part in range(2):
-            small[part, 0:rows, 0:flat] += dot(
+            small[part * rows : (part + 1) * rows, 0:flat] += dot(
                 feats[step, part], weights[step], ((1,), (1,))
             )
+    turned = small[...].T[0:bc_rows, 0 : 2 * rows].astype(jnp.bfloat16)
+    for at in range(bc_ref.shape[0]):
+        bc_ref[at] = turned
     for part in range(2):
-        turned = small[part].T
-        bc_ref[:, part, :] = turned[0:bc_rows, 0:rows].astype(jnp.bfloat16)
-        turned = small[part, HALO:rows].T
+        turned = small[part * rows + HALO : (part + 1) * rows].T
         dt_ref[:, part * tokens : (part + 1) * tokens] = turned[bc_rows:flat]
 
 
@@ -154,7 +156,7 @@
                 x_ref[part] = (acc[part] + found).astype(jnp.bfloat16)
 
 
-def narrow_project(where, own, other, weights, bc_rows, dt_rows):
+def narrow_project(where, own, other, weights, bc_rows, dt_rows, copies):
     _, _, rows, depth = own.shape
     blocks = len(weights)
     flat = bc_rows + dt_rows
@@ -166,12 +168,12 @@
         scratch_shapes=[
             pltpu.VMEM((blocks, 2, rows, depth), jnp.bfloat16),
             pltpu.VMEM((blocks, flat, depth), jnp.bfloat16),
-            pltpu.VMEM((2, (rows + 127) // 128 * 128, 128), jnp.float32),
+            pltpu.VMEM(((2 * rows + 127) // 128 * 128, 128), jnp.float32),
             pltpu.SemaphoreType.DMA((blocks,)),
             pltpu.SemaphoreType.DMA((blocks,)),
         ],
         out_shape=[
-            jax.ShapeDtypeStruct((bc_rows, 2, rows), jnp.bfloat16),
+            jax.ShapeDtypeStruct((copies, bc_rows, 2 * rows), jnp.bfloat16),
             jax.ShapeDtypeStruct((dt_rows, 2 * (rows - HALO)), jnp.float32),
         ],
         compiler_params=pltpu.CompilerParams(vmem_limit_bytes=ALL_VMEM),
@@ -225,7 +227,7 @@
             x_ref[at, on] = convolved(values, conv_ref[:, on], local)
     raw = dt_ref[...] + head_ref[:, 0:1]
     step_size = jnp.maximum(raw, 0.0) + jnp.log1p(jnp.exp(-jnp.abs(raw)))
-    log_decay = -step_size * head_ref[:, 1:2]
+    log_decay = -step_size * head_ref[:, 64:65]
     step_ref[...] = step_size
     upper = jnp.where(
         lax.broadcasted_iota(jnp.int32, (GROUP, GROUP), 0)
@@ -247,15 +249,19 @@
 def state_kernel(
     mine_ref, bc_ref, conv_ref, cum_ref, scaled_ref, bconv_ref, pay_ref, local_ref
 ):
-    halves, rows, _ = bc_ref.shape
+    rows = bc_ref.shape[1] // 2
     channels, tokens = scaled_ref.shape
-    local = tokens // halves
+    local = tokens // 2
     heads = cum_ref.shape[0]
-    for part in range(halves):
-        at = slice(part * local, (part + 1) * local)
-        for lane in range(0, 2 * N, 128):
-            on = slice(lane, lane + 128)
-            values = bc_ref[part, :, on].astype(jnp.float32)
+    row = lax.broadcasted_iota(jnp.int32, (128, 128), 0)
+    column = lax.broadcasted_iota(jnp.int32, (128, 128), 1)
+    same = jnp.where(row == column, 1.0, 0.0).astype(jnp.bfloat16)
+    for lane in range(0, 2 * N, 128):
+        on = slice(lane, lane + 128)
+        turned = dot(bc_ref[on], same, ((0,), (0,)))
+        for part in range(2):
+            at = slice(part * local, (part + 1) * local)
+            values = turned[part * rows : (part + 1) * rows]
             bconv_ref[at, on] = convolved(values, conv_ref[:, on], local)
     total = jnp.zeros((heads, 1), jnp.float32)
     blocks = tokens // GROUP
@@ -290,18 +296,6 @@
             pay_ref[part, 16:] = tail
 
 
-def block_kernel(
-    mine_ref, pre_ref, bc_ref, dt_ref, conv_x_ref, conv_bc_ref, head_ref,
-    x_ref, bconv_ref, cum_ref, step_ref, pay_ref, local_ref, scaled_ref,
-):
-    conv_kernel(
-        mine_ref, pre_ref, dt_ref, conv_x_ref, head_ref, x_ref, cum_ref, step_ref, scaled_ref
-    )
-    state_kernel(
-        mine_ref, bc_ref, conv_bc_ref, cum_ref, scaled_ref, bconv_ref, pay_ref, local_ref
-    )
-
-
 def prefix_kernel(at_ref, got_ref, start_ref, out_ref):
     running = start_ref[...]
     for source in range(got_ref.shape[0]):
@@ -393,7 +387,7 @@
             out_ref[:, on] = (normed - penalty * factor).astype(jnp.bfloat16)
 
 
-def prepare_parameters(d_skip, norm_gain, steer, dt_bias, decay_rate, z):
+def prepare_parameters(d_skip, norm_gain, steer, dt_bias, decay_rate, z, start, at):
     channel_rows = jnp.concatenate(
         [
             jnp.repeat(d_skip, HEAD)[None], norm_gain[None], steer[None],
@@ -401,12 +395,16 @@
         ],
         0,
     )
-    head_columns = jnp.stack([dt_bias, decay_rate], 1)
+    wide = (dt_bias.shape[0], 64)
+    head_columns = jnp.concatenate(
+        [jnp.broadcast_to(dt_bias[:, None], wide), jnp.broadcast_to(decay_rate[:, None], wide)], 1
+    )
     source = (z + jnp.array(OFFSETS, jnp.int32)) % SIZES["z"]
     where = jnp.concatenate(
         [source // 2, (source % 2 == lax.axis_index("c")).astype(jnp.int32)]
     )
-    return channel_rows, head_columns, where
+    start = lax.dynamic_slice_in_dim(start, at, start.shape[0] // SHARES, 0)
+    return channel_rows, head_columns, where, start
 
 
 def ring(block, depth, axis, prepare, raw):
@@ -476,6 +474,7 @@
         fan, panel.shape[1], half
     )
     got = lax.all_to_all(panel, ("x", "yl"), 0, 0)
+    copies, got = lax.optimization_barrier((copies, got))
     tall = got[:, :k_rows].reshape(fan * k_rows, half)
     flat = got[:, k_rows : k_rows + packed_rows].reshape(
         fan, packed_rows, half // k_rows, k_rows
@@ -484,56 +483,58 @@
     block = jnp.concatenate([tall, flat], 0)
     pieces, far, ready = ring(
         block, fan * k_rows, "z", prepare_parameters,
-        (d_skip, norm_gain, steer, dt_bias, decay_rate, z.astype(jnp.int32)),
-    )
-    channel_rows, head_columns, where = ready
-
-    copies = lax.optimization_barrier((copies, got))[0]
+        (
+            d_skip, norm_gain, steer, dt_bias, decay_rate, z.astype(jnp.int32),
+            initial_state.reshape(channels, N),
+            (lax.axis_index(("yl", "z", "x")) * (channels // SHARES)).astype(jnp.int32),
+        ),
+    )
+    channel_rows, head_columns, where, start = ready
+
     own = lax.all_to_all(copies, ("yh", "yl"), 0, 0).reshape(
         SIZES["yh"], 2, local + HALO, width
     )
-    own = lax.optimization_barrier((own, pieces[5], pieces[6]))[0]
+    own = lax.optimization_barrier((own, pieces[5]))[0]
     other = lax.ppermute(own, "c", [(0, 1), (1, 0)])
 
-    bc_pre, dt_raw = narrow_project(where, own, other, pieces[:-1] + [far], bc_rows, heads)
+    bc_pre, dt_raw = narrow_project(where, own, other, pieces[:-1] + [far], bc_rows, heads, 2 * tp_count)
     pieces[-1] = lax.optimization_barrier((pieces[-1], bc_pre))[0]
     x_pre = project(where, own, other, pieces)
-    bc_all = lax.all_to_all(
-        jnp.broadcast_to(
-            bc_pre.reshape(1, bc_rows, -1), (2 * tp_count, bc_rows, 2 * (local + HALO))
-        ),
-        ("yh", "c", "yl"), 0, 0,
-    )
-    bc_all = bc_all.reshape(2 * N, -1).T.reshape(2, local + HALO, 2 * N)
+    bc_all = lax.all_to_all(bc_pre, ("yh", "c", "yl"), 0, 0).reshape(2 * N, -1)
 
     pair = 2 * local
     plane = SIZES["z"] * SIZES["x"]
     share = half // plane
-    x_conv, bc_conv, cumulative, step_size, payload, locals_ = call(
-        block_kernel,
+    x_conv, cumulative, step_size, scaled = call(
+        conv_kernel,
         [
             jax.ShapeDtypeStruct((pair, half), bf16),
-            jax.ShapeDtypeStruct((pair, 2 * N), bf16),
             jax.ShapeDtypeStruct((heads, pair), f32),
             jax.ShapeDtypeStruct((heads, pair), f32),
+            jax.ShapeDtypeStruct((half, pair), bf16),
+        ],
+        mine, x_pre, dt_raw, conv_x, head_columns,
+        blocks={
+            2: ((conv_x.shape[0], half), lambda i, s: (0, s[0])),
+            3: ((heads, 128), lambda i, s: (s[0], 0)),
+        },
+        flops=10**9, bytes_accessed=8 * pair * half, grant=ALL_VMEM,
+    )
+    bc_conv, payload, locals_ = call(
+        state_kernel,
+        [
+            jax.ShapeDtypeStruct((pair, 2 * N), bf16),
             jax.ShapeDtypeStruct((plane, share + 8, N), bf16),
             jax.ShapeDtypeStruct((pair // GROUP, half, N), f32),
         ],
-        mine, x_pre, bc_all, dt_raw, conv_x, conv_bc, head_columns,
-        blocks={
-            3: ((conv_x.shape[0], half), lambda i, s: (0, s[0])),
-            5: ((heads, 2), lambda i, s: (s[0], 0)),
-        },
-        scratch=[pltpu.VMEM((half, pair), bf16)],
+        mine, bc_all, conv_bc, cumulative, scaled,
         grant=ALL_VMEM,
     )
     states = lax.all_to_all(payload, ("z", "x"), 0, 0)
-    place = mine * plane + lax.axis_index(("z", "x")).astype(jnp.int32)
     (prefixes,) = call(
         prefix_kernel,
         [jax.ShapeDtypeStruct((plane, share, N), bf16)],
-        place, states, initial_state.reshape(channels, N),
-        blocks={1: ((share, N), lambda i, s: (s[0], 0))},
+        mine, states, start,
     )
     entering = lax.all_to_all(prefixes, ("z", "x"), 0, 0).reshape(half, N)
 
@@ -555,12 +556,12 @@
         mine, inside, growth, bc_conv, entering, channel_rows,
         blocks={4: lanes},
     )
-    swapped = lax.ppermute(send, "yl", [(0, 1), (1, 0)])
     shape = (SIZES["yh"], 2, SIZES["c"], 1, local)
     partials = lax.all_to_all(
         jnp.broadcast_to(dots[None, :, None], shape).reshape(2 * tp_count, 1, local),
         ("yh", "yl", "c"), 0, 0,
     )
+    swapped = lax.ppermute(send, "yl", [(0, 1), (1, 0)])
     factor = 1.0 / math.sqrt(channels * tp_count)
     (out,) = call(
         functools.partial(steer_kernel, factor),

time: 182 us -> 179 us (0.984)
  blocking collectives: 14 us -> 31.5 us
  waiting for transfers between devices: 41.2 us -> 28.9 us
  starting transfers between devices: 80 us -> 73.1 us
  local copies, waits for them, and re-layouts: 17.7 us -> 12.7 us
  Pallas kernels: 24.6 us -> 26.9 us
    all_to_all x0 -> x1, blocking collectives: none -> 15.5 us  [per_device(): states = lax.all_to_all(payload, ('z', 'x'), 0, 0)]
    all_to_all x2 -> x1, waiting for transfers between devices: 14.5 us -> 0.01 us  [per_device(): bc_all = lax.all_to_all(bc_pre, ('yh', 'c', 'yl'), 0, 0).reshape(2 * N, -1)]
    ppermute x3, starting transfers between devices: 12.6 us -> 6.27 us  [ring(): ahead = lax.ppermute(ahead, axis, forward)]
    ppermute x3, starting transfers between devices: 14.5 us -> 20.2 us  [ring(): behind = lax.ppermute(behind, axis, backward)]
    all_to_all x2 -> x1, starting transfers between devices: 12.8 us -> 7.1 us  [per_device(): bc_all = lax.all_to_all(bc_pre, ('yh', 'c', 'yl'), 0, 0).reshape(2 * N, -1)]
    ppermute x1, waiting for transfers between devices: 5.08 us -> 8.29 us  [ring(): far = lax.ppermute(block[depth:], axis, across)]
    ppermute x3, waiting for transfers between devices: 3.2 us -> 0.75 us  [ring(): behind = lax.ppermute(behind, axis, backward)]
    pallas_call x5 -> x6, Pallas kernels: 13.1 us -> 15.3 us  [call(): pl.pallas_call(kernel, grid_spec=pltpu.PrefetchScalarGridSpec(num_scalar_...]
  transfers between devices with their start and end apart: 16 -> 15, of which waited for: 13 -> 12; matrix products, arithmetic and copies ran while one was open for 3% -> 2% of each run, Pallas kernels for 8% -> 10%
where the time goes in v7:
time: 179 us; the launch traced here: 177 us
  starting transfers between devices  73.1 us (41%)
  blocking collectives  31.5 us (18%)
  waiting for transfers between devices  28.9 us (16%)
  Pallas kernels  26.9 us (15%)
  local copies, waits for them, and re-layouts  12.7 us (7%)
  other arithmetic  3.71 us (2%)
    ppermute x3, starting transfers between devices, ring(): behind = lax.ppermute(behind, axis, backward)  20.2 us
    all_to_all x1, blocking collectives, per_device(): lax.all_to_all(jnp.broadcast_to(dots[None, :, None], shape).reshape(2 * t...  16 us
    all_to_all x1, blocking collectives, per_device(): states = lax.all_to_all(payload, ('z', 'x'), 0, 0)  15.5 us
    pallas_call x6, Pallas kernels, call(): pl.pallas_call(kernel, grid_spec=pltpu.PrefetchScalarGridSpec(num_scalar_...  15.3 us
    ppermute x3, waiting for transfers between devices, ring(): ahead = lax.ppermute(ahead, axis, forward)  10.8 us
    unnamed x44, local copies, waits for them, and re-layouts  8.38 us
    ppermute x1, waiting for transfers between devices, ring(): far = lax.ppermute(block[depth:], axis, across)  8.29 us
    all_to_all x1, starting transfers between devices, per_device(): lax.all_to_all(copies, ('yh', 'yl'), 0, 0)  7.91 us
  transfers between devices with their start and end apart: 15, of which 12 were waited for; matrix products, arithmetic and copies ran while one was open for 2% of the time, Pallas kernels for 10%

profile of v7, /device:TPU:1, one launch (start us, length us, event | category | flops | bytes accessed | tf_op | source)
XLA Modules:
  0.0 177.2 jit_solution(4400710045113361072)
XLA Ops:
  0.0 0.8 pad_maximum_fusion.2
  0.8 0.1 reshape.57
  0.9 1.0 reshape.54
  1.9 0.1 pad.12.clone
  1.9 0.2 maximum_maximum_fusion
  2.2 0.9 broadcast_in_dim.51
  3.1 5.9 %all-to-all-start = ((bf16[8,72,512]{2,1,0:T(8,128)(2,1)}), bf16[8,72,512]{2,1,0:T(8,128)(2,1)S(1)}, u32[]{:S(2)}, u32[]{:S(2)}) async-start(bf16[8,72,512]{2,1,0:T(8,128)(2,1)} %bitcast.6), calls=%async_computation | async-start | bytes 1179648 | tf_op jit(solution)/shard_map/all_to_all | solution.py:476
  9.0 3.4 %collective-permute-start = (bf16[16,512]{1,0:T(8,128)(2,1)S(1)}, bf16[16,512]{1,0:T(8,128)(2,1)S(1)}, u32[]{:S(2)}, u32[]{:S(2)}) collective-permute-start(bf16[16,512]{1,0:T(8,128)(2,1)S(1)} %slice.9), channel_id=1, source_target_pairs={{0,8},{8,16},{16,24},{24,32},{32,40},{40,48},{48,56},{56,64},{64,7... | collective-permute-start | bytes 49160 | tf_op jit(solution)/shard_map/ppermute | solution.py:449
  12.3 0.9 collective-permute-done
  13.2 3.6 %all-to-all-done = bf16[8,72,512]{2,1,0:T(8,128)(2,1)S(1)} async-done(((bf16[8,72,512]{2,1,0:T(8,128)(2,1)}), bf16[8,72,512]{2,1,0:T(8,128)(2,1)S(1)}, u32[]{:S(2)}, u32[]{:S(2)}) %all-to-all-start) | async-done | bytes 589856 | tf_op jit(solution)/shard_map/all_to_all | solution.py:476
  16.8 1.6 broadcast_in_dim.24
  18.4 7.9 %all-to-all-start.1 = ((bf16[8,272,512]{2,1,0:T(8,128)(2,1)}), bf16[8,272,512]{2,1,0:T(8,128)(2,1)S(1)}, u32[]{:S(2)}, u32[]{:S(2)}) async-start(bf16[8,272,512]{2,1,0:T(8,128)(2,1)} %broadcast_in_dim.24), calls=%async_computation.1 | async-start | bytes 4456448 | tf_op jit(solution)/shard_map/all_to_all | solution.py:494
  26.3 0.0 copy-start.17
  26.5 0.1 reshape.60
  26.6 0.1 reshape.61
  26.7 10.8 %collective-permute-start.2 = (bf16[536,512]{1,0:T(8,128)(2,1)S(1)}, bf16[536,512]{1,0:T(8,128)(2,1)S(1)}, u32[]{:S(2)}, u32[]{:S(2)}) collective-permute-start(bf16[536,512]{1,0:T(8,128)(2,1)S(1)} %pad_maximum_fusion.w0), channel_id=1, source_target_pairs={{0,448},{64,0},{128,64},{192,128},{256,192},{320,256},{384,320},{4... | collective-permute-start | bytes 1646600 | tf_op jit(solution)/shard_map/ppermute | solution.py:419
  37.5 1.9 %collective-permute-start.1 = (bf16[536,512]{1,0:T(8,128)(2,1)S(1)}, bf16[536,512]{1,0:T(8,128)(2,1)}, u32[]{:S(2)}, u32[]{:S(2)}) collective-permute-start(bf16[536,512]{1,0:T(8,128)(2,1)S(1)} %pad_maximum_fusion.w0), channel_id=1, source_target_pairs={{0,64},{64,128},{128,192},{192,256},{256,320},{320,384},{384,448},... | collective-permute-start | bytes 1646600 | tf_op jit(solution)/shard_map/ppermute | solution.py:418
  39.4 3.2 %collective-permute-start.3 = (bf16[24,512]{1,0:T(8,128)(2,1)S(1)}, bf16[24,512]{1,0:T(8,128)(2,1)S(1)}, u32[]{:S(2)}, u32[]{:S(2)}) collective-permute-start(bf16[24,512]{1,0:T(8,128)(2,1)S(1)} %reshape.61), channel_id=1, source_target_pairs={{0,256},{64,320},{128,384},{192,448},{256,0},{320,64},{384,128},{4... | collective-permute-start | bytes 73736 | tf_op jit(solution)/shard_map/ppermute | solution.py:421
  42.7 0.1 pad.7.clone
  42.8 8.3 %collective-permute-done.3.w7 = bf16[24,512]{1,0:T(8,128)(2,1)S(1)} collective-permute-done((bf16[24,512]{1,0:T(8,128)(2,1)S(1)}, bf16[24,512]{1,0:T(8,128)(2,1)S(1)}, u32[]{:S(2)}, u32[]{:S(2)}) %collective-permute-start.3) | collective-permute-done | bytes 24608 | tf_op jit(solution)/shard_map/ppermute | solution.py:421
  51.1 1.4 collective-permute-done.1.w1
  52.5 1.9 %collective-permute-start.4 = (bf16[536,512]{1,0:T(8,128)(2,1)}, bf16[536,512]{1,0:T(8,128)(2,1)}, u32[]{:S(2)}, u32[]{:S(2)}) collective-permute-start(bf16[536,512]{1,0:T(8,128)(2,1)} %collective-permute-done.1.w1), channel_id=1, source_target_pairs={{0,64},{64,128},{128,192},{192,256},{256,320},{320,384},{384,448},... | collective-permute-start | bytes 1646600 | tf_op jit(solution)/shard_map/ppermute | solution.py:418
  54.4 4.6 %collective-permute-start.5 = (bf16[536,512]{1,0:T(8,128)(2,1)S(1)}, bf16[536,512]{1,0:T(8,128)(2,1)}, u32[]{:S(2)}, u32[]{:S(2)}) collective-permute-start(bf16[536,512]{1,0:T(8,128)(2,1)S(1)} %collective-permute-done.2.w2), channel_id=1, source_target_pairs={{0,448},{64,0},{128,64},{192,128},{256,192},{320,256},{384,320},{4... | collective-permute-start | bytes 1646600 | tf_op jit(solution)/shard_map/ppermute | solution.py:419
  59.0 0.1 broadcast_in_dim.52
  59.1 0.1 broadcast_in_dim_reshape.3
  59.2 0.6 pad_add_fusion.where_ref
  59.8 0.1 broadcast_in_dim.56
  59.8 0.1 broadcast_in_dim.57
  59.9 1.4 pad_maximum_fusion.3
  61.3 0.7 maximum_maximum_fusion.1.chan_ref
  62.0 3.7 %collective-permute-done.4.w3 = bf16[536,512]{1,0:T(8,128)(2,1)} collective-permute-done((bf16[536,512]{1,0:T(8,128)(2,1)}, bf16[536,512]{1,0:T(8,128)(2,1)}, u32[]{:S(2)}, u32[]{:S(2)}) %collective-permute-start.4) | collective-permute-done | bytes 548896 | tf_op jit(solution)/shard_map/ppermute | solution.py:418
  65.7 0.6 collective-permute-done.5.w4
  66.3 2.4 %collective-permute-start.6 = (bf16[536,512]{1,0:T(8,128)(2,1)}, bf16[536,512]{1,0:T(8,128)(2,1)S(1)}, u32[]{:S(2)}, u32[]{:S(2)}) collective-permute-start(bf16[536,512]{1,0:T(8,128)(2,1)} %collective-permute-done.4.w3), channel_id=1, source_target_pairs={{0,64},{64,128},{128,192},{192,256},{256,320},{320,384},{384,448},... | collective-permute-start | bytes 1646600 | tf_op jit(solution)/shard_map/ppermute | solution.py:418
  68.7 4.9 %collective-permute-start.7 = (bf16[536,512]{1,0:T(8,128)(2,1)}, bf16[536,512]{1,0:T(8,128)(2,1)}, u32[]{:S(2)}, u32[]{:S(2)}) collective-permute-start(bf16[536,512]{1,0:T(8,128)(2,1)} %collective-permute-done.5.w4), channel_id=1, source_target_pairs={{0,448},{64,0},{128,64},{192,128},{256,192},{320,256},{384,320},{4... | collective-permute-start | bytes 1646600 | tf_op jit(solution)/shard_map/ppermute | solution.py:419
  73.6 5.7 %collective-permute-done.6.w5 = bf16[536,512]{1,0:T(8,128)(2,1)S(1)} collective-permute-done((bf16[536,512]{1,0:T(8,128)(2,1)}, bf16[536,512]{1,0:T(8,128)(2,1)S(1)}, u32[]{:S(2)}, u32[]{:S(2)}) %collective-permute-start.6) | collective-permute-done | bytes 548896 | tf_op jit(solution)/shard_map/ppermute | solution.py:418
  79.3 0.8 copy-done.12
  80.2 0.2 collective-permute-done.7.w6
  80.3 0.5 all-to-all-done.1
  80.8 1.4 copy-done.9
  82.2 7.7 %collective-permute-start.8 = (bf16[4,2,272,512]{3,2,1,0:T(8,128)(2,1)S(1)}, bf16[4,2,272,512]{3,2,1,0:T(8,128)(2,1)}, u32[]{:S(2)}, u32[]{:S(2)}) collective-permute-start(bf16[4,2,272,512]{3,2,1,0:T(8,128)(2,1)S(1)} %bitcast.29), channel_id=1, source_target_pairs={{0,1},{1,0},{2,3},{3,2},{4,5},{5,4},{6,7},{7,6},{8,9},{9,8},{10,11... | collective-permute-start | bytes 6684680 | tf_op jit(solution)/shard_map/ppermute | solution.py:498
  89.9 3.7 %collective-permute-start.9 = (bf16[536,512]{1,0:T(8,128)(2,1)}, bf16[536,512]{1,0:T(8,128)(2,1)}, u32[]{:S(2)}, u32[]{:S(2)}) collective-permute-start(bf16[536,512]{1,0:T(8,128)(2,1)} %copy-done.12), channel_id=1, source_target_pairs={{0,64},{64,128},{128,192},{192,256},{256,320},{320,384},{384,448},... | collective-permute-start | bytes 1646600 | tf_op jit(solution)/shard_map/ppermute | solution.py:429
  93.7 0.3 collective-permute-done.8.other_ref
  94.0 5.4 %shard_map.127 = (bf16[16,16,544]{2,1,0:T(8,128)(2,1)}, f32[8,512]{1,0:T(8,128)}) custom-call(s32[16]{0:T(128)} %pad_add_fusion.where_ref, bf16[4,2,272,512]{3,2,1,0:T(8,128)(2,1)} %bitcast.30, bf16[4,2,272,512]{3,2,1,0:T(8,128)(2,1)} %collective-permute-done.8.other_ref, bf16[536,512]{1,0:T(8,128)(2,1)} %copy-done.10, ...), custom_call_target="tpu_custom_call" | custom-call | flops 1000000000 | bytes 10000000 | tf_op jit(solution)/shard_map/pallas_call | solution.py:163
  99.4 7.1 %all-to-all-start.2 = ((bf16[16,16,544]{2,1,0:T(8,128)(2,1)}), bf16[16,16,544]{2,1,0:T(8,128)(2,1)}, u32[]{:S(2)}, u32[]{:S(2)}) async-start(bf16[16,16,544]{2,1,0:T(8,128)(2,1)} %get-tuple-element.61), calls=%async_computation.2 | async-start | bytes 655360 | tf_op jit(solution)/shard_map/all_to_all | solution.py:503
  106.5 2.0 %collective-permute-done.9.w7 = bf16[536,512]{1,0:T(8,128)(2,1)} collective-permute-done((bf16[536,512]{1,0:T(8,128)(2,1)}, bf16[536,512]{1,0:T(8,128)(2,1)}, u32[]{:S(2)}, u32[]{:S(2)}) %collective-permute-start.9) | collective-permute-done | bytes 548896 | tf_op jit(solution)/shard_map/ppermute | solution.py:429
  108.5 6.2 %shard_map.128.pre_ref = bf16[2,272,512]{2,1,0:T(8,128)(2,1)} custom-call(s32[16]{0:T(128)} %pad_add_fusion.where_ref, bf16[4,2,272,512]{3,2,1,0:T(8,128)(2,1)} %bitcast.31, bf16[4,2,272,512]{3,2,1,0:T(8,128)(2,1)} %collective-permute-done.8.other_ref, bf16[536,512]{1,0:T(8,128)(2,1)} %copy-done.10, bf16[536,512]{1,0:T(8,128)(2,1)} %collective-permute-done.1.w1, ...), custom_call_target="tpu_custom_call" | custom-call | flops 3000000000 | bytes 10000000 | tf_op jit(solution)/shard_map/pallas_call | solution.py:188
  114.6 4.3 %shard_map.129 = (bf16[512,512]{1,0:T(8,128)(2,1)}, f32[8,512]{1,0:T(8,128)}, f32[8,512]{1,0:T(8,128)}, bf16[512,512]{1,0:T(8,128)(2,1)}) custom-call(s32[1]{0:T(128)} %bitcast.mine_ref.at_ref, bf16[2,272,512]{2,1,0:T(8,128)(2,1)} %shard_map.128.pre_ref, f32[8,512]{1,0:T(8,128)} %get-tuple-element.63.dt_ref, f32[4,1024]{1,0:T(4,128)} %conv_ref.2, ...), custom_call_target="tpu_custom_call" | custom-call | flops 1000000000 | bytes 2097152 | tf_op jit(solution)/shard_map/pallas_call | solution.py:41
  118.9 3.1 %shard_map.130 = (bf16[512,256]{1,0:T(8,128)(2,1)}, bf16[32,24,128]{2,1,0:T(8,128)(2,1)}, f32[4,512,128]{2,1,0:T(8,128)}) custom-call(s32[1]{0:T(128)} %bitcast.mine_ref.at_ref, bf16[256,544]{1,0:T(8,128)(2,1)} %bitcast.13.bc_ref, f32[4,256]{1,0:T(4,128)} %conv_ref.3, f32[8,512]{1,0:T(8,128)} %get-tuple-element.66.cum_ref, ...), custom_call_target="tpu_custom_call" | custom-call | tf_op jit(solution)/shard_map/pallas_call | solution.py:41
  122.1 15.5 %all_to_all.30.got_ref = bf16[32,24,128]{2,1,0:T(8,128)(2,1)S(1)} all-to-all(bf16[32,24,128]{2,1,0:T(8,128)(2,1)} %get-tuple-element.74), channel_id=1, replica_groups=mesh['z'=8,'x'=4,'yl'=2,'yh'=4,'c'=2] {'z','x'}, dimensions={0} | all-to-all | bytes 393216 | tf_op jit(solution)/shard_map/all_to_all | solution.py:533
  137.6 0.7 copy-done.4
  138.3 0.7 shard_map.132
  139.0 4.6 %all-to-all-start.4 = ((bf16[32,16,128]{2,1,0:T(8,128)(2,1)}), bf16[32,16,128]{2,1,0:T(8,128)(2,1)S(1)}, u32[]{:S(2)}, u32[]{:S(2)}) async-start(bf16[32,16,128]{2,1,0:T(8,128)(2,1)} %shard_map.132), calls=%async_computation.4 | async-start | bytes 262144 | tf_op jit(solution)/shard_map/all_to_all | solution.py:539
  143.6 0.7 copy-done
  144.3 0.9 copy-done.2
  145.3 0.7 copy-done.5
  146.0 1.2 copy-done.6
  147.2 1.0 copy-done.7
  148.3 0.7 copy-done.8
  149.0 2.1 %shard_map.131 = (f32[512,512]{1,0:T(8,128)S(1)}, f32[512,512]{1,0:T(8,128)S(1)}) custom-call(s32[1]{0:T(128)} %bitcast.mine_ref.at_ref, bf16[512,512]{1,0:T(8,128)(2,1)S(1)} %copy-done.7, bf16[512,256]{1,0:T(8,128)(2,1)S(1)} %copy-done.2, f32[8,512]{1,0:T(8,128)S(1)} %copy-done.5, f32[8,512]{1,0:T(8,128)S(1)} %copy-done.8, f32[4,512,128]{2,1,0:T(8,128)S(1)} %copy-done.6, ...), custom_call_target="tpu_custom_call" | custom-call | flops 1000000000 | bytes 3145728 | tf_op jit(solution)/shard_map/pallas_call | solution.py:41
  151.1 1.8 %all-to-all-done.4 = bf16[32,16,128]{2,1,0:T(8,128)(2,1)S(1)} async-done(((bf16[32,16,128]{2,1,0:T(8,128)(2,1)}), bf16[32,16,128]{2,1,0:T(8,128)(2,1)S(1)}, u32[]{:S(2)}, u32[]{:S(2)}) %all-to-all-start.4) | async-done | bytes 131104 | tf_op jit(solution)/shard_map/all_to_all | solution.py:539
  152.9 3.3 %shard_map.133 = (f32[256,512]{1,0:T(8,128)S(1)}, bf16[256,512]{1,0:T(8,128)(2,1)S(1)}, f32[2,1,256]{2,1,0:T(1,128)S(1)}) custom-call(s32[1]{0:T(128)} %bitcast.mine_ref.at_ref, f32[512,512]{1,0:T(8,128)S(1)} %get-tuple-element.72.inside_ref, f32[512,512]{1,0:T(8,128)S(1)} %get-tuple-element.73.growth_ref, bf16[512,256]{1,0:T(8,128)(2,1)S(1)} %copy-done.3, ...), custom_call_target="tpu_custom_call" | custom-call | tf_op jit(solution)/shard_map/pallas_call | solution.py:41
  156.2 3.1 %collective-permute-start.10 = (bf16[256,512]{1,0:T(8,128)(2,1)S(1)}, bf16[256,512]{1,0:T(8,128)(2,1)S(1)}, u32[]{:S(2)}, u32[]{:S(2)}) collective-permute-start(bf16[256,512]{1,0:T(8,128)(2,1)S(1)} %get-tuple-element.77), channel_id=1, source_target_pairs={{0,8},{8,0},{1,9},{9,1},{2,10},{10,2},{3,11},{11,3},{4,12},{12,4},... | collective-permute-start | bytes 786440 | tf_op jit(solution)/shard_map/ppermute | solution.py:564
  159.4 16.0 %all_to_all.31 = f32[16,1,256]{2,1,0:T(1,128)S(1)} all-to-all(f32[16,1,256]{2,1,0:T(1,128)S(1)} %broadcast_in_dim.60), channel_id=1, replica_groups=mesh['z'=8,'x'=4,'yl'=2,'yh'=4,'c'=2] {'yh','yl','c'}, dimensions={0} | all-to-all | bytes 32768 | tf_op jit(solution)/shard_map/all_to_all | solution.py:560
  175.4 1.8 %shard_map.134 = bf16[256,1024]{1,0:T(8,128)(2,1)} custom-call(s32[1]{0:T(128)} %bitcast.mine_ref.at_ref, f32[256,512]{1,0:T(8,128)S(1)} %get-tuple-element.76.keep_ref, bf16[256,512]{1,0:T(8,128)(2,1)S(1)} %collective-permute-done.10.other_ref, f32[16,256]{1,0:T(8,128)S(1)} %bitcast.28, f32[8,1024]{1,0:T(8,128)S(1)} %copy-done.1), custom_call_target="tpu_custom_call" | custom-call | tf_op jit(solution)/shard_map/pallas_call | solution.py:41
  (52 shorter events, 0.3 us)
Async XLA Ops:
  0.0 8.9 %copy-start.13 = (bf16[256,512]{1,0:T(8,128)(2,1)S(1)}, bf16[256,512]{1,0:T(8,128)(2,1)}, u32[]{:S(2)}) copy-start(bf16[256,512]{1,0:T(8,128)(2,1)} %param.13) | copy-start | bytes 786436
  3.1 13.8 %all-to-all-start = ((bf16[8,72,512]{2,1,0:T(8,128)(2,1)}), bf16[8,72,512]{2,1,0:T(8,128)(2,1)S(1)}, u32[]{:S(2)}, u32[]{:S(2)}) async-start(bf16[8,72,512]{2,1,0:T(8,128)(2,1)} %bitcast.6), calls=%async_computation | async-start | bytes 1179648 | tf_op jit(solution)/shard_map/all_to_all | solution.py:476
  9.0 4.2 %collective-permute-start = (bf16[16,512]{1,0:T(8,128)(2,1)S(1)}, bf16[16,512]{1,0:T(8,128)(2,1)S(1)}, u32[]{:S(2)}, u32[]{:S(2)}) collective-permute-start(bf16[16,512]{1,0:T(8,128)(2,1)S(1)} %slice.9), channel_id=1, source_target_pairs={{0,8},{8,16},{16,24},{24,32},{32,40},{40,48},{48,56},{56,64},{64,7... | collective-permute-start | bytes 49160 | tf_op jit(solution)/shard_map/ppermute | solution.py:449
  18.4 62.4 %all-to-all-start.1 = ((bf16[8,272,512]{2,1,0:T(8,128)(2,1)}), bf16[8,272,512]{2,1,0:T(8,128)(2,1)S(1)}, u32[]{:S(2)}, u32[]{:S(2)}) async-start(bf16[8,272,512]{2,1,0:T(8,128)(2,1)} %broadcast_in_dim.24), calls=%async_computation.1 | async-start | bytes 4456448 | tf_op jit(solution)/shard_map/all_to_all | solution.py:494
  26.3 24.8 %copy-start.20 = (s32[8]{0:T(128)S(1)}, s32[8]{0:T(128)}, u32[]{:S(2)}) copy-start(s32[8]{0:T(128)} %constant.70.clone) | copy-start | bytes 100
  26.3 32.7 %copy-start.17 = (f32[16]{0:T(128)S(1)}, f32[16]{0:T(128)}, u32[]{:S(2)}) copy-start(f32[16]{0:T(128)} %param.21) | copy-start | bytes 196
  26.3 33.4 %copy-start.18 = (f32[16]{0:T(128)S(1)}, f32[16]{0:T(128)}, u32[]{:S(2)}) copy-start(f32[16]{0:T(128)} %param.19) | copy-start | bytes 196
  26.3 33.5 %copy-start.19 = (f32[16]{0:T(128)S(1)}, f32[16]{0:T(128)}, u32[]{:S(2)}) copy-start(f32[16]{0:T(128)} %param.20) | copy-start | bytes 196
  26.3 34.9 %copy-start.15 = (f32[1024]{0:T(1024)S(1)}, f32[1024]{0:T(1024)}, u32[]{:S(2)}) copy-start(f32[1024]{0:T(1024)} %param.24) | copy-start | bytes 12292
  26.4 34.9 %copy-start.16 = (f32[1024]{0:T(1024)S(1)}, f32[1024]{0:T(1024)}, u32[]{:S(2)}) copy-start(f32[1024]{0:T(1024)} %param.22) | copy-start | bytes 12292
  26.7 63.2 %copy-start.10 = (bf16[536,512]{1,0:T(8,128)(2,1)}, bf16[536,512]{1,0:T(8,128)(2,1)S(1)}, u32[]{:S(2)}) copy-start(bf16[536,512]{1,0:T(8,128)(2,1)S(1)} %pad_maximum_fusion.w0) | copy-start | bytes 1646596
  26.7 24.4 %collective-permute-start.2 = (bf16[536,512]{1,0:T(8,128)(2,1)S(1)}, bf16[536,512]{1,0:T(8,128)(2,1)S(1)}, u32[]{:S(2)}, u32[]{:S(2)}) collective-permute-start(bf16[536,512]{1,0:T(8,128)(2,1)S(1)} %pad_maximum_fusion.w0), channel_id=1, source_target_pairs={{0,448},{64,0},{128,64},{192,128},{256,192},{320,256},{384,320},{4... | collective-permute-start | bytes 1646600 | tf_op jit(solution)/shard_map/ppermute | solution.py:419
  37.5 15.0 %collective-permute-start.1 = (bf16[536,512]{1,0:T(8,128)(2,1)S(1)}, bf16[536,512]{1,0:T(8,128)(2,1)}, u32[]{:S(2)}, u32[]{:S(2)}) collective-permute-start(bf16[536,512]{1,0:T(8,128)(2,1)S(1)} %pad_maximum_fusion.w0), channel_id=1, source_target_pairs={{0,64},{64,128},{128,192},{192,256},{256,320},{320,384},{384,448},... | collective-permute-start | bytes 1646600 | tf_op jit(solution)/shard_map/ppermute | solution.py:418
  39.4 11.6 %collective-permute-start.3 = (bf16[24,512]{1,0:T(8,128)(2,1)S(1)}, bf16[24,512]{1,0:T(8,128)(2,1)S(1)}, u32[]{:S(2)}, u32[]{:S(2)}) collective-permute-start(bf16[24,512]{1,0:T(8,128)(2,1)S(1)} %reshape.61), channel_id=1, source_target_pairs={{0,256},{64,320},{128,384},{192,448},{256,0},{320,64},{384,128},{4... | collective-permute-start | bytes 73736 | tf_op jit(solution)/shard_map/ppermute | solution.py:421
  51.1 42.6 %copy-start.14 = (bf16[24,512]{1,0:T(8,128)(2,1)}, bf16[24,512]{1,0:T(8,128)(2,1)S(1)}, u32[]{:S(2)}) copy-start(bf16[24,512]{1,0:T(8,128)(2,1)S(1)} %collective-permute-done.3.w7) | copy-start | bytes 73732
  51.1 42.5 %copy-start.11 = (bf16[536,512]{1,0:T(8,128)(2,1)}, bf16[536,512]{1,0:T(8,128)(2,1)S(1)}, u32[]{:S(2)}) copy-start(bf16[536,512]{1,0:T(8,128)(2,1)S(1)} %collective-permute-done.2.w2) | copy-start | bytes 1646596
  52.5 13.2 %collective-permute-start.4 = (bf16[536,512]{1,0:T(8,128)(2,1)}, bf16[536,512]{1,0:T(8,128)(2,1)}, u32[]{:S(2)}, u32[]{:S(2)}) collective-permute-start(bf16[536,512]{1,0:T(8,128)(2,1)} %collective-permute-done.1.w1), channel_id=1, source_target_pairs={{0,64},{64,128},{128,192},{192,256},{256,320},{320,384},{384,448},... | collective-permute-start | bytes 1646600 | tf_op jit(solution)/shard_map/ppermute | solution.py:418
  54.4 11.9 %collective-permute-start.5 = (bf16[536,512]{1,0:T(8,128)(2,1)S(1)}, bf16[536,512]{1,0:T(8,128)(2,1)}, u32[]{:S(2)}, u32[]{:S(2)}) collective-permute-start(bf16[536,512]{1,0:T(8,128)(2,1)S(1)} %collective-permute-done.2.w2), channel_id=1, source_target_pairs={{0,448},{64,0},{128,64},{192,128},{256,192},{320,256},{384,320},{4... | collective-permute-start | bytes 1646600 | tf_op jit(solution)/shard_map/ppermute | solution.py:419
  66.3 13.0 %collective-permute-start.6 = (bf16[536,512]{1,0:T(8,128)(2,1)}, bf16[536,512]{1,0:T(8,128)(2,1)S(1)}, u32[]{:S(2)}, u32[]{:S(2)}) collective-permute-start(bf16[536,512]{1,0:T(8,128)(2,1)} %collective-permute-done.4.w3), channel_id=1, source_target_pairs={{0,64},{64,128},{128,192},{192,256},{256,320},{320,384},{384,448},... | collective-permute-start | bytes 1646600 | tf_op jit(solution)/shard_map/ppermute | solution.py:418
  68.7 11.6 %collective-permute-start.7 = (bf16[536,512]{1,0:T(8,128)(2,1)}, bf16[536,512]{1,0:T(8,128)(2,1)}, u32[]{:S(2)}, u32[]{:S(2)}) collective-permute-start(bf16[536,512]{1,0:T(8,128)(2,1)} %collective-permute-done.5.w4), channel_id=1, source_target_pairs={{0,448},{64,0},{128,64},{192,128},{256,192},{320,256},{384,320},{4... | collective-permute-start | bytes 1646600 | tf_op jit(solution)/shard_map/ppermute | solution.py:419
  79.3 0.8 copy-start.12
  80.8 1.4 copy-start.9
  82.2 11.8 %collective-permute-start.8 = (bf16[4,2,272,512]{3,2,1,0:T(8,128)(2,1)S(1)}, bf16[4,2,272,512]{3,2,1,0:T(8,128)(2,1)}, u32[]{:S(2)}, u32[]{:S(2)}) collective-permute-start(bf16[4,2,272,512]{3,2,1,0:T(8,128)(2,1)S(1)} %bitcast.29), channel_id=1, source_target_pairs={{0,1},{1,0},{2,3},{3,2},{4,5},{5,4},{6,7},{7,6},{8,9},{9,8},{10,11... | collective-permute-start | bytes 6684680 | tf_op jit(solution)/shard_map/ppermute | solution.py:498
  89.9 18.6 %collective-permute-start.9 = (bf16[536,512]{1,0:T(8,128)(2,1)}, bf16[536,512]{1,0:T(8,128)(2,1)}, u32[]{:S(2)}, u32[]{:S(2)}) collective-permute-start(bf16[536,512]{1,0:T(8,128)(2,1)} %copy-done.12), channel_id=1, source_target_pairs={{0,64},{64,128},{128,192},{192,256},{256,320},{320,384},{384,448},... | collective-permute-start | bytes 1646600 | tf_op jit(solution)/shard_map/ppermute | solution.py:429
  99.4 19.5 %all-to-all-start.2 = ((bf16[16,16,544]{2,1,0:T(8,128)(2,1)}), bf16[16,16,544]{2,1,0:T(8,128)(2,1)}, u32[]{:S(2)}, u32[]{:S(2)}) async-start(bf16[16,16,544]{2,1,0:T(8,128)(2,1)} %get-tuple-element.61), calls=%async_computation.2 | async-start | bytes 655360 | tf_op jit(solution)/shard_map/all_to_all | solution.py:503
  137.6 0.7 copy-start.4
  138.3 14.7 %copy-start.1 = (f32[8,1024]{1,0:T(8,128)S(1)}, f32[8,1024]{1,0:T(8,128)}, u32[]{:S(2)}) copy-start(f32[8,1024]{1,0:T(8,128)} %maximum_maximum_fusion.1.chan_ref) | copy-start | bytes 98308
  138.3 14.7 %copy-start.3 = (bf16[512,256]{1,0:T(8,128)(2,1)S(1)}, bf16[512,256]{1,0:T(8,128)(2,1)}, u32[]{:S(2)}) copy-start(bf16[512,256]{1,0:T(8,128)(2,1)} %get-tuple-element.68.bc_ref) | copy-start | bytes 786436
  139.0 13.9 %all-to-all-start.4 = ((bf16[32,16,128]{2,1,0:T(8,128)(2,1)}), bf16[32,16,128]{2,1,0:T(8,128)(2,1)S(1)}, u32[]{:S(2)}, u32[]{:S(2)}) async-start(bf16[32,16,128]{2,1,0:T(8,128)(2,1)} %shard_map.132), calls=%async_computation.4 | async-start | bytes 262144 | tf_op jit(solution)/shard_map/all_to_all | solution.py:539
  143.6 0.8 copy-start
  144.3 0.9 copy-start.2
  145.3 0.7 copy-start.5
  146.0 1.2 copy-start.6
  147.2 1.0 copy-start.7
  148.3 0.7 copy-start.8
  156.2 19.2 %collective-permute-start.10 = (bf16[256,512]{1,0:T(8,128)(2,1)S(1)}, bf16[256,512]{1,0:T(8,128)(2,1)S(1)}, u32[]{:S(2)}, u32[]{:S(2)}) collective-permute-start(bf16[256,512]{1,0:T(8,128)(2,1)S(1)} %get-tuple-element.77), channel_id=1, source_target_pairs={{0,8},{8,0},{1,9},{9,1},{2,10},{10,2},{3,11},{11,3},{4,12},{12,4},... | collective-permute-start | bytes 786440 | tf_op jit(solution)/shard_map/ppermute | solution.py:564

commit v8 on v7

--- a/solution.py
+++ b/solution.py
@@ -132,8 +132,8 @@
 
 
 def project_kernel(
-    where_ref, own_ref, other_ref, w0, w1, w2, w3, w4, w5, w6, w7,
-    x_ref, feats, weights, acc, sem, weight_sem,
+    where_ref, dt_ref, conv_ref, head_ref, own_ref, other_ref, w0, w1, w2, w3, w4, w5, w6, w7,
+    x_ref, cum_ref, step_ref, scaled_ref, feats, weights, acc, pre, sem, weight_sem,
 ):
     blocks, depth = weights.shape[0], weights.shape[1]
     fetch_tokens(where_ref, own_ref, other_ref, feats, sem)
@@ -153,7 +153,15 @@
             elif step < blocks - 1:
                 acc[part] += found
             else:
-                x_ref[part] = (acc[part] + found).astype(jnp.bfloat16)
+                pre[part] = (acc[part] + found).astype(jnp.bfloat16)
+    mine = where_ref[2 * blocks]
+    heads, channels = dt_ref.shape[0], x_ref.shape[1]
+    convolve_block(
+        pre, dt_ref,
+        conv_ref.at[:, pl.ds(pl.multiple_of(mine * channels, channels), channels)],
+        head_ref.at[pl.ds(pl.multiple_of(mine * heads, heads), heads)],
+        x_ref, cum_ref, step_ref, scaled_ref,
+    )
 
 
 def narrow_project(where, own, other, weights, bc_rows, dt_rows, copies):
@@ -181,28 +189,36 @@
     )(where, own, other, *weights)
 
 
-def project(where, own, other, weights):
+def project(where, dt_raw, conv_x, head_columns, own, other, weights):
     _, _, rows, depth = own.shape
     channels = weights[0].shape[1]
     blocks = len(weights)
+    heads, tokens = dt_raw.shape
+    vmem = pl.BlockSpec(memory_space=pltpu.VMEM)
     return pl.pallas_call(
         project_kernel,
-        in_specs=[pl.BlockSpec(memory_space=pltpu.SMEM)]
+        in_specs=[pl.BlockSpec(memory_space=pltpu.SMEM), vmem, vmem, vmem]
         + [pl.BlockSpec(memory_space=pl.ANY)] * (len(weights) + 2),
-        out_specs=pl.BlockSpec(memory_space=pltpu.VMEM),
+        out_specs=[vmem] * 4,
         scratch_shapes=[
             pltpu.VMEM((blocks, 2, rows, depth), jnp.bfloat16),
             pltpu.VMEM((blocks, depth, channels), jnp.bfloat16),
             pltpu.VMEM((2, rows, channels), jnp.float32),
+            pltpu.VMEM((2, rows, channels), jnp.bfloat16),
             pltpu.SemaphoreType.DMA((blocks,)),
             pltpu.SemaphoreType.DMA((blocks,)),
         ],
-        out_shape=jax.ShapeDtypeStruct((2, rows, channels), jnp.bfloat16),
+        out_shape=[
+            jax.ShapeDtypeStruct((tokens, channels), jnp.bfloat16),
+            jax.ShapeDtypeStruct((heads, tokens), jnp.float32),
+            jax.ShapeDtypeStruct((heads, tokens), jnp.float32),
+            jax.ShapeDtypeStruct((channels, tokens), jnp.bfloat16),
+        ],
         compiler_params=pltpu.CompilerParams(vmem_limit_bytes=ALL_VMEM),
         cost_estimate=pl.CostEstimate(
             flops=3 * 10**9, bytes_accessed=10**7, transcendentals=0
         ),
-    )(where, own, other, *weights)
+    )(where, dt_raw, conv_x, head_columns, own, other, *weights)
 
 
 def convolved(values, taps, tokens):
@@ -212,9 +228,7 @@
     return (summed / (1.0 + jnp.exp(-summed))).astype(jnp.bfloat16)
 
 
-def conv_kernel(
-    mine_ref, pre_ref, dt_ref, conv_ref, head_ref, x_ref, cum_ref, step_ref, scaled_ref
-):
+def convolve_block(pre_ref, dt_ref, conv_ref, head_ref, x_ref, cum_ref, step_ref, scaled_ref):
     tokens, channels = x_ref.shape
     halves, rows, _ = pre_ref.shape
     local = tokens // halves
@@ -401,7 +415,10 @@
     )
     source = (z + jnp.array(OFFSETS, jnp.int32)) % SIZES["z"]
     where = jnp.concatenate(
-        [source // 2, (source % 2 == lax.axis_index("c")).astype(jnp.int32)]
+        [
+            source // 2, (source % 2 == lax.axis_index("c")).astype(jnp.int32),
+            lax.axis_index("yl").astype(jnp.int32).reshape(1),
+        ]
     )
     start = lax.dynamic_slice_in_dim(start, at, start.shape[0] // SHARES, 0)
     return channel_rows, head_columns, where, start
@@ -464,7 +481,7 @@
     ).reshape(2, packed_rows, half)
     panel = jnp.concatenate(
         [
-            x_weight.reshape(k_rows, 2, half).transpose(1, 0, 2),
+            jnp.stack([x_weight[:, :half], x_weight[:, half:]]),
             packed,
             jnp.zeros((2, -packed_rows % 8, half), bf16),
         ],
@@ -499,27 +516,14 @@
 
     bc_pre, dt_raw = narrow_project(where, own, other, pieces[:-1] + [far], bc_rows, heads, 2 * tp_count)
     pieces[-1] = lax.optimization_barrier((pieces[-1], bc_pre))[0]
-    x_pre = project(where, own, other, pieces)
+    x_conv, cumulative, step_size, scaled = project(
+        where, dt_raw, conv_x, head_columns, own, other, pieces
+    )
     bc_all = lax.all_to_all(bc_pre, ("yh", "c", "yl"), 0, 0).reshape(2 * N, -1)
 
     pair = 2 * local
     plane = SIZES["z"] * SIZES["x"]
     share = half // plane
-    x_conv, cumulative, step_size, scaled = call(
-        conv_kernel,
-        [
-            jax.ShapeDtypeStruct((pair, half), bf16),
-            jax.ShapeDtypeStruct((heads, pair), f32),
-            jax.ShapeDtypeStruct((heads, pair), f32),
-            jax.ShapeDtypeStruct((half, pair), bf16),
-        ],
-        mine, x_pre, dt_raw, conv_x, head_columns,
-        blocks={
-            2: ((conv_x.shape[0], half), lambda i, s: (0, s[0])),
-            3: ((heads, 128), lambda i, s: (s[0], 0)),
-        },
-        flops=10**9, bytes_accessed=8 * pair * half, grant=ALL_VMEM,
-    )
     bc_conv, payload, locals_ = call(
         state_kernel,
         [

time: 179 us -> 176 us (0.983)
  Pallas kernels: 26.9 us -> 24.1 us
    pallas_call x6 -> x5, Pallas kernels: 15.3 us -> 11.1 us  [call(): pl.pallas_call(kernel, grid_spec=pltpu.PrefetchScalarGridSpec(num_scalar_...]
    all_to_all x1, blocking collectives: 16 us -> 14 us  [per_device(): lax.all_to_all(jnp.broadcast_to(dots[None, :, None], shape).reshape(2 * t...]
  transfers between devices with their start and end apart: 15 -> 15, of which waited for: 12 -> 13; matrix products, arithmetic and copies ran while one was open for 2% -> 2% of each run, Pallas kernels for 10% -> 9%
where the time goes in v8:
time: 176 us; the launch traced here: 175 us
  starting transfers between devices  72.9 us (41%)
  blocking collectives  30.9 us (18%)
  waiting for transfers between devices  30.6 us (17%)
  Pallas kernels  24.1 us (14%)
  local copies, waits for them, and re-layouts  12.6 us (7%)
  other arithmetic  3.55 us (2%)
    ppermute x3, starting transfers between devices, ring(): behind = lax.ppermute(behind, axis, backward)  20.2 us
    all_to_all x1, blocking collectives, per_device(): states = lax.all_to_all(payload, ('z', 'x'), 0, 0)  16.9 us
    all_to_all x1, blocking collectives, per_device(): lax.all_to_all(jnp.broadcast_to(dots[None, :, None], shape).reshape(2 * t...  14 us
    pallas_call x5, Pallas kernels, call(): pl.pallas_call(kernel, grid_spec=pltpu.PrefetchScalarGridSpec(num_scalar_...  11.1 us
    ppermute x3, waiting for transfers between devices, ring(): ahead = lax.ppermute(ahead, axis, forward)  10.8 us
    unnamed x44, local copies, waits for them, and re-layouts  8.4 us
    ppermute x1, waiting for transfers between devices, ring(): far = lax.ppermute(block[depth:], axis, across)  8.29 us
    all_to_all x1, starting transfers between devices, per_device(): lax.all_to_all(copies, ('yh', 'yl'), 0, 0)  7.91 us
  transfers between devices with their start and end apart: 15, of which 13 were waited for; matrix products, arithmetic and copies ran while one was open for 2% of the time, Pallas kernels for 9%

profile of v8, /device:TPU:1, one launch (start us, length us, event | category | flops | bytes accessed | tf_op | source)
XLA Modules:
  0.0 175.1 jit_solution(4635309958381953914)
XLA Ops:
  0.0 0.8 pad_maximum_fusion.2
  0.8 0.1 reshape.54
  0.9 0.9 slice_bitcast_fusion.1
  1.7 0.1 pad.14.clone
  1.8 0.1 maximum_maximum_fusion
  1.9 0.9 broadcast_in_dim.51
  2.8 5.9 %all-to-all-start = ((bf16[8,72,512]{2,1,0:T(8,128)(2,1)}), bf16[8,72,512]{2,1,0:T(8,128)(2,1)S(1)}, u32[]{:S(2)}, u32[]{:S(2)}) async-start(bf16[8,72,512]{2,1,0:T(8,128)(2,1)} %bitcast.7), calls=%async_computation | async-start | bytes 1179648 | tf_op jit(solution)/shard_map/all_to_all | solution.py:493
  8.7 3.4 %collective-permute-start = (bf16[16,512]{1,0:T(8,128)(2,1)S(1)}, bf16[16,512]{1,0:T(8,128)(2,1)S(1)}, u32[]{:S(2)}, u32[]{:S(2)}) collective-permute-start(bf16[16,512]{1,0:T(8,128)(2,1)S(1)} %slice.15), channel_id=1, source_target_pairs={{0,8},{8,16},{16,24},{24,32},{32,40},{40,48},{48,56},{56,64},{64,7... | collective-permute-start | bytes 49160 | tf_op jit(solution)/shard_map/ppermute | solution.py:466
  12.0 0.9 collective-permute-done
  12.9 3.6 %all-to-all-done = bf16[8,72,512]{2,1,0:T(8,128)(2,1)S(1)} async-done(((bf16[8,72,512]{2,1,0:T(8,128)(2,1)}), bf16[8,72,512]{2,1,0:T(8,128)(2,1)S(1)}, u32[]{:S(2)}, u32[]{:S(2)}) %all-to-all-start) | async-done | bytes 589856 | tf_op jit(solution)/shard_map/all_to_all | solution.py:493
  16.5 1.6 broadcast_in_dim.24
  18.1 7.9 %all-to-all-start.1 = ((bf16[8,272,512]{2,1,0:T(8,128)(2,1)}), bf16[8,272,512]{2,1,0:T(8,128)(2,1)S(1)}, u32[]{:S(2)}, u32[]{:S(2)}) async-start(bf16[8,272,512]{2,1,0:T(8,128)(2,1)} %broadcast_in_dim.24), calls=%async_computation.1 | async-start | bytes 4456448 | tf_op jit(solution)/shard_map/all_to_all | solution.py:511
  26.1 0.0 copy-start.19
  26.2 0.1 reshape.57
  26.3 0.1 reshape.58
  26.5 10.8 %collective-permute-start.2 = (bf16[536,512]{1,0:T(8,128)(2,1)S(1)}, bf16[536,512]{1,0:T(8,128)(2,1)S(1)}, u32[]{:S(2)}, u32[]{:S(2)}) collective-permute-start(bf16[536,512]{1,0:T(8,128)(2,1)S(1)} %pad_maximum_fusion.w0), channel_id=1, source_target_pairs={{0,448},{64,0},{128,64},{192,128},{256,192},{320,256},{384,320},{4... | collective-permute-start | bytes 1646600 | tf_op jit(solution)/shard_map/ppermute | solution.py:436
  37.2 1.9 %collective-permute-start.1 = (bf16[536,512]{1,0:T(8,128)(2,1)S(1)}, bf16[536,512]{1,0:T(8,128)(2,1)}, u32[]{:S(2)}, u32[]{:S(2)}) collective-permute-start(bf16[536,512]{1,0:T(8,128)(2,1)S(1)} %pad_maximum_fusion.w0), channel_id=1, source_target_pairs={{0,64},{64,128},{128,192},{192,256},{256,320},{320,384},{384,448},... | collective-permute-start | bytes 1646600 | tf_op jit(solution)/shard_map/ppermute | solution.py:435
  39.2 3.2 %collective-permute-start.3 = (bf16[24,512]{1,0:T(8,128)(2,1)S(1)}, bf16[24,512]{1,0:T(8,128)(2,1)S(1)}, u32[]{:S(2)}, u32[]{:S(2)}) collective-permute-start(bf16[24,512]{1,0:T(8,128)(2,1)S(1)} %reshape.58), channel_id=1, source_target_pairs={{0,256},{64,320},{128,384},{192,448},{256,0},{320,64},{384,128},{4... | collective-permute-start | bytes 73736 | tf_op jit(solution)/shard_map/ppermute | solution.py:438
  42.4 0.1 pad.8.clone
  42.5 8.3 %collective-permute-done.3.w7 = bf16[24,512]{1,0:T(8,128)(2,1)S(1)} collective-permute-done((bf16[24,512]{1,0:T(8,128)(2,1)S(1)}, bf16[24,512]{1,0:T(8,128)(2,1)S(1)}, u32[]{:S(2)}, u32[]{:S(2)}) %collective-permute-start.3) | collective-permute-done | bytes 24608 | tf_op jit(solution)/shard_map/ppermute | solution.py:438
  50.8 1.4 collective-permute-done.1.w1
  52.2 1.9 %collective-permute-start.4 = (bf16[536,512]{1,0:T(8,128)(2,1)}, bf16[536,512]{1,0:T(8,128)(2,1)}, u32[]{:S(2)}, u32[]{:S(2)}) collective-permute-start(bf16[536,512]{1,0:T(8,128)(2,1)} %collective-permute-done.1.w1), channel_id=1, source_target_pairs={{0,64},{64,128},{128,192},{192,256},{256,320},{320,384},{384,448},... | collective-permute-start | bytes 1646600 | tf_op jit(solution)/shard_map/ppermute | solution.py:435
  54.1 4.6 %collective-permute-start.5 = (bf16[536,512]{1,0:T(8,128)(2,1)S(1)}, bf16[536,512]{1,0:T(8,128)(2,1)}, u32[]{:S(2)}, u32[]{:S(2)}) collective-permute-start(bf16[536,512]{1,0:T(8,128)(2,1)S(1)} %collective-permute-done.2.w2), channel_id=1, source_target_pairs={{0,448},{64,0},{128,64},{192,128},{256,192},{320,256},{384,320},{4... | collective-permute-start | bytes 1646600 | tf_op jit(solution)/shard_map/ppermute | solution.py:436
  58.7 0.1 broadcast_in_dim.52
  58.8 0.1 broadcast_in_dim_reshape.3
  58.9 0.6 pad_add_fusion.where_ref
  59.5 0.1 broadcast_in_dim.56
  59.5 0.1 broadcast_in_dim.57
  59.6 1.4 pad_maximum_fusion.3
  61.0 0.7 maximum_maximum_fusion.1.chan_ref
  61.7 3.8 %collective-permute-done.4.w3 = bf16[536,512]{1,0:T(8,128)(2,1)} collective-permute-done((bf16[536,512]{1,0:T(8,128)(2,1)}, bf16[536,512]{1,0:T(8,128)(2,1)}, u32[]{:S(2)}, u32[]{:S(2)}) %collective-permute-start.4) | collective-permute-done | bytes 548896 | tf_op jit(solution)/shard_map/ppermute | solution.py:435
  65.4 0.6 collective-permute-done.5.w4
  66.0 2.4 %collective-permute-start.6 = (bf16[536,512]{1,0:T(8,128)(2,1)}, bf16[536,512]{1,0:T(8,128)(2,1)S(1)}, u32[]{:S(2)}, u32[]{:S(2)}) collective-permute-start(bf16[536,512]{1,0:T(8,128)(2,1)} %collective-permute-done.4.w3), channel_id=1, source_target_pairs={{0,64},{64,128},{128,192},{192,256},{256,320},{320,384},{384,448},... | collective-permute-start | bytes 1646600 | tf_op jit(solution)/shard_map/ppermute | solution.py:435
  68.5 4.9 %collective-permute-start.7 = (bf16[536,512]{1,0:T(8,128)(2,1)}, bf16[536,512]{1,0:T(8,128)(2,1)}, u32[]{:S(2)}, u32[]{:S(2)}) collective-permute-start(bf16[536,512]{1,0:T(8,128)(2,1)} %collective-permute-done.5.w4), channel_id=1, source_target_pairs={{0,448},{64,0},{128,64},{192,128},{256,192},{320,256},{384,320},{4... | collective-permute-start | bytes 1646600 | tf_op jit(solution)/shard_map/ppermute | solution.py:436
  73.4 5.7 %collective-permute-done.6.w5 = bf16[536,512]{1,0:T(8,128)(2,1)S(1)} collective-permute-done((bf16[536,512]{1,0:T(8,128)(2,1)}, bf16[536,512]{1,0:T(8,128)(2,1)S(1)}, u32[]{:S(2)}, u32[]{:S(2)}) %collective-permute-start.6) | collective-permute-done | bytes 548896 | tf_op jit(solution)/shard_map/ppermute | solution.py:435
  79.0 0.9 copy-done.12
  79.9 0.1 collective-permute-done.7.w6
  80.0 0.5 all-to-all-done.1
  80.5 1.4 copy-done.9
  81.9 7.7 %collective-permute-start.8 = (bf16[4,2,272,512]{3,2,1,0:T(8,128)(2,1)S(1)}, bf16[4,2,272,512]{3,2,1,0:T(8,128)(2,1)}, u32[]{:S(2)}, u32[]{:S(2)}) collective-permute-start(bf16[4,2,272,512]{3,2,1,0:T(8,128)(2,1)S(1)} %bitcast.32), channel_id=1, source_target_pairs={{0,1},{1,0},{2,3},{3,2},{4,5},{5,4},{6,7},{7,6},{8,9},{9,8},{10,11... | collective-permute-start | bytes 6684680 | tf_op jit(solution)/shard_map/ppermute | solution.py:515
  89.6 3.7 %collective-permute-start.9 = (bf16[536,512]{1,0:T(8,128)(2,1)}, bf16[536,512]{1,0:T(8,128)(2,1)}, u32[]{:S(2)}, u32[]{:S(2)}) collective-permute-start(bf16[536,512]{1,0:T(8,128)(2,1)} %copy-done.12), channel_id=1, source_target_pairs={{0,64},{64,128},{128,192},{192,256},{256,320},{320,384},{384,448},... | collective-permute-start | bytes 1646600 | tf_op jit(solution)/shard_map/ppermute | solution.py:446
  93.4 0.3 collective-permute-done.8.other_ref
  93.7 5.3 %shard_map.127 = (bf16[16,16,544]{2,1,0:T(8,128)(2,1)}, f32[8,512]{1,0:T(8,128)}) custom-call(s32[17]{0:T(128)} %pad_add_fusion.where_ref, bf16[4,2,272,512]{3,2,1,0:T(8,128)(2,1)} %bitcast.33, bf16[4,2,272,512]{3,2,1,0:T(8,128)(2,1)} %collective-permute-done.8.other_ref, bf16[536,512]{1,0:T(8,128)(2,1)} %copy-done.10, ...), custom_call_target="tpu_custom_call" | custom-call | flops 1000000000 | bytes 10000000 | tf_op jit(solution)/shard_map/pallas_call | solution.py:171
  99.0 7.1 %all-to-all-start.2 = ((bf16[16,16,544]{2,1,0:T(8,128)(2,1)}), bf16[16,16,544]{2,1,0:T(8,128)(2,1)}, u32[]{:S(2)}, u32[]{:S(2)}) async-start(bf16[16,16,544]{2,1,0:T(8,128)(2,1)} %get-tuple-element.63), calls=%async_computation.2 | async-start | bytes 655360 | tf_op jit(solution)/shard_map/all_to_all | solution.py:522
  106.1 2.1 %collective-permute-done.9.w7 = bf16[536,512]{1,0:T(8,128)(2,1)} collective-permute-done((bf16[536,512]{1,0:T(8,128)(2,1)}, bf16[536,512]{1,0:T(8,128)(2,1)}, u32[]{:S(2)}, u32[]{:S(2)}) %collective-permute-start.9) | collective-permute-done | bytes 548896 | tf_op jit(solution)/shard_map/ppermute | solution.py:446
  108.2 7.8 %shard_map.128 = (bf16[512,512]{1,0:T(8,128)(2,1)}, f32[8,512]{1,0:T(8,128)}, f32[8,512]{1,0:T(8,128)}, bf16[512,512]{1,0:T(8,128)(2,1)}) custom-call(s32[17]{0:T(128)} %pad_add_fusion.where_ref, f32[8,512]{1,0:T(8,128)} %get-tuple-element.61.dt_ref, f32[4,1024]{1,0:T(4,128)} %conv_ref.2, f32[16,128]{1,0:T(8,128)} %get-tuple-element.62.head_ref, ...), custom_call_target="tpu_custom_call" | custom-call | flops 3000000000 | bytes 10000000 | tf_op jit(solution)/shard_map/pallas_call | solution.py:198
  115.9 1.7 all-to-all-done.2
  117.6 3.1 %shard_map.129 = (bf16[512,256]{1,0:T(8,128)(2,1)}, bf16[32,24,128]{2,1,0:T(8,128)(2,1)}, f32[4,512,128]{2,1,0:T(8,128)}) custom-call(s32[1]{0:T(128)} %bitcast.mine_ref.at_ref, bf16[256,544]{1,0:T(8,128)(2,1)} %bitcast.14.bc_ref, f32[4,256]{1,0:T(4,128)} %conv_ref.3, f32[8,512]{1,0:T(8,128)} %get-tuple-element.66.cum_ref, ...), custom_call_target="tpu_custom_call" | custom-call | tf_op jit(solution)/shard_map/pallas_call | solution.py:41
  120.8 16.9 %all_to_all.30.got_ref = bf16[32,24,128]{2,1,0:T(8,128)(2,1)S(1)} all-to-all(bf16[32,24,128]{2,1,0:T(8,128)(2,1)} %get-tuple-element.74), channel_id=1, replica_groups=mesh['z'=8,'x'=4,'yl'=2,'yh'=4,'c'=2] {'z','x'}, dimensions={0} | all-to-all | bytes 393216 | tf_op jit(solution)/shard_map/all_to_all | solution.py:537
  137.7 0.7 copy-done.4
  138.4 0.7 shard_map.131
  139.1 4.2 %all-to-all-start.4 = ((bf16[32,16,128]{2,1,0:T(8,128)(2,1)}), bf16[32,16,128]{2,1,0:T(8,128)(2,1)S(1)}, u32[]{:S(2)}, u32[]{:S(2)}) async-start(bf16[32,16,128]{2,1,0:T(8,128)(2,1)} %shard_map.131), calls=%async_computation.4 | async-start | bytes 262144 | tf_op jit(solution)/shard_map/all_to_all | solution.py:543
  143.2 0.7 copy-done
  144.0 0.9 copy-done.2
  145.0 0.7 copy-done.5
  145.7 1.2 copy-done.6
  146.9 1.0 copy-done.7
  147.9 0.7 copy-done.8
  148.7 2.1 %shard_map.130 = (f32[512,512]{1,0:T(8,128)S(1)}, f32[512,512]{1,0:T(8,128)S(1)}) custom-call(s32[1]{0:T(128)} %bitcast.mine_ref.at_ref, bf16[512,512]{1,0:T(8,128)(2,1)S(1)} %copy-done.7, bf16[512,256]{1,0:T(8,128)(2,1)S(1)} %copy-done.2, f32[8,512]{1,0:T(8,128)S(1)} %copy-done.5, f32[8,512]{1,0:T(8,128)S(1)} %copy-done.8, f32[4,512,128]{2,1,0:T(8,128)S(1)} %copy-done.6, ...), custom_call_target="tpu_custom_call" | custom-call | flops 1000000000 | bytes 3145728 | tf_op jit(solution)/shard_map/pallas_call | solution.py:41
  150.8 1.8 %all-to-all-done.4 = bf16[32,16,128]{2,1,0:T(8,128)(2,1)S(1)} async-done(((bf16[32,16,128]{2,1,0:T(8,128)(2,1)}), bf16[32,16,128]{2,1,0:T(8,128)(2,1)S(1)}, u32[]{:S(2)}, u32[]{:S(2)}) %all-to-all-start.4) | async-done | bytes 131104 | tf_op jit(solution)/shard_map/all_to_all | solution.py:543
  152.6 3.3 %shard_map.132 = (f32[256,512]{1,0:T(8,128)S(1)}, bf16[256,512]{1,0:T(8,128)(2,1)S(1)}, f32[2,1,256]{2,1,0:T(1,128)S(1)}) custom-call(s32[1]{0:T(128)} %bitcast.mine_ref.at_ref, f32[512,512]{1,0:T(8,128)S(1)} %get-tuple-element.72.inside_ref, f32[512,512]{1,0:T(8,128)S(1)} %get-tuple-element.73.growth_ref, bf16[512,256]{1,0:T(8,128)(2,1)S(1)} %copy-done.3, ...), custom_call_target="tpu_custom_call" | custom-call | tf_op jit(solution)/shard_map/pallas_call | solution.py:41
  155.9 3.3 %collective-permute-start.10 = (bf16[256,512]{1,0:T(8,128)(2,1)S(1)}, bf16[256,512]{1,0:T(8,128)(2,1)S(1)}, u32[]{:S(2)}, u32[]{:S(2)}) collective-permute-start(bf16[256,512]{1,0:T(8,128)(2,1)S(1)} %get-tuple-element.77), channel_id=1, source_target_pairs={{0,8},{8,0},{1,9},{9,1},{2,10},{10,2},{3,11},{11,3},{4,12},{12,4},... | collective-permute-start | bytes 786440 | tf_op jit(solution)/shard_map/ppermute | solution.py:568
  159.3 14.0 %all_to_all.31 = f32[16,1,256]{2,1,0:T(1,128)S(1)} all-to-all(f32[16,1,256]{2,1,0:T(1,128)S(1)} %broadcast_in_dim.60), channel_id=1, replica_groups=mesh['z'=8,'x'=4,'yl'=2,'yh'=4,'c'=2] {'yh','yl','c'}, dimensions={0} | all-to-all | bytes 32768 | tf_op jit(solution)/shard_map/all_to_all | solution.py:564
  173.3 1.8 %shard_map.133 = bf16[256,1024]{1,0:T(8,128)(2,1)} custom-call(s32[1]{0:T(128)} %bitcast.mine_ref.at_ref, f32[256,512]{1,0:T(8,128)S(1)} %get-tuple-element.76.keep_ref, bf16[256,512]{1,0:T(8,128)(2,1)S(1)} %collective-permute-done.10.other_ref, f32[16,256]{1,0:T(8,128)S(1)} %bitcast.31, f32[8,1024]{1,0:T(8,128)S(1)} %copy-done.1), custom_call_target="tpu_custom_call" | custom-call | tf_op jit(solution)/shard_map/pallas_call | solution.py:41
  (49 shorter events, 0.3 us)
Async XLA Ops:
  0.0 8.7 %copy-start.13 = (bf16[256,512]{1,0:T(8,128)(2,1)S(1)}, bf16[256,512]{1,0:T(8,128)(2,1)}, u32[]{:S(2)}) copy-start(bf16[256,512]{1,0:T(8,128)(2,1)} %param.13) | copy-start | bytes 786436
  2.8 13.8 %all-to-all-start = ((bf16[8,72,512]{2,1,0:T(8,128)(2,1)}), bf16[8,72,512]{2,1,0:T(8,128)(2,1)S(1)}, u32[]{:S(2)}, u32[]{:S(2)}) async-start(bf16[8,72,512]{2,1,0:T(8,128)(2,1)} %bitcast.7), calls=%async_computation | async-start | bytes 1179648 | tf_op jit(solution)/shard_map/all_to_all | solution.py:493
  8.7 4.2 %collective-permute-start = (bf16[16,512]{1,0:T(8,128)(2,1)S(1)}, bf16[16,512]{1,0:T(8,128)(2,1)S(1)}, u32[]{:S(2)}, u32[]{:S(2)}) collective-permute-start(bf16[16,512]{1,0:T(8,128)(2,1)S(1)} %slice.15), channel_id=1, source_target_pairs={{0,8},{8,16},{16,24},{24,32},{32,40},{40,48},{48,56},{56,64},{64,7... | collective-permute-start | bytes 49160 | tf_op jit(solution)/shard_map/ppermute | solution.py:466
  18.1 62.4 %all-to-all-start.1 = ((bf16[8,272,512]{2,1,0:T(8,128)(2,1)}), bf16[8,272,512]{2,1,0:T(8,128)(2,1)S(1)}, u32[]{:S(2)}, u32[]{:S(2)}) async-start(bf16[8,272,512]{2,1,0:T(8,128)(2,1)} %broadcast_in_dim.24), calls=%async_computation.1 | async-start | bytes 4456448 | tf_op jit(solution)/shard_map/all_to_all | solution.py:511
  26.0 24.8 %copy-start.20 = (s32[8]{0:T(128)S(1)}, s32[8]{0:T(128)}, u32[]{:S(2)}) copy-start(s32[8]{0:T(128)} %constant.70.clone) | copy-start | bytes 100
  26.0 32.7 %copy-start.17 = (f32[16]{0:T(128)S(1)}, f32[16]{0:T(128)}, u32[]{:S(2)}) copy-start(f32[16]{0:T(128)} %param.21) | copy-start | bytes 196
  26.0 33.4 %copy-start.18 = (f32[16]{0:T(128)S(1)}, f32[16]{0:T(128)}, u32[]{:S(2)}) copy-start(f32[16]{0:T(128)} %param.19) | copy-start | bytes 196
  26.1 33.5 %copy-start.19 = (f32[16]{0:T(128)S(1)}, f32[16]{0:T(128)}, u32[]{:S(2)}) copy-start(f32[16]{0:T(128)} %param.20) | copy-start | bytes 196
  26.1 34.9 %copy-start.15 = (f32[1024]{0:T(1024)S(1)}, f32[1024]{0:T(1024)}, u32[]{:S(2)}) copy-start(f32[1024]{0:T(1024)} %param.24) | copy-start | bytes 12292
  26.1 34.9 %copy-start.16 = (f32[1024]{0:T(1024)S(1)}, f32[1024]{0:T(1024)}, u32[]{:S(2)}) copy-start(f32[1024]{0:T(1024)} %param.22) | copy-start | bytes 12292
  26.4 63.2 %copy-start.10 = (bf16[536,512]{1,0:T(8,128)(2,1)}, bf16[536,512]{1,0:T(8,128)(2,1)S(1)}, u32[]{:S(2)}) copy-start(bf16[536,512]{1,0:T(8,128)(2,1)S(1)} %pad_maximum_fusion.w0) | copy-start | bytes 1646596
  26.5 24.4 %collective-permute-start.2 = (bf16[536,512]{1,0:T(8,128)(2,1)S(1)}, bf16[536,512]{1,0:T(8,128)(2,1)S(1)}, u32[]{:S(2)}, u32[]{:S(2)}) collective-permute-start(bf16[536,512]{1,0:T(8,128)(2,1)S(1)} %pad_maximum_fusion.w0), channel_id=1, source_target_pairs={{0,448},{64,0},{128,64},{192,128},{256,192},{320,256},{384,320},{4... | collective-permute-start | bytes 1646600 | tf_op jit(solution)/shard_map/ppermute | solution.py:436
  37.2 15.0 %collective-permute-start.1 = (bf16[536,512]{1,0:T(8,128)(2,1)S(1)}, bf16[536,512]{1,0:T(8,128)(2,1)}, u32[]{:S(2)}, u32[]{:S(2)}) collective-permute-start(bf16[536,512]{1,0:T(8,128)(2,1)S(1)} %pad_maximum_fusion.w0), channel_id=1, source_target_pairs={{0,64},{64,128},{128,192},{192,256},{256,320},{320,384},{384,448},... | collective-permute-start | bytes 1646600 | tf_op jit(solution)/shard_map/ppermute | solution.py:435
  39.2 11.6 %collective-permute-start.3 = (bf16[24,512]{1,0:T(8,128)(2,1)S(1)}, bf16[24,512]{1,0:T(8,128)(2,1)S(1)}, u32[]{:S(2)}, u32[]{:S(2)}) collective-permute-start(bf16[24,512]{1,0:T(8,128)(2,1)S(1)} %reshape.58), channel_id=1, source_target_pairs={{0,256},{64,320},{128,384},{192,448},{256,0},{320,64},{384,128},{4... | collective-permute-start | bytes 73736 | tf_op jit(solution)/shard_map/ppermute | solution.py:438
  50.8 42.6 %copy-start.14 = (bf16[24,512]{1,0:T(8,128)(2,1)}, bf16[24,512]{1,0:T(8,128)(2,1)S(1)}, u32[]{:S(2)}) copy-start(bf16[24,512]{1,0:T(8,128)(2,1)S(1)} %collective-permute-done.3.w7) | copy-start | bytes 73732
  50.8 42.5 %copy-start.11 = (bf16[536,512]{1,0:T(8,128)(2,1)}, bf16[536,512]{1,0:T(8,128)(2,1)S(1)}, u32[]{:S(2)}) copy-start(bf16[536,512]{1,0:T(8,128)(2,1)S(1)} %collective-permute-done.2.w2) | copy-start | bytes 1646596
  52.2 13.2 %collective-permute-start.4 = (bf16[536,512]{1,0:T(8,128)(2,1)}, bf16[536,512]{1,0:T(8,128)(2,1)}, u32[]{:S(2)}, u32[]{:S(2)}) collective-permute-start(bf16[536,512]{1,0:T(8,128)(2,1)} %collective-permute-done.1.w1), channel_id=1, source_target_pairs={{0,64},{64,128},{128,192},{192,256},{256,320},{320,384},{384,448},... | collective-permute-start | bytes 1646600 | tf_op jit(solution)/shard_map/ppermute | solution.py:435
  54.1 11.9 %collective-permute-start.5 = (bf16[536,512]{1,0:T(8,128)(2,1)S(1)}, bf16[536,512]{1,0:T(8,128)(2,1)}, u32[]{:S(2)}, u32[]{:S(2)}) collective-permute-start(bf16[536,512]{1,0:T(8,128)(2,1)S(1)} %collective-permute-done.2.w2), channel_id=1, source_target_pairs={{0,448},{64,0},{128,64},{192,128},{256,192},{320,256},{384,320},{4... | collective-permute-start | bytes 1646600 | tf_op jit(solution)/shard_map/ppermute | solution.py:436
  66.0 13.0 %collective-permute-start.6 = (bf16[536,512]{1,0:T(8,128)(2,1)}, bf16[536,512]{1,0:T(8,128)(2,1)S(1)}, u32[]{:S(2)}, u32[]{:S(2)}) collective-permute-start(bf16[536,512]{1,0:T(8,128)(2,1)} %collective-permute-done.4.w3), channel_id=1, source_target_pairs={{0,64},{64,128},{128,192},{192,256},{256,320},{320,384},{384,448},... | collective-permute-start | bytes 1646600 | tf_op jit(solution)/shard_map/ppermute | solution.py:435
  68.5 11.6 %collective-permute-start.7 = (bf16[536,512]{1,0:T(8,128)(2,1)}, bf16[536,512]{1,0:T(8,128)(2,1)}, u32[]{:S(2)}, u32[]{:S(2)}) collective-permute-start(bf16[536,512]{1,0:T(8,128)(2,1)} %collective-permute-done.5.w4), channel_id=1, source_target_pairs={{0,448},{64,0},{128,64},{192,128},{256,192},{320,256},{384,320},{4... | collective-permute-start | bytes 1646600 | tf_op jit(solution)/shard_map/ppermute | solution.py:436
  79.0 0.9 copy-start.12
  80.5 1.4 copy-start.9
  81.9 11.8 %collective-permute-start.8 = (bf16[4,2,272,512]{3,2,1,0:T(8,128)(2,1)S(1)}, bf16[4,2,272,512]{3,2,1,0:T(8,128)(2,1)}, u32[]{:S(2)}, u32[]{:S(2)}) collective-permute-start(bf16[4,2,272,512]{3,2,1,0:T(8,128)(2,1)S(1)} %bitcast.32), channel_id=1, source_target_pairs={{0,1},{1,0},{2,3},{3,2},{4,5},{5,4},{6,7},{7,6},{8,9},{9,8},{10,11... | collective-permute-start | bytes 6684680 | tf_op jit(solution)/shard_map/ppermute | solution.py:515
  89.6 18.6 %collective-permute-start.9 = (bf16[536,512]{1,0:T(8,128)(2,1)}, bf16[536,512]{1,0:T(8,128)(2,1)}, u32[]{:S(2)}, u32[]{:S(2)}) collective-permute-start(bf16[536,512]{1,0:T(8,128)(2,1)} %copy-done.12), channel_id=1, source_target_pairs={{0,64},{64,128},{128,192},{192,256},{256,320},{320,384},{384,448},... | collective-permute-start | bytes 1646600 | tf_op jit(solution)/shard_map/ppermute | solution.py:446
  99.0 18.6 %all-to-all-start.2 = ((bf16[16,16,544]{2,1,0:T(8,128)(2,1)}), bf16[16,16,544]{2,1,0:T(8,128)(2,1)}, u32[]{:S(2)}, u32[]{:S(2)}) async-start(bf16[16,16,544]{2,1,0:T(8,128)(2,1)} %get-tuple-element.63), calls=%async_computation.2 | async-start | bytes 655360 | tf_op jit(solution)/shard_map/all_to_all | solution.py:522
  137.7 0.7 copy-start.4
  138.3 14.2 %copy-start.1 = (f32[8,1024]{1,0:T(8,128)S(1)}, f32[8,1024]{1,0:T(8,128)}, u32[]{:S(2)}) copy-start(f32[8,1024]{1,0:T(8,128)} %maximum_maximum_fusion.1.chan_ref) | copy-start | bytes 98308
  138.4 14.2 %copy-start.3 = (bf16[512,256]{1,0:T(8,128)(2,1)S(1)}, bf16[512,256]{1,0:T(8,128)(2,1)}, u32[]{:S(2)}) copy-start(bf16[512,256]{1,0:T(8,128)(2,1)} %get-tuple-element.68.bc_ref) | copy-start | bytes 786436
  139.1 13.5 %all-to-all-start.4 = ((bf16[32,16,128]{2,1,0:T(8,128)(2,1)}), bf16[32,16,128]{2,1,0:T(8,128)(2,1)S(1)}, u32[]{:S(2)}, u32[]{:S(2)}) async-start(bf16[32,16,128]{2,1,0:T(8,128)(2,1)} %shard_map.131), calls=%async_computation.4 | async-start | bytes 262144 | tf_op jit(solution)/shard_map/all_to_all | solution.py:543
  143.2 0.8 copy-start
  144.0 0.9 copy-start.2
  144.9 0.7 copy-start.5
  145.7 1.2 copy-start.6
  146.9 1.0 copy-start.7
  147.9 0.7 copy-start.8
  155.9 17.4 %collective-permute-start.10 = (bf16[256,512]{1,0:T(8,128)(2,1)S(1)}, bf16[256,512]{1,0:T(8,128)(2,1)S(1)}, u32[]{:S(2)}, u32[]{:S(2)}) collective-permute-start(bf16[256,512]{1,0:T(8,128)(2,1)S(1)} %get-tuple-element.77), channel_id=1, source_target_pairs={{0,8},{8,0},{1,9},{9,1},{2,10},{10,2},{3,11},{11,3},{4,12},{12,4},... | collective-permute-start | bytes 786440 | tf_op jit(solution)/shard_map/ppermute | solution.py:568

commit v9 on v8

--- a/solution.py
+++ b/solution.py
@@ -184,7 +184,7 @@
             jax.ShapeDtypeStruct((copies, bc_rows, 2 * rows), jnp.bfloat16),
             jax.ShapeDtypeStruct((dt_rows, 2 * (rows - HALO)), jnp.float32),
         ],
-        compiler_params=pltpu.CompilerParams(vmem_limit_bytes=ALL_VMEM),
+        compiler_params=pltpu.CompilerParams(vmem_limit_bytes=64000000),
         cost_estimate=pl.CostEstimate(flops=10**9, bytes_accessed=10**7, transcendentals=0),
     )(where, own, other, *weights)
 
@@ -214,7 +214,7 @@
             jax.ShapeDtypeStruct((heads, tokens), jnp.float32),
             jax.ShapeDtypeStruct((channels, tokens), jnp.bfloat16),
         ],
-        compiler_params=pltpu.CompilerParams(vmem_limit_bytes=ALL_VMEM),
+        compiler_params=pltpu.CompilerParams(vmem_limit_bytes=64000000),
         cost_estimate=pl.CostEstimate(
             flops=3 * 10**9, bytes_accessed=10**7, transcendentals=0
         ),
@@ -434,12 +434,13 @@
     for hop in range(1, count // 2):
         ahead = lax.ppermute(ahead, axis, forward)
         behind = lax.ppermute(behind, axis, backward)
-        if hop == 1:
-            far = lax.ppermute(block[depth:], axis, across)
-            ready = prepare(*lax.optimization_barrier((raw, far))[0])
-            ahead, behind, far = lax.optimization_barrier((ahead, behind, far))
-        elif hop == 2:
-            ahead, behind, ready = lax.optimization_barrier((ahead, behind, ready))
+        if hop == 2:
+            ready = prepare(*raw)
+            far = lax.ppermute(small, axis, across)
+            ahead, behind, ready, far = lax.optimization_barrier((ahead, behind, ready, far))
+        elif hop == 1:
+            ahead, behind = lax.optimization_barrier((ahead, behind))
+            small, raw = lax.optimization_barrier((block[depth:], raw, ahead))[:2]
         else:
             ahead, behind = lax.optimization_barrier((ahead, behind))
         pieces += [ahead, behind]

time: 176 us -> 182 us (1.034)
  waiting for transfers between devices: 30.6 us -> 37.8 us
  starting transfers between devices: 72.9 us -> 70.5 us
    ppermute x3, waiting for transfers between devices: 0.73 us -> 15 us  [ring(): behind = lax.ppermute(behind, axis, backward)]
    ppermute x1, waiting for transfers between devices: 8.29 us -> 0.12 us  [ring(): far = lax.ppermute(small, axis, across)]
    unnamed x44 -> x42, local copies, waits for them, and re-layouts: 8.4 us -> 7.01 us
  transfers between devices with their start and end apart: 15 -> 15, of which waited for: 13 -> 12; matrix products, arithmetic and copies ran while one was open for 2% -> 3% of each run, Pallas kernels for 9% -> 8%
where the time goes in v9:
time: 182 us; the launch traced here: 180 us
  starting transfers between devices  70.5 us (39%)
  waiting for transfers between devices  37.8 us (21%)
  blocking collectives  30.7 us (17%)
  Pallas kernels  24.2 us (13%)
  local copies, waits for them, and re-layouts  12 us (7%)
  other arithmetic  4.62 us (3%)
    ppermute x3, starting transfers between devices, ring(): behind = lax.ppermute(behind, axis, backward)  20.3 us
    all_to_all x1, blocking collectives, per_device(): states = lax.all_to_all(payload, ('z', 'x'), 0, 0)  16.8 us
    ppermute x3, waiting for transfers between devices, ring(): behind = lax.ppermute(behind, axis, backward)  15 us
    all_to_all x1, blocking collectives, per_device(): lax.all_to_all(jnp.broadcast_to(dots[None, :, None], shape).reshape(2 * t...  14 us
    ppermute x3, waiting for transfers between devices, ring(): ahead = lax.ppermute(ahead, axis, forward)  11.9 us
    pallas_call x5, Pallas kernels, call(): pl.pallas_call(kernel, grid_spec=pltpu.PrefetchScalarGridSpec(num_scalar_...  11.1 us
    all_to_all x1, starting transfers between devices, per_device(): lax.all_to_all(copies, ('yh', 'yl'), 0, 0)  7.91 us
    pallas_call x1, Pallas kernels, project(): pl.pallas_call(project_kernel, in_specs=[pl.BlockSpec(memory_space=pltpu....  7.77 us
  transfers between devices with their start and end apart: 15, of which 12 were waited for; matrix products, arithmetic and copies ran while one was open for 3% of the time, Pallas kernels for 8%

profile of v9, /device:TPU:1, one launch (start us, length us, event | category | flops | bytes accessed | tf_op | source)
XLA Modules:
  0.0 180.2 jit_solution(12944608664540315256)
XLA Ops:
  0.0 0.8 pad_maximum_fusion.2
  0.8 0.1 reshape.54
  0.9 0.9 slice_bitcast_fusion.1
  1.7 0.1 pad.14.clone
  1.8 0.1 maximum_maximum_fusion
  1.9 0.9 broadcast_in_dim.51
  2.8 5.9 %all-to-all-start = ((bf16[8,72,512]{2,1,0:T(8,128)(2,1)}), bf16[8,72,512]{2,1,0:T(8,128)(2,1)S(1)}, u32[]{:S(2)}, u32[]{:S(2)}) async-start(bf16[8,72,512]{2,1,0:T(8,128)(2,1)} %bitcast.7), calls=%async_computation | async-start | bytes 1179648 | tf_op jit(solution)/shard_map/all_to_all | solution.py:494
  8.7 3.4 %collective-permute-start = (bf16[16,512]{1,0:T(8,128)(2,1)S(1)}, bf16[16,512]{1,0:T(8,128)(2,1)S(1)}, u32[]{:S(2)}, u32[]{:S(2)}) collective-permute-start(bf16[16,512]{1,0:T(8,128)(2,1)S(1)} %slice.15), channel_id=1, source_target_pairs={{0,8},{8,16},{16,24},{24,32},{32,40},{40,48},{48,56},{56,64},{64,7... | collective-permute-start | bytes 49160 | tf_op jit(solution)/shard_map/ppermute | solution.py:467
  12.0 0.9 collective-permute-done
  12.9 3.6 %all-to-all-done = bf16[8,72,512]{2,1,0:T(8,128)(2,1)S(1)} async-done(((bf16[8,72,512]{2,1,0:T(8,128)(2,1)}), bf16[8,72,512]{2,1,0:T(8,128)(2,1)S(1)}, u32[]{:S(2)}, u32[]{:S(2)}) %all-to-all-start) | async-done | bytes 589856 | tf_op jit(solution)/shard_map/all_to_all | solution.py:494
  16.5 1.6 broadcast_in_dim.24
  18.1 7.9 %all-to-all-start.1 = ((bf16[8,272,512]{2,1,0:T(8,128)(2,1)}), bf16[8,272,512]{2,1,0:T(8,128)(2,1)S(1)}, u32[]{:S(2)}, u32[]{:S(2)}) async-start(bf16[8,272,512]{2,1,0:T(8,128)(2,1)} %broadcast_in_dim.24), calls=%async_computation.1 | async-start | bytes 4456448 | tf_op jit(solution)/shard_map/all_to_all | solution.py:512
  26.1 0.0 copy-start.19
  26.1 0.8 slice.18
  27.0 0.1 reshape.57
  27.1 0.1 reshape.58
  27.2 1.1 pad_maximum_fusion.w0
  28.3 10.8 %collective-permute-start.2 = (bf16[536,512]{1,0:T(8,128)(2,1)S(1)}, bf16[536,512]{1,0:T(8,128)(2,1)}, u32[]{:S(2)}, u32[]{:S(2)}) collective-permute-start(bf16[536,512]{1,0:T(8,128)(2,1)S(1)} %pad_maximum_fusion.w0), channel_id=1, source_target_pairs={{0,448},{64,0},{128,64},{192,128},{256,192},{320,256},{384,320},{4... | collective-permute-start | bytes 1646600 | tf_op jit(solution)/shard_map/ppermute | solution.py:436
  39.1 1.9 %collective-permute-start.1 = (bf16[536,512]{1,0:T(8,128)(2,1)S(1)}, bf16[536,512]{1,0:T(8,128)(2,1)}, u32[]{:S(2)}, u32[]{:S(2)}) collective-permute-start(bf16[536,512]{1,0:T(8,128)(2,1)S(1)} %pad_maximum_fusion.w0), channel_id=1, source_target_pairs={{0,64},{64,128},{128,192},{192,256},{256,320},{320,384},{384,448},... | collective-permute-start | bytes 1646600 | tf_op jit(solution)/shard_map/ppermute | solution.py:435
  41.0 0.1 pad.8.clone
  41.1 7.3 %collective-permute-done.2.w2 = bf16[536,512]{1,0:T(8,128)(2,1)} collective-permute-done((bf16[536,512]{1,0:T(8,128)(2,1)S(1)}, bf16[536,512]{1,0:T(8,128)(2,1)}, u32[]{:S(2)}, u32[]{:S(2)}) %collective-permute-start.2) | collective-permute-done | bytes 548896 | tf_op jit(solution)/shard_map/ppermute | solution.py:436
  48.4 5.2 %collective-permute-done.1.w1 = bf16[536,512]{1,0:T(8,128)(2,1)} collective-permute-done((bf16[536,512]{1,0:T(8,128)(2,1)S(1)}, bf16[536,512]{1,0:T(8,128)(2,1)}, u32[]{:S(2)}, u32[]{:S(2)}) %collective-permute-start.1) | collective-permute-done | bytes 548896 | tf_op jit(solution)/shard_map/ppermute | solution.py:435
  53.5 1.9 %collective-permute-start.3 = (bf16[536,512]{1,0:T(8,128)(2,1)}, bf16[536,512]{1,0:T(8,128)(2,1)}, u32[]{:S(2)}, u32[]{:S(2)}) collective-permute-start(bf16[536,512]{1,0:T(8,128)(2,1)} %collective-permute-done.1.w1), channel_id=1, source_target_pairs={{0,64},{64,128},{128,192},{192,256},{256,320},{320,384},{384,448},... | collective-permute-start | bytes 1646600 | tf_op jit(solution)/shard_map/ppermute | solution.py:435
  55.4 0.1 broadcast_in_dim.52
  55.5 0.1 broadcast_in_dim_reshape.3
  55.6 2.1 %collective-permute-start.5 = (bf16[24,512]{1,0:T(8,128)(2,1)S(1)}, bf16[24,512]{1,0:T(8,128)(2,1)S(1)}, u32[]{:S(2)}, u32[]{:S(2)}) collective-permute-start(bf16[24,512]{1,0:T(8,128)(2,1)S(1)} %reshape.58), channel_id=1, source_target_pairs={{0,256},{64,320},{128,384},{192,448},{256,0},{320,64},{384,128},{4... | collective-permute-start | bytes 73736 | tf_op jit(solution)/shard_map/ppermute | solution.py:439
  57.7 4.6 %collective-permute-start.4 = (bf16[536,512]{1,0:T(8,128)(2,1)}, bf16[536,512]{1,0:T(8,128)(2,1)}, u32[]{:S(2)}, u32[]{:S(2)}) collective-permute-start(bf16[536,512]{1,0:T(8,128)(2,1)} %collective-permute-done.2.w2), channel_id=1, source_target_pairs={{0,448},{64,0},{128,64},{192,128},{256,192},{320,256},{384,320},{4... | collective-permute-start | bytes 1646600 | tf_op jit(solution)/shard_map/ppermute | solution.py:436
  62.3 0.1 broadcast_in_dim.56
  62.4 0.1 broadcast_in_dim.57
  62.4 1.4 pad_maximum_fusion.3
  63.9 0.7 maximum_maximum_fusion.1.chan_ref
  64.5 0.6 pad_add_fusion.where_ref
  65.1 0.1 collective-permute-done.5.w7
  65.3 6.5 %collective-permute-done.4.w4 = bf16[536,512]{1,0:T(8,128)(2,1)} collective-permute-done((bf16[536,512]{1,0:T(8,128)(2,1)}, bf16[536,512]{1,0:T(8,128)(2,1)}, u32[]{:S(2)}, u32[]{:S(2)}) %collective-permute-start.4) | collective-permute-done | bytes 548896 | tf_op jit(solution)/shard_map/ppermute | solution.py:436
  71.8 2.3 %collective-permute-start.6 = (bf16[536,512]{1,0:T(8,128)(2,1)}, bf16[536,512]{1,0:T(8,128)(2,1)S(1)}, u32[]{:S(2)}, u32[]{:S(2)}) collective-permute-start(bf16[536,512]{1,0:T(8,128)(2,1)} %collective-permute-done.3.w3), channel_id=1, source_target_pairs={{0,64},{64,128},{128,192},{192,256},{256,320},{320,384},{384,448},... | collective-permute-start | bytes 1646600 | tf_op jit(solution)/shard_map/ppermute | solution.py:435
  74.1 4.9 %collective-permute-start.7 = (bf16[536,512]{1,0:T(8,128)(2,1)}, bf16[536,512]{1,0:T(8,128)(2,1)}, u32[]{:S(2)}, u32[]{:S(2)}) collective-permute-start(bf16[536,512]{1,0:T(8,128)(2,1)} %collective-permute-done.4.w4), channel_id=1, source_target_pairs={{0,448},{64,0},{128,64},{192,128},{256,192},{320,256},{384,320},{4... | collective-permute-start | bytes 1646600 | tf_op jit(solution)/shard_map/ppermute | solution.py:436
  79.0 6.8 %collective-permute-done.6.w5 = bf16[536,512]{1,0:T(8,128)(2,1)S(1)} collective-permute-done((bf16[536,512]{1,0:T(8,128)(2,1)}, bf16[536,512]{1,0:T(8,128)(2,1)S(1)}, u32[]{:S(2)}, u32[]{:S(2)}) %collective-permute-start.6) | collective-permute-done | bytes 548896 | tf_op jit(solution)/shard_map/ppermute | solution.py:435
  85.8 0.8 copy-done.11
  86.6 1.2 collective-permute-done.7.w6
  87.9 7.1 %collective-permute-start.8 = (bf16[4,2,272,512]{3,2,1,0:T(8,128)(2,1)S(1)}, bf16[4,2,272,512]{3,2,1,0:T(8,128)(2,1)}, u32[]{:S(2)}, u32[]{:S(2)}) collective-permute-start(bf16[4,2,272,512]{3,2,1,0:T(8,128)(2,1)S(1)} %bitcast.32), channel_id=1, source_target_pairs={{0,1},{1,0},{2,3},{3,2},{4,5},{5,4},{6,7},{7,6},{8,9},{9,8},{10,11... | collective-permute-start | bytes 6684680 | tf_op jit(solution)/shard_map/ppermute | solution.py:516
  95.0 3.4 %collective-permute-start.9 = (bf16[536,512]{1,0:T(8,128)(2,1)}, bf16[536,512]{1,0:T(8,128)(2,1)}, u32[]{:S(2)}, u32[]{:S(2)}) collective-permute-start(bf16[536,512]{1,0:T(8,128)(2,1)} %copy-done.11), channel_id=1, source_target_pairs={{0,64},{64,128},{128,192},{192,256},{256,320},{320,384},{384,448},... | collective-permute-start | bytes 1646600 | tf_op jit(solution)/shard_map/ppermute | solution.py:447
  98.4 0.7 collective-permute-done.8.other_ref
  99.1 5.3 %shard_map.127 = (bf16[16,16,544]{2,1,0:T(8,128)(2,1)}, f32[8,512]{1,0:T(8,128)}) custom-call(s32[17]{0:T(128)} %pad_add_fusion.where_ref, bf16[4,2,272,512]{3,2,1,0:T(8,128)(2,1)} %bitcast.33, bf16[4,2,272,512]{3,2,1,0:T(8,128)(2,1)} %collective-permute-done.8.other_ref, bf16[536,512]{1,0:T(8,128)(2,1)} %copy-done.10, ...), custom_call_target="tpu_custom_call" | custom-call | flops 1000000000 | bytes 10000000 | tf_op jit(solution)/shard_map/pallas_call | solution.py:171
  104.4 6.9 %all-to-all-start.2 = ((bf16[16,16,544]{2,1,0:T(8,128)(2,1)}), bf16[16,16,544]{2,1,0:T(8,128)(2,1)}, u32[]{:S(2)}, u32[]{:S(2)}) async-start(bf16[16,16,544]{2,1,0:T(8,128)(2,1)} %get-tuple-element.65), calls=%async_computation.2 | async-start | bytes 655360 | tf_op jit(solution)/shard_map/all_to_all | solution.py:523
  111.4 1.1 collective-permute-done.9.w7
  112.5 7.8 %shard_map.128 = (bf16[512,512]{1,0:T(8,128)(2,1)}, f32[8,512]{1,0:T(8,128)}, f32[8,512]{1,0:T(8,128)}, bf16[512,512]{1,0:T(8,128)(2,1)}) custom-call(s32[17]{0:T(128)} %pad_add_fusion.where_ref, f32[8,512]{1,0:T(8,128)} %get-tuple-element.63.dt_ref, f32[4,1024]{1,0:T(4,128)} %conv_ref.2, f32[16,128]{1,0:T(8,128)} %get-tuple-element.64.head_ref, ...), custom_call_target="tpu_custom_call" | custom-call | flops 3000000000 | bytes 10000000 | tf_op jit(solution)/shard_map/pallas_call | solution.py:198
  120.3 2.6 %all-to-all-done.2 = bf16[16,16,544]{2,1,0:T(8,128)(2,1)} async-done(((bf16[16,16,544]{2,1,0:T(8,128)(2,1)}), bf16[16,16,544]{2,1,0:T(8,128)(2,1)}, u32[]{:S(2)}, u32[]{:S(2)}) %all-to-all-start.2) | async-done | bytes 278560 | tf_op jit(solution)/shard_map/all_to_all | solution.py:523
  122.9 3.1 %shard_map.129 = (bf16[512,256]{1,0:T(8,128)(2,1)}, bf16[32,24,128]{2,1,0:T(8,128)(2,1)}, f32[4,512,128]{2,1,0:T(8,128)}) custom-call(s32[1]{0:T(128)} %bitcast.mine_ref.at_ref, bf16[256,544]{1,0:T(8,128)(2,1)} %bitcast.14.bc_ref, f32[4,256]{1,0:T(4,128)} %conv_ref.3, f32[8,512]{1,0:T(8,128)} %get-tuple-element.68.cum_ref, ...), custom_call_target="tpu_custom_call" | custom-call | tf_op jit(solution)/shard_map/pallas_call | solution.py:41
  126.0 16.8 %all_to_all.30.got_ref = bf16[32,24,128]{2,1,0:T(8,128)(2,1)S(1)} all-to-all(bf16[32,24,128]{2,1,0:T(8,128)(2,1)} %get-tuple-element.76), channel_id=1, replica_groups=mesh['z'=8,'x'=4,'yl'=2,'yh'=4,'c'=2] {'z','x'}, dimensions={0} | all-to-all | bytes 393216 | tf_op jit(solution)/shard_map/all_to_all | solution.py:538
  142.8 0.7 copy-done.4
  143.5 0.7 shard_map.131
  144.2 4.2 %all-to-all-start.4 = ((bf16[32,16,128]{2,1,0:T(8,128)(2,1)}), bf16[32,16,128]{2,1,0:T(8,128)(2,1)S(1)}, u32[]{:S(2)}, u32[]{:S(2)}) async-start(bf16[32,16,128]{2,1,0:T(8,128)(2,1)} %shard_map.131), calls=%async_computation.4 | async-start | bytes 262144 | tf_op jit(solution)/shard_map/all_to_all | solution.py:544
  148.4 0.7 copy-done
  149.1 0.9 copy-done.2
  150.1 0.7 copy-done.5
  150.8 1.2 copy-done.6
  152.0 1.0 copy-done.7
  153.1 0.7 copy-done.8
  153.8 2.1 %shard_map.130 = (f32[512,512]{1,0:T(8,128)S(1)}, f32[512,512]{1,0:T(8,128)S(1)}) custom-call(s32[1]{0:T(128)} %bitcast.mine_ref.at_ref, bf16[512,512]{1,0:T(8,128)(2,1)S(1)} %copy-done.7, bf16[512,256]{1,0:T(8,128)(2,1)S(1)} %copy-done.2, f32[8,512]{1,0:T(8,128)S(1)} %copy-done.5, f32[8,512]{1,0:T(8,128)S(1)} %copy-done.8, f32[4,512,128]{2,1,0:T(8,128)S(1)} %copy-done.6, ...), custom_call_target="tpu_custom_call" | custom-call | flops 1000000000 | bytes 3145728 | tf_op jit(solution)/shard_map/pallas_call | solution.py:41
  155.9 1.8 all-to-all-done.4
  157.7 3.3 %shard_map.132 = (f32[256,512]{1,0:T(8,128)S(1)}, bf16[256,512]{1,0:T(8,128)(2,1)S(1)}, f32[2,1,256]{2,1,0:T(1,128)S(1)}) custom-call(s32[1]{0:T(128)} %bitcast.mine_ref.at_ref, f32[512,512]{1,0:T(8,128)S(1)} %get-tuple-element.74.inside_ref, f32[512,512]{1,0:T(8,128)S(1)} %get-tuple-element.75.growth_ref, bf16[512,256]{1,0:T(8,128)(2,1)S(1)} %copy-done.3, ...), custom_call_target="tpu_custom_call" | custom-call | tf_op jit(solution)/shard_map/pallas_call | solution.py:41
  161.0 3.3 %collective-permute-start.10 = (bf16[256,512]{1,0:T(8,128)(2,1)S(1)}, bf16[256,512]{1,0:T(8,128)(2,1)S(1)}, u32[]{:S(2)}, u32[]{:S(2)}) collective-permute-start(bf16[256,512]{1,0:T(8,128)(2,1)S(1)} %get-tuple-element.79), channel_id=1, source_target_pairs={{0,8},{8,0},{1,9},{9,1},{2,10},{10,2},{3,11},{11,3},{4,12},{12,4},... | collective-permute-start | bytes 786440 | tf_op jit(solution)/shard_map/ppermute | solution.py:569
  164.4 14.0 %all_to_all.31 = f32[16,1,256]{2,1,0:T(1,128)S(1)} all-to-all(f32[16,1,256]{2,1,0:T(1,128)S(1)} %broadcast_in_dim.60), channel_id=1, replica_groups=mesh['z'=8,'x'=4,'yl'=2,'yh'=4,'c'=2] {'yh','yl','c'}, dimensions={0} | all-to-all | bytes 32768 | tf_op jit(solution)/shard_map/all_to_all | solution.py:565
  178.4 1.8 %shard_map.133 = bf16[256,1024]{1,0:T(8,128)(2,1)} custom-call(s32[1]{0:T(128)} %bitcast.mine_ref.at_ref, f32[256,512]{1,0:T(8,128)S(1)} %get-tuple-element.78.keep_ref, bf16[256,512]{1,0:T(8,128)(2,1)S(1)} %collective-permute-done.10.other_ref, f32[16,256]{1,0:T(8,128)S(1)} %bitcast.31, f32[8,1024]{1,0:T(8,128)S(1)} %copy-done.1), custom_call_target="tpu_custom_call" | custom-call | tf_op jit(solution)/shard_map/pallas_call | solution.py:41
  (47 shorter events, 0.2 us)
Async XLA Ops:
  0.0 8.7 %copy-start.12 = (bf16[256,512]{1,0:T(8,128)(2,1)S(1)}, bf16[256,512]{1,0:T(8,128)(2,1)}, u32[]{:S(2)}) copy-start(bf16[256,512]{1,0:T(8,128)(2,1)} %param.13) | copy-start | bytes 786436
  2.8 13.8 %all-to-all-start = ((bf16[8,72,512]{2,1,0:T(8,128)(2,1)}), bf16[8,72,512]{2,1,0:T(8,128)(2,1)S(1)}, u32[]{:S(2)}, u32[]{:S(2)}) async-start(bf16[8,72,512]{2,1,0:T(8,128)(2,1)} %bitcast.7), calls=%async_computation | async-start | bytes 1179648 | tf_op jit(solution)/shard_map/all_to_all | solution.py:494
  8.7 4.2 %collective-permute-start = (bf16[16,512]{1,0:T(8,128)(2,1)S(1)}, bf16[16,512]{1,0:T(8,128)(2,1)S(1)}, u32[]{:S(2)}, u32[]{:S(2)}) collective-permute-start(bf16[16,512]{1,0:T(8,128)(2,1)S(1)} %slice.15), channel_id=1, source_target_pairs={{0,8},{8,16},{16,24},{24,32},{32,40},{40,48},{48,56},{56,64},{64,7... | collective-permute-start | bytes 49160 | tf_op jit(solution)/shard_map/ppermute | solution.py:467
  18.1 69.8 %all-to-all-start.1 = ((bf16[8,272,512]{2,1,0:T(8,128)(2,1)}), bf16[8,272,512]{2,1,0:T(8,128)(2,1)S(1)}, u32[]{:S(2)}, u32[]{:S(2)}) async-start(bf16[8,272,512]{2,1,0:T(8,128)(2,1)} %broadcast_in_dim.24), calls=%async_computation.1 | async-start | bytes 4456448 | tf_op jit(solution)/shard_map/all_to_all | solution.py:512
  26.0 29.4 %copy-start.16 = (f32[16]{0:T(128)S(1)}, f32[16]{0:T(128)}, u32[]{:S(2)}) copy-start(f32[16]{0:T(128)} %param.21) | copy-start | bytes 196
  26.0 36.3 %copy-start.17 = (f32[16]{0:T(128)S(1)}, f32[16]{0:T(128)}, u32[]{:S(2)}) copy-start(f32[16]{0:T(128)} %param.19) | copy-start | bytes 196
  26.0 36.3 %copy-start.18 = (f32[16]{0:T(128)S(1)}, f32[16]{0:T(128)}, u32[]{:S(2)}) copy-start(f32[16]{0:T(128)} %param.20) | copy-start | bytes 196
  26.1 37.8 %copy-start.19 = (s32[8]{0:T(128)S(1)}, s32[8]{0:T(128)}, u32[]{:S(2)}) copy-start(s32[8]{0:T(128)} %constant.70.clone) | copy-start | bytes 100
  26.1 37.8 %copy-start.14 = (f32[1024]{0:T(1024)S(1)}, f32[1024]{0:T(1024)}, u32[]{:S(2)}) copy-start(f32[1024]{0:T(1024)} %param.24) | copy-start | bytes 12292
  26.1 37.8 %copy-start.15 = (f32[1024]{0:T(1024)S(1)}, f32[1024]{0:T(1024)}, u32[]{:S(2)}) copy-start(f32[1024]{0:T(1024)} %param.22) | copy-start | bytes 12292
  28.3 70.8 %copy-start.10 = (bf16[536,512]{1,0:T(8,128)(2,1)}, bf16[536,512]{1,0:T(8,128)(2,1)S(1)}, u32[]{:S(2)}) copy-start(bf16[536,512]{1,0:T(8,128)(2,1)S(1)} %pad_maximum_fusion.w0) | copy-start | bytes 1646596
  28.3 20.1 %collective-permute-start.2 = (bf16[536,512]{1,0:T(8,128)(2,1)S(1)}, bf16[536,512]{1,0:T(8,128)(2,1)}, u32[]{:S(2)}, u32[]{:S(2)}) collective-permute-start(bf16[536,512]{1,0:T(8,128)(2,1)S(1)} %pad_maximum_fusion.w0), channel_id=1, source_target_pairs={{0,448},{64,0},{128,64},{192,128},{256,192},{320,256},{384,320},{4... | collective-permute-start | bytes 1646600 | tf_op jit(solution)/shard_map/ppermute | solution.py:436
  39.1 14.5 %collective-permute-start.1 = (bf16[536,512]{1,0:T(8,128)(2,1)S(1)}, bf16[536,512]{1,0:T(8,128)(2,1)}, u32[]{:S(2)}, u32[]{:S(2)}) collective-permute-start(bf16[536,512]{1,0:T(8,128)(2,1)S(1)} %pad_maximum_fusion.w0), channel_id=1, source_target_pairs={{0,64},{64,128},{128,192},{192,256},{256,320},{320,384},{384,448},... | collective-permute-start | bytes 1646600 | tf_op jit(solution)/shard_map/ppermute | solution.py:435
  53.5 18.3 %collective-permute-start.3 = (bf16[536,512]{1,0:T(8,128)(2,1)}, bf16[536,512]{1,0:T(8,128)(2,1)}, u32[]{:S(2)}, u32[]{:S(2)}) collective-permute-start(bf16[536,512]{1,0:T(8,128)(2,1)} %collective-permute-done.1.w1), channel_id=1, source_target_pairs={{0,64},{64,128},{128,192},{192,256},{256,320},{320,384},{384,448},... | collective-permute-start | bytes 1646600 | tf_op jit(solution)/shard_map/ppermute | solution.py:435
  55.6 9.7 %collective-permute-start.5 = (bf16[24,512]{1,0:T(8,128)(2,1)S(1)}, bf16[24,512]{1,0:T(8,128)(2,1)S(1)}, u32[]{:S(2)}, u32[]{:S(2)}) collective-permute-start(bf16[24,512]{1,0:T(8,128)(2,1)S(1)} %reshape.58), channel_id=1, source_target_pairs={{0,256},{64,320},{128,384},{192,448},{256,0},{320,64},{384,128},{4... | collective-permute-start | bytes 73736 | tf_op jit(solution)/shard_map/ppermute | solution.py:439
  57.7 14.1 %collective-permute-start.4 = (bf16[536,512]{1,0:T(8,128)(2,1)}, bf16[536,512]{1,0:T(8,128)(2,1)}, u32[]{:S(2)}, u32[]{:S(2)}) collective-permute-start(bf16[536,512]{1,0:T(8,128)(2,1)} %collective-permute-done.2.w2), channel_id=1, source_target_pairs={{0,448},{64,0},{128,64},{192,128},{256,192},{320,256},{384,320},{4... | collective-permute-start | bytes 1646600 | tf_op jit(solution)/shard_map/ppermute | solution.py:436
  65.2 33.9 %copy-start.13 = (bf16[24,512]{1,0:T(8,128)(2,1)}, bf16[24,512]{1,0:T(8,128)(2,1)S(1)}, u32[]{:S(2)}) copy-start(bf16[24,512]{1,0:T(8,128)(2,1)S(1)} %collective-permute-done.5.w7) | copy-start | bytes 73732
  71.8 14.0 %collective-permute-start.6 = (bf16[536,512]{1,0:T(8,128)(2,1)}, bf16[536,512]{1,0:T(8,128)(2,1)S(1)}, u32[]{:S(2)}, u32[]{:S(2)}) collective-permute-start(bf16[536,512]{1,0:T(8,128)(2,1)} %collective-permute-done.3.w3), channel_id=1, source_target_pairs={{0,64},{64,128},{128,192},{192,256},{256,320},{320,384},{384,448},... | collective-permute-start | bytes 1646600 | tf_op jit(solution)/shard_map/ppermute | solution.py:435
  74.1 13.8 %collective-permute-start.7 = (bf16[536,512]{1,0:T(8,128)(2,1)}, bf16[536,512]{1,0:T(8,128)(2,1)}, u32[]{:S(2)}, u32[]{:S(2)}) collective-permute-start(bf16[536,512]{1,0:T(8,128)(2,1)} %collective-permute-done.4.w4), channel_id=1, source_target_pairs={{0,448},{64,0},{128,64},{192,128},{256,192},{320,256},{384,320},{4... | collective-permute-start | bytes 1646600 | tf_op jit(solution)/shard_map/ppermute | solution.py:436
  85.8 0.9 copy-start.11
  87.9 11.2 %copy-start.9 = (bf16[8,272,512]{2,1,0:T(8,128)(2,1)}, bf16[8,272,512]{2,1,0:T(8,128)(2,1)S(1)}, u32[]{:S(2)}) copy-start(bf16[8,272,512]{2,1,0:T(8,128)(2,1)S(1)} %all-to-all-done.1) | copy-start | bytes 6684676
  87.9 11.2 %collective-permute-start.8 = (bf16[4,2,272,512]{3,2,1,0:T(8,128)(2,1)S(1)}, bf16[4,2,272,512]{3,2,1,0:T(8,128)(2,1)}, u32[]{:S(2)}, u32[]{:S(2)}) collective-permute-start(bf16[4,2,272,512]{3,2,1,0:T(8,128)(2,1)S(1)} %bitcast.32), channel_id=1, source_target_pairs={{0,1},{1,0},{2,3},{3,2},{4,5},{5,4},{6,7},{7,6},{8,9},{9,8},{10,11... | collective-permute-start | bytes 6684680 | tf_op jit(solution)/shard_map/ppermute | solution.py:516
  95.0 17.5 %collective-permute-start.9 = (bf16[536,512]{1,0:T(8,128)(2,1)}, bf16[536,512]{1,0:T(8,128)(2,1)}, u32[]{:S(2)}, u32[]{:S(2)}) collective-permute-start(bf16[536,512]{1,0:T(8,128)(2,1)} %copy-done.11), channel_id=1, source_target_pairs={{0,64},{64,128},{128,192},{192,256},{256,320},{320,384},{384,448},... | collective-permute-start | bytes 1646600 | tf_op jit(solution)/shard_map/ppermute | solution.py:447
  104.4 18.4 %all-to-all-start.2 = ((bf16[16,16,544]{2,1,0:T(8,128)(2,1)}), bf16[16,16,544]{2,1,0:T(8,128)(2,1)}, u32[]{:S(2)}, u32[]{:S(2)}) async-start(bf16[16,16,544]{2,1,0:T(8,128)(2,1)} %get-tuple-element.65), calls=%async_computation.2 | async-start | bytes 655360 | tf_op jit(solution)/shard_map/all_to_all | solution.py:523
  142.8 0.7 copy-start.4
  143.5 14.3 %copy-start.1 = (f32[8,1024]{1,0:T(8,128)S(1)}, f32[8,1024]{1,0:T(8,128)}, u32[]{:S(2)}) copy-start(f32[8,1024]{1,0:T(8,128)} %maximum_maximum_fusion.1.chan_ref) | copy-start | bytes 98308
  143.5 14.3 %copy-start.3 = (bf16[512,256]{1,0:T(8,128)(2,1)S(1)}, bf16[512,256]{1,0:T(8,128)(2,1)}, u32[]{:S(2)}) copy-start(bf16[512,256]{1,0:T(8,128)(2,1)} %get-tuple-element.70.bc_ref) | copy-start | bytes 786436
  144.2 13.5 %all-to-all-start.4 = ((bf16[32,16,128]{2,1,0:T(8,128)(2,1)}), bf16[32,16,128]{2,1,0:T(8,128)(2,1)S(1)}, u32[]{:S(2)}, u32[]{:S(2)}) async-start(bf16[32,16,128]{2,1,0:T(8,128)(2,1)} %shard_map.131), calls=%async_computation.4 | async-start | bytes 262144 | tf_op jit(solution)/shard_map/all_to_all | solution.py:544
  148.4 0.8 copy-start
  149.1 0.9 copy-start.2
  150.1 0.7 copy-start.5
  150.8 1.2 copy-start.6
  152.0 1.0 copy-start.7
  153.1 0.7 copy-start.8
  161.0 17.4 %collective-permute-start.10 = (bf16[256,512]{1,0:T(8,128)(2,1)S(1)}, bf16[256,512]{1,0:T(8,128)(2,1)S(1)}, u32[]{:S(2)}, u32[]{:S(2)}) collective-permute-start(bf16[256,512]{1,0:T(8,128)(2,1)S(1)} %get-tuple-element.79), channel_id=1, source_target_pairs={{0,8},{8,0},{1,9},{9,1},{2,10},{10,2},{3,11},{11,3},{4,12},{12,4},... | collective-permute-start | bytes 786440 | tf_op jit(solution)/shard_map/ppermute | solution.py:569

commit v10 on v8

--- a/solution.py
+++ b/solution.py
@@ -94,6 +94,12 @@
         @pl.when(jnp.logical_not(mine))
         def _():
             pltpu.make_async_copy(other_ref.at[line], feats.at[step], sem.at[step]).start()
+
+
+def token_kernel(earlier_ref, tokens_ref, out_ref):
+    for at in range(out_ref.shape[0]):
+        out_ref[at, 0:HALO] = earlier_ref[...]
+        out_ref[at, HALO:] = tokens_ref[...]
 
 
 def narrow_kernel(
@@ -466,9 +472,15 @@
     earlier = lax.ppermute(
         tokens[local - HALO :], SEQ, [(i, i + 1) for i in range(seq_count - 1)]
     )
-    extended = jnp.concatenate([earlier, tokens], 0)
     line = SIZES["yh"] * 2
-    copies = jnp.broadcast_to(extended[None], (line,) + extended.shape)
+    copies = pl.pallas_call(
+        token_kernel,
+        out_shape=jax.ShapeDtypeStruct((line, local + HALO, width), bf16),
+        compiler_params=pltpu.CompilerParams(vmem_limit_bytes=8388608),
+        cost_estimate=pl.CostEstimate(
+            flops=0, bytes_accessed=3 * line * local * width, transcendentals=0
+        ),
+    )(earlier, tokens)
 
     fan = SIZES["x"] * SIZES["yl"]
     packed_rows = small * k_rows // half

time: 176 us -> 176 us (level)
  starting transfers between devices: 72.9 us -> 74.7 us
  transfers between devices with their start and end apart: 15 -> 15, of which waited for: 13 -> 12; matrix products, arithmetic and copies ran while one was open for 2% -> 2% of each run, Pallas kernels for 9% -> 10%
where the time goes in v10:
time: 176 us; the launch traced here: 175 us
  starting transfers between devices  74.7 us (42%)
  blocking collectives  30.9 us (18%)
  waiting for transfers between devices  28.9 us (16%)
  Pallas kernels  25.6 us (15%)
  local copies, waits for them, and re-layouts  11 us (6%)
  other arithmetic  3.53 us (2%)
    ppermute x3, starting transfers between devices, ring(): behind = lax.ppermute(behind, axis, backward)  21.7 us
    all_to_all x1, blocking collectives, per_device(): states = lax.all_to_all(payload, ('z', 'x'), 0, 0)  16.9 us
    all_to_all x1, blocking collectives, per_device(): lax.all_to_all(jnp.broadcast_to(dots[None, :, None], shape).reshape(2 * t...  14 us
    pallas_call x5, Pallas kernels, call(): pl.pallas_call(kernel, grid_spec=pltpu.PrefetchScalarGridSpec(num_scalar_...  11.1 us
    ppermute x3, waiting for transfers between devices, ring(): ahead = lax.ppermute(ahead, axis, forward)  10.8 us
    ppermute x1, waiting for transfers between devices, ring(): far = lax.ppermute(block[depth:], axis, across)  8.52 us
    unnamed x44, local copies, waits for them, and re-layouts  8.4 us
    ppermute x1, starting transfers between devices, per_device(): other = lax.ppermute(own, 'c', [(0, 1), (1, 0)])  8.17 us
  transfers between devices with their start and end apart: 15, of which 12 were waited for; matrix products, arithmetic and copies ran while one was open for 2% of the time, Pallas kernels for 10%

profile of v10, /device:TPU:1, one launch (start us, length us, event | category | flops | bytes accessed | tf_op | source)
XLA Modules:
  0.0 175.0 jit_solution(3893479549888937512)
XLA Ops:
  0.0 0.8 pad_maximum_fusion.1
  0.8 0.1 reshape.53
  0.9 0.9 slice_bitcast_fusion.1
  1.7 0.1 pad.14.clone
  1.8 0.1 maximum_maximum_fusion
  1.9 0.9 broadcast_in_dim.44
  2.8 5.9 %all-to-all-start = ((bf16[8,72,512]{2,1,0:T(8,128)(2,1)}), bf16[8,72,512]{2,1,0:T(8,128)(2,1)S(1)}, u32[]{:S(2)}, u32[]{:S(2)}) async-start(bf16[8,72,512]{2,1,0:T(8,128)(2,1)} %bitcast.7), calls=%async_computation | async-start | bytes 1179648 | tf_op jit(solution)/shard_map/all_to_all | solution.py:505
  8.7 3.4 %collective-permute-start = (bf16[16,512]{1,0:T(8,128)(2,1)S(1)}, bf16[16,512]{1,0:T(8,128)(2,1)S(1)}, u32[]{:S(2)}, u32[]{:S(2)}) collective-permute-start(bf16[16,512]{1,0:T(8,128)(2,1)S(1)} %slice.15), channel_id=1, source_target_pairs={{0,8},{8,16},{16,24},{24,32},{32,40},{40,48},{48,56},{56,64},{64,7... | collective-permute-start | bytes 49160 | tf_op jit(solution)/shard_map/ppermute | solution.py:472
  12.0 0.9 collective-permute-done.earlier_ref
  12.9 1.5 shard_map.127
  14.4 2.1 %all-to-all-done = bf16[8,72,512]{2,1,0:T(8,128)(2,1)S(1)} async-done(((bf16[8,72,512]{2,1,0:T(8,128)(2,1)}), bf16[8,72,512]{2,1,0:T(8,128)(2,1)S(1)}, u32[]{:S(2)}, u32[]{:S(2)}) %all-to-all-start) | async-done | bytes 589856 | tf_op jit(solution)/shard_map/all_to_all | solution.py:505
  16.5 7.9 %all-to-all-start.1 = ((bf16[8,272,512]{2,1,0:T(8,128)(2,1)}), bf16[8,272,512]{2,1,0:T(8,128)(2,1)S(1)}, u32[]{:S(2)}, u32[]{:S(2)}) async-start(bf16[8,272,512]{2,1,0:T(8,128)(2,1)} %shard_map.127), calls=%async_computation.1 | async-start | bytes 4456448 | tf_op jit(solution)/shard_map/all_to_all | solution.py:523
  24.5 0.0 copy-start.17
  24.5 0.0 copy-start.18
  24.6 0.1 reshape.56
  24.7 0.1 reshape.57
  24.9 12.3 %collective-permute-start.2 = (bf16[536,512]{1,0:T(8,128)(2,1)S(1)}, bf16[536,512]{1,0:T(8,128)(2,1)S(1)}, u32[]{:S(2)}, u32[]{:S(2)}) collective-permute-start(bf16[536,512]{1,0:T(8,128)(2,1)S(1)} %pad_maximum_fusion.w0), channel_id=1, source_target_pairs={{0,448},{64,0},{128,64},{192,128},{256,192},{320,256},{384,320},{4... | collective-permute-start | bytes 1646600 | tf_op jit(solution)/shard_map/ppermute | solution.py:442
  37.2 1.9 %collective-permute-start.1 = (bf16[536,512]{1,0:T(8,128)(2,1)S(1)}, bf16[536,512]{1,0:T(8,128)(2,1)}, u32[]{:S(2)}, u32[]{:S(2)}) collective-permute-start(bf16[536,512]{1,0:T(8,128)(2,1)S(1)} %pad_maximum_fusion.w0), channel_id=1, source_target_pairs={{0,64},{64,128},{128,192},{192,256},{256,320},{320,384},{384,448},... | collective-permute-start | bytes 1646600 | tf_op jit(solution)/shard_map/ppermute | solution.py:441
  39.1 3.1 %collective-permute-start.3 = (bf16[24,512]{1,0:T(8,128)(2,1)S(1)}, bf16[24,512]{1,0:T(8,128)(2,1)S(1)}, u32[]{:S(2)}, u32[]{:S(2)}) collective-permute-start(bf16[24,512]{1,0:T(8,128)(2,1)S(1)} %reshape.57), channel_id=1, source_target_pairs={{0,256},{64,320},{128,384},{192,448},{256,0},{320,64},{384,128},{4... | collective-permute-start | bytes 73736 | tf_op jit(solution)/shard_map/ppermute | solution.py:444
  42.2 0.1 pad.8.clone
  42.3 8.5 %collective-permute-done.3.w7 = bf16[24,512]{1,0:T(8,128)(2,1)S(1)} collective-permute-done((bf16[24,512]{1,0:T(8,128)(2,1)S(1)}, bf16[24,512]{1,0:T(8,128)(2,1)S(1)}, u32[]{:S(2)}, u32[]{:S(2)}) %collective-permute-start.3) | collective-permute-done | bytes 24608 | tf_op jit(solution)/shard_map/ppermute | solution.py:444
  50.8 1.3 collective-permute-done.1.w1
  52.1 1.9 %collective-permute-start.4 = (bf16[536,512]{1,0:T(8,128)(2,1)}, bf16[536,512]{1,0:T(8,128)(2,1)}, u32[]{:S(2)}, u32[]{:S(2)}) collective-permute-start(bf16[536,512]{1,0:T(8,128)(2,1)} %collective-permute-done.1.w1), channel_id=1, source_target_pairs={{0,64},{64,128},{128,192},{192,256},{256,320},{320,384},{384,448},... | collective-permute-start | bytes 1646600 | tf_op jit(solution)/shard_map/ppermute | solution.py:441
  54.1 4.6 %collective-permute-start.5 = (bf16[536,512]{1,0:T(8,128)(2,1)S(1)}, bf16[536,512]{1,0:T(8,128)(2,1)}, u32[]{:S(2)}, u32[]{:S(2)}) collective-permute-start(bf16[536,512]{1,0:T(8,128)(2,1)S(1)} %collective-permute-done.2.w2), channel_id=1, source_target_pairs={{0,448},{64,0},{128,64},{192,128},{256,192},{320,256},{384,320},{4... | collective-permute-start | bytes 1646600 | tf_op jit(solution)/shard_map/ppermute | solution.py:442
  58.7 0.1 broadcast_in_dim.45
  58.7 0.1 broadcast_in_dim_reshape.3
  58.8 0.6 pad_add_fusion.where_ref
  59.4 0.1 broadcast_in_dim.49
  59.4 0.1 broadcast_in_dim.50
  59.5 1.4 pad_maximum_fusion.2
  60.9 0.7 maximum_maximum_fusion.1.chan_ref
  61.6 3.8 %collective-permute-done.4.w3 = bf16[536,512]{1,0:T(8,128)(2,1)} collective-permute-done((bf16[536,512]{1,0:T(8,128)(2,1)}, bf16[536,512]{1,0:T(8,128)(2,1)}, u32[]{:S(2)}, u32[]{:S(2)}) %collective-permute-start.4) | collective-permute-done | bytes 548896 | tf_op jit(solution)/shard_map/ppermute | solution.py:441
  65.3 0.6 collective-permute-done.5.w4
  65.9 2.4 %collective-permute-start.6 = (bf16[536,512]{1,0:T(8,128)(2,1)}, bf16[536,512]{1,0:T(8,128)(2,1)S(1)}, u32[]{:S(2)}, u32[]{:S(2)}) collective-permute-start(bf16[536,512]{1,0:T(8,128)(2,1)} %collective-permute-done.4.w3), channel_id=1, source_target_pairs={{0,64},{64,128},{128,192},{192,256},{256,320},{320,384},{384,448},... | collective-permute-start | bytes 1646600 | tf_op jit(solution)/shard_map/ppermute | solution.py:441
  68.4 4.9 %collective-permute-start.7 = (bf16[536,512]{1,0:T(8,128)(2,1)}, bf16[536,512]{1,0:T(8,128)(2,1)}, u32[]{:S(2)}, u32[]{:S(2)}) collective-permute-start(bf16[536,512]{1,0:T(8,128)(2,1)} %collective-permute-done.5.w4), channel_id=1, source_target_pairs={{0,448},{64,0},{128,64},{192,128},{256,192},{320,256},{384,320},{4... | collective-permute-start | bytes 1646600 | tf_op jit(solution)/shard_map/ppermute | solution.py:442
  73.3 5.7 %collective-permute-done.6.w5 = bf16[536,512]{1,0:T(8,128)(2,1)S(1)} collective-permute-done((bf16[536,512]{1,0:T(8,128)(2,1)}, bf16[536,512]{1,0:T(8,128)(2,1)S(1)}, u32[]{:S(2)}, u32[]{:S(2)}) %collective-permute-start.6) | collective-permute-done | bytes 548896 | tf_op jit(solution)/shard_map/ppermute | solution.py:441
  79.0 0.9 copy-done.13
  79.8 0.1 collective-permute-done.7.w6
  80.0 1.4 copy-done.10
  81.3 8.2 %collective-permute-start.8 = (bf16[4,2,272,512]{3,2,1,0:T(8,128)(2,1)S(1)}, bf16[4,2,272,512]{3,2,1,0:T(8,128)(2,1)}, u32[]{:S(2)}, u32[]{:S(2)}) collective-permute-start(bf16[4,2,272,512]{3,2,1,0:T(8,128)(2,1)S(1)} %bitcast.32), channel_id=1, source_target_pairs={{0,1},{1,0},{2,3},{3,2},{4,5},{5,4},{6,7},{7,6},{8,9},{9,8},{10,11... | collective-permute-start | bytes 6684680 | tf_op jit(solution)/shard_map/ppermute | solution.py:527
  89.5 3.7 %collective-permute-start.9 = (bf16[536,512]{1,0:T(8,128)(2,1)}, bf16[536,512]{1,0:T(8,128)(2,1)}, u32[]{:S(2)}, u32[]{:S(2)}) collective-permute-start(bf16[536,512]{1,0:T(8,128)(2,1)} %copy-done.13), channel_id=1, source_target_pairs={{0,64},{64,128},{128,192},{192,256},{256,320},{320,384},{384,448},... | collective-permute-start | bytes 1646600 | tf_op jit(solution)/shard_map/ppermute | solution.py:452
  93.3 0.3 collective-permute-done.8.other_ref
  93.6 5.3 %shard_map.128 = (bf16[16,16,544]{2,1,0:T(8,128)(2,1)}, f32[8,512]{1,0:T(8,128)}) custom-call(s32[17]{0:T(128)} %pad_add_fusion.where_ref, bf16[4,2,272,512]{3,2,1,0:T(8,128)(2,1)} %bitcast.33, bf16[4,2,272,512]{3,2,1,0:T(8,128)(2,1)} %collective-permute-done.8.other_ref, bf16[536,512]{1,0:T(8,128)(2,1)} %copy-done.11, ...), custom_call_target="tpu_custom_call" | custom-call | flops 1000000000 | bytes 10000000 | tf_op jit(solution)/shard_map/pallas_call | solution.py:177
  98.9 7.1 %all-to-all-start.2 = ((bf16[16,16,544]{2,1,0:T(8,128)(2,1)}), bf16[16,16,544]{2,1,0:T(8,128)(2,1)}, u32[]{:S(2)}, u32[]{:S(2)}) async-start(bf16[16,16,544]{2,1,0:T(8,128)(2,1)} %get-tuple-element.63), calls=%async_computation.2 | async-start | bytes 655360 | tf_op jit(solution)/shard_map/all_to_all | solution.py:534
  106.0 2.1 %collective-permute-done.9.w7 = bf16[536,512]{1,0:T(8,128)(2,1)} collective-permute-done((bf16[536,512]{1,0:T(8,128)(2,1)}, bf16[536,512]{1,0:T(8,128)(2,1)}, u32[]{:S(2)}, u32[]{:S(2)}) %collective-permute-start.9) | collective-permute-done | bytes 548896 | tf_op jit(solution)/shard_map/ppermute | solution.py:452
  108.1 7.8 %shard_map.129 = (bf16[512,512]{1,0:T(8,128)(2,1)}, f32[8,512]{1,0:T(8,128)}, f32[8,512]{1,0:T(8,128)}, bf16[512,512]{1,0:T(8,128)(2,1)}) custom-call(s32[17]{0:T(128)} %pad_add_fusion.where_ref, f32[8,512]{1,0:T(8,128)} %get-tuple-element.61.dt_ref, f32[4,1024]{1,0:T(4,128)} %conv_ref.2, f32[16,128]{1,0:T(8,128)} %get-tuple-element.62.head_ref, ...), custom_call_target="tpu_custom_call" | custom-call | flops 3000000000 | bytes 10000000 | tf_op jit(solution)/shard_map/pallas_call | solution.py:204
  115.9 1.7 all-to-all-done.2
  117.5 3.1 %shard_map.130 = (bf16[512,256]{1,0:T(8,128)(2,1)}, bf16[32,24,128]{2,1,0:T(8,128)(2,1)}, f32[4,512,128]{2,1,0:T(8,128)}) custom-call(s32[1]{0:T(128)} %bitcast.mine_ref.at_ref, bf16[256,544]{1,0:T(8,128)(2,1)} %bitcast.14.bc_ref, f32[4,256]{1,0:T(4,128)} %conv_ref.3, f32[8,512]{1,0:T(8,128)} %get-tuple-element.66.cum_ref, ...), custom_call_target="tpu_custom_call" | custom-call | tf_op jit(solution)/shard_map/pallas_call | solution.py:41
  120.7 16.9 %all_to_all.30.got_ref = bf16[32,24,128]{2,1,0:T(8,128)(2,1)S(1)} all-to-all(bf16[32,24,128]{2,1,0:T(8,128)(2,1)} %get-tuple-element.74), channel_id=1, replica_groups=mesh['z'=8,'x'=4,'yl'=2,'yh'=4,'c'=2] {'z','x'}, dimensions={0} | all-to-all | bytes 393216 | tf_op jit(solution)/shard_map/all_to_all | solution.py:549
  137.6 0.7 copy-done.5
  138.3 0.7 shard_map.132
  139.0 4.2 %all-to-all-start.4 = ((bf16[32,16,128]{2,1,0:T(8,128)(2,1)}), bf16[32,16,128]{2,1,0:T(8,128)(2,1)S(1)}, u32[]{:S(2)}, u32[]{:S(2)}) async-start(bf16[32,16,128]{2,1,0:T(8,128)(2,1)} %shard_map.132), calls=%async_computation.4 | async-start | bytes 262144 | tf_op jit(solution)/shard_map/all_to_all | solution.py:555
  143.2 0.7 copy-done.1
  143.9 0.9 copy-done.3
  144.9 0.7 copy-done.6
  145.6 1.2 copy-done.7
  146.8 1.0 copy-done.8
  147.9 0.7 copy-done.9
  148.6 2.1 %shard_map.131 = (f32[512,512]{1,0:T(8,128)S(1)}, f32[512,512]{1,0:T(8,128)S(1)}) custom-call(s32[1]{0:T(128)} %bitcast.mine_ref.at_ref, bf16[512,512]{1,0:T(8,128)(2,1)S(1)} %copy-done.8, bf16[512,256]{1,0:T(8,128)(2,1)S(1)} %copy-done.3, f32[8,512]{1,0:T(8,128)S(1)} %copy-done.6, f32[8,512]{1,0:T(8,128)S(1)} %copy-done.9, f32[4,512,128]{2,1,0:T(8,128)S(1)} %copy-done.7, ...), custom_call_target="tpu_custom_call" | custom-call | flops 1000000000 | bytes 3145728 | tf_op jit(solution)/shard_map/pallas_call | solution.py:41
  150.7 1.8 %all-to-all-done.4 = bf16[32,16,128]{2,1,0:T(8,128)(2,1)S(1)} async-done(((bf16[32,16,128]{2,1,0:T(8,128)(2,1)}), bf16[32,16,128]{2,1,0:T(8,128)(2,1)S(1)}, u32[]{:S(2)}, u32[]{:S(2)}) %all-to-all-start.4) | async-done | bytes 131104 | tf_op jit(solution)/shard_map/all_to_all | solution.py:555
  152.5 3.3 %shard_map.133 = (f32[256,512]{1,0:T(8,128)S(1)}, bf16[256,512]{1,0:T(8,128)(2,1)S(1)}, f32[2,1,256]{2,1,0:T(1,128)S(1)}) custom-call(s32[1]{0:T(128)} %bitcast.mine_ref.at_ref, f32[512,512]{1,0:T(8,128)S(1)} %get-tuple-element.72.inside_ref, f32[512,512]{1,0:T(8,128)S(1)} %get-tuple-element.73.growth_ref, bf16[512,256]{1,0:T(8,128)(2,1)S(1)} %copy-done.4, ...), custom_call_target="tpu_custom_call" | custom-call | tf_op jit(solution)/shard_map/pallas_call | solution.py:41
  155.8 3.3 %collective-permute-start.10 = (bf16[256,512]{1,0:T(8,128)(2,1)S(1)}, bf16[256,512]{1,0:T(8,128)(2,1)S(1)}, u32[]{:S(2)}, u32[]{:S(2)}) collective-permute-start(bf16[256,512]{1,0:T(8,128)(2,1)S(1)} %get-tuple-element.77), channel_id=1, source_target_pairs={{0,8},{8,0},{1,9},{9,1},{2,10},{10,2},{3,11},{11,3},{4,12},{12,4},... | collective-permute-start | bytes 786440 | tf_op jit(solution)/shard_map/ppermute | solution.py:580
  159.2 14.0 %all_to_all.31 = f32[16,1,256]{2,1,0:T(1,128)S(1)} all-to-all(f32[16,1,256]{2,1,0:T(1,128)S(1)} %broadcast_in_dim.53), channel_id=1, replica_groups=mesh['z'=8,'x'=4,'yl'=2,'yh'=4,'c'=2] {'yh','yl','c'}, dimensions={0} | all-to-all | bytes 32768 | tf_op jit(solution)/shard_map/all_to_all | solution.py:576
  173.2 1.8 %shard_map.134 = bf16[256,1024]{1,0:T(8,128)(2,1)} custom-call(s32[1]{0:T(128)} %bitcast.mine_ref.at_ref, f32[256,512]{1,0:T(8,128)S(1)} %get-tuple-element.76.keep_ref, bf16[256,512]{1,0:T(8,128)(2,1)S(1)} %collective-permute-done.10.other_ref, f32[16,256]{1,0:T(8,128)S(1)} %bitcast.31, f32[8,1024]{1,0:T(8,128)S(1)} %copy-done.2), custom_call_target="tpu_custom_call" | custom-call | tf_op jit(solution)/shard_map/pallas_call | solution.py:41
  (48 shorter events, 0.3 us)
Async XLA Ops:
  0.0 8.7 %copy-start = (bf16[256,512]{1,0:T(8,128)(2,1)S(1)}, bf16[256,512]{1,0:T(8,128)(2,1)}, u32[]{:S(2)}) copy-start(bf16[256,512]{1,0:T(8,128)(2,1)} %tokens_ref.1) | copy-start | bytes 786436
  2.8 13.8 %all-to-all-start = ((bf16[8,72,512]{2,1,0:T(8,128)(2,1)}), bf16[8,72,512]{2,1,0:T(8,128)(2,1)S(1)}, u32[]{:S(2)}, u32[]{:S(2)}) async-start(bf16[8,72,512]{2,1,0:T(8,128)(2,1)} %bitcast.7), calls=%async_computation | async-start | bytes 1179648 | tf_op jit(solution)/shard_map/all_to_all | solution.py:505
  8.7 4.2 %collective-permute-start = (bf16[16,512]{1,0:T(8,128)(2,1)S(1)}, bf16[16,512]{1,0:T(8,128)(2,1)S(1)}, u32[]{:S(2)}, u32[]{:S(2)}) collective-permute-start(bf16[16,512]{1,0:T(8,128)(2,1)S(1)} %slice.15), channel_id=1, source_target_pairs={{0,8},{8,16},{16,24},{24,32},{32,40},{40,48},{48,56},{56,64},{64,7... | collective-permute-start | bytes 49160 | tf_op jit(solution)/shard_map/ppermute | solution.py:472
  16.5 63.4 %all-to-all-start.1 = ((bf16[8,272,512]{2,1,0:T(8,128)(2,1)}), bf16[8,272,512]{2,1,0:T(8,128)(2,1)S(1)}, u32[]{:S(2)}, u32[]{:S(2)}) async-start(bf16[8,272,512]{2,1,0:T(8,128)(2,1)} %shard_map.127), calls=%async_computation.1 | async-start | bytes 4456448 | tf_op jit(solution)/shard_map/all_to_all | solution.py:523
  24.5 26.3 %copy-start.20 = (s32[8]{0:T(128)S(1)}, s32[8]{0:T(128)}, u32[]{:S(2)}) copy-start(s32[8]{0:T(128)} %constant.70.clone) | copy-start | bytes 100
  24.5 34.2 %copy-start.17 = (f32[16]{0:T(128)S(1)}, f32[16]{0:T(128)}, u32[]{:S(2)}) copy-start(f32[16]{0:T(128)} %param.21) | copy-start | bytes 196
  24.5 34.9 %copy-start.18 = (f32[16]{0:T(128)S(1)}, f32[16]{0:T(128)}, u32[]{:S(2)}) copy-start(f32[16]{0:T(128)} %param.19) | copy-start | bytes 196
  24.5 35.0 %copy-start.19 = (f32[16]{0:T(128)S(1)}, f32[16]{0:T(128)}, u32[]{:S(2)}) copy-start(f32[16]{0:T(128)} %param.20) | copy-start | bytes 196
  24.5 36.4 %copy-start.15 = (f32[1024]{0:T(1024)S(1)}, f32[1024]{0:T(1024)}, u32[]{:S(2)}) copy-start(f32[1024]{0:T(1024)} %param.24) | copy-start | bytes 12292
  24.5 36.4 %copy-start.16 = (f32[1024]{0:T(1024)S(1)}, f32[1024]{0:T(1024)}, u32[]{:S(2)}) copy-start(f32[1024]{0:T(1024)} %param.22) | copy-start | bytes 12292
  24.9 64.7 %copy-start.11 = (bf16[536,512]{1,0:T(8,128)(2,1)}, bf16[536,512]{1,0:T(8,128)(2,1)S(1)}, u32[]{:S(2)}) copy-start(bf16[536,512]{1,0:T(8,128)(2,1)S(1)} %pad_maximum_fusion.w0) | copy-start | bytes 1646596
  24.9 25.9 %collective-permute-start.2 = (bf16[536,512]{1,0:T(8,128)(2,1)S(1)}, bf16[536,512]{1,0:T(8,128)(2,1)S(1)}, u32[]{:S(2)}, u32[]{:S(2)}) collective-permute-start(bf16[536,512]{1,0:T(8,128)(2,1)S(1)} %pad_maximum_fusion.w0), channel_id=1, source_target_pairs={{0,448},{64,0},{128,64},{192,128},{256,192},{320,256},{384,320},{4... | collective-permute-start | bytes 1646600 | tf_op jit(solution)/shard_map/ppermute | solution.py:442
  37.2 15.0 %collective-permute-start.1 = (bf16[536,512]{1,0:T(8,128)(2,1)S(1)}, bf16[536,512]{1,0:T(8,128)(2,1)}, u32[]{:S(2)}, u32[]{:S(2)}) collective-permute-start(bf16[536,512]{1,0:T(8,128)(2,1)S(1)} %pad_maximum_fusion.w0), channel_id=1, source_target_pairs={{0,64},{64,128},{128,192},{192,256},{256,320},{320,384},{384,448},... | collective-permute-start | bytes 1646600 | tf_op jit(solution)/shard_map/ppermute | solution.py:441
  39.1 11.7 %collective-permute-start.3 = (bf16[24,512]{1,0:T(8,128)(2,1)S(1)}, bf16[24,512]{1,0:T(8,128)(2,1)S(1)}, u32[]{:S(2)}, u32[]{:S(2)}) collective-permute-start(bf16[24,512]{1,0:T(8,128)(2,1)S(1)} %reshape.57), channel_id=1, source_target_pairs={{0,256},{64,320},{128,384},{192,448},{256,0},{320,64},{384,128},{4... | collective-permute-start | bytes 73736 | tf_op jit(solution)/shard_map/ppermute | solution.py:444
  50.8 42.5 %copy-start.14 = (bf16[24,512]{1,0:T(8,128)(2,1)}, bf16[24,512]{1,0:T(8,128)(2,1)S(1)}, u32[]{:S(2)}) copy-start(bf16[24,512]{1,0:T(8,128)(2,1)S(1)} %collective-permute-done.3.w7) | copy-start | bytes 73732
  50.8 42.5 %copy-start.12 = (bf16[536,512]{1,0:T(8,128)(2,1)}, bf16[536,512]{1,0:T(8,128)(2,1)S(1)}, u32[]{:S(2)}) copy-start(bf16[536,512]{1,0:T(8,128)(2,1)S(1)} %collective-permute-done.2.w2) | copy-start | bytes 1646596
  52.1 13.2 %collective-permute-start.4 = (bf16[536,512]{1,0:T(8,128)(2,1)}, bf16[536,512]{1,0:T(8,128)(2,1)}, u32[]{:S(2)}, u32[]{:S(2)}) collective-permute-start(bf16[536,512]{1,0:T(8,128)(2,1)} %collective-permute-done.1.w1), channel_id=1, source_target_pairs={{0,64},{64,128},{128,192},{192,256},{256,320},{320,384},{384,448},... | collective-permute-start | bytes 1646600 | tf_op jit(solution)/shard_map/ppermute | solution.py:441
  54.1 11.9 %collective-permute-start.5 = (bf16[536,512]{1,0:T(8,128)(2,1)S(1)}, bf16[536,512]{1,0:T(8,128)(2,1)}, u32[]{:S(2)}, u32[]{:S(2)}) collective-permute-start(bf16[536,512]{1,0:T(8,128)(2,1)S(1)} %collective-permute-done.2.w2), channel_id=1, source_target_pairs={{0,448},{64,0},{128,64},{192,128},{256,192},{320,256},{384,320},{4... | collective-permute-start | bytes 1646600 | tf_op jit(solution)/shard_map/ppermute | solution.py:442
  65.9 13.0 %collective-permute-start.6 = (bf16[536,512]{1,0:T(8,128)(2,1)}, bf16[536,512]{1,0:T(8,128)(2,1)S(1)}, u32[]{:S(2)}, u32[]{:S(2)}) collective-permute-start(bf16[536,512]{1,0:T(8,128)(2,1)} %collective-permute-done.4.w3), channel_id=1, source_target_pairs={{0,64},{64,128},{128,192},{192,256},{256,320},{320,384},{384,448},... | collective-permute-start | bytes 1646600 | tf_op jit(solution)/shard_map/ppermute | solution.py:441
  68.4 11.6 %collective-permute-start.7 = (bf16[536,512]{1,0:T(8,128)(2,1)}, bf16[536,512]{1,0:T(8,128)(2,1)}, u32[]{:S(2)}, u32[]{:S(2)}) collective-permute-start(bf16[536,512]{1,0:T(8,128)(2,1)} %collective-permute-done.5.w4), channel_id=1, source_target_pairs={{0,448},{64,0},{128,64},{192,128},{256,192},{320,256},{384,320},{4... | collective-permute-start | bytes 1646600 | tf_op jit(solution)/shard_map/ppermute | solution.py:442
  79.0 0.9 copy-start.13
  80.0 1.4 copy-start.10
  81.3 12.3 %collective-permute-start.8 = (bf16[4,2,272,512]{3,2,1,0:T(8,128)(2,1)S(1)}, bf16[4,2,272,512]{3,2,1,0:T(8,128)(2,1)}, u32[]{:S(2)}, u32[]{:S(2)}) collective-permute-start(bf16[4,2,272,512]{3,2,1,0:T(8,128)(2,1)S(1)} %bitcast.32), channel_id=1, source_target_pairs={{0,1},{1,0},{2,3},{3,2},{4,5},{5,4},{6,7},{7,6},{8,9},{9,8},{10,11... | collective-permute-start | bytes 6684680 | tf_op jit(solution)/shard_map/ppermute | solution.py:527
  89.5 18.6 %collective-permute-start.9 = (bf16[536,512]{1,0:T(8,128)(2,1)}, bf16[536,512]{1,0:T(8,128)(2,1)}, u32[]{:S(2)}, u32[]{:S(2)}) collective-permute-start(bf16[536,512]{1,0:T(8,128)(2,1)} %copy-done.13), channel_id=1, source_target_pairs={{0,64},{64,128},{128,192},{192,256},{256,320},{320,384},{384,448},... | collective-permute-start | bytes 1646600 | tf_op jit(solution)/shard_map/ppermute | solution.py:452
  98.9 18.6 %all-to-all-start.2 = ((bf16[16,16,544]{2,1,0:T(8,128)(2,1)}), bf16[16,16,544]{2,1,0:T(8,128)(2,1)}, u32[]{:S(2)}, u32[]{:S(2)}) async-start(bf16[16,16,544]{2,1,0:T(8,128)(2,1)} %get-tuple-element.63), calls=%async_computation.2 | async-start | bytes 655360 | tf_op jit(solution)/shard_map/all_to_all | solution.py:534
  137.6 0.7 copy-start.5
  138.3 14.2 %copy-start.2 = (f32[8,1024]{1,0:T(8,128)S(1)}, f32[8,1024]{1,0:T(8,128)}, u32[]{:S(2)}) copy-start(f32[8,1024]{1,0:T(8,128)} %maximum_maximum_fusion.1.chan_ref) | copy-start | bytes 98308
  138.3 14.2 %copy-start.4 = (bf16[512,256]{1,0:T(8,128)(2,1)S(1)}, bf16[512,256]{1,0:T(8,128)(2,1)}, u32[]{:S(2)}) copy-start(bf16[512,256]{1,0:T(8,128)(2,1)} %get-tuple-element.68.bc_ref) | copy-start | bytes 786436
  139.0 13.5 %all-to-all-start.4 = ((bf16[32,16,128]{2,1,0:T(8,128)(2,1)}), bf16[32,16,128]{2,1,0:T(8,128)(2,1)S(1)}, u32[]{:S(2)}, u32[]{:S(2)}) async-start(bf16[32,16,128]{2,1,0:T(8,128)(2,1)} %shard_map.132), calls=%async_computation.4 | async-start | bytes 262144 | tf_op jit(solution)/shard_map/all_to_all | solution.py:555
  143.2 0.8 copy-start.1
  143.9 0.9 copy-start.3
  144.9 0.7 copy-start.6
  145.6 1.2 copy-start.7
  146.8 1.0 copy-start.8
  147.9 0.7 copy-start.9
  155.8 17.4 %collective-permute-start.10 = (bf16[256,512]{1,0:T(8,128)(2,1)S(1)}, bf16[256,512]{1,0:T(8,128)(2,1)S(1)}, u32[]{:S(2)}, u32[]{:S(2)}) collective-permute-start(bf16[256,512]{1,0:T(8,128)(2,1)S(1)} %get-tuple-element.77), channel_id=1, source_target_pairs={{0,8},{8,0},{1,9},{9,1},{2,10},{10,2},{3,11},{11,3},{4,12},{12,4},... | collective-permute-start | bytes 786440 | tf_op jit(solution)/shard_map/ppermute | solution.py:580

commit v11 on v10

--- a/solution.py
+++ b/solution.py
@@ -190,7 +190,7 @@
             jax.ShapeDtypeStruct((copies, bc_rows, 2 * rows), jnp.bfloat16),
             jax.ShapeDtypeStruct((dt_rows, 2 * (rows - HALO)), jnp.float32),
         ],
-        compiler_params=pltpu.CompilerParams(vmem_limit_bytes=ALL_VMEM),
+        compiler_params=pltpu.CompilerParams(vmem_limit_bytes=64000000),
         cost_estimate=pl.CostEstimate(flops=10**9, bytes_accessed=10**7, transcendentals=0),
     )(where, own, other, *weights)
 
@@ -220,7 +220,7 @@
             jax.ShapeDtypeStruct((heads, tokens), jnp.float32),
             jax.ShapeDtypeStruct((channels, tokens), jnp.bfloat16),
         ],
-        compiler_params=pltpu.CompilerParams(vmem_limit_bytes=ALL_VMEM),
+        compiler_params=pltpu.CompilerParams(vmem_limit_bytes=64000000),
         cost_estimate=pl.CostEstimate(
             flops=3 * 10**9, bytes_accessed=10**7, transcendentals=0
         ),

time: 176 us -> 177 us (level)
    unnamed x44 -> x42, local copies, waits for them, and re-layouts: 8.4 us -> 7.01 us
  transfers between devices with their start and end apart: 15 -> 15, of which waited for: 12 -> 12; matrix products, arithmetic and copies ran while one was open for 2% -> 3% of each run, Pallas kernels for 10% -> 10%
where the time goes in v11:
time: 177 us; the launch traced here: 176 us
  starting transfers between devices  74.5 us (42%)
  blocking collectives  30.9 us (17%)
  waiting for transfers between devices  29.2 us (16%)
  Pallas kernels  25.8 us (15%)
  local copies, waits for them, and re-layouts  10.4 us (6%)
  other arithmetic  4.6 us (3%)
    ppermute x3, starting transfers between devices, ring(): behind = lax.ppermute(behind, axis, backward)  21.8 us
    all_to_all x1, blocking collectives, per_device(): states = lax.all_to_all(payload, ('z', 'x'), 0, 0)  17 us
    all_to_all x1, blocking collectives, per_device(): lax.all_to_all(jnp.broadcast_to(dots[None, :, None], shape).reshape(2 * t...  14 us
    pallas_call x5, Pallas kernels, call(): pl.pallas_call(kernel, grid_spec=pltpu.PrefetchScalarGridSpec(num_scalar_...  11.1 us
    ppermute x3, waiting for transfers between devices, ring(): ahead = lax.ppermute(ahead, axis, forward)  10.7 us
    ppermute x1, waiting for transfers between devices, ring(): far = lax.ppermute(block[depth:], axis, across)  8.52 us
    ppermute x1, starting transfers between devices, per_device(): other = lax.ppermute(own, 'c', [(0, 1), (1, 0)])  8.17 us
    all_to_all x1, starting transfers between devices, per_device(): lax.all_to_all(copies, ('yh', 'yl'), 0, 0)  7.91 us
  transfers between devices with their start and end apart: 15, of which 12 were waited for; matrix products, arithmetic and copies ran while one was open for 3% of the time, Pallas kernels for 10%

profile of v11, /device:TPU:1, one launch (start us, length us, event | category | flops | bytes accessed | tf_op | source)
XLA Modules:
  0.0 175.8 jit_solution(13453129490681348436)
XLA Ops:
  0.0 0.8 pad_maximum_fusion.1
  0.8 0.1 reshape.53
  0.9 0.9 slice_bitcast_fusion.1
  1.7 0.1 pad.14.clone
  1.8 0.1 maximum_maximum_fusion
  1.9 0.9 broadcast_in_dim.44
  2.8 5.9 %all-to-all-start = ((bf16[8,72,512]{2,1,0:T(8,128)(2,1)}), bf16[8,72,512]{2,1,0:T(8,128)(2,1)S(1)}, u32[]{:S(2)}, u32[]{:S(2)}) async-start(bf16[8,72,512]{2,1,0:T(8,128)(2,1)} %bitcast.7), calls=%async_computation | async-start | bytes 1179648 | tf_op jit(solution)/shard_map/all_to_all | solution.py:505
  8.7 3.4 %collective-permute-start = (bf16[16,512]{1,0:T(8,128)(2,1)S(1)}, bf16[16,512]{1,0:T(8,128)(2,1)S(1)}, u32[]{:S(2)}, u32[]{:S(2)}) collective-permute-start(bf16[16,512]{1,0:T(8,128)(2,1)S(1)} %slice.15), channel_id=1, source_target_pairs={{0,8},{8,16},{16,24},{24,32},{32,40},{40,48},{48,56},{56,64},{64,7... | collective-permute-start | bytes 49160 | tf_op jit(solution)/shard_map/ppermute | solution.py:472
  12.0 0.9 collective-permute-done.earlier_ref
  12.9 1.5 shard_map.127
  14.4 2.1 %all-to-all-done = bf16[8,72,512]{2,1,0:T(8,128)(2,1)S(1)} async-done(((bf16[8,72,512]{2,1,0:T(8,128)(2,1)}), bf16[8,72,512]{2,1,0:T(8,128)(2,1)S(1)}, u32[]{:S(2)}, u32[]{:S(2)}) %all-to-all-start) | async-done | bytes 589856 | tf_op jit(solution)/shard_map/all_to_all | solution.py:505
  16.5 7.9 %all-to-all-start.1 = ((bf16[8,272,512]{2,1,0:T(8,128)(2,1)}), bf16[8,272,512]{2,1,0:T(8,128)(2,1)S(1)}, u32[]{:S(2)}, u32[]{:S(2)}) async-start(bf16[8,272,512]{2,1,0:T(8,128)(2,1)} %shard_map.127), calls=%async_computation.1 | async-start | bytes 4456448 | tf_op jit(solution)/shard_map/all_to_all | solution.py:523
  24.5 0.0 copy-start.17
  24.5 0.8 slice.18
  25.4 0.1 reshape.56
  25.5 0.1 reshape.57
  25.6 1.1 pad_maximum_fusion.w0
  26.7 12.3 %collective-permute-start.2 = (bf16[536,512]{1,0:T(8,128)(2,1)S(1)}, bf16[536,512]{1,0:T(8,128)(2,1)}, u32[]{:S(2)}, u32[]{:S(2)}) collective-permute-start(bf16[536,512]{1,0:T(8,128)(2,1)S(1)} %pad_maximum_fusion.w0), channel_id=1, source_target_pairs={{0,448},{64,0},{128,64},{192,128},{256,192},{320,256},{384,320},{4... | collective-permute-start | bytes 1646600 | tf_op jit(solution)/shard_map/ppermute | solution.py:442
  39.0 1.9 %collective-permute-start.1 = (bf16[536,512]{1,0:T(8,128)(2,1)S(1)}, bf16[536,512]{1,0:T(8,128)(2,1)}, u32[]{:S(2)}, u32[]{:S(2)}) collective-permute-start(bf16[536,512]{1,0:T(8,128)(2,1)S(1)} %pad_maximum_fusion.w0), channel_id=1, source_target_pairs={{0,64},{64,128},{128,192},{192,256},{256,320},{320,384},{384,448},... | collective-permute-start | bytes 1646600 | tf_op jit(solution)/shard_map/ppermute | solution.py:441
  40.9 3.1 %collective-permute-start.3 = (bf16[24,512]{1,0:T(8,128)(2,1)S(1)}, bf16[24,512]{1,0:T(8,128)(2,1)S(1)}, u32[]{:S(2)}, u32[]{:S(2)}) collective-permute-start(bf16[24,512]{1,0:T(8,128)(2,1)S(1)} %reshape.57), channel_id=1, source_target_pairs={{0,256},{64,320},{128,384},{192,448},{256,0},{320,64},{384,128},{4... | collective-permute-start | bytes 73736 | tf_op jit(solution)/shard_map/ppermute | solution.py:444
  44.0 0.1 pad.8.clone
  44.1 8.5 %collective-permute-done.3.w7 = bf16[24,512]{1,0:T(8,128)(2,1)S(1)} collective-permute-done((bf16[24,512]{1,0:T(8,128)(2,1)S(1)}, bf16[24,512]{1,0:T(8,128)(2,1)S(1)}, u32[]{:S(2)}, u32[]{:S(2)}) %collective-permute-start.3) | collective-permute-done | bytes 24608 | tf_op jit(solution)/shard_map/ppermute | solution.py:444
  52.6 1.3 collective-permute-done.1.w1
  54.0 1.9 %collective-permute-start.4 = (bf16[536,512]{1,0:T(8,128)(2,1)}, bf16[536,512]{1,0:T(8,128)(2,1)}, u32[]{:S(2)}, u32[]{:S(2)}) collective-permute-start(bf16[536,512]{1,0:T(8,128)(2,1)} %collective-permute-done.1.w1), channel_id=1, source_target_pairs={{0,64},{64,128},{128,192},{192,256},{256,320},{320,384},{384,448},... | collective-permute-start | bytes 1646600 | tf_op jit(solution)/shard_map/ppermute | solution.py:441
  55.9 4.6 %collective-permute-start.5 = (bf16[536,512]{1,0:T(8,128)(2,1)}, bf16[536,512]{1,0:T(8,128)(2,1)}, u32[]{:S(2)}, u32[]{:S(2)}) collective-permute-start(bf16[536,512]{1,0:T(8,128)(2,1)} %collective-permute-done.2.w2), channel_id=1, source_target_pairs={{0,448},{64,0},{128,64},{192,128},{256,192},{320,256},{384,320},{4... | collective-permute-start | bytes 1646600 | tf_op jit(solution)/shard_map/ppermute | solution.py:442
  60.5 0.1 broadcast_in_dim.45
  60.6 0.1 broadcast_in_dim_reshape.3
  60.6 0.6 pad_add_fusion.where_ref
  61.2 0.1 broadcast_in_dim.49
  61.3 0.1 broadcast_in_dim.50
  61.4 1.4 pad_maximum_fusion.2
  62.8 0.7 maximum_maximum_fusion.1.chan_ref
  63.4 3.7 %collective-permute-done.4.w3 = bf16[536,512]{1,0:T(8,128)(2,1)} collective-permute-done((bf16[536,512]{1,0:T(8,128)(2,1)}, bf16[536,512]{1,0:T(8,128)(2,1)}, u32[]{:S(2)}, u32[]{:S(2)}) %collective-permute-start.4) | collective-permute-done | bytes 548896 | tf_op jit(solution)/shard_map/ppermute | solution.py:441
  67.2 0.9 collective-permute-done.5.w4
  68.1 2.3 %collective-permute-start.6 = (bf16[536,512]{1,0:T(8,128)(2,1)}, bf16[536,512]{1,0:T(8,128)(2,1)S(1)}, u32[]{:S(2)}, u32[]{:S(2)}) collective-permute-start(bf16[536,512]{1,0:T(8,128)(2,1)} %collective-permute-done.4.w3), channel_id=1, source_target_pairs={{0,64},{64,128},{128,192},{192,256},{256,320},{320,384},{384,448},... | collective-permute-start | bytes 1646600 | tf_op jit(solution)/shard_map/ppermute | solution.py:441
  70.4 4.9 %collective-permute-start.7 = (bf16[536,512]{1,0:T(8,128)(2,1)}, bf16[536,512]{1,0:T(8,128)(2,1)}, u32[]{:S(2)}, u32[]{:S(2)}) collective-permute-start(bf16[536,512]{1,0:T(8,128)(2,1)} %collective-permute-done.5.w4), channel_id=1, source_target_pairs={{0,448},{64,0},{128,64},{192,128},{256,192},{320,256},{384,320},{4... | collective-permute-start | bytes 1646600 | tf_op jit(solution)/shard_map/ppermute | solution.py:442
  75.3 5.7 %collective-permute-done.6.w5 = bf16[536,512]{1,0:T(8,128)(2,1)S(1)} collective-permute-done((bf16[536,512]{1,0:T(8,128)(2,1)}, bf16[536,512]{1,0:T(8,128)(2,1)S(1)}, u32[]{:S(2)}, u32[]{:S(2)}) %collective-permute-start.6) | collective-permute-done | bytes 548896 | tf_op jit(solution)/shard_map/ppermute | solution.py:441
  81.0 0.8 copy-done.12
  81.8 0.2 collective-permute-done.7.w6
  82.0 8.2 %collective-permute-start.8 = (bf16[4,2,272,512]{3,2,1,0:T(8,128)(2,1)S(1)}, bf16[4,2,272,512]{3,2,1,0:T(8,128)(2,1)}, u32[]{:S(2)}, u32[]{:S(2)}) collective-permute-start(bf16[4,2,272,512]{3,2,1,0:T(8,128)(2,1)S(1)} %bitcast.32), channel_id=1, source_target_pairs={{0,1},{1,0},{2,3},{3,2},{4,5},{5,4},{6,7},{7,6},{8,9},{9,8},{10,11... | collective-permute-start | bytes 6684680 | tf_op jit(solution)/shard_map/ppermute | solution.py:527
  90.2 3.7 %collective-permute-start.9 = (bf16[536,512]{1,0:T(8,128)(2,1)}, bf16[536,512]{1,0:T(8,128)(2,1)}, u32[]{:S(2)}, u32[]{:S(2)}) collective-permute-start(bf16[536,512]{1,0:T(8,128)(2,1)} %copy-done.12), channel_id=1, source_target_pairs={{0,64},{64,128},{128,192},{192,256},{256,320},{320,384},{384,448},... | collective-permute-start | bytes 1646600 | tf_op jit(solution)/shard_map/ppermute | solution.py:452
  93.9 0.4 collective-permute-done.8.other_ref
  94.3 5.4 %shard_map.128 = (bf16[16,16,544]{2,1,0:T(8,128)(2,1)}, f32[8,512]{1,0:T(8,128)}) custom-call(s32[17]{0:T(128)} %pad_add_fusion.where_ref, bf16[4,2,272,512]{3,2,1,0:T(8,128)(2,1)} %bitcast.33, bf16[4,2,272,512]{3,2,1,0:T(8,128)(2,1)} %collective-permute-done.8.other_ref, bf16[536,512]{1,0:T(8,128)(2,1)} %copy-done.11, ...), custom_call_target="tpu_custom_call" | custom-call | flops 1000000000 | bytes 10000000 | tf_op jit(solution)/shard_map/pallas_call | solution.py:177
  99.7 7.1 %all-to-all-start.2 = ((bf16[16,16,544]{2,1,0:T(8,128)(2,1)}), bf16[16,16,544]{2,1,0:T(8,128)(2,1)}, u32[]{:S(2)}, u32[]{:S(2)}) async-start(bf16[16,16,544]{2,1,0:T(8,128)(2,1)} %get-tuple-element.63), calls=%async_computation.2 | async-start | bytes 655360 | tf_op jit(solution)/shard_map/all_to_all | solution.py:534
  106.7 1.9 %collective-permute-done.9.w7 = bf16[536,512]{1,0:T(8,128)(2,1)} collective-permute-done((bf16[536,512]{1,0:T(8,128)(2,1)}, bf16[536,512]{1,0:T(8,128)(2,1)}, u32[]{:S(2)}, u32[]{:S(2)}) %collective-permute-start.9) | collective-permute-done | bytes 548896 | tf_op jit(solution)/shard_map/ppermute | solution.py:452
  108.6 7.8 %shard_map.129 = (bf16[512,512]{1,0:T(8,128)(2,1)}, f32[8,512]{1,0:T(8,128)}, f32[8,512]{1,0:T(8,128)}, bf16[512,512]{1,0:T(8,128)(2,1)}) custom-call(s32[17]{0:T(128)} %pad_add_fusion.where_ref, f32[8,512]{1,0:T(8,128)} %get-tuple-element.61.dt_ref, f32[4,1024]{1,0:T(4,128)} %conv_ref.2, f32[16,128]{1,0:T(8,128)} %get-tuple-element.62.head_ref, ...), custom_call_target="tpu_custom_call" | custom-call | flops 3000000000 | bytes 10000000 | tf_op jit(solution)/shard_map/pallas_call | solution.py:204
  116.4 1.8 %all-to-all-done.2 = bf16[16,16,544]{2,1,0:T(8,128)(2,1)} async-done(((bf16[16,16,544]{2,1,0:T(8,128)(2,1)}), bf16[16,16,544]{2,1,0:T(8,128)(2,1)}, u32[]{:S(2)}, u32[]{:S(2)}) %all-to-all-start.2) | async-done | bytes 278560 | tf_op jit(solution)/shard_map/all_to_all | solution.py:534
  118.2 3.1 %shard_map.130 = (bf16[512,256]{1,0:T(8,128)(2,1)}, bf16[32,24,128]{2,1,0:T(8,128)(2,1)}, f32[4,512,128]{2,1,0:T(8,128)}) custom-call(s32[1]{0:T(128)} %bitcast.mine_ref.at_ref, bf16[256,544]{1,0:T(8,128)(2,1)} %bitcast.14.bc_ref, f32[4,256]{1,0:T(4,128)} %conv_ref.3, f32[8,512]{1,0:T(8,128)} %get-tuple-element.66.cum_ref, ...), custom_call_target="tpu_custom_call" | custom-call | tf_op jit(solution)/shard_map/pallas_call | solution.py:41
  121.4 17.0 %all_to_all.30.got_ref = bf16[32,24,128]{2,1,0:T(8,128)(2,1)S(1)} all-to-all(bf16[32,24,128]{2,1,0:T(8,128)(2,1)} %get-tuple-element.74), channel_id=1, replica_groups=mesh['z'=8,'x'=4,'yl'=2,'yh'=4,'c'=2] {'z','x'}, dimensions={0} | all-to-all | bytes 393216 | tf_op jit(solution)/shard_map/all_to_all | solution.py:549
  138.3 0.7 copy-done.5
  139.0 0.7 shard_map.132
  139.8 4.2 %all-to-all-start.4 = ((bf16[32,16,128]{2,1,0:T(8,128)(2,1)}), bf16[32,16,128]{2,1,0:T(8,128)(2,1)S(1)}, u32[]{:S(2)}, u32[]{:S(2)}) async-start(bf16[32,16,128]{2,1,0:T(8,128)(2,1)} %shard_map.132), calls=%async_computation.4 | async-start | bytes 262144 | tf_op jit(solution)/shard_map/all_to_all | solution.py:555
  143.9 0.7 copy-done.1
  144.7 0.9 copy-done.3
  145.6 0.7 copy-done.6
  146.4 1.2 copy-done.7
  147.6 1.0 copy-done.8
  148.6 0.7 copy-done.9
  149.3 2.1 %shard_map.131 = (f32[512,512]{1,0:T(8,128)S(1)}, f32[512,512]{1,0:T(8,128)S(1)}) custom-call(s32[1]{0:T(128)} %bitcast.mine_ref.at_ref, bf16[512,512]{1,0:T(8,128)(2,1)S(1)} %copy-done.8, bf16[512,256]{1,0:T(8,128)(2,1)S(1)} %copy-done.3, f32[8,512]{1,0:T(8,128)S(1)} %copy-done.6, f32[8,512]{1,0:T(8,128)S(1)} %copy-done.9, f32[4,512,128]{2,1,0:T(8,128)S(1)} %copy-done.7, ...), custom_call_target="tpu_custom_call" | custom-call | flops 1000000000 | bytes 3145728 | tf_op jit(solution)/shard_map/pallas_call | solution.py:41
  151.5 1.8 %all-to-all-done.4 = bf16[32,16,128]{2,1,0:T(8,128)(2,1)S(1)} async-done(((bf16[32,16,128]{2,1,0:T(8,128)(2,1)}), bf16[32,16,128]{2,1,0:T(8,128)(2,1)S(1)}, u32[]{:S(2)}, u32[]{:S(2)}) %all-to-all-start.4) | async-done | bytes 131104 | tf_op jit(solution)/shard_map/all_to_all | solution.py:555
  153.3 3.3 %shard_map.133 = (f32[256,512]{1,0:T(8,128)S(1)}, bf16[256,512]{1,0:T(8,128)(2,1)S(1)}, f32[2,1,256]{2,1,0:T(1,128)S(1)}) custom-call(s32[1]{0:T(128)} %bitcast.mine_ref.at_ref, f32[512,512]{1,0:T(8,128)S(1)} %get-tuple-element.72.inside_ref, f32[512,512]{1,0:T(8,128)S(1)} %get-tuple-element.73.growth_ref, bf16[512,256]{1,0:T(8,128)(2,1)S(1)} %copy-done.4, ...), custom_call_target="tpu_custom_call" | custom-call | tf_op jit(solution)/shard_map/pallas_call | solution.py:41
  156.6 3.3 %collective-permute-start.10 = (bf16[256,512]{1,0:T(8,128)(2,1)S(1)}, bf16[256,512]{1,0:T(8,128)(2,1)S(1)}, u32[]{:S(2)}, u32[]{:S(2)}) collective-permute-start(bf16[256,512]{1,0:T(8,128)(2,1)S(1)} %get-tuple-element.77), channel_id=1, source_target_pairs={{0,8},{8,0},{1,9},{9,1},{2,10},{10,2},{3,11},{11,3},{4,12},{12,4},... | collective-permute-start | bytes 786440 | tf_op jit(solution)/shard_map/ppermute | solution.py:580
  160.0 14.0 %all_to_all.31 = f32[16,1,256]{2,1,0:T(1,128)S(1)} all-to-all(f32[16,1,256]{2,1,0:T(1,128)S(1)} %broadcast_in_dim.53), channel_id=1, replica_groups=mesh['z'=8,'x'=4,'yl'=2,'yh'=4,'c'=2] {'yh','yl','c'}, dimensions={0} | all-to-all | bytes 32768 | tf_op jit(solution)/shard_map/all_to_all | solution.py:576
  174.0 1.8 %shard_map.134 = bf16[256,1024]{1,0:T(8,128)(2,1)} custom-call(s32[1]{0:T(128)} %bitcast.mine_ref.at_ref, f32[256,512]{1,0:T(8,128)S(1)} %get-tuple-element.76.keep_ref, bf16[256,512]{1,0:T(8,128)(2,1)S(1)} %collective-permute-done.10.other_ref, f32[16,256]{1,0:T(8,128)S(1)} %bitcast.31, f32[8,1024]{1,0:T(8,128)S(1)} %copy-done.2), custom_call_target="tpu_custom_call" | custom-call | tf_op jit(solution)/shard_map/pallas_call | solution.py:41
  (46 shorter events, 0.2 us)
Async XLA Ops:
  0.0 8.7 %copy-start = (bf16[256,512]{1,0:T(8,128)(2,1)S(1)}, bf16[256,512]{1,0:T(8,128)(2,1)}, u32[]{:S(2)}) copy-start(bf16[256,512]{1,0:T(8,128)(2,1)} %tokens_ref.1) | copy-start | bytes 786436
  2.8 13.8 %all-to-all-start = ((bf16[8,72,512]{2,1,0:T(8,128)(2,1)}), bf16[8,72,512]{2,1,0:T(8,128)(2,1)S(1)}, u32[]{:S(2)}, u32[]{:S(2)}) async-start(bf16[8,72,512]{2,1,0:T(8,128)(2,1)} %bitcast.7), calls=%async_computation | async-start | bytes 1179648 | tf_op jit(solution)/shard_map/all_to_all | solution.py:505
  8.7 4.2 %collective-permute-start = (bf16[16,512]{1,0:T(8,128)(2,1)S(1)}, bf16[16,512]{1,0:T(8,128)(2,1)S(1)}, u32[]{:S(2)}, u32[]{:S(2)}) collective-permute-start(bf16[16,512]{1,0:T(8,128)(2,1)S(1)} %slice.15), channel_id=1, source_target_pairs={{0,8},{8,16},{16,24},{24,32},{32,40},{40,48},{48,56},{56,64},{64,7... | collective-permute-start | bytes 49160 | tf_op jit(solution)/shard_map/ppermute | solution.py:472
  16.5 65.5 %all-to-all-start.1 = ((bf16[8,272,512]{2,1,0:T(8,128)(2,1)}), bf16[8,272,512]{2,1,0:T(8,128)(2,1)S(1)}, u32[]{:S(2)}, u32[]{:S(2)}) async-start(bf16[8,272,512]{2,1,0:T(8,128)(2,1)} %shard_map.127), calls=%async_computation.1 | async-start | bytes 4456448 | tf_op jit(solution)/shard_map/all_to_all | solution.py:523
  24.5 28.2 %copy-start.19 = (s32[8]{0:T(128)S(1)}, s32[8]{0:T(128)}, u32[]{:S(2)}) copy-start(s32[8]{0:T(128)} %constant.70.clone) | copy-start | bytes 100
  24.5 36.0 %copy-start.16 = (f32[16]{0:T(128)S(1)}, f32[16]{0:T(128)}, u32[]{:S(2)}) copy-start(f32[16]{0:T(128)} %param.21) | copy-start | bytes 196
  24.5 36.8 %copy-start.17 = (f32[16]{0:T(128)S(1)}, f32[16]{0:T(128)}, u32[]{:S(2)}) copy-start(f32[16]{0:T(128)} %param.19) | copy-start | bytes 196
  24.5 36.8 %copy-start.18 = (f32[16]{0:T(128)S(1)}, f32[16]{0:T(128)}, u32[]{:S(2)}) copy-start(f32[16]{0:T(128)} %param.20) | copy-start | bytes 196
  24.5 38.3 %copy-start.14 = (f32[1024]{0:T(1024)S(1)}, f32[1024]{0:T(1024)}, u32[]{:S(2)}) copy-start(f32[1024]{0:T(1024)} %param.24) | copy-start | bytes 12292
  24.5 38.2 %copy-start.15 = (f32[1024]{0:T(1024)S(1)}, f32[1024]{0:T(1024)}, u32[]{:S(2)}) copy-start(f32[1024]{0:T(1024)} %param.22) | copy-start | bytes 12292
  26.7 67.6 %copy-start.11 = (bf16[536,512]{1,0:T(8,128)(2,1)}, bf16[536,512]{1,0:T(8,128)(2,1)S(1)}, u32[]{:S(2)}) copy-start(bf16[536,512]{1,0:T(8,128)(2,1)S(1)} %pad_maximum_fusion.w0) | copy-start | bytes 1646596
  26.7 25.9 %collective-permute-start.2 = (bf16[536,512]{1,0:T(8,128)(2,1)S(1)}, bf16[536,512]{1,0:T(8,128)(2,1)}, u32[]{:S(2)}, u32[]{:S(2)}) collective-permute-start(bf16[536,512]{1,0:T(8,128)(2,1)S(1)} %pad_maximum_fusion.w0), channel_id=1, source_target_pairs={{0,448},{64,0},{128,64},{192,128},{256,192},{320,256},{384,320},{4... | collective-permute-start | bytes 1646600 | tf_op jit(solution)/shard_map/ppermute | solution.py:442
  39.0 15.0 %collective-permute-start.1 = (bf16[536,512]{1,0:T(8,128)(2,1)S(1)}, bf16[536,512]{1,0:T(8,128)(2,1)}, u32[]{:S(2)}, u32[]{:S(2)}) collective-permute-start(bf16[536,512]{1,0:T(8,128)(2,1)S(1)} %pad_maximum_fusion.w0), channel_id=1, source_target_pairs={{0,64},{64,128},{128,192},{192,256},{256,320},{320,384},{384,448},... | collective-permute-start | bytes 1646600 | tf_op jit(solution)/shard_map/ppermute | solution.py:441
  40.9 11.7 %collective-permute-start.3 = (bf16[24,512]{1,0:T(8,128)(2,1)S(1)}, bf16[24,512]{1,0:T(8,128)(2,1)S(1)}, u32[]{:S(2)}, u32[]{:S(2)}) collective-permute-start(bf16[24,512]{1,0:T(8,128)(2,1)S(1)} %reshape.57), channel_id=1, source_target_pairs={{0,256},{64,320},{128,384},{192,448},{256,0},{320,64},{384,128},{4... | collective-permute-start | bytes 73736 | tf_op jit(solution)/shard_map/ppermute | solution.py:444
  52.6 41.7 %copy-start.13 = (bf16[24,512]{1,0:T(8,128)(2,1)}, bf16[24,512]{1,0:T(8,128)(2,1)S(1)}, u32[]{:S(2)}) copy-start(bf16[24,512]{1,0:T(8,128)(2,1)S(1)} %collective-permute-done.3.w7) | copy-start | bytes 73732
  54.0 13.2 %collective-permute-start.4 = (bf16[536,512]{1,0:T(8,128)(2,1)}, bf16[536,512]{1,0:T(8,128)(2,1)}, u32[]{:S(2)}, u32[]{:S(2)}) collective-permute-start(bf16[536,512]{1,0:T(8,128)(2,1)} %collective-permute-done.1.w1), channel_id=1, source_target_pairs={{0,64},{64,128},{128,192},{192,256},{256,320},{320,384},{384,448},... | collective-permute-start | bytes 1646600 | tf_op jit(solution)/shard_map/ppermute | solution.py:441
  55.9 12.2 %collective-permute-start.5 = (bf16[536,512]{1,0:T(8,128)(2,1)}, bf16[536,512]{1,0:T(8,128)(2,1)}, u32[]{:S(2)}, u32[]{:S(2)}) collective-permute-start(bf16[536,512]{1,0:T(8,128)(2,1)} %collective-permute-done.2.w2), channel_id=1, source_target_pairs={{0,448},{64,0},{128,64},{192,128},{256,192},{320,256},{384,320},{4... | collective-permute-start | bytes 1646600 | tf_op jit(solution)/shard_map/ppermute | solution.py:442
  68.1 12.9 %collective-permute-start.6 = (bf16[536,512]{1,0:T(8,128)(2,1)}, bf16[536,512]{1,0:T(8,128)(2,1)S(1)}, u32[]{:S(2)}, u32[]{:S(2)}) collective-permute-start(bf16[536,512]{1,0:T(8,128)(2,1)} %collective-permute-done.4.w3), channel_id=1, source_target_pairs={{0,64},{64,128},{128,192},{192,256},{256,320},{320,384},{384,448},... | collective-permute-start | bytes 1646600 | tf_op jit(solution)/shard_map/ppermute | solution.py:441
  70.4 11.6 %collective-permute-start.7 = (bf16[536,512]{1,0:T(8,128)(2,1)}, bf16[536,512]{1,0:T(8,128)(2,1)}, u32[]{:S(2)}, u32[]{:S(2)}) collective-permute-start(bf16[536,512]{1,0:T(8,128)(2,1)} %collective-permute-done.5.w4), channel_id=1, source_target_pairs={{0,448},{64,0},{128,64},{192,128},{256,192},{320,256},{384,320},{4... | collective-permute-start | bytes 1646600 | tf_op jit(solution)/shard_map/ppermute | solution.py:442
  81.0 0.9 copy-start.12
  82.0 12.3 %copy-start.10 = (bf16[8,272,512]{2,1,0:T(8,128)(2,1)}, bf16[8,272,512]{2,1,0:T(8,128)(2,1)S(1)}, u32[]{:S(2)}) copy-start(bf16[8,272,512]{2,1,0:T(8,128)(2,1)S(1)} %all-to-all-done.1) | copy-start | bytes 6684676
  82.0 12.3 %collective-permute-start.8 = (bf16[4,2,272,512]{3,2,1,0:T(8,128)(2,1)S(1)}, bf16[4,2,272,512]{3,2,1,0:T(8,128)(2,1)}, u32[]{:S(2)}, u32[]{:S(2)}) collective-permute-start(bf16[4,2,272,512]{3,2,1,0:T(8,128)(2,1)S(1)} %bitcast.32), channel_id=1, source_target_pairs={{0,1},{1,0},{2,3},{3,2},{4,5},{5,4},{6,7},{7,6},{8,9},{9,8},{10,11... | collective-permute-start | bytes 6684680 | tf_op jit(solution)/shard_map/ppermute | solution.py:527
  90.2 18.4 %collective-permute-start.9 = (bf16[536,512]{1,0:T(8,128)(2,1)}, bf16[536,512]{1,0:T(8,128)(2,1)}, u32[]{:S(2)}, u32[]{:S(2)}) collective-permute-start(bf16[536,512]{1,0:T(8,128)(2,1)} %copy-done.12), channel_id=1, source_target_pairs={{0,64},{64,128},{128,192},{192,256},{256,320},{320,384},{384,448},... | collective-permute-start | bytes 1646600 | tf_op jit(solution)/shard_map/ppermute | solution.py:452
  99.7 18.6 %all-to-all-start.2 = ((bf16[16,16,544]{2,1,0:T(8,128)(2,1)}), bf16[16,16,544]{2,1,0:T(8,128)(2,1)}, u32[]{:S(2)}, u32[]{:S(2)}) async-start(bf16[16,16,544]{2,1,0:T(8,128)(2,1)} %get-tuple-element.63), calls=%async_computation.2 | async-start | bytes 655360 | tf_op jit(solution)/shard_map/all_to_all | solution.py:534
  138.3 0.7 copy-start.5
  139.0 14.3 %copy-start.2 = (f32[8,1024]{1,0:T(8,128)S(1)}, f32[8,1024]{1,0:T(8,128)}, u32[]{:S(2)}) copy-start(f32[8,1024]{1,0:T(8,128)} %maximum_maximum_fusion.1.chan_ref) | copy-start | bytes 98308
  139.0 14.3 %copy-start.4 = (bf16[512,256]{1,0:T(8,128)(2,1)S(1)}, bf16[512,256]{1,0:T(8,128)(2,1)}, u32[]{:S(2)}) copy-start(bf16[512,256]{1,0:T(8,128)(2,1)} %get-tuple-element.68.bc_ref) | copy-start | bytes 786436
  139.8 13.5 %all-to-all-start.4 = ((bf16[32,16,128]{2,1,0:T(8,128)(2,1)}), bf16[32,16,128]{2,1,0:T(8,128)(2,1)S(1)}, u32[]{:S(2)}, u32[]{:S(2)}) async-start(bf16[32,16,128]{2,1,0:T(8,128)(2,1)} %shard_map.132), calls=%async_computation.4 | async-start | bytes 262144 | tf_op jit(solution)/shard_map/all_to_all | solution.py:555
  143.9 0.8 copy-start.1
  144.7 0.9 copy-start.3
  145.6 0.7 copy-start.6
  146.4 1.2 copy-start.7
  147.6 1.0 copy-start.8
  148.6 0.7 copy-start.9
  156.6 17.4 %collective-permute-start.10 = (bf16[256,512]{1,0:T(8,128)(2,1)S(1)}, bf16[256,512]{1,0:T(8,128)(2,1)S(1)}, u32[]{:S(2)}, u32[]{:S(2)}) collective-permute-start(bf16[256,512]{1,0:T(8,128)(2,1)S(1)} %get-tuple-element.77), channel_id=1, source_target_pairs={{0,8},{8,0},{1,9},{9,1},{2,10},{10,2},{3,11},{11,3},{4,12},{12,4},... | collective-permute-start | bytes 786440 | tf_op jit(solution)/shard_map/ppermute | solution.py:580

commit v12 on v10

--- a/solution.py
+++ b/solution.py
@@ -446,8 +446,6 @@
             ahead, behind, far = lax.optimization_barrier((ahead, behind, far))
         elif hop == 2:
             ahead, behind, ready = lax.optimization_barrier((ahead, behind, ready))
-        else:
-            ahead, behind = lax.optimization_barrier((ahead, behind))
         pieces += [ahead, behind]
     pieces.append(lax.ppermute(ahead, axis, forward))
     return pieces, far, ready

time: 176 us -> 187 us (1.062)
  waiting for transfers between devices: 28.9 us -> 43.7 us
  starting transfers between devices: 74.7 us -> 72.1 us
    ppermute x3, waiting for transfers between devices: 0.73 us -> 10.8 us  [ring(): behind = lax.ppermute(behind, axis, backward)]
    ppermute x3, waiting for transfers between devices: 10.8 us -> 15.8 us  [ring(): ahead = lax.ppermute(ahead, axis, forward)]
    all_to_all x1, starting transfers between devices: 7.12 us -> 4.91 us  [per_device(): bc_all = lax.all_to_all(bc_pre, ('yh', 'c', 'yl'), 0, 0).reshape(2 * N, -1)]
    all_to_all x1, waiting for transfers between devices: 1.67 us -> 3.81 us  [per_device(): bc_all = lax.all_to_all(bc_pre, ('yh', 'c', 'yl'), 0, 0).reshape(2 * N, -1)]
    ppermute x1, waiting for transfers between devices: 2.06 us -> 0.01 us  [ring(): pieces.append(lax.ppermute(ahead, axis, forward))]
    unnamed x44 -> x42, local copies, waits for them, and re-layouts: 8.4 us -> 7.54 us
  transfers between devices with their start and end apart: 15 -> 15, of which waited for: 12 -> 10; matrix products, arithmetic and copies ran while one was open for 2% -> 2% of each run, Pallas kernels for 10% -> 9%
where the time goes in v12:
time: 187 us; the launch traced here: 186 us
  starting transfers between devices  72.1 us (39%)
  waiting for transfers between devices  43.7 us (23%)
  blocking collectives  30.2 us (16%)
  Pallas kernels  25.7 us (14%)
  local copies, waits for them, and re-layouts  10.1 us (5%)
  other arithmetic  3.56 us (2%)
    ppermute x3, starting transfers between devices, ring(): behind = lax.ppermute(behind, axis, backward)  23.5 us
    all_to_all x1, blocking collectives, per_device(): states = lax.all_to_all(payload, ('z', 'x'), 0, 0)  16.3 us
    ppermute x3, waiting for transfers between devices, ring(): ahead = lax.ppermute(ahead, axis, forward)  15.8 us
    all_to_all x1, blocking collectives, per_device(): lax.all_to_all(jnp.broadcast_to(dots[None, :, None], shape).reshape(2 * t...  14 us
    pallas_call x5, Pallas kernels, call(): pl.pallas_call(kernel, grid_spec=pltpu.PrefetchScalarGridSpec(num_scalar_...  11.1 us
    ppermute x3, waiting for transfers between devices, ring(): behind = lax.ppermute(behind, axis, backward)  10.8 us
    ppermute x1, waiting for transfers between devices, ring(): far = lax.ppermute(block[depth:], axis, across)  8.52 us
    all_to_all x1, starting transfers between devices, per_device(): lax.all_to_all(copies, ('yh', 'yl'), 0, 0)  7.91 us
  transfers between devices with their start and end apart: 15, of which 10 were waited for; matrix products, arithmetic and copies ran while one was open for 2% of the time, Pallas kernels for 9%

profile of v12, /device:TPU:1, one launch (start us, length us, event | category | flops | bytes accessed | tf_op | source)
XLA Modules:
  0.0 185.8 jit_solution(17782155693289091164)
XLA Ops:
  0.0 0.8 pad_maximum_fusion.1
  0.8 0.1 reshape.53
  0.9 0.9 slice_bitcast_fusion.1
  1.7 0.1 pad.14.clone
  1.8 0.1 maximum_maximum_fusion
  1.9 0.9 broadcast_in_dim.44
  2.8 5.9 %all-to-all-start = ((bf16[8,72,512]{2,1,0:T(8,128)(2,1)}), bf16[8,72,512]{2,1,0:T(8,128)(2,1)S(1)}, u32[]{:S(2)}, u32[]{:S(2)}) async-start(bf16[8,72,512]{2,1,0:T(8,128)(2,1)} %bitcast.7), calls=%async_computation | async-start | bytes 1179648 | tf_op jit(solution)/shard_map/all_to_all | solution.py:503
  8.7 3.4 %collective-permute-start = (bf16[16,512]{1,0:T(8,128)(2,1)S(1)}, bf16[16,512]{1,0:T(8,128)(2,1)S(1)}, u32[]{:S(2)}, u32[]{:S(2)}) collective-permute-start(bf16[16,512]{1,0:T(8,128)(2,1)S(1)} %slice.15), channel_id=1, source_target_pairs={{0,8},{8,16},{16,24},{24,32},{32,40},{40,48},{48,56},{56,64},{64,7... | collective-permute-start | bytes 49160 | tf_op jit(solution)/shard_map/ppermute | solution.py:470
  12.0 0.9 collective-permute-done.earlier_ref
  12.9 1.5 shard_map.127
  14.4 2.1 %all-to-all-done = bf16[8,72,512]{2,1,0:T(8,128)(2,1)S(1)} async-done(((bf16[8,72,512]{2,1,0:T(8,128)(2,1)}), bf16[8,72,512]{2,1,0:T(8,128)(2,1)S(1)}, u32[]{:S(2)}, u32[]{:S(2)}) %all-to-all-start) | async-done | bytes 589856 | tf_op jit(solution)/shard_map/all_to_all | solution.py:503
  16.5 7.9 %all-to-all-start.1 = ((bf16[8,272,512]{2,1,0:T(8,128)(2,1)}), bf16[8,272,512]{2,1,0:T(8,128)(2,1)S(1)}, u32[]{:S(2)}, u32[]{:S(2)}) async-start(bf16[8,272,512]{2,1,0:T(8,128)(2,1)} %shard_map.127), calls=%async_computation.1 | async-start | bytes 4456448 | tf_op jit(solution)/shard_map/all_to_all | solution.py:521
  24.5 0.0 copy-start.16
  24.5 0.0 copy-start.17
  24.5 0.0 copy-start.18
  24.5 0.0 copy-start.14
  24.5 0.0 copy-start.15
  24.6 0.1 reshape.56
  24.7 0.1 reshape.57
  24.9 12.3 %collective-permute-start.2 = (bf16[536,512]{1,0:T(8,128)(2,1)S(1)}, bf16[536,512]{1,0:T(8,128)(2,1)S(1)}, u32[]{:S(2)}, u32[]{:S(2)}) collective-permute-start(bf16[536,512]{1,0:T(8,128)(2,1)S(1)} %pad_maximum_fusion.w0), channel_id=1, source_target_pairs={{0,448},{64,0},{128,64},{192,128},{256,192},{320,256},{384,320},{4... | collective-permute-start | bytes 1646600 | tf_op jit(solution)/shard_map/ppermute | solution.py:442
  37.2 1.9 %collective-permute-start.1 = (bf16[536,512]{1,0:T(8,128)(2,1)S(1)}, bf16[536,512]{1,0:T(8,128)(2,1)}, u32[]{:S(2)}, u32[]{:S(2)}) collective-permute-start(bf16[536,512]{1,0:T(8,128)(2,1)S(1)} %pad_maximum_fusion.w0), channel_id=1, source_target_pairs={{0,64},{64,128},{128,192},{192,256},{256,320},{320,384},{384,448},... | collective-permute-start | bytes 1646600 | tf_op jit(solution)/shard_map/ppermute | solution.py:441
  39.1 3.1 %collective-permute-start.3 = (bf16[24,512]{1,0:T(8,128)(2,1)S(1)}, bf16[24,512]{1,0:T(8,128)(2,1)S(1)}, u32[]{:S(2)}, u32[]{:S(2)}) collective-permute-start(bf16[24,512]{1,0:T(8,128)(2,1)S(1)} %reshape.57), channel_id=1, source_target_pairs={{0,256},{64,320},{128,384},{192,448},{256,0},{320,64},{384,128},{4... | collective-permute-start | bytes 73736 | tf_op jit(solution)/shard_map/ppermute | solution.py:444
  42.2 0.1 pad.8.clone
  42.3 8.5 %collective-permute-done.3.w7 = bf16[24,512]{1,0:T(8,128)(2,1)S(1)} collective-permute-done((bf16[24,512]{1,0:T(8,128)(2,1)S(1)}, bf16[24,512]{1,0:T(8,128)(2,1)S(1)}, u32[]{:S(2)}, u32[]{:S(2)}) %collective-permute-start.3) | collective-permute-done | bytes 24608 | tf_op jit(solution)/shard_map/ppermute | solution.py:444
  50.8 1.3 collective-permute-done.1.w1
  52.1 1.9 %collective-permute-start.4 = (bf16[536,512]{1,0:T(8,128)(2,1)}, bf16[536,512]{1,0:T(8,128)(2,1)}, u32[]{:S(2)}, u32[]{:S(2)}) collective-permute-start(bf16[536,512]{1,0:T(8,128)(2,1)} %collective-permute-done.1.w1), channel_id=1, source_target_pairs={{0,64},{64,128},{128,192},{192,256},{256,320},{320,384},{384,448},... | collective-permute-start | bytes 1646600 | tf_op jit(solution)/shard_map/ppermute | solution.py:441
  54.1 4.6 %collective-permute-start.5 = (bf16[536,512]{1,0:T(8,128)(2,1)S(1)}, bf16[536,512]{1,0:T(8,128)(2,1)}, u32[]{:S(2)}, u32[]{:S(2)}) collective-permute-start(bf16[536,512]{1,0:T(8,128)(2,1)S(1)} %collective-permute-done.2.w2), channel_id=1, source_target_pairs={{0,448},{64,0},{128,64},{192,128},{256,192},{320,256},{384,320},{4... | collective-permute-start | bytes 1646600 | tf_op jit(solution)/shard_map/ppermute | solution.py:442
  58.7 0.1 broadcast_in_dim.45
  58.7 0.1 broadcast_in_dim_reshape.3
  58.8 0.6 pad_add_fusion.where_ref
  59.4 0.1 broadcast_in_dim.49
  59.5 0.1 broadcast_in_dim.50
  59.5 1.4 pad_maximum_fusion.2
  60.9 0.7 maximum_maximum_fusion.1.chan_ref
  61.6 3.7 %collective-permute-done.4.w3 = bf16[536,512]{1,0:T(8,128)(2,1)} collective-permute-done((bf16[536,512]{1,0:T(8,128)(2,1)}, bf16[536,512]{1,0:T(8,128)(2,1)}, u32[]{:S(2)}, u32[]{:S(2)}) %collective-permute-start.4) | collective-permute-done | bytes 548896 | tf_op jit(solution)/shard_map/ppermute | solution.py:441
  65.3 0.6 collective-permute-done.5.w4
  65.9 2.4 %collective-permute-start.6 = (bf16[536,512]{1,0:T(8,128)(2,1)}, bf16[536,512]{1,0:T(8,128)(2,1)}, u32[]{:S(2)}, u32[]{:S(2)}) collective-permute-start(bf16[536,512]{1,0:T(8,128)(2,1)} %collective-permute-done.4.w3), channel_id=1, source_target_pairs={{0,64},{64,128},{128,192},{192,256},{256,320},{320,384},{384,448},... | collective-permute-start | bytes 1646600 | tf_op jit(solution)/shard_map/ppermute | solution.py:441
  68.4 10.7 %collective-permute-done.6.w5 = bf16[536,512]{1,0:T(8,128)(2,1)} collective-permute-done((bf16[536,512]{1,0:T(8,128)(2,1)}, bf16[536,512]{1,0:T(8,128)(2,1)}, u32[]{:S(2)}, u32[]{:S(2)}) %collective-permute-start.6) | collective-permute-done | bytes 548896 | tf_op jit(solution)/shard_map/ppermute | solution.py:441
  79.1 1.4 copy-done.10
  80.5 7.9 %collective-permute-start.7 = (bf16[4,2,272,512]{3,2,1,0:T(8,128)(2,1)S(1)}, bf16[4,2,272,512]{3,2,1,0:T(8,128)(2,1)}, u32[]{:S(2)}, u32[]{:S(2)}) collective-permute-start(bf16[4,2,272,512]{3,2,1,0:T(8,128)(2,1)S(1)} %bitcast.32), channel_id=1, source_target_pairs={{0,1},{1,0},{2,3},{3,2},{4,5},{5,4},{6,7},{7,6},{8,9},{9,8},{10,11... | collective-permute-start | bytes 6684680 | tf_op jit(solution)/shard_map/ppermute | solution.py:525
  88.4 6.6 %collective-permute-start.8 = (bf16[536,512]{1,0:T(8,128)(2,1)}, bf16[536,512]{1,0:T(8,128)(2,1)}, u32[]{:S(2)}, u32[]{:S(2)}) collective-permute-start(bf16[536,512]{1,0:T(8,128)(2,1)} %collective-permute-done.5.w4), channel_id=1, source_target_pairs={{0,448},{64,0},{128,64},{192,128},{256,192},{320,256},{384,320},{4... | collective-permute-start | bytes 1646600 | tf_op jit(solution)/shard_map/ppermute | solution.py:442
  95.0 1.9 %collective-permute-start.9 = (bf16[536,512]{1,0:T(8,128)(2,1)}, bf16[536,512]{1,0:T(8,128)(2,1)}, u32[]{:S(2)}, u32[]{:S(2)}) collective-permute-start(bf16[536,512]{1,0:T(8,128)(2,1)} %collective-permute-done.6.w5), channel_id=1, source_target_pairs={{0,64},{64,128},{128,192},{192,256},{256,320},{320,384},{384,448},... | collective-permute-start | bytes 1646600 | tf_op jit(solution)/shard_map/ppermute | solution.py:450
  96.9 10.2 %collective-permute-done.8.w6 = bf16[536,512]{1,0:T(8,128)(2,1)} collective-permute-done((bf16[536,512]{1,0:T(8,128)(2,1)}, bf16[536,512]{1,0:T(8,128)(2,1)}, u32[]{:S(2)}, u32[]{:S(2)}) %collective-permute-start.8) | collective-permute-done | bytes 548896 | tf_op jit(solution)/shard_map/ppermute | solution.py:442
  107.2 5.3 %shard_map.128 = (bf16[16,16,544]{2,1,0:T(8,128)(2,1)}, f32[8,512]{1,0:T(8,128)}) custom-call(s32[17]{0:T(128)} %pad_add_fusion.where_ref, bf16[4,2,272,512]{3,2,1,0:T(8,128)(2,1)} %bitcast.33, bf16[4,2,272,512]{3,2,1,0:T(8,128)(2,1)} %collective-permute-done.7.other_ref, bf16[536,512]{1,0:T(8,128)(2,1)} %copy-done.11, ...), custom_call_target="tpu_custom_call" | custom-call | flops 1000000000 | bytes 10000000 | tf_op jit(solution)/shard_map/pallas_call | solution.py:177
  112.5 4.9 %all-to-all-start.2 = ((bf16[16,16,544]{2,1,0:T(8,128)(2,1)}), bf16[16,16,544]{2,1,0:T(8,128)(2,1)}, u32[]{:S(2)}, u32[]{:S(2)}) async-start(bf16[16,16,544]{2,1,0:T(8,128)(2,1)} %get-tuple-element.59), calls=%async_computation.2 | async-start | bytes 655360 | tf_op jit(solution)/shard_map/all_to_all | solution.py:532
  117.4 7.8 %shard_map.129 = (bf16[512,512]{1,0:T(8,128)(2,1)}, f32[8,512]{1,0:T(8,128)}, f32[8,512]{1,0:T(8,128)}, bf16[512,512]{1,0:T(8,128)(2,1)}) custom-call(s32[17]{0:T(128)} %pad_add_fusion.where_ref, f32[8,512]{1,0:T(8,128)} %get-tuple-element.57.dt_ref, f32[4,1024]{1,0:T(4,128)} %conv_ref.2, f32[16,128]{1,0:T(8,128)} %get-tuple-element.58.head_ref, ...), custom_call_target="tpu_custom_call" | custom-call | flops 3000000000 | bytes 10000000 | tf_op jit(solution)/shard_map/pallas_call | solution.py:204
  125.2 3.8 %all-to-all-done.2 = bf16[16,16,544]{2,1,0:T(8,128)(2,1)} async-done(((bf16[16,16,544]{2,1,0:T(8,128)(2,1)}), bf16[16,16,544]{2,1,0:T(8,128)(2,1)}, u32[]{:S(2)}, u32[]{:S(2)}) %all-to-all-start.2) | async-done | bytes 278560 | tf_op jit(solution)/shard_map/all_to_all | solution.py:532
  129.0 3.1 %shard_map.130 = (bf16[512,256]{1,0:T(8,128)(2,1)}, bf16[32,24,128]{2,1,0:T(8,128)(2,1)}, f32[4,512,128]{2,1,0:T(8,128)}) custom-call(s32[1]{0:T(128)} %bitcast.mine_ref.at_ref, bf16[256,544]{1,0:T(8,128)(2,1)} %bitcast.14.bc_ref, f32[4,256]{1,0:T(4,128)} %conv_ref.3, f32[8,512]{1,0:T(8,128)} %get-tuple-element.62.cum_ref, ...), custom_call_target="tpu_custom_call" | custom-call | tf_op jit(solution)/shard_map/pallas_call | solution.py:41
  132.1 16.3 %all_to_all.30.got_ref = bf16[32,24,128]{2,1,0:T(8,128)(2,1)S(1)} all-to-all(bf16[32,24,128]{2,1,0:T(8,128)(2,1)} %get-tuple-element.70), channel_id=1, replica_groups=mesh['z'=8,'x'=4,'yl'=2,'yh'=4,'c'=2] {'z','x'}, dimensions={0} | all-to-all | bytes 393216 | tf_op jit(solution)/shard_map/all_to_all | solution.py:547
  148.4 0.7 copy-done.5
  149.1 0.7 shard_map.132
  149.8 4.2 %all-to-all-start.4 = ((bf16[32,16,128]{2,1,0:T(8,128)(2,1)}), bf16[32,16,128]{2,1,0:T(8,128)(2,1)S(1)}, u32[]{:S(2)}, u32[]{:S(2)}) async-start(bf16[32,16,128]{2,1,0:T(8,128)(2,1)} %shard_map.132), calls=%async_computation.4 | async-start | bytes 262144 | tf_op jit(solution)/shard_map/all_to_all | solution.py:553
  154.0 0.7 copy-done.1
  154.8 0.9 copy-done.3
  155.7 0.7 copy-done.6
  156.4 1.2 copy-done.7
  157.6 1.0 copy-done.8
  158.7 0.7 copy-done.9
  159.4 2.1 %shard_map.131 = (f32[512,512]{1,0:T(8,128)S(1)}, f32[512,512]{1,0:T(8,128)S(1)}) custom-call(s32[1]{0:T(128)} %bitcast.mine_ref.at_ref, bf16[512,512]{1,0:T(8,128)(2,1)S(1)} %copy-done.8, bf16[512,256]{1,0:T(8,128)(2,1)S(1)} %copy-done.3, f32[8,512]{1,0:T(8,128)S(1)} %copy-done.6, f32[8,512]{1,0:T(8,128)S(1)} %copy-done.9, f32[4,512,128]{2,1,0:T(8,128)S(1)} %copy-done.7, ...), custom_call_target="tpu_custom_call" | custom-call | flops 1000000000 | bytes 3145728 | tf_op jit(solution)/shard_map/pallas_call | solution.py:41
  161.5 1.8 all-to-all-done.4
  163.3 3.3 %shard_map.133 = (f32[256,512]{1,0:T(8,128)S(1)}, bf16[256,512]{1,0:T(8,128)(2,1)S(1)}, f32[2,1,256]{2,1,0:T(1,128)S(1)}) custom-call(s32[1]{0:T(128)} %bitcast.mine_ref.at_ref, f32[512,512]{1,0:T(8,128)S(1)} %get-tuple-element.68.inside_ref, f32[512,512]{1,0:T(8,128)S(1)} %get-tuple-element.69.growth_ref, bf16[512,256]{1,0:T(8,128)(2,1)S(1)} %copy-done.4, ...), custom_call_target="tpu_custom_call" | custom-call | tf_op jit(solution)/shard_map/pallas_call | solution.py:41
  166.6 3.3 %collective-permute-start.10 = (bf16[256,512]{1,0:T(8,128)(2,1)S(1)}, bf16[256,512]{1,0:T(8,128)(2,1)S(1)}, u32[]{:S(2)}, u32[]{:S(2)}) collective-permute-start(bf16[256,512]{1,0:T(8,128)(2,1)S(1)} %get-tuple-element.73), channel_id=1, source_target_pairs={{0,8},{8,0},{1,9},{9,1},{2,10},{10,2},{3,11},{11,3},{4,12},{12,4},... | collective-permute-start | bytes 786440 | tf_op jit(solution)/shard_map/ppermute | solution.py:578
  170.0 14.0 %all_to_all.31 = f32[16,1,256]{2,1,0:T(1,128)S(1)} all-to-all(f32[16,1,256]{2,1,0:T(1,128)S(1)} %broadcast_in_dim.53), channel_id=1, replica_groups=mesh['z'=8,'x'=4,'yl'=2,'yh'=4,'c'=2] {'yh','yl','c'}, dimensions={0} | all-to-all | bytes 32768 | tf_op jit(solution)/shard_map/all_to_all | solution.py:574
  184.0 1.8 shard_map.134
  (46 shorter events, 0.3 us)
Async XLA Ops:
  0.0 8.7 %copy-start = (bf16[256,512]{1,0:T(8,128)(2,1)S(1)}, bf16[256,512]{1,0:T(8,128)(2,1)}, u32[]{:S(2)}) copy-start(bf16[256,512]{1,0:T(8,128)(2,1)} %tokens_ref.1) | copy-start | bytes 786436
  2.8 13.8 %all-to-all-start = ((bf16[8,72,512]{2,1,0:T(8,128)(2,1)}), bf16[8,72,512]{2,1,0:T(8,128)(2,1)S(1)}, u32[]{:S(2)}, u32[]{:S(2)}) async-start(bf16[8,72,512]{2,1,0:T(8,128)(2,1)} %bitcast.7), calls=%async_computation | async-start | bytes 1179648 | tf_op jit(solution)/shard_map/all_to_all | solution.py:503
  8.7 4.2 %collective-permute-start = (bf16[16,512]{1,0:T(8,128)(2,1)S(1)}, bf16[16,512]{1,0:T(8,128)(2,1)S(1)}, u32[]{:S(2)}, u32[]{:S(2)}) collective-permute-start(bf16[16,512]{1,0:T(8,128)(2,1)S(1)} %slice.15), channel_id=1, source_target_pairs={{0,8},{8,16},{16,24},{24,32},{32,40},{40,48},{48,56},{56,64},{64,7... | collective-permute-start | bytes 49160 | tf_op jit(solution)/shard_map/ppermute | solution.py:470
  16.5 62.5 %all-to-all-start.1 = ((bf16[8,272,512]{2,1,0:T(8,128)(2,1)}), bf16[8,272,512]{2,1,0:T(8,128)(2,1)S(1)}, u32[]{:S(2)}, u32[]{:S(2)}) async-start(bf16[8,272,512]{2,1,0:T(8,128)(2,1)} %shard_map.127), calls=%async_computation.1 | async-start | bytes 4456448 | tf_op jit(solution)/shard_map/all_to_all | solution.py:521
  24.5 26.3 %copy-start.19 = (s32[8]{0:T(128)S(1)}, s32[8]{0:T(128)}, u32[]{:S(2)}) copy-start(s32[8]{0:T(128)} %constant.70.clone) | copy-start | bytes 100
  24.5 34.2 %copy-start.16 = (f32[16]{0:T(128)S(1)}, f32[16]{0:T(128)}, u32[]{:S(2)}) copy-start(f32[16]{0:T(128)} %param.21) | copy-start | bytes 196
  24.5 34.9 %copy-start.17 = (f32[16]{0:T(128)S(1)}, f32[16]{0:T(128)}, u32[]{:S(2)}) copy-start(f32[16]{0:T(128)} %param.19) | copy-start | bytes 196
  24.5 35.0 %copy-start.18 = (f32[16]{0:T(128)S(1)}, f32[16]{0:T(128)}, u32[]{:S(2)}) copy-start(f32[16]{0:T(128)} %param.20) | copy-start | bytes 196
  24.5 36.4 %copy-start.14 = (f32[1024]{0:T(1024)S(1)}, f32[1024]{0:T(1024)}, u32[]{:S(2)}) copy-start(f32[1024]{0:T(1024)} %param.24) | copy-start | bytes 12292
  24.5 36.4 %copy-start.15 = (f32[1024]{0:T(1024)S(1)}, f32[1024]{0:T(1024)}, u32[]{:S(2)}) copy-start(f32[1024]{0:T(1024)} %param.22) | copy-start | bytes 12292
  24.9 63.5 %copy-start.11 = (bf16[536,512]{1,0:T(8,128)(2,1)}, bf16[536,512]{1,0:T(8,128)(2,1)S(1)}, u32[]{:S(2)}) copy-start(bf16[536,512]{1,0:T(8,128)(2,1)S(1)} %pad_maximum_fusion.w0) | copy-start | bytes 1646596
  24.9 25.9 %collective-permute-start.2 = (bf16[536,512]{1,0:T(8,128)(2,1)S(1)}, bf16[536,512]{1,0:T(8,128)(2,1)S(1)}, u32[]{:S(2)}, u32[]{:S(2)}) collective-permute-start(bf16[536,512]{1,0:T(8,128)(2,1)S(1)} %pad_maximum_fusion.w0), channel_id=1, source_target_pairs={{0,448},{64,0},{128,64},{192,128},{256,192},{320,256},{384,320},{4... | collective-permute-start | bytes 1646600 | tf_op jit(solution)/shard_map/ppermute | solution.py:442
  37.2 15.0 %collective-permute-start.1 = (bf16[536,512]{1,0:T(8,128)(2,1)S(1)}, bf16[536,512]{1,0:T(8,128)(2,1)}, u32[]{:S(2)}, u32[]{:S(2)}) collective-permute-start(bf16[536,512]{1,0:T(8,128)(2,1)S(1)} %pad_maximum_fusion.w0), channel_id=1, source_target_pairs={{0,64},{64,128},{128,192},{192,256},{256,320},{320,384},{384,448},... | collective-permute-start | bytes 1646600 | tf_op jit(solution)/shard_map/ppermute | solution.py:441
  39.1 11.7 %collective-permute-start.3 = (bf16[24,512]{1,0:T(8,128)(2,1)S(1)}, bf16[24,512]{1,0:T(8,128)(2,1)S(1)}, u32[]{:S(2)}, u32[]{:S(2)}) collective-permute-start(bf16[24,512]{1,0:T(8,128)(2,1)S(1)} %reshape.57), channel_id=1, source_target_pairs={{0,256},{64,320},{128,384},{192,448},{256,0},{320,64},{384,128},{4... | collective-permute-start | bytes 73736 | tf_op jit(solution)/shard_map/ppermute | solution.py:444
  50.8 46.2 %copy-start.13 = (bf16[24,512]{1,0:T(8,128)(2,1)}, bf16[24,512]{1,0:T(8,128)(2,1)S(1)}, u32[]{:S(2)}) copy-start(bf16[24,512]{1,0:T(8,128)(2,1)S(1)} %collective-permute-done.3.w7) | copy-start | bytes 73732
  50.8 44.2 %copy-start.12 = (bf16[536,512]{1,0:T(8,128)(2,1)}, bf16[536,512]{1,0:T(8,128)(2,1)S(1)}, u32[]{:S(2)}) copy-start(bf16[536,512]{1,0:T(8,128)(2,1)S(1)} %collective-permute-done.2.w2) | copy-start | bytes 1646596
  52.1 13.2 %collective-permute-start.4 = (bf16[536,512]{1,0:T(8,128)(2,1)}, bf16[536,512]{1,0:T(8,128)(2,1)}, u32[]{:S(2)}, u32[]{:S(2)}) collective-permute-start(bf16[536,512]{1,0:T(8,128)(2,1)} %collective-permute-done.1.w1), channel_id=1, source_target_pairs={{0,64},{64,128},{128,192},{192,256},{256,320},{320,384},{384,448},... | collective-permute-start | bytes 1646600 | tf_op jit(solution)/shard_map/ppermute | solution.py:441
  54.1 11.9 %collective-permute-start.5 = (bf16[536,512]{1,0:T(8,128)(2,1)S(1)}, bf16[536,512]{1,0:T(8,128)(2,1)}, u32[]{:S(2)}, u32[]{:S(2)}) collective-permute-start(bf16[536,512]{1,0:T(8,128)(2,1)S(1)} %collective-permute-done.2.w2), channel_id=1, source_target_pairs={{0,448},{64,0},{128,64},{192,128},{256,192},{320,256},{384,320},{4... | collective-permute-start | bytes 1646600 | tf_op jit(solution)/shard_map/ppermute | solution.py:442
  65.9 13.1 %collective-permute-start.6 = (bf16[536,512]{1,0:T(8,128)(2,1)}, bf16[536,512]{1,0:T(8,128)(2,1)}, u32[]{:S(2)}, u32[]{:S(2)}) collective-permute-start(bf16[536,512]{1,0:T(8,128)(2,1)} %collective-permute-done.4.w3), channel_id=1, source_target_pairs={{0,64},{64,128},{128,192},{192,256},{256,320},{320,384},{384,448},... | collective-permute-start | bytes 1646600 | tf_op jit(solution)/shard_map/ppermute | solution.py:441
  79.1 1.4 copy-start.10
  80.5 26.7 %collective-permute-start.7 = (bf16[4,2,272,512]{3,2,1,0:T(8,128)(2,1)S(1)}, bf16[4,2,272,512]{3,2,1,0:T(8,128)(2,1)}, u32[]{:S(2)}, u32[]{:S(2)}) collective-permute-start(bf16[4,2,272,512]{3,2,1,0:T(8,128)(2,1)S(1)} %bitcast.32), channel_id=1, source_target_pairs={{0,1},{1,0},{2,3},{3,2},{4,5},{5,4},{6,7},{7,6},{8,9},{9,8},{10,11... | collective-permute-start | bytes 6684680 | tf_op jit(solution)/shard_map/ppermute | solution.py:525
  88.4 18.8 %collective-permute-start.8 = (bf16[536,512]{1,0:T(8,128)(2,1)}, bf16[536,512]{1,0:T(8,128)(2,1)}, u32[]{:S(2)}, u32[]{:S(2)}) collective-permute-start(bf16[536,512]{1,0:T(8,128)(2,1)} %collective-permute-done.5.w4), channel_id=1, source_target_pairs={{0,448},{64,0},{128,64},{192,128},{256,192},{320,256},{384,320},{4... | collective-permute-start | bytes 1646600 | tf_op jit(solution)/shard_map/ppermute | solution.py:442
  95.0 22.4 %collective-permute-start.9 = (bf16[536,512]{1,0:T(8,128)(2,1)}, bf16[536,512]{1,0:T(8,128)(2,1)}, u32[]{:S(2)}, u32[]{:S(2)}) collective-permute-start(bf16[536,512]{1,0:T(8,128)(2,1)} %collective-permute-done.6.w5), channel_id=1, source_target_pairs={{0,64},{64,128},{128,192},{192,256},{256,320},{320,384},{384,448},... | collective-permute-start | bytes 1646600 | tf_op jit(solution)/shard_map/ppermute | solution.py:450
  112.5 16.5 %all-to-all-start.2 = ((bf16[16,16,544]{2,1,0:T(8,128)(2,1)}), bf16[16,16,544]{2,1,0:T(8,128)(2,1)}, u32[]{:S(2)}, u32[]{:S(2)}) async-start(bf16[16,16,544]{2,1,0:T(8,128)(2,1)} %get-tuple-element.59), calls=%async_computation.2 | async-start | bytes 655360 | tf_op jit(solution)/shard_map/all_to_all | solution.py:532
  148.4 0.7 copy-start.5
  149.1 14.3 %copy-start.2 = (f32[8,1024]{1,0:T(8,128)S(1)}, f32[8,1024]{1,0:T(8,128)}, u32[]{:S(2)}) copy-start(f32[8,1024]{1,0:T(8,128)} %maximum_maximum_fusion.1.chan_ref) | copy-start | bytes 98308
  149.1 14.3 %copy-start.4 = (bf16[512,256]{1,0:T(8,128)(2,1)S(1)}, bf16[512,256]{1,0:T(8,128)(2,1)}, u32[]{:S(2)}) copy-start(bf16[512,256]{1,0:T(8,128)(2,1)} %get-tuple-element.64.bc_ref) | copy-start | bytes 786436
  149.8 13.5 %all-to-all-start.4 = ((bf16[32,16,128]{2,1,0:T(8,128)(2,1)}), bf16[32,16,128]{2,1,0:T(8,128)(2,1)S(1)}, u32[]{:S(2)}, u32[]{:S(2)}) async-start(bf16[32,16,128]{2,1,0:T(8,128)(2,1)} %shard_map.132), calls=%async_computation.4 | async-start | bytes 262144 | tf_op jit(solution)/shard_map/all_to_all | solution.py:553
  154.0 0.8 copy-start.1
  154.8 0.9 copy-start.3
  155.7 0.7 copy-start.6
  156.4 1.2 copy-start.7
  157.6 1.0 copy-start.8
  158.7 0.7 copy-start.9
  166.6 17.4 %collective-permute-start.10 = (bf16[256,512]{1,0:T(8,128)(2,1)S(1)}, bf16[256,512]{1,0:T(8,128)(2,1)S(1)}, u32[]{:S(2)}, u32[]{:S(2)}) collective-permute-start(bf16[256,512]{1,0:T(8,128)(2,1)S(1)} %get-tuple-element.73), channel_id=1, source_target_pairs={{0,8},{8,0},{1,9},{9,1},{2,10},{10,2},{3,11},{11,3},{4,12},{12,4},... | collective-permute-start | bytes 786440 | tf_op jit(solution)/shard_map/ppermute | solution.py:578
